TPU v7x, 32 devices: a whole 2x2x4 slice. The times are simulated.
32 devices in a mesh: dp: 4 (over y, core), tensor: 8 (over z, x).
Axes of the slice: x: 2, y: 2, z: 4, core: 2. Of those that a mesh axis runs over, the one named last changes fastest.
Arguments:
- inputs: bfloat16 [8192, 1024], P(('dp', 'tensor')), may hold values from -6 to 6
- qkv_weight: bfloat16 [1024, 3072], P(None, 'tensor'), may hold values from -0.1875 to 0.1875
- qkv_bias: bfloat16 [3072], P('tensor'), may hold values from -3 to 3
- dense_weight: bfloat16 [1024, 1024], P('tensor'), may hold values from -1 to 1
- up_weight: bfloat16 [1024, 4096], P(None, 'tensor'), may hold values from -0.1875 to 0.1875
- up_bias: bfloat16 [4096], P('tensor'), may hold values from -3 to 3
- down_weight: bfloat16 [4096, 1024], P('tensor'), may hold values from -0.09375 to 0.09375
- out_bias: bfloat16 [1024], replicated, may hold values from -3 to 3
- gain_one: bfloat16 [1024], replicated, may hold values from 0.099609375 to 1.8984375
- shift_one: bfloat16 [1024], replicated, may hold values from -2 to 2
- gain_two: bfloat16 [1024], replicated, may hold values from 0.099609375 to 1.8984375
- shift_two: bfloat16 [1024], replicated, may hold values from -2 to 2
- feature_omega: float32 [64, 64], replicated, may hold values from -0.75 to 0.75
- doc_ids: int32 [4, 2048], P('dp'), may hold values from 0 to 7, never falling along the last dimension, each value on 1 to 1024 neighbouring positions
- out_grad: bfloat16 [8192, 1024], P(('dp', 'tensor')), may hold values from -6 to 6
Outputs:
- layer_out: bfloat16 [8192, 1024], P(('dp', 'tensor'))
- input_grad: float32 [8192, 1024], P(('dp', 'tensor'))
- qkv_weight_grad: float32 [1024, 3072], P(None, 'tensor')
- qkv_bias_grad: float32 [3072], P('tensor')
- dense_weight_grad: float32 [1024, 1024], P('tensor')
- up_weight_grad: float32 [1024, 4096], P(None, 'tensor')
- up_bias_grad: float32 [4096], P('tensor')
- down_weight_grad: float32 [4096, 1024], P('tensor')
- out_bias_grad: float32 [1024], P('tensor')
- gain_one_grad: float32 [1024], P('tensor')
- shift_one_grad: float32 [1024], P('tensor')
- gain_two_grad: float32 [1024], P('tensor')
- shift_two_grad: float32 [1024], P('tensor')
Inputs may be any that keep to these rules, and one draw needn't show every extreme that they name: `doc_ids`: in each packed row the document numbers never fall; a document holds at most 1024 tokens and some document holds exactly that many.
All inputs are finite; a program needn't handle non-finite values.
Results may differ from a plain program's by a relative error of at most 0.0072.
Values may be sent and summed in bfloat16 or wider, within the bound.
No kernel may reach another device: no remote copies, remote signals or barrier semaphores. Data moves between devices by JAX's collectives and lax.ppermute only.
A program may use at most 192 MiB of HBM per device.

v0:
```python
import jax
import jax.numpy as jnp
from jax import lax
from jax.sharding import PartitionSpec as P

HEAD_DIM = 64
ROT = 16
LEN = 2048


EPS = 1e-05
EXACT = lax.Precision.HIGHEST


def layer_norm(values, gain_row, offset):
    row_mean = jnp.mean(values, axis=-1, keepdims=True)
    centred = values - row_mean
    spread = jnp.mean(centred * centred, axis=-1, keepdims=True)
    return centred * lax.rsqrt(spread + EPS) * gain_row + offset


def both_norms(token_rows, first_gain, first_offset, second_gain, second_offset):
    return (
        layer_norm(token_rows, first_gain, first_offset),
        layer_norm(token_rows, second_gain, second_offset),
    )


def exact_gelu(values):
    return jax.nn.gelu(values, approximate=False)


def dct_matrix(extent):
    indices = jnp.arange(extent, dtype=jnp.float32)
    cosines = jnp.cos(jnp.pi * (indices[:, None] + 0.5) * indices[None, :] / extent)
    scales = jnp.where(indices == 0, jnp.sqrt(1.0 / extent), jnp.sqrt(2.0 / extent))
    return cosines * scales[None, :]


def rotary_tables(positions, turned):
    half_rot = turned // 2
    frequencies = 10000.0 ** (-(jnp.arange(half_rot, dtype=jnp.float32) * 2.0 / turned))
    angles = positions.astype(jnp.float32)[:, None] * frequencies[None, :]
    return (jnp.cos(angles), jnp.sin(angles))


def rotate(values, cosine_table, sine_table):
    half_rot = cosine_table.shape[-1]
    leading = values[..., :half_rot]
    trailing = values[..., half_rot : 2 * half_rot]
    return jnp.concatenate(
        [
            leading * cosine_table - trailing * sine_table,
            trailing * cosine_table + leading * sine_table,
            values[..., 2 * half_rot :],
        ],
        axis=-1,
    )


def feature_map(values, cosine_table, sine_table, mixing):
    return jnp.exp(jnp.dot(rotate(values, cosine_table, sine_table), mixing, precision=EXACT))


def to_blocks(values, sequences, block_rows):
    shaped = values.reshape(
        (sequences, values.shape[0] // (sequences * block_rows), block_rows) + values.shape[1:]
    )
    return jnp.swapaxes(shaped, 0, 1)


def from_blocks(values):
    joined = jnp.swapaxes(values, 0, 1)
    return joined.reshape((-1,) + joined.shape[3:])


def allowed_pairs(doc_block):
    block_width = doc_block.shape[-1]
    places = jnp.arange(block_width)
    causal = places[:, None] >= places[None, :]
    return (doc_block[:, :, None] == doc_block[:, None, :]) & causal[None]


def attend_forward(query_blocks, key_blocks, value_blocks, doc_blocks, before_docs):
    sequences = query_blocks.shape[1]
    features = query_blocks.shape[-1]
    initial = (
        jnp.zeros((sequences, features, value_blocks.shape[-1]), jnp.float32),
        jnp.zeros((sequences, features), jnp.float32),
    )

    def advance(running, pieces):
        memory, totals = running
        query_rows, key_rows, value_rows, doc_block, before_doc = pieces
        query_wide = query_rows.astype(jnp.float32)
        value_wide = value_rows.astype(jnp.float32)
        weights = jnp.where(
            allowed_pairs(doc_block),
            jnp.einsum("sbf,scf->sbc", query_rows, key_rows, preferred_element_type=jnp.float32),
            0.0,
        )
        carried = (doc_block == before_doc[:, None]).astype(jnp.float32)[:, :, None]
        numerator = jnp.einsum(
            "sbc,sce->sbe", weights, value_wide, precision=EXACT
        ) + carried * jnp.einsum("sbf,sfe->sbe", query_wide, memory, precision=EXACT)
        denominator = (
            jnp.sum(weights, axis=-1, keepdims=True)
            + carried * jnp.einsum("sbf,sf->sb", query_wide, totals, precision=EXACT)[:, :, None]
        )
        last_doc = doc_block[:, -1]
        retained = (last_doc == before_doc).astype(jnp.float32)
        chosen = key_rows * (doc_block == last_doc[:, None]).astype(jnp.bfloat16)[:, :, None]
        new_memory = retained[:, None, None] * memory + jnp.einsum(
            "sbf,sbe->sfe", chosen, value_rows, preferred_element_type=jnp.float32
        )
        new_totals = retained[:, None] * totals + jnp.sum(chosen.astype(jnp.float32), axis=1)
        return ((new_memory, new_totals), (numerator / denominator, denominator, memory, totals))

    final_running, stored = lax.scan(
        advance, initial, (query_blocks, key_blocks, value_blocks, doc_blocks, before_docs)
    )
    return stored


def attend_backward(
    query_blocks,
    key_blocks,
    value_blocks,
    doc_blocks,
    before_docs,
    after_docs,
    stored,
    result_grads,
):
    result_blocks, denominators, memories, totals_before = stored
    sequences = query_blocks.shape[1]
    features = query_blocks.shape[-1]
    initial = (
        jnp.zeros((sequences, features, value_blocks.shape[-1]), jnp.float32),
        jnp.zeros((sequences, features), jnp.float32),
    )

    def retreat(running, pieces):
        later, later_totals = running
        (
            query_rows,
            key_rows,
            value_rows,
            doc_block,
            before_doc,
            after_doc,
            result_rows,
            denominator,
            memory,
            totals,
            result_grad,
        ) = pieces
        query_wide = query_rows.astype(jnp.float32)
        key_wide = key_rows.astype(jnp.float32)
        value_wide = value_rows.astype(jnp.float32)
        allowed = allowed_pairs(doc_block)
        weights = jnp.where(
            allowed,
            jnp.einsum("sbf,scf->sbc", query_rows, key_rows, preferred_element_type=jnp.float32),
            0.0,
        )
        numerator_grad = result_grad / denominator
        denominator_grad = -jnp.sum(result_grad * result_rows, axis=-1, keepdims=True) / denominator
        weight_grad = jnp.where(
            allowed,
            jnp.einsum("sbe,sce->sbc", numerator_grad, value_wide, precision=EXACT)
            + denominator_grad,
            0.0,
        )
        carried = (doc_block == before_doc[:, None]).astype(jnp.float32)[:, :, None]
        query_grad = jnp.einsum(
            "sbc,scf->sbf", weight_grad, key_wide, precision=EXACT
        ) + carried * (
            jnp.einsum("sbe,sfe->sbf", numerator_grad, memory, precision=EXACT)
            + denominator_grad * totals[:, None, :]
        )
        linked = (doc_block == after_doc[:, None]).astype(jnp.float32)[:, :, None]
        key_grad = jnp.einsum("sbc,sbf->scf", weight_grad, query_wide, precision=EXACT) + linked * (
            jnp.einsum("sbe,sfe->sbf", value_wide, later, precision=EXACT)
            + later_totals[:, None, :]
        )
        value_grad = jnp.einsum(
            "sbc,sbe->sce", weights, numerator_grad, precision=EXACT
        ) + linked * jnp.einsum("sbf,sfe->sbe", key_wide, later, precision=EXACT)
        first_doc = doc_block[:, 0]
        retained = (first_doc == after_doc).astype(jnp.float32)
        chosen = query_wide * (doc_block == first_doc[:, None]).astype(jnp.float32)[:, :, None]
        new_later = retained[:, None, None] * later + jnp.einsum(
            "sbf,sbe->sfe", chosen, numerator_grad, precision=EXACT
        )
        new_totals = retained[:, None] * later_totals + jnp.sum(chosen * denominator_grad, axis=1)
        return ((new_later, new_totals), (query_grad, key_grad, value_grad))

    final_running, grads = lax.scan(
        retreat,
        initial,
        (
            query_blocks,
            key_blocks,
            value_blocks,
            doc_blocks,
            before_docs,
            after_docs,
            result_blocks,
            denominators,
            memories,
            totals_before,
            result_grads,
        ),
        reverse=True,
    )
    return grads


def on_device(
    inputs,
    qkv_weight,
    qkv_bias,
    dense_weight,
    up_weight,
    up_bias,
    down_weight,
    out_bias,
    gain_one,
    shift_one,
    gain_two,
    shift_two,
    feature_omega,
    doc_ids,
    out_grad,
):
    local_rows = inputs.astype(jnp.float32)
    model_width = local_rows.shape[1]
    first_gain = gain_one.astype(jnp.float32)
    second_gain = gain_two.astype(jnp.float32)
    norm_values, norm_pull = jax.vjp(
        both_norms,
        local_rows,
        first_gain,
        shift_one.astype(jnp.float32),
        second_gain,
        shift_two.astype(jnp.float32),
    )
    whole_one, whole_two = (
        lax.all_gather(norm_values[0].astype(jnp.bfloat16), "tensor", axis=0, tiled=True),
        lax.all_gather(norm_values[1].astype(jnp.bfloat16), "tensor", axis=0, tiled=True),
    )
    group_rows = whole_one.shape[0]
    sequences = doc_ids.shape[0]
    block_rows = min(512, LEN // 4)
    projected = jnp.dot(
        whole_one, qkv_weight, preferred_element_type=jnp.float32
    ) + qkv_bias.astype(jnp.float32)
    hidden = jnp.dot(whole_two, up_weight, preferred_element_type=jnp.float32) + up_bias.astype(
        jnp.float32
    )
    activated_exact, gelu_pull = jax.vjp(exact_gelu, hidden)
    activated = activated_exact.astype(jnp.bfloat16)
    cosine_table, sine_table = rotary_tables(jnp.arange(group_rows) % LEN, ROT)
    mixing = jnp.dot(dct_matrix(HEAD_DIM), feature_omega, precision=EXACT)
    doc_blocks = to_blocks(doc_ids.reshape(group_rows), sequences, block_rows)
    before_docs = jnp.concatenate(
        [jnp.full((1, sequences), -1, jnp.int32), doc_blocks[:-1, :, -1]], axis=0
    )
    after_docs = jnp.concatenate(
        [doc_blocks[1:, :, 0], jnp.full((1, sequences), -1, jnp.int32)], axis=0
    )

    def features_of(token_rows):
        return feature_map(token_rows, cosine_table, sine_table, mixing)

    local_heads = qkv_weight.shape[1] // (3 * HEAD_DIM)
    head_saved = []
    head_results = []
    for head_index in range(local_heads):
        column_base = head_index * 3 * HEAD_DIM
        query_exact, query_pull = jax.vjp(
            features_of, projected[:, column_base : column_base + HEAD_DIM]
        )
        key_exact, key_pull = jax.vjp(
            features_of, projected[:, column_base + HEAD_DIM : column_base + 2 * HEAD_DIM]
        )
        value_rows = projected[:, column_base + 2 * HEAD_DIM : column_base + 3 * HEAD_DIM].astype(
            jnp.bfloat16
        )
        blocks = (
            to_blocks(query_exact.astype(jnp.bfloat16), sequences, block_rows),
            to_blocks(key_exact.astype(jnp.bfloat16), sequences, block_rows),
            to_blocks(value_rows, sequences, block_rows),
        )
        stored = attend_forward(blocks[0], blocks[1], blocks[2], doc_blocks, before_docs)
        head_results.append(from_blocks(stored[0]))
        head_saved.append((blocks, stored, query_pull, key_pull))
    merged = jnp.concatenate(head_results, axis=1).astype(jnp.bfloat16)
    branch_total = lax.psum_scatter(
        jnp.dot(merged, dense_weight, preferred_element_type=jnp.float32),
        "tensor",
        scatter_dimension=0,
        tiled=True,
    ) + lax.psum_scatter(
        jnp.dot(activated, down_weight, preferred_element_type=jnp.float32).astype(jnp.bfloat16),
        "tensor",
        scatter_dimension=0,
        tiled=True,
    ).astype(
        jnp.float32
    )
    layer_out = (local_rows + branch_total + out_bias.astype(jnp.float32)).astype(jnp.bfloat16)
    grad_whole = lax.all_gather(out_grad, "tensor", axis=0, tiled=True)
    merged_grad = jnp.einsum(
        "td,ed->te", grad_whole, dense_weight, preferred_element_type=jnp.float32
    )
    dense_weight_grad = jnp.einsum(
        "te,td->ed", merged, grad_whole, preferred_element_type=jnp.float32
    )
    down_weight_grad = jnp.einsum(
        "tf,td->fd", activated, grad_whole, preferred_element_type=jnp.float32
    )
    activated_grad = jnp.einsum(
        "td,fd->tf", grad_whole, down_weight, preferred_element_type=jnp.float32
    )
    hidden_grad = gelu_pull(activated_grad)[0].astype(jnp.bfloat16)
    up_weight_grad = jnp.einsum(
        "td,tf->df", whole_two, hidden_grad, preferred_element_type=jnp.float32
    )
    up_bias_grad = jnp.sum(hidden_grad, axis=0, dtype=jnp.float32)
    column_grads = []
    for head_index in range(local_heads):
        blocks, stored, query_pull, key_pull = head_saved[head_index]
        result_grads = to_blocks(
            merged_grad[:, head_index * HEAD_DIM : (head_index + 1) * HEAD_DIM],
            sequences,
            block_rows,
        )
        query_grad, key_grad, value_grad = attend_backward(
            blocks[0],
            blocks[1],
            blocks[2],
            doc_blocks,
            before_docs,
            after_docs,
            stored,
            result_grads,
        )
        column_grads.extend(
            [
                query_pull(from_blocks(query_grad))[0],
                key_pull(from_blocks(key_grad))[0],
                from_blocks(value_grad),
            ]
        )
    qkv_grad = jnp.concatenate(column_grads, axis=1).astype(jnp.bfloat16)
    qkv_weight_grad = jnp.einsum(
        "td,tc->dc", whole_one, qkv_grad, preferred_element_type=jnp.float32
    )
    qkv_bias_grad = jnp.sum(qkv_grad, axis=0, dtype=jnp.float32)
    local_grad = out_grad.astype(jnp.float32)
    norm_grads = lax.psum_scatter(
        jnp.concatenate(
            [
                jnp.einsum("tc,dc->td", qkv_grad, qkv_weight, preferred_element_type=jnp.float32),
                jnp.einsum("tf,df->td", hidden_grad, up_weight, preferred_element_type=jnp.float32),
            ],
            axis=1,
        ),
        "tensor",
        scatter_dimension=0,
        tiled=True,
    )
    row_part, first_gain_grad, first_shift_grad, second_gain_grad, second_shift_grad = norm_pull(
        (norm_grads[:, :model_width], norm_grads[:, model_width:])
    )
    input_grad = local_grad + row_part
    vector_part = lax.psum_scatter(
        jnp.stack(
            [
                first_gain_grad,
                first_shift_grad,
                second_gain_grad,
                second_shift_grad,
                jnp.sum(local_grad, axis=0),
            ]
        ),
        "tensor",
        scatter_dimension=1,
        tiled=True,
    )
    summed = lax.psum(
        (
            qkv_weight_grad,
            qkv_bias_grad,
            dense_weight_grad,
            up_weight_grad,
            up_bias_grad,
            down_weight_grad,
            vector_part,
        ),
        "dp",
    )
    vectors = summed[6]
    return (
        layer_out,
        input_grad,
        summed[0],
        summed[1],
        summed[2],
        summed[3],
        summed[4],
        summed[5],
        vectors[4],
        vectors[0],
        vectors[1],
        vectors[2],
        vectors[3],
    )


def solution(mesh):
    in_specs = (
        P(("dp", "tensor"), None),
        P(None, "tensor"),
        P("tensor"),
        P("tensor", None),
        P(None, "tensor"),
        P("tensor"),
        P("tensor", None),
        P(),
        P(),
        P(),
        P(),
        P(),
        P(),
        P("dp", None),
        P(("dp", "tensor"), None),
    )
    out_specs = (
        P(("dp", "tensor"), None),
        P(("dp", "tensor"), None),
        P(None, "tensor"),
        P("tensor"),
        P("tensor", None),
        P(None, "tensor"),
        P("tensor"),
        P("tensor", None),
        P("tensor"),
        P("tensor"),
        P("tensor"),
        P("tensor"),
        P("tensor"),
    )
    return jax.shard_map(
        on_device, mesh=mesh, in_specs=in_specs, out_specs=out_specs, check_vma=False
    )
```

profile of v0, /device:TPU:0, one launch (start us, length us, event | category | flops | bytes accessed | tf_op | source)
XLA Modules:
  0.0 1256.4 jit_solution(18088975919537195365)
XLA Ops:
  22.2 64.1 %all-gather.8.cloned.1.call-done = bf16[2048,1024]{1,0:T(8,128)(2,1)} async-done(((bf16[256,1024]{1,0:T(8,128)(2,1)}), bf16[2048,1024]{1,0:T(8,128)(2,1)}) %all-gather.8.cloned.1.call-update) | async-done | bytes 4194320 | tf_op jit(solution)/shard_map/all_gather | solution.py:314
  86.4 3.7 fusion.330
  91.8 68.9 %all-gather.4.cloned.1.call-done = bf16[2048,1024]{1,0:T(8,128)(2,1)} async-done(((bf16[256,1024]{1,0:T(8,128)(2,1)}), bf16[2048,1024]{1,0:T(8,128)(2,1)}) %all-gather.4.cloned.1.call-update) | async-done | bytes 4194320 | tf_op jit(solution)/shard_map/all_gather | solution.py:250
  160.7 5.7 fusion.325
  179.6 37.0 %while.89 = (s32[]{:T(128)}, f32[1,64,64]{2,1,0:T(8,128)S(1)}, f32[1,64]{1,0:T(1,128)S(1)}, f32[4,1,512,64]{2,3,1,0:T(8,128)}, f32[4,1,512,1]{2,3,1,0:T(1,128)},...) while((s32[]{:T(128)}, f32[1,64,64]{2,1,0:T(8,128)S(1)}, ...), condition=%wide.region_9.10_spmd.clone, body=%wide.region_6.9_spmd.clone.sunk | while | flops 266197760 | bytes 3668453 | solution.py:119
  218.4 125.6 %while.91 = (s32[]{:T(128)}, f32[1,64,64]{2,1,0:T(8,128)}, f32[1,64]{1,0:T(1,128)}, f32[4,1,512,64]{2,0,3,1:T(4,128)}, f32[4,1,512,64]{2,0,3,1:T(4,128)}, /*inde...) while((s32[]{:T(128)}, f32[1,64,64]{2,1,0:T(8,128)}, ...), condition=%wide.region_19.20_spmd.clone, body=%wide.region_16.19_spmd.clone.sunk | while | flops 942595712 | bytes 11318790 | solution.py:199
  236.6 3.6 dynamic_update_slice.133
  240.3 3.6 dynamic_update_slice.132
  268.2 3.6 dynamic_update_slice.133
  271.8 3.6 dynamic_update_slice.132
  299.8 3.6 dynamic_update_slice.133
  303.4 3.6 dynamic_update_slice.132
  331.3 3.6 dynamic_update_slice.133
  335.0 3.6 dynamic_update_slice.132
  350.4 35.3 %while.88 = (s32[]{:T(128)}, f32[1,64,64]{2,1,0:T(8,128)S(1)}, f32[1,64]{1,0:T(1,128)S(1)}, f32[4,1,512,64]{2,3,1,0:T(8,128)}, f32[4,1,512,1]{2,3,1,0:T(1,128)S(...) while((s32[]{:T(128)}, f32[1,64,64]{2,1,0:T(8,128)S(1)}, ...), condition=%wide.region_5.6_spmd.clone, body=%wide.region_2.5_spmd.clone.sunk | while | flops 266197760 | bytes 3668709 | solution.py:119
  387.4 108.1 %while.90 = (s32[]{:T(128)}, f32[1,64,64]{2,1,0:T(8,128)}, f32[1,64]{1,0:T(1,128)}, f32[4,1,512,64]{2,0,3,1:T(4,128)}, f32[4,1,512,64]{2,0,3,1:T(4,128)}, /*inde...) while((s32[]{:T(128)}, f32[1,64,64]{2,1,0:T(8,128)}, ...), condition=%wide.region_15.16_spmd.clone, body=%wide.region_12.15_spmd.clone.sunk | while | flops 942595712 | bytes 11392122 | solution.py:199
  392.8 2.5 compare_convert_fusion.14
  403.6 3.6 dynamic_update_slice.130
  407.2 3.6 dynamic_update_slice.129
  419.2 2.5 compare_convert_fusion.14
  430.6 3.6 dynamic_update_slice.130
  434.3 3.6 dynamic_update_slice.129
  446.3 2.5 compare_convert_fusion.14
  457.7 3.6 dynamic_update_slice.130
  461.3 3.6 dynamic_update_slice.129
  473.4 2.5 compare_convert_fusion.14
  484.8 3.6 dynamic_update_slice.130
  488.4 3.6 dynamic_update_slice.129
  504.5 5.7 fusion.331
  510.2 5.0 fusion.329
  515.3 13.5 %convert_reduce_fusion.2 = (f32[512]{0:T(512)S(1)}, bf16[2048,512]{1,0:T(8,128)(2,1)S(1)}, f32[2048,512]{1,0:T(8,128)}) fusion(f32[2048,512]{1,0:T(8,128)S(1)} %fusion.329, f32[512]{0:T(512)S(1)} %copy-done.62, bf16[2048,1024]{1,0:T(8,128)(2,1)S(1)} %copy-done.1, bf16[512,1024]{1,0:T(8,128)(2,1)S(1)} %copy-done), kind=kOutput, calls=%fused_computation.269 | convolution fusion | flops 2226126336 | bytes 15732736 | tf_op jit(solution)/shard_map/td,fd->tf/dot_general | solution.py:324
  532.6 6.3 pad_maximum_fusion
  538.9 4.6 multiply_convert_fusion
  544.9 4.3 convolution_convert_fusion
  552.8 4.6 fusion.328
  558.0 5.9 fusion.333
  563.9 3.7 fusion.335
  567.6 3.7 fusion.336
  571.3 248.1 %reduce-scatter.9.cloned.1.call-done = f32[256,2048]{1,0:T(8,128)} async-done(((f32[2048,2048]{1,0:T(8,128)}), f32[256,2048]{1,0:T(8,128)}) %reduce-scatter.9.cloned.1.call-update) | async-done | bytes 2097168 | tf_op jit(solution)/shard_map/reduce_scatter | solution.py:363
  821.7 2.6 fusion.205
  824.4 85.9 %reduce-scatter.7.cloned.1.call-done = bf16[256,1024]{1,0:T(8,128)(2,1)} async-done(((bf16[2048,1024]{1,0:T(8,128)(2,1)}), bf16[256,1024]{1,0:T(8,128)(2,1)}) %reduce-scatter.7.cloned.1.call-update) | async-done | bytes 524304 | tf_op jit(solution)/shard_map/reduce_scatter | solution.py:305
  910.3 152.3 %reduce-scatter.5.cloned.1.call-done = f32[256,1024]{1,0:T(8,128)} async-done(((f32[2048,1024]{1,0:T(8,128)}), f32[256,1024]{1,0:T(8,128)}) %reduce-scatter.5.cloned.1.call-update) | async-done | bytes 1048592 | tf_op jit(solution)/shard_map/reduce_scatter | solution.py:300
  1062.6 3.5 convert_reduce_fusion.5
  1066.8 3.9 fusion.334
  1072.4 47.0 %reduce-scatter.11.cloned.1.call-done = f32[5,128]{1,0:T(8,128)} async-done(((f32[5,1024]{1,0:T(8,128)}), f32[5,128]{1,0:T(8,128)}) %reduce-scatter.11.cloned.1.call-update) | async-done | bytes 2576 | tf_op jit(solution)/shard_map/reduce_scatter | solution.py:379
  1119.5 6.4 all-reduce.12
  1126.4 115.6 %all-reduce.16.cloned.1.call-done = (f32[1024,384]{1,0:T(8,128)}, f32[128,1024]{1,0:T(8,128)}, f32[1024,512]{1,0:T(8,128)}, f32[512,1024]{1,0:T(8,128)}) async-done(((f32[1024,384]{1,0:T(8,128)}, f32[128,1024]{1,0:T(8,128)}, f32[1024,512]{1,0:T(8,128)}, f32[512,1024]{1,0:T(8,128)}), (f32[1024,384]{1,0:T(8,128)}, f32[128,1024]{1,0:T(8,128)}, f32[1024,512]{1,0:T(8,128)}, ...) | async-done | bytes 6291472 | tf_op jit(solution)/shard_map/psum | solution.py:393
  1242.0 2.8 copy.249
  (705 shorter events, 292.0 us)
Async XLA Ops:
  7.2 508.0 %copy-start = (bf16[512,1024]{1,0:T(8,128)(2,1)S(1)}, bf16[512,1024]{1,0:T(8,128)(2,1)}, u32[]{:S(2)}) copy-start(bf16[512,1024]{1,0:T(8,128)(2,1)} %param.29) | copy-start | bytes 3145732
  7.2 14.1 %copy-start.68 = (bf16[512]{0:T(512)(128)(2,1)S(1)}, bf16[512]{0:T(512)(128)(2,1)}, u32[]{:S(2)}) copy-start(bf16[512]{0:T(512)(128)(2,1)} %param.28) | copy-start | bytes 3076
  7.2 14.6 %copy-start.69 = (bf16[384]{0:T(512)(128)(2,1)S(1)}, bf16[384]{0:T(512)(128)(2,1)}, u32[]{:S(2)}) copy-start(bf16[384]{0:T(512)(128)(2,1)} %param.25) | copy-start | bytes 2308
  7.2 14.6 %copy-start.56 = (f32[64,64]{1,0:T(8,128)S(1)}, f32[64,64]{1,0:T(8,128)}, u32[]{:S(2)}) copy-start(f32[64,64]{1,0:T(8,128)} %param.35) | copy-start | bytes 49156
  7.2 79.1 %copy-start.30 = (bf16[128,1024]{1,0:T(8,128)(2,1)S(1)}, bf16[128,1024]{1,0:T(8,128)(2,1)}, u32[]{:S(2)}) copy-start(bf16[128,1024]{1,0:T(8,128)(2,1)} %param.26) | copy-start | bytes 786436
  7.2 79.1 %all-gather.8.cloned.1.call-start = ((), (), s32[]{:S(2)}) async-start(), calls=%async_computation.8 | async-start | bytes 4718592 | tf_op jit(solution)/shard_map/all_gather | solution.py:314
  8.0 152.7 %all-gather.4.cloned.1.call-start = ((), (), s32[]{:S(2)}) async-start(), calls=%async_computation.4 | async-start | bytes 4718592 | tf_op jit(solution)/shard_map/all_gather | solution.py:250
  8.7 77.6 %copy-start.46 = (f32[1024]{0:T(1024)}, f32[1024]{0:T(1024)S(1)}, u32[]{:S(2)}) copy-start(f32[1024]{0:T(1024)S(1)} %convert_element_type.410) | copy-start | bytes 12292
  9.4 76.9 %copy-start.48 = (f32[1024]{0:T(1024)}, f32[1024]{0:T(1024)S(1)}, u32[]{:S(2)}) copy-start(f32[1024]{0:T(1024)S(1)} %convert_element_type.419) | copy-start | bytes 12292
  12.0 74.4 %copy-start.54 = (f32[256]{0:T(256)}, f32[256]{0:T(256)S(1)}, u32[]{:S(2)}) copy-start(f32[256]{0:T(256)S(1)} %broadcast_multiply_fusion) | copy-start | bytes 3076
  13.3 73.0 %copy-start.60 = (f32[256]{0:T(256)}, f32[256]{0:T(256)S(1)}, u32[]{:S(2)}) copy-start(f32[256]{0:T(256)S(1)} %fusion.206) | copy-start | bytes 3076
  13.3 73.0 %copy-start.58 = (f32[256]{0:T(256)}, f32[256]{0:T(256)S(1)}, u32[]{:S(2)}) copy-start(f32[256]{0:T(256)S(1)} %fusion.304) | copy-start | bytes 3076
  15.7 494.5 %all-gather.6.cloned.1.call-start = ((), (), s32[]{:S(2)}) async-start(), calls=%async_computation.6 | async-start | bytes 4718592 | tf_op jit(solution)/shard_map/all_gather | solution.py:251
  16.5 802.9 %reduce-scatter.9.cloned.1.call-start = ((), (), s32[]{:S(2)}) async-start(), calls=%async_computation.9 | async-start | bytes 18874368 | tf_op jit(solution)/shard_map/reduce_scatter | solution.py:363
  22.2 152.6 %copy-start.15 = (f32[64,64]{1,0:T(8,128)}, f32[64,64]{1,0:T(8,128)S(1)}, u32[]{:S(2)}) copy-start(f32[64,64]{1,0:T(8,128)S(1)} %fusion.291) | copy-start | bytes 49156
  90.1 70.7 %copy-start.33 = (bf16[1024,384]{1,0:T(8,128)(2,1)S(1)}, bf16[1024,384]{1,0:T(8,128)(2,1)}, u32[]{:S(2)}) copy-start(bf16[1024,384]{1,0:T(8,128)(2,1)} %param.24) | copy-start | bytes 2359300
  228.2 15.7 %copy-start.38 = (s32[1,1,512]{2,1,0:T(1,128)S(1)}, s32[1,1,512]{2,1,0:T(1,128)}, u32[]{:S(2)}) copy-start(s32[1,1,512]{2,1,0:T(1,128)} %copy-done.37) | copy-start | bytes 6148 | tf_op jit(solution)/shard_map/while
  233.4 12.6 %copy-start.13 = (f32[1,64,64]{2,1,0:T(8,128)S(1)}, f32[1,64,64]{2,1,0:T(8,128)}, u32[]{:S(2)}) copy-start(f32[1,64,64]{2,1,0:T(8,128)} %get-tuple-element.1812) | copy-start | bytes 49156 | tf_op jit(solution)/shard_map/while
  259.1 16.4 %copy-start.38 = (s32[1,1,512]{2,1,0:T(1,128)S(1)}, s32[1,1,512]{2,1,0:T(1,128)}, u32[]{:S(2)}) copy-start(s32[1,1,512]{2,1,0:T(1,128)} %copy-done.37) | copy-start | bytes 6148 | tf_op jit(solution)/shard_map/while
  265.0 12.6 %copy-start.13 = (f32[1,64,64]{2,1,0:T(8,128)S(1)}, f32[1,64,64]{2,1,0:T(8,128)}, u32[]{:S(2)}) copy-start(f32[1,64,64]{2,1,0:T(8,128)} %get-tuple-element.1812) | copy-start | bytes 49156 | tf_op jit(solution)/shard_map/while
  290.7 16.4 %copy-start.38 = (s32[1,1,512]{2,1,0:T(1,128)S(1)}, s32[1,1,512]{2,1,0:T(1,128)}, u32[]{:S(2)}) copy-start(s32[1,1,512]{2,1,0:T(1,128)} %copy-done.37) | copy-start | bytes 6148 | tf_op jit(solution)/shard_map/while
  296.5 12.6 %copy-start.13 = (f32[1,64,64]{2,1,0:T(8,128)S(1)}, f32[1,64,64]{2,1,0:T(8,128)}, u32[]{:S(2)}) copy-start(f32[1,64,64]{2,1,0:T(8,128)} %get-tuple-element.1812) | copy-start | bytes 49156 | tf_op jit(solution)/shard_map/while
  322.2 16.4 %copy-start.38 = (s32[1,1,512]{2,1,0:T(1,128)S(1)}, s32[1,1,512]{2,1,0:T(1,128)}, u32[]{:S(2)}) copy-start(s32[1,1,512]{2,1,0:T(1,128)} %copy-done.37) | copy-start | bytes 6148 | tf_op jit(solution)/shard_map/while
  328.1 12.6 %copy-start.13 = (f32[1,64,64]{2,1,0:T(8,128)S(1)}, f32[1,64,64]{2,1,0:T(8,128)}, u32[]{:S(2)}) copy-start(f32[1,64,64]{2,1,0:T(8,128)} %get-tuple-element.1812) | copy-start | bytes 49156 | tf_op jit(solution)/shard_map/while
  396.4 14.4 %copy-start.40 = (s32[1,1,512]{2,1,0:T(1,128)S(1)}, s32[1,1,512]{2,1,0:T(1,128)}, u32[]{:S(2)}) copy-start(s32[1,1,512]{2,1,0:T(1,128)} %copy-done.39) | copy-start | bytes 6148 | tf_op jit(solution)/shard_map/while
  402.1 12.2 copy-start.53
  422.9 15.0 %copy-start.40 = (s32[1,1,512]{2,1,0:T(1,128)S(1)}, s32[1,1,512]{2,1,0:T(1,128)}, u32[]{:S(2)}) copy-start(s32[1,1,512]{2,1,0:T(1,128)} %copy-done.39) | copy-start | bytes 6148 | tf_op jit(solution)/shard_map/while
  429.1 12.2 copy-start.53
  449.9 15.1 %copy-start.40 = (s32[1,1,512]{2,1,0:T(1,128)S(1)}, s32[1,1,512]{2,1,0:T(1,128)}, u32[]{:S(2)}) copy-start(s32[1,1,512]{2,1,0:T(1,128)} %copy-done.39) | copy-start | bytes 6148 | tf_op jit(solution)/shard_map/while
  456.2 12.3 copy-start.53
  456.2 12.2 copy-start.67
  477.0 15.1 %copy-start.40 = (s32[1,1,512]{2,1,0:T(1,128)S(1)}, s32[1,1,512]{2,1,0:T(1,128)}, u32[]{:S(2)}) copy-start(s32[1,1,512]{2,1,0:T(1,128)} %copy-done.39) | copy-start | bytes 6148 | tf_op jit(solution)/shard_map/while
  483.3 12.3 copy-start.53
  504.5 53.5 %copy-start.4 = (bf16[2048,384]{0,1:T(8,128)(2,1)}, bf16[2048,384]{0,1:T(8,128)(2,1)S(1)}, u32[]{:S(2)}) copy-start(bf16[2048,384]{0,1:T(8,128)(2,1)S(1)} %constant_dynamic-update-slice_fusion.6) | copy-start | bytes 4718596
  510.2 22.3 %slice-start = ((s8[8388608]{0:T(1024)(128)(4,1)}), s8[4194304]{0:T(1024)(128)(4,1)S(1)}, s32[]{:S(2)}) async-start(s8[8388608]{0:T(1024)(128)(4,1)} %bitcast.597), calls=%async_computation.12 | async-start | bytes 8388608
  515.3 13.6 %copy-start.9 = (f32[2048,512]{1,0:T(8,128)}, f32[2048,512]{1,0:T(8,128)S(1)}, u32[]{:S(2)}) copy-start(f32[2048,512]{1,0:T(8,128)S(1)} %fusion.329) | copy-start | bytes 12582916
  515.3 14.9 %copy-start.70 = (bf16[1024,512]{1,0:T(8,128)(2,1)S(1)}, bf16[1024,512]{1,0:T(8,128)(2,1)}, u32[]{:S(2)}) copy-start(bf16[1024,512]{1,0:T(8,128)(2,1)} %param.27) | copy-start | bytes 3145732
  515.3 17.3 %slice-start.1 = ((s8[8388608]{0:T(1024)(128)(4,1)}), s8[4194304]{0:T(1024)(128)(4,1)S(1)}, s32[]{:S(2)}) async-start(s8[8388608]{0:T(1024)(128)(4,1)} %bitcast.597), calls=%async_computation.13 | async-start | bytes 8388608
  538.9 371.4 %reduce-scatter.7.cloned.1.call-start = ((), (), s32[]{:S(2)}) async-start(), calls=%async_computation.7 | async-start | bytes 4718592 | tf_op jit(solution)/shard_map/reduce_scatter | solution.py:305
  549.2 513.4 %reduce-scatter.5.cloned.1.call-start = ((), (), s32[]{:S(2)}) async-start(), calls=%async_computation.5 | async-start | bytes 9437184 | tf_op jit(solution)/shard_map/reduce_scatter | solution.py:300
  557.4 562.1 %reduce-scatter.11.cloned.1.call-start = ((), (), s32[]{:S(2)}) async-start(), calls=%async_computation.10 | async-start | bytes 36864 | tf_op jit(solution)/shard_map/reduce_scatter | solution.py:379
  567.6 251.8 %copy-start.47 = (f32[1024]{0:T(1024)S(1)}, f32[1024]{0:T(1024)}, u32[]{:S(2)}) copy-start(f32[1024]{0:T(1024)} %copy-done.46) | copy-start | bytes 12292
  567.6 251.8 %copy-start.49 = (f32[1024]{0:T(1024)S(1)}, f32[1024]{0:T(1024)}, u32[]{:S(2)}) copy-start(f32[1024]{0:T(1024)} %copy-done.48) | copy-start | bytes 12292
  567.6 251.8 %copy-start.55 = (f32[256]{0:T(256)S(1)}, f32[256]{0:T(256)}, u32[]{:S(2)}) copy-start(f32[256]{0:T(256)} %copy-done.54) | copy-start | bytes 3076
  567.6 254.1 %copy-start.61 = (f32[256]{0:T(256)S(1)}, f32[256]{0:T(256)}, u32[]{:S(2)}) copy-start(f32[256]{0:T(256)} %copy-done.60) | copy-start | bytes 3076
  567.6 254.1 %copy-start.59 = (f32[256]{0:T(256)S(1)}, f32[256]{0:T(256)}, u32[]{:S(2)}) copy-start(f32[256]{0:T(256)} %copy-done.58) | copy-start | bytes 3076
  819.4 243.2 %copy-start.3 = (f32[256,2048]{1,0:T(8,128)S(1)}, f32[256,2048]{1,0:T(8,128)}, u32[]{:S(2)}) copy-start(f32[256,2048]{1,0:T(8,128)} %reduce-scatter.9.cloned.1.call-done) | copy-start | bytes 6291460
  1066.8 175.2 %all-reduce.16.cloned.1.call-start = ((), (), s32[]{:S(2)}) async-start(), calls=%async_computation.11 | async-start | bytes 12582912 | tf_op jit(solution)/shard_map/psum | solution.py:393
  (87 other events, 506.3 us)
Sparse Core Ops, SparseCore 0:
  10.2 76.0 all-gather.7
  89.0 71.6 all-gather.3
  163.4 71.6 all-gather.5
  539.0 280.3 reduce-scatter.8
  823.3 86.9 reduce-scatter.6
  913.8 148.7 reduce-scatter.4
  1066.9 52.4 reduce-scatter.10
  1122.8 119.1 all-reduce.15
where the time goes:
time: 1270 us; the launch traced here: 1260 us
  waiting for transfers between devices  783 us (62%)
  matrix products  180 us (14%)
  local copies, waits for them, and re-layouts  143 us (11%)
  other arithmetic  115 us (9%)
  between operations  15.3 us (1%)
  loops' own time  12.9 us (1%)
    reduce_scatter x1, waiting for transfers between devices, on_device(): lax.psum_scatter(jnp.concatenate([jnp.einsum('tc,dc->td', qkv_grad, qkv_w...  248 us
    reduce_scatter x1, waiting for transfers between devices, on_device(): lax.psum_scatter(jnp.dot(merged, dense_weight, preferred_element_type=jnp...  152 us
    psum x1, waiting for transfers between devices, on_device(): lax.psum((qkv_weight_grad, qkv_bias_grad, dense_weight_grad, up_weight_gr...  116 us
    reduce_scatter x1, waiting for transfers between devices, on_device(): lax.psum_scatter(jnp.dot(activated, down_weight, preferred_element_type=j...  85.9 us
    all_gather x1, waiting for transfers between devices, on_device(): lax.all_gather(norm_values[0].astype(jnp.bfloat16), 'tensor', axis=0, til...  68.9 us
    all_gather x1, waiting for transfers between devices, on_device(): grad_whole = lax.all_gather(out_grad, 'tensor', axis=0, tiled=True)  64.1 us
    dynamic_update_slice x40, local copies, waits for them, and re-layouts, attend_forward(): lax.scan(advance, initial, (query_blocks, key_blocks, value_blocks, doc_b...  62.8 us
    reduce_scatter x1, waiting for transfers between devices, on_device(): lax.psum_scatter(jnp.stack([first_gain_grad, first_shift_grad, second_gai...  47 us
  transfers between devices with their start and end apart: 8, of which 7 were waited for; matrix products, arithmetic and copies ran while one was open for 31% of the time, Pallas kernels for 0%

commit v1 on v0

v1 whole, which is shorter than its diff:
```python
import functools

import jax
import jax.numpy as jnp
import numpy as np
from jax import lax
from jax.experimental import pallas as pl
from jax.experimental.pallas import tpu as pltpu
from jax.sharding import PartitionSpec as P

HEAD_DIM = 64
ROT = 16
LANES = 128
EPS = 1e-05
EXACT = lax.Precision.HIGHEST
F32 = jnp.float32
BF16 = jnp.bfloat16
AXES = ("dp", "tensor")
VMEM_LIMIT = 16 * 1024 * 1024
QUARTERS = 4

NN = ((1,), (0,))
NT = ((1,), (1,))
TN = ((0,), (0,))


def dot(a, b, dims=NN, precision=None):
    return lax.dot_general(a, b, (dims, ((), ())), precision=precision, preferred_element_type=F32)


def halves(values):
    high = values.astype(BF16)
    return high, (values - high.astype(F32)).astype(BF16)


def lane_of(dims):
    return lax.broadcasted_iota(jnp.int32, dims, len(dims) - 1)


def prepare_kernel(table, rates, omega, keep, ahead, behind, mix_high, mix_low, turned_high, turned_low):
    rows = keep.shape[0]
    start = (table[1] * pl.num_programs(0) + pl.program_id(0)) * rows
    places = start + lax.broadcasted_iota(jnp.int32, (rows, LANES), 0)
    angles = places.astype(F32) * rates[...]
    inner = lane_of((rows, LANES)) % HEAD_DIM
    cosine, sine = jnp.cos(angles), jnp.sin(angles)
    half = ROT // 2
    keep[...] = jnp.where(inner < ROT, cosine, 1.0)
    ahead[...] = jnp.where(inner < half, -sine, 0.0)
    behind[...] = jnp.where((inner >= half) & (inner < ROT), sine, 0.0)

    @pl.when(pl.program_id(0) == 0)
    def _():
        extent = HEAD_DIM
        n = lax.broadcasted_iota(jnp.int32, (LANES, LANES), 0)
        k = lax.broadcasted_iota(jnp.int32, (LANES, LANES), 1)
        same = (n // extent) == (k // extent)
        n, k = (n % extent).astype(F32), (k % extent).astype(F32)
        scale = jnp.where(k == 0, float(np.sqrt(1.0 / extent)), float(np.sqrt(2.0 / extent)))
        matrix = jnp.where(same, jnp.cos(np.pi * (n + 0.5) * k / extent) * scale, 0.0)
        row = jnp.concatenate([omega[...]] * 2, axis=1)
        spread = jnp.where(same, jnp.concatenate([row] * 2, axis=0), 0.0)
        mixing = dot(matrix, spread, precision=EXACT)
        mix_high[...], mix_low[...] = halves(mixing)
        turned_high[...], turned_low[...] = halves(mixing.T)


def turn(values, keep, ahead, behind, sign):
    half = ROT // 2
    moved = (
        pltpu.roll(values, LANES - half, axis=1) * ahead + pltpu.roll(values, half, axis=1) * behind
    )
    return values * keep + sign * moved


def mixed_dot(values, high, low):
    first, second = halves(values)
    return dot(first, high) + (dot(second, high) + dot(first, low))


def head_columns(values, which, count):
    parts = [
        values[:, (3 * j + which) * HEAD_DIM : (3 * j + which + 1) * HEAD_DIM] for j in range(count)
    ]
    return parts[0] if count == 1 else jnp.concatenate(parts, axis=1)


def masked_stack(values, count):
    if count == 1:
        return values
    lane = (lane_of(values.shape) % (count * HEAD_DIM)) // HEAD_DIM
    zero = jnp.zeros_like(values)
    return jnp.concatenate([jnp.where(lane == j, values, zero) for j in range(count)], axis=0)


def side_by_side(stack, count):
    rows = stack.shape[0] // count
    if count == 1:
        return stack
    return jnp.concatenate([stack[j * rows : (j + 1) * rows] for j in range(count)], axis=1)


def own_block(dims):
    rows = lax.broadcasted_iota(jnp.int32, dims, 0) // HEAD_DIM
    return rows == (lane_of(dims) % dims[0]) // HEAD_DIM


def compress(state, count):
    width = count * HEAD_DIM
    sides = []
    for base in (0, width):
        part = state[:, base : base + HEAD_DIM]
        for j in range(1, count):
            rows = lax.broadcasted_iota(jnp.int32, part.shape, 0) // HEAD_DIM
            here = state[:, base + j * HEAD_DIM : base + (j + 1) * HEAD_DIM]
            part = jnp.where(rows == j, here, part)
        sides.append(part)
    return jnp.concatenate(sides, axis=1)


def expand(packed, count):
    values, totals = packed[:, :HEAD_DIM], packed[:, HEAD_DIM:]
    wide = jnp.concatenate([values] * count + [totals] * count, axis=1)
    return jnp.where(own_block(wide.shape), wide, 0.0)


def project(count, one, weight, bias, turns, mix_high, mix_low, chosen, feat_out, value_out, state):
    width = count * HEAD_DIM
    projected = dot(one, weight) + bias
    value = head_columns(projected, 2, count).astype(BF16)
    pairs = [head_columns(projected, which, count) for which in (0, 1)]
    if count == 1:
        pairs = [jnp.concatenate(pairs, axis=1)]
    feats = []
    for pair in pairs:
        feats.append(jnp.exp(mixed_dot(turn(pair, *turns, 1.0), mix_high, mix_low)))
    feat = feats[0] if count == 1 else jnp.concatenate(feats, axis=1)
    feat_out[...] = feat
    value_out[...] = value
    key = jnp.where(chosen, feat[:, width:], 0.0).astype(BF16)
    state[...] += dot(key, jnp.concatenate([value, jnp.ones_like(value)], axis=1), TN)


def own_features_kernel(count, blocks, table, docs, *refs):
    x_refs = refs[:blocks]
    (
        affine,
        weight,
        bias,
        keep,
        ahead,
        behind,
        mix_high,
        mix_low,
        docs_col,
        norm_one,
        norm_two,
        unit_out,
        feat_out,
        value_out,
        state_out,
        state,
        x_keep,
    ) = refs[blocks:]

    @pl.when(pl.program_id(0) == 0)
    def _():
        state[...] = jnp.zeros_like(state)

    for k in range(blocks):

        @pl.when(pl.program_id(0) == k)
        def _(k=k):
            x_keep[...] = x_refs[k][...]

    rows = x_keep.shape[0]
    x = x_keep[...].astype(F32)
    mean = jnp.mean(x, axis=-1, keepdims=True)
    centred = x - mean
    scale = lax.rsqrt(jnp.mean(centred * centred, axis=-1, keepdims=True) + EPS)
    unit = centred * scale
    one = (unit * affine[0:1] + affine[1:2]).astype(BF16)
    norm_one[...] = one
    norm_two[...] = (unit * affine[2:3] + affine[3:4]).astype(BF16)
    unit_out[...] = unit.astype(BF16)
    chosen = docs_col[...] == docs[(table[1] + 1) * blocks * rows - 1]
    project(
        count,
        one,
        weight[...],
        bias[...].astype(F32),
        (keep[...], ahead[...], behind[...]),
        mix_high[...],
        mix_low[...],
        chosen,
        feat_out,
        value_out,
        state,
    )

    @pl.when(pl.program_id(0) == pl.num_programs(0) - 1)
    def _():
        state_out[...] = compress(state[...], count)


def far_features_kernel(
    count,
    table,
    docs,
    norm_one,
    weight,
    bias,
    keep,
    ahead,
    behind,
    mix_high,
    mix_low,
    docs_col,
    near_state,
    feat_out,
    value_out,
    state_out,
    state,
):
    @pl.when(pl.program_id(0) == 0)
    def _():
        state[...] = jnp.zeros_like(state)

    rows = norm_one.shape[0]
    chosen = docs_col[...] == docs[(table[1] + 1) * pl.num_programs(0) * rows - 1]
    project(
        count,
        norm_one[...],
        weight[...],
        bias[0:1, : weight.shape[1]].astype(F32),
        (keep[...], ahead[...], behind[...]),
        mix_high[...],
        mix_low[...],
        chosen,
        feat_out,
        value_out,
        state,
    )

    @pl.when(pl.program_id(0) == pl.num_programs(0) - 1)
    def _():
        state_out[0] = near_state[...]
        state_out[1] = compress(state[...], count)


def allowed_pairs(docs_col, docs_row, count):
    size = docs_col.shape[0]
    rows = lax.broadcasted_iota(jnp.int32, (size, size), 0)
    cols = lax.broadcasted_iota(jnp.int32, (size, size), 1)
    allowed = ((docs_col == docs_row) & (rows >= cols)).astype(F32)
    return allowed if count == 1 else jnp.concatenate([allowed] * count, axis=0)


def forward_kernel(
    count,
    table,
    docs,
    own_feat,
    far_feat,
    own_value,
    far_value,
    docs_col,
    docs_row,
    first_state,
    mixed_out,
    merged_out,
    inverse_out,
    states_out,
    state,
):
    step = pl.program_id(0)
    width = count * HEAD_DIM
    rows = own_feat.shape[0]

    @pl.when(step == 0)
    def _():
        for side in range(2):
            state[side] = expand(first_state[1 - side], count)

    start = (table[1] * pl.num_programs(0) + step) * rows
    before = jnp.where(start > 0, docs[jnp.maximum(start - 1, 0)], -1)
    last = docs[start + rows - 1]
    kept = (last == before).astype(F32)
    allowed = allowed_pairs(docs_col[...], docs_row[0], count)
    carried = docs_col[...] == before
    chosen = docs_col[...] == last
    for side in range(2):
        feat_ref, value_ref = ((own_feat, own_value), (far_feat, far_value))[side]
        query = feat_ref[:, :width].astype(BF16)
        key = feat_ref[:, width:]
        value = value_ref[...]
        both = jnp.concatenate([value, jnp.ones_like(value)], axis=1)
        memory = state[side]
        states_out[0, side] = memory
        high, low = halves(memory)
        weights = (dot(masked_stack(query, count), key.astype(BF16), NT) * allowed).astype(BF16)
        sums = dot(side_by_side(weights, count), masked_stack(both, count)) + jnp.where(
            carried, dot(query, high) + dot(query, low), 0.0
        )
        inverse = 1.0 / sums[:, width:]
        mixed = sums[:, :width] * inverse
        mixed_out[:, side * width : (side + 1) * width] = mixed
        merged_out[:, side * width : (side + 1) * width] = mixed.astype(BF16)
        inverse_out[:, side * width : (side + 1) * width] = inverse
        picked = jnp.where(chosen, key, 0.0).astype(BF16)
        added = dot(picked, both, TN)
        state[side] = kept * memory + jnp.where(own_block(added.shape), added, 0.0)


def pair_grads(grad, inverse, mixed):
    part = (grad * inverse).astype(BF16)
    high, low = halves(-(part.astype(F32) * mixed))
    return part, high, low


def later_kernel(
    count,
    table,
    docs,
    grad_ref,
    own_dense,
    far_dense,
    own_feat,
    far_feat,
    mixed_ref,
    inverse_ref,
    docs_col,
    merged_grad,
    later_out,
    later,
):
    @pl.when(pl.program_id(0) == 0)
    def _():
        later[...] = jnp.zeros_like(later)

    width = count * HEAD_DIM
    rows = own_feat.shape[0]
    chosen = docs_col[...] == docs[table[1] * pl.num_programs(0) * rows]
    for side, dense in enumerate((own_dense, far_dense)):
        span = slice(side * width, (side + 1) * width)
        grad = dot(grad_ref[...], dense[...], NT)
        merged_grad[:, span] = grad
        part, high, low = pair_grads(grad, inverse_ref[:, span], mixed_ref[:, span])
        query = (own_feat, far_feat)[side][:, :width]
        query = jnp.where(chosen, query, 0.0).astype(BF16)
        later[side, :, :width] += dot(query, part, TN)
        later[side, :, width:] += dot(query, high, TN) + dot(query, low, TN)

    @pl.when(pl.program_id(0) == pl.num_programs(0) - 1)
    def _():
        for side in range(2):
            later_out[side] = compress(later[side], count)


def backward_kernel(
    count,
    table,
    docs,
    own_feat,
    far_feat,
    own_value,
    far_value,
    mixed_ref,
    inverse_ref,
    grad_ref,
    docs_col,
    docs_row,
    states_ref,
    first_later,
    keep,
    ahead,
    behind,
    turned_high,
    turned_low,
    own_out,
    far_out,
    later,
):
    blocks = pl.num_programs(0)
    step = blocks - 1 - pl.program_id(0)
    width = count * HEAD_DIM
    rows = own_feat.shape[0]

    @pl.when(pl.program_id(0) == 0)
    def _():
        for side in range(2):
            later[side] = expand(first_later[1 - side], count)

    start = (table[1] * blocks + step) * rows
    total = docs.shape[0]
    before = jnp.where(start > 0, docs[jnp.maximum(start - 1, 0)], -1)
    after = jnp.where(start + rows < total, docs[jnp.minimum(start + rows, total - 1)], -1)
    first = docs[start]
    kept = (first == after).astype(F32)
    allowed = allowed_pairs(docs_col[...], docs_row[0], count)
    carried = docs_col[...] == before
    linked = docs_col[...] == after
    chosen = docs_col[...] == first
    for side in range(2):
        span = slice(side * width, (side + 1) * width)
        feat = (own_feat, far_feat)[side][...]
        query, key = feat[:, :width].astype(BF16), feat[:, width:].astype(BF16)
        value = (own_value, far_value)[side][...]
        ones = jnp.ones_like(value)
        both = jnp.concatenate([value, ones], axis=1)
        part, high, low = pair_grads(grad_ref[:, span], inverse_ref[:, span], mixed_ref[:, span])
        first_two = jnp.concatenate([part, high], axis=1)
        queries = masked_stack(query, count)
        weights = (dot(queries, key, NT) * allowed).astype(BF16)
        weight_grad = dot(masked_stack(first_two, count), both, NT)
        weight_grad += dot(masked_stack(low, count), ones, NT)
        weight_grad = (weight_grad * allowed).astype(BF16)
        mem_high, mem_low = halves(states_ref[0, side])
        late = later[side]
        late_high, late_low = halves(late)
        query_grad = dot(side_by_side(weight_grad, count), masked_stack(key, count)) + jnp.where(
            carried,
            dot(first_two, mem_high, NT) + dot(first_two, mem_low, NT) + dot(low, mem_high[:, width:], NT),
            0.0,
        )
        key_grad = dot(weight_grad, queries, TN) + jnp.where(
            linked, dot(both, late_high, NT) + dot(both, late_low, NT), 0.0
        )
        value_grad = dot(weights, masked_stack(part, count), TN) + jnp.where(
            linked, dot(key, late_high[:, :width]) + dot(key, late_low[:, :width]), 0.0
        )
        picked = jnp.where(chosen, query.astype(F32), 0.0).astype(BF16)
        block = own_block(late.shape)
        added = jnp.concatenate(
            [dot(picked, part, TN), dot(picked, high, TN) + dot(picked, low, TN)], axis=1
        )
        later[side] = kept * late + jnp.where(block, added, 0.0)
        inner = jnp.concatenate([query_grad, key_grad], axis=1) * feat
        pairs = []
        for base in range(0, 2 * width, LANES):
            pair = mixed_dot(inner[:, base : base + LANES], turned_high[...], turned_low[...])
            pairs.append(turn(pair, keep[...], ahead[...], behind[...], -1.0))
        flat = pairs[0] if count == 1 else jnp.concatenate(pairs, axis=1)
        pieces = []
        for j in range(count):
            lanes = slice(j * HEAD_DIM, (j + 1) * HEAD_DIM)
            pieces += [flat[:, :width][:, lanes], flat[:, width:][:, lanes], value_grad[:, lanes]]
        out = own_out if side == 0 else far_out
        out[...] = jnp.concatenate(pieces, axis=1).astype(BF16)


def up_kernel(norm_ref, weight, bias, active_out, slope_out):
    hidden = dot(norm_ref[...], weight[...], NT) + bias[...]
    normal = 0.5 * (1.0 + lax.erf(hidden * 0.7071067811865476))
    density = jnp.exp(-0.5 * hidden * hidden) * 0.3989422804014327
    active_out[...] = (hidden * normal).astype(BF16)
    slope_out[...] = (normal + hidden * density).astype(BF16)


def down_back_kernel(grad_ref, weight, slope, hidden_out, sums_out):
    hidden = (dot(grad_ref[...], weight[...], NT) * slope[...].astype(F32)).astype(BF16)
    hidden_out[...] = hidden

    @pl.when(pl.program_id(0) == 0)
    def _():
        sums_out[...] = jnp.zeros_like(sums_out)

    sums_out[0:1] += jnp.sum(hidden.astype(F32), axis=0, keepdims=True)


def out_kernel(merged, own_active, far_active, own_dense, far_dense, own_down, far_down, *outs):
    width = own_dense.shape[0]
    total = dot(own_active[...], own_down[...]) + dot(far_active[...], far_down[...])
    total += dot(merged[:, :width], own_dense[...]) + dot(merged[:, width:], far_dense[...])
    write_block(outs, total.astype(BF16))


def write_block(outs, values):
    for k, out in enumerate(outs):

        @pl.when(pl.program_id(0) == k)
        def _(out=out):
            out[...] = values


def norm_grad_kernel(
    own_pg,
    far_pg,
    own_hg,
    far_hg,
    own_qkv,
    far_qkv,
    own_up,
    far_up,
    unit_ref,
    affine,
    grad_sums,
    sums_out,
    *outs,
):
    @pl.when(pl.program_id(0) == 0)
    def _():
        sums_out[...] = jnp.zeros_like(sums_out)
        sums_out[4:5] = grad_sums[0:1]

    down = lambda values: jnp.sum(values, axis=0, keepdims=True)
    unit = unit_ref[...].astype(F32)
    one = dot(own_pg[...], own_qkv[...], NT) + dot(far_pg[...], far_qkv[...], NT)
    sums_out[0:1] += down(one * unit)
    sums_out[1:2] += down(one)
    two = dot(own_hg[...], own_up[...]) + dot(far_hg[...], far_up[...])
    sums_out[2:3] += down(two * unit)
    sums_out[3:4] += down(two)
    write_block(outs, (one * affine[0:1] + two * affine[2:3]).astype(BF16))


def first_pack_kernel(table, weight, dense, bias, out):
    rows, small = weight.shape[0], dense.shape[0]
    if out.shape[1] > min(weight.shape[1], dense.shape[1]):
        out[...] = jnp.zeros_like(out)
    out[:rows, : weight.shape[1]] = weight[...]
    out[rows : rows + small, : dense.shape[1]] = dense[...]
    out[rows + small :, : bias.shape[1]] = jnp.broadcast_to(bias[...], (16, bias.shape[1]))


def arrange_kernel(table, up, down, bias, own_up, own_down, own_bias, pack, turned):
    part = table[2]
    step = down.shape[0] // QUARTERS
    turned[...] = up[...].T
    for k in range(QUARTERS):
        begin = pl.multiple_of((part ^ k) * step, step)
        own_up[k * step : (k + 1) * step] = turned[pl.ds(begin, step)]
        own_down[k * step : (k + 1) * step] = down[pl.ds(begin, step)]
    own_bias[...] = jnp.concatenate([bias[part ^ k].astype(F32) for k in range(QUARTERS)], axis=1)
    pack[:step] = own_up[:step]
    pack[step : 2 * step] = own_down[:step]
    pack[2 * step :] = jnp.zeros((16, pack.shape[1]), BF16)
    pack[2 * step :, :step] = jnp.broadcast_to(bias[part], (16, step))


def collect_first_kernel(table, mine, others, third, far_qkv, far_dense):
    part = table[2]
    step = far_qkv.shape[0] // QUARTERS
    small = far_dense.shape[0]
    size = mine.shape[0]
    for k, (ref, base) in enumerate(((mine, 0), (others, 0), (third, 0), (others, size))):
        begin = pl.multiple_of((part ^ k) * step, step)
        far_qkv[pl.ds(begin, step)] = ref[base : base + step, : far_qkv.shape[1]]
        far_dense[:, pl.ds(begin, step)] = ref[base + step : base + step + small, :step]


def collect_second_kernel(table, mine, others, third, far_up, far_down, far_bias):
    step = far_down.shape[0] // QUARTERS
    size = mine.shape[0]
    biases = []
    for k, (ref, base) in enumerate(((mine, 0), (others, 0), (third, 0), (others, size))):
        far_up[k * step : (k + 1) * step] = ref[base : base + step]
        far_down[k * step : (k + 1) * step] = ref[base + step : base + 2 * step]
        tail = ref[base + 2 * step : base + size].astype(F32)
        biases.append(tail[0:1, :step])
    far_bias[...] = jnp.concatenate(biases, axis=1)


def collect_grad_kernel(*refs):
    blocks, (whole, sums) = refs[:-2], refs[-2:]
    rows = blocks[0].shape[0]
    for k, ref in enumerate(blocks):
        whole[k * rows : (k + 1) * rows] = ref[...]
    sums[...] = jnp.zeros_like(sums)
    sums[0:1] = jnp.sum(blocks[0][...].astype(F32), axis=0, keepdims=True)


def bias_rows(values, cols):
    tile = jnp.zeros((16, values.shape[1]), F32)
    row = lax.broadcasted_iota(jnp.int32, tile.shape, 0)
    high = values.astype(BF16).astype(F32)
    tile = jnp.where(row == 0, high, jnp.where(row == 1, values - high, tile)).astype(BF16)
    if values.shape[1] == cols:
        return tile
    return jnp.concatenate([tile, jnp.zeros((16, cols - values.shape[1]), BF16)], axis=1)


def hidden_weights_kernel(
    table, active, hidden_grad, merged, grad, norm_two, hidden_sums, kept, sent, dense
):
    part = table[2]
    step, small = active.shape[1] // QUARTERS, merged.shape[1] // QUARTERS
    cols = kept.shape[2]
    dense[...] = dot(merged[...], grad[...], TN).astype(BF16)
    down = dot(active[...], grad[...], TN).astype(BF16)
    up = dot(hidden_grad[...], norm_two[...], TN).astype(BF16)
    for k in range(QUARTERS):
        out = (kept, sent)[k % 2].at[k // 2]
        span = slice(k * step, (k + 1) * step)
        out[:step] = up[span]
        out[step : 2 * step] = down[span]
        begin = pl.multiple_of((part ^ k) * small, small)
        out[2 * step : 2 * step + small] = dense[pl.ds(begin, small)]
        out[2 * step + small :] = bias_rows(hidden_sums[0:1, span], cols)


def qkv_weights_kernel(table, own_pg, far_pg, norm_one, kept, sent, full):
    part = table[2]
    cols = kept.shape[2]
    step = full.shape[0] // QUARTERS
    for side, grad in enumerate((own_pg, far_pg)):
        full[...] = dot(norm_one[...], grad[...], TN).astype(BF16)
        tail = bias_rows(jnp.sum(grad[...].astype(F32), axis=0, keepdims=True), cols)
        for k in range(QUARTERS):
            out = (kept, sent)[k % 2].at[2 * (k // 2) + side]
            begin = pl.multiple_of((part ^ k) * step, step)
            out[:step] = full[pl.ds(begin, step)]
            out[step:] = tail


def finish_hidden_kernel(
    table, mine, near, third, last, up_grad, down_grad, dense_grad, bias_grad, turned
):
    part = table[2]
    step, small = down_grad.shape[0] // QUARTERS, dense_grad.shape[0] // QUARTERS
    size = mine.shape[0]
    for k, ref in enumerate((mine, near, third, last)):
        begin = pl.multiple_of((part ^ k) * step, step)
        turned[pl.ds(begin, step)] = ref[:step].astype(F32)
        down_grad[pl.ds(begin, step)] = ref[step : 2 * step].astype(F32)
        begin = pl.multiple_of((part ^ k) * small, small)
        dense_grad[pl.ds(begin, small)] = ref[2 * step : 2 * step + small].astype(F32)
        tail = ref[2 * step + small : size].astype(F32)
        bias_grad[part ^ k] = tail[0:1, :step] + tail[1:2, :step]
    up_grad[...] = turned[...].T


def finish_qkv_kernel(table, mine, near, third, last, weight_grad, bias_grad):
    part = table[2]
    step = weight_grad.shape[0] // QUARTERS
    for k, ref in enumerate((mine, near, third, last)):
        begin = pl.multiple_of((part ^ k) * step, step)
        weight_grad[pl.ds(begin, step)] = ref[:step].astype(F32)
    tail = mine[step:].astype(F32)
    bias_grad[...] = tail[0:1] + tail[1:2]


def finish_out_kernel(x_ref, bias, *refs):
    parts, out = refs[:-1], refs[-1]
    total = x_ref[...].astype(F32) + bias[...].astype(F32)
    for ref in parts:
        total += ref[...].astype(F32)
    out[...] = total.astype(BF16)


def finish_in_kernel(x_ref, grad_ref, *refs):
    parts, out = refs[:-1], refs[-1]
    x = x_ref[...].astype(F32)
    mean = jnp.mean(x, axis=-1, keepdims=True)
    centred = x - mean
    scale = lax.rsqrt(jnp.mean(centred * centred, axis=-1, keepdims=True) + EPS)
    unit = centred * scale
    total = parts[0][...].astype(F32)
    for ref in parts[1:]:
        total += ref[...].astype(F32)
    along = jnp.mean(total * unit, axis=-1, keepdims=True)
    out[...] = grad_ref[...].astype(F32) + scale * (
        total - jnp.mean(total, axis=-1, keepdims=True) - unit * along
    )


def params():
    return pltpu.CompilerParams(
        dimension_semantics=("arbitrary",), vmem_limit_bytes=VMEM_LIMIT
    )


def after(value, *others):
    return lax.optimization_barrier((value,) + others)[0]


def shape(dims, kind):
    return jax.ShapeDtypeStruct(dims, kind)


def cost(flops, nbytes, trans=0):
    return pl.CostEstimate(flops=1000, bytes_accessed=1000, transcendentals=0)


def on_device(
    dp_size,
    tensor_size,
    inputs,
    qkv_weight,
    qkv_bias,
    dense_weight,
    up_weight,
    up_bias,
    down_weight,
    out_bias,
    gain_one,
    shift_one,
    gain_two,
    shift_two,
    feature_omega,
    doc_ids,
    out_grad,
):
    rows, model = inputs.shape
    inner = tensor_size // 2
    tokens = rows * inner
    qkv_cols = qkv_weight.shape[1]
    count = qkv_cols // (3 * HEAD_DIM)
    width = count * HEAD_DIM
    hidden_cols = up_weight.shape[1]
    dense_part, hidden_part, model_part = width // QUARTERS, hidden_cols // QUARTERS, model // QUARTERS
    member = lax.axis_index("dp")
    place = lax.axis_index("tensor")
    half, slot = place // inner, place % inner
    part = member % QUARTERS

    def swap(values, over_dp, over_tensor):
        pairs = [
            (p * tensor_size + t, (p ^ over_dp) * tensor_size + (t ^ over_tensor))
            for p in range(dp_size)
            for t in range(tensor_size)
        ]
        return lax.ppermute(values, AXES, pairs)

    def across(values, source_half):
        pairs = [
            (p * tensor_size + source_half * inner + t, p * tensor_size + (1 - source_half) * inner + t)
            for p in range(dp_size)
            for t in range(inner)
        ]
        return lax.ppermute(values, AXES, pairs)

    def gather(block):
        return [block] + [swap(block, 0, k) for k in range(1, inner)]

    line = []

    def run(step, *operands, gate=0, wait=()):
        operands = list(operands)
        held = tuple(line[-1:]) + tuple(wait)
        if held:
            operands[gate] = after(operands[gate], *held)
        result = step(*operands)
        line.append(result[0] if isinstance(result, (tuple, list)) else result)
        return result

    table = jnp.stack([slot, half, part]).astype(jnp.int32)
    plain = lambda cols: pl.BlockSpec((rows, cols), lambda k, *s: (k, 0))
    moved = lambda cols: pl.BlockSpec((rows, cols), lambda k, table, *s: (k ^ table[0], 0))
    whole = lambda *dims: pl.BlockSpec(dims, lambda k, *s: (0,) * len(dims))
    spec = lambda values: whole(*values.shape)

    def call(kernel, name, outs, in_specs, out_specs, price, prefetch=1, scratch=(), steps=inner):
        return pl.pallas_call(
            kernel,
            out_shape=outs,
            grid_spec=pltpu.PrefetchScalarGridSpec(
                num_scalar_prefetch=prefetch,
                grid=(steps,),
                in_specs=in_specs,
                out_specs=out_specs,
                scratch_shapes=list(scratch),
            ),
            compiler_params=params(),
            cost_estimate=price,
            name=name,
        )

    def once(kernel, name, outs, prefetch=1, scratch=()):
        single = not isinstance(outs, (tuple, list))
        listed = (outs,) if single else tuple(outs)

        def step(*operands):
            result = call(
                kernel,
                name,
                listed,
                [spec(v) for v in operands[prefetch:]],
                [whole(*v.shape) for v in listed],
                cost(0, 0),
                prefetch,
                scratch,
                1,
            )(*operands)
            return result[0] if single else result

        return step

    docs = doc_ids.reshape(-1)
    docs_col = docs.reshape(-1, 1)
    docs_row = docs.reshape(tensor_size, 1, rows)
    affine = jnp.stack([gain_one, shift_one, gain_two, shift_two]).astype(F32)
    lane = np.arange(LANES) % HEAD_DIM
    rates = np.where(lane < ROT, 10000.0 ** (-(lane % (ROT // 2)) * 2.0 / ROT), 0.0)
    rates = jnp.asarray(rates[None, :], F32)
    own_bias = qkv_bias.reshape(1, -1)

    x_blocks = gather(inputs)
    first_rows, first_cols = model_part + width + 16, max(qkv_cols, model_part)
    first_pack = run(
        call(
            first_pack_kernel,
            "first_pack",
            shape((first_rows, first_cols), BF16),
            [
                pl.BlockSpec((model_part, qkv_cols), lambda k, table: (table[2], 0)),
                pl.BlockSpec((width, model_part), lambda k, table: (0, table[2])),
                whole(1, qkv_cols),
            ],
            whole(first_rows, first_cols),
            cost(1e5, 4e5),
            steps=1,
        ),
        table,
        qkv_weight,
        dense_weight,
        own_bias,
    )
    first_mine = swap(first_pack, 0, inner)
    pack_rows = 2 * hidden_part + dense_part + 16
    second_rows = 2 * hidden_part + 16
    own_up, own_down, own_up_bias, second_pack = run(
        once(
            arrange_kernel,
            "arrange",
            (
                shape((hidden_cols, model), BF16),
                shape((hidden_cols, model), BF16),
                shape((1, hidden_cols), F32),
                shape((second_rows, model), BF16),
            ),
            scratch=[pltpu.VMEM((hidden_cols, model), BF16)],
        ),
        table,
        up_weight,
        down_weight,
        up_bias.reshape(QUARTERS, 1, hidden_part),
        gate=3,
    )
    second_mine = swap(second_pack, 0, inner)
    square = whole(LANES, LANES)
    keep, ahead, behind, mix_high, mix_low, turned_high, turned_low = run(
        call(
            prepare_kernel,
            "prepare",
            (shape((tokens, LANES), F32),) * 3 + (shape((LANES, LANES), BF16),) * 4,
            [whole(1, LANES), whole(HEAD_DIM, HEAD_DIM)],
            [plain(LANES)] * 3 + [square] * 4,
            cost(1e6, 2e6),
        ),
        table,
        rates,
        feature_omega,
        gate=2,
    )

    wide = pltpu.VMEM((2, width, 2 * width), F32)
    narrow = pltpu.VMEM((width, 2 * width), F32)
    mine_col = pl.BlockSpec(
        (rows, 1), lambda k, table, docs: ((k ^ table[0]) + table[1] * inner, 0)
    )
    norm_one, norm_two, unit, own_feat, own_value, near_state = run(
        call(
            functools.partial(own_features_kernel, count, inner),
            "own_features",
            (
                shape((tokens, model), BF16),
                shape((tokens, model), BF16),
                shape((tokens, model), BF16),
                shape((tokens, 2 * width), F32),
                shape((tokens, width), BF16),
                shape((width, LANES), F32),
            ),
            [whole(rows, model)] * inner
            + [
                whole(4, model),
                whole(model, qkv_cols),
                whole(1, qkv_cols),
                moved(LANES),
                moved(LANES),
                moved(LANES),
                square,
                square,
                mine_col,
            ],
            [
                plain(model),
                plain(model),
                plain(model),
                plain(2 * width),
                plain(width),
                whole(width, LANES),
            ],
            cost(2 * tokens * model * qkv_cols, 12e6),
            prefetch=2,
            scratch=[narrow, pltpu.VMEM((rows, model), BF16)],
        ),
        table,
        docs,
        *x_blocks,
        affine,
        qkv_weight,
        own_bias,
        keep,
        ahead,
        behind,
        mix_high,
        mix_low,
        docs_col,
        gate=2 + inner,
        wait=(first_mine,),
    )
    here_x = tuple(x_blocks[1:]) + (keep,)
    first_third = swap(after(first_mine, *here_x), 2, 0)
    grad_blocks = gather(after(out_grad, *here_x))
    first_others = swap(
        run(lambda a, b: jnp.concatenate([a, b], axis=0), first_mine, first_third), 1, 0
    )
    far_qkv, far_dense = run(
        once(
            collect_first_kernel,
            "collect_first",
            (shape((model, qkv_cols), BF16), shape((width, model), BF16)),
        ),
        table,
        first_mine,
        first_others,
        first_third,
        gate=1,
        wait=(second_mine,),
    )
    second_third = swap(second_mine, 2, 0)
    far_feat, far_value, state = run(
        call(
            functools.partial(far_features_kernel, count),
            "far_features",
            (
                shape((tokens, 2 * width), F32),
                shape((tokens, width), BF16),
                shape((2, width, LANES), F32),
            ),
            [
                plain(model),
                whole(model, qkv_cols),
                pl.BlockSpec((16, first_cols), lambda k, *s: ((model_part + width) // 16, 0)),
                moved(LANES),
                moved(LANES),
                moved(LANES),
                square,
                square,
                mine_col,
                whole(width, LANES),
            ],
            [plain(2 * width), plain(width), whole(2, width, LANES)],
            cost(2 * tokens * model * qkv_cols, 8e6),
            prefetch=2,
            scratch=[narrow],
        ),
        table,
        docs,
        norm_one,
        far_qkv,
        first_mine,
        keep,
        ahead,
        behind,
        mix_high,
        mix_low,
        docs_col,
        near_state,
        gate=2,
    )
    first_state = across(state, 0)

    def simple(kernel, name, outs, in_specs, out_specs, price):
        return call(kernel, name, outs, in_specs, out_specs, price, prefetch=0)

    def up_projection(weight, bias):
        return run(
            simple(
                up_kernel,
                "up",
                (shape((tokens, hidden_cols), BF16),) * 2,
                [plain(model), whole(hidden_cols, model), whole(1, hidden_cols)],
                [plain(hidden_cols)] * 2,
                cost(2 * tokens * model * hidden_cols, 5e6, 2 * tokens * hidden_cols),
            ),
            norm_two,
            weight,
            bias,
        )

    own_active, own_slope = up_projection(own_up, own_up_bias)

    block_row = pl.BlockSpec((1, 1, rows), lambda m, table, docs: (m + table[1] * inner, 0, 0))
    block_col = pl.BlockSpec((rows, 1), lambda m, table, docs: (m + table[1] * inner, 0))
    mixed, merged, inverse, states = run(
        call(
            functools.partial(forward_kernel, count),
            "attend",
            (
                shape((tokens, 2 * width), F32),
                shape((tokens, 2 * width), BF16),
                shape((tokens, 2 * width), F32),
                shape((inner, 2, width, 2 * width), F32),
            ),
            [
                moved(2 * width),
                moved(2 * width),
                moved(width),
                moved(width),
                block_col,
                block_row,
                whole(2, width, LANES),
            ],
            [
                moved(2 * width),
                moved(2 * width),
                moved(2 * width),
                pl.BlockSpec((1, 2, width, 2 * width), lambda m, *s: (m, 0, 0, 0)),
            ],
            cost(2 * count * tokens * rows * 800, 5e6),
            prefetch=2,
            scratch=[wide],
        ),
        table,
        docs,
        own_feat,
        far_feat,
        own_value,
        far_value,
        docs_col,
        docs_row,
        first_state,
        gate=2,
    )
    grad_all, grad_sums = run(
        once(
            collect_grad_kernel,
            "collect_grad",
            (shape((tokens, model), BF16), shape((8, model), F32)),
            prefetch=0,
        ),
        *grad_blocks,
        gate=1,
    )
    both_second = run(lambda a, b: jnp.concatenate([a, b], axis=0), second_mine, second_third)
    second_others = swap(both_second, 1, 0)
    merged_grad, later = run(
        call(
            functools.partial(later_kernel, count),
            "later",
            (shape((tokens, 2 * width), F32), shape((2, width, LANES), F32)),
            [
                plain(model),
                whole(width, model),
                whole(width, model),
                plain(2 * width),
                plain(2 * width),
                plain(2 * width),
                plain(2 * width),
                mine_col,
            ],
            [plain(2 * width), whole(2, width, LANES)],
            cost(2 * count * tokens * 64 * 256, 5e6),
            prefetch=2,
            scratch=[wide],
        ),
        *(table, docs, grad_all, dense_weight, far_dense, own_feat, far_feat, mixed, inverse, docs_col),
        gate=2,
    )
    first_later = across(later, 1)

    def down_back(weight, slope):
        return run(
            simple(
                down_back_kernel,
                "down_back",
                (shape((tokens, hidden_cols), BF16), shape((8, hidden_cols), F32)),
                [plain(model), whole(hidden_cols, model), plain(hidden_cols)],
                [plain(hidden_cols), whole(8, hidden_cols)],
                cost(2 * tokens * model * hidden_cols, 5e6),
            ),
            grad_all,
            weight,
            slope,
            gate=2,
        )

    def add(a, b):
        return (a.astype(F32) + b.astype(F32)).astype(BF16)

    def rest(total):
        step = QUARTERS
        while step < dp_size:
            total = add(total, swap(total, step, 0))
            step *= 2
        return total

    def hidden_weights(active, hidden_grad, side, sums_row):
        return run(
            call(
                hidden_weights_kernel,
                "hidden_weights",
                (shape((2, pack_rows, model), BF16),) * 2,
                [
                    whole(tokens, hidden_cols),
                    whole(tokens, hidden_cols),
                    pl.BlockSpec((tokens, width), lambda k, table: (0, side))
                    if width % LANES == 0
                    else whole(tokens, width),
                    whole(tokens, model),
                    whole(tokens, model),
                    whole(8, hidden_cols),
                ],
                [whole(2, pack_rows, model)] * 2,
                cost(2 * tokens * model * (2 * hidden_cols + width), 9e6),
                scratch=[pltpu.VMEM((width, model), BF16)],
                steps=1,
            ),
            table,
            active,
            hidden_grad,
            merged if width % LANES == 0 else merged[:, side * width : (side + 1) * width],
            grad_all,
            norm_two,
            sums_row,
            gate=2,
        )

    own_hidden_grad, own_up_sums = down_back(own_down, own_slope)
    own_kept, own_sent = hidden_weights(own_active, own_hidden_grad, 0, own_up_sums)
    own_got = swap(own_sent, 1, 0)
    far_up, far_down, far_up_bias = run(
        once(
            collect_second_kernel,
            "collect_second",
            (
                shape((hidden_cols, model), BF16),
                shape((hidden_cols, model), BF16),
                shape((1, hidden_cols), F32),
            ),
        ),
        table,
        second_mine,
        second_others,
        second_third,
        gate=1,
    )
    far_active, far_slope = up_projection(far_up, far_up_bias)
    partial_out = run(
        simple(
            out_kernel,
            "out",
            (shape((rows, model), BF16),) * inner,
            [
                plain(2 * width),
                plain(hidden_cols),
                plain(hidden_cols),
                whole(width, model),
                whole(width, model),
                whole(hidden_cols, model),
                whole(hidden_cols, model),
            ],
            [whole(rows, model)] * inner,
            cost(4 * tokens * model * (width + hidden_cols), 8e6),
        ),
        merged,
        own_active,
        far_active,
        dense_weight,
        far_dense,
        own_down,
        far_down,
    )

    def scatter(blocks):
        return [blocks[0]] + [swap(blocks[k], 0, k) for k in range(1, inner)]

    out_parts = scatter(partial_out)

    far_hidden_grad, far_up_sums = down_back(far_down, far_slope)
    own_next = run(add, own_kept[1], own_got[1])
    own_cross = swap(own_next, 2, 0)
    far_kept, far_sent = hidden_weights(far_active, far_hidden_grad, 1, far_up_sums)
    far_got = swap(far_sent, 1, 0)

    back = lambda cols: pl.BlockSpec((rows, cols), lambda m, table, docs: ((inner - 1 - m) ^ table[0], 0))
    back_straight = lambda cols: pl.BlockSpec((rows, cols), lambda m, *s: (inner - 1 - m, 0))
    own_pg, far_pg = run(
        call(
            functools.partial(backward_kernel, count),
            "attend_back",
            (shape((tokens, qkv_cols), BF16),) * 2,
            [
                back(2 * width),
                back(2 * width),
                back(width),
                back(width),
                back(2 * width),
                back(2 * width),
                back(2 * width),
                pl.BlockSpec(
                    (rows, 1), lambda m, table, docs: (inner - 1 - m + table[1] * inner, 0)
                ),
                pl.BlockSpec(
                    (1, 1, rows), lambda m, table, docs: (inner - 1 - m + table[1] * inner, 0, 0)
                ),
                pl.BlockSpec((1, 2, width, 2 * width), lambda m, *s: (inner - 1 - m, 0, 0, 0)),
                whole(2, width, LANES),
                back_straight(LANES),
                back_straight(LANES),
                back_straight(LANES),
                square,
                square,
            ],
            [back(qkv_cols), back(qkv_cols)],
            cost(2 * count * tokens * rows * 2000, 8e6),
            prefetch=2,
            scratch=[wide],
        ),
        table,
        docs,
        own_feat,
        far_feat,
        own_value,
        far_value,
        mixed,
        inverse,
        merged_grad,
        docs_col,
        docs_row,
        states,
        first_later,
        keep,
        ahead,
        behind,
        turned_high,
        turned_low,
        gate=8,
    )
    far_next = run(add, far_kept[1], far_got[1])
    far_cross = swap(far_next, 2, 0)
    own_quad = run(lambda a, b, c: add(add(a, b), c), own_kept[0], own_got[0], own_cross)
    layer_out = run(
        once(finish_out_kernel, "finish_out", shape((rows, model), BF16), prefetch=0),
        inputs,
        out_bias.reshape(1, -1),
        *out_parts,
        gate=2,
    )
    kept, sent = run(
        once(
            qkv_weights_kernel,
            "qkv_weights",
            (shape((4, model_part + 16, qkv_cols), BF16),) * 2,
            scratch=[pltpu.VMEM((model, qkv_cols), BF16)],
        ),
        table,
        own_pg,
        far_pg,
        norm_one,
        gate=3,
    )
    got = swap(sent, 1, 0)
    norm_grads = run(
        simple(
            norm_grad_kernel,
            "norm_grad",
            (shape((8, model), F32),) + (shape((rows, model), BF16),) * inner,
            [
                plain(qkv_cols),
                plain(qkv_cols),
                plain(hidden_cols),
                plain(hidden_cols),
                whole(model, qkv_cols),
                whole(model, qkv_cols),
                whole(hidden_cols, model),
                whole(hidden_cols, model),
                plain(model),
                whole(4, model),
                whole(8, model),
            ],
            [whole(8, model)] + [whole(rows, model)] * inner,
            cost(4 * tokens * model * (qkv_cols + hidden_cols), 12e6),
        ),
        own_pg,
        far_pg,
        own_hidden_grad,
        far_hidden_grad,
        qkv_weight,
        far_qkv,
        own_up,
        far_up,
        unit,
        affine,
        grad_sums,
        gate=8,
    )
    e_parts = scatter(norm_grads[1:])
    cross_sent = run(add, kept[2:], got[2:])
    crossed = swap(cross_sent, 2, 0)
    far_quad = run(lambda a, b, c: add(add(a, b), c), far_kept[0], far_got[0], far_cross)
    far_home = swap(far_quad, 0, inner)
    far_piece = run(lambda a, b, c: add(add(a, b), c), kept[1], got[1], crossed[1])
    far_piece_home = swap(far_piece, 0, inner)
    own_piece = run(lambda a, b, c: add(add(a, b), c), kept[0], got[0], crossed[0])
    input_grad = run(
        once(finish_in_kernel, "finish_in", shape((rows, model), F32), prefetch=0),
        inputs,
        out_grad,
        *e_parts,
        gate=2,
    )
    upper_mine = rest(run(add, own_piece, far_piece_home))
    upper_third = swap(upper_mine, 2, 0)
    upper_near = swap(upper_mine, 1, 0)
    lower_mine = rest(run(add, own_quad, far_home))
    lower_third = swap(lower_mine, 2, 0)
    lower_near = swap(lower_mine, 1, 0)
    upper = (upper_mine, upper_near, upper_third, swap(upper_third, 1, 0))
    lower = (lower_mine, lower_near, lower_third, swap(lower_third, 1, 0))

    small = after(norm_grads[0], input_grad)
    step = 1
    while step < dp_size:
        small = small + swap(small, step, 0)
        step *= 2
    step = 1
    while step < tensor_size:
        small = small + swap(small, 0, step)
        step *= 2
    cols = model // tensor_size
    small = lax.dynamic_slice_in_dim(small, place * cols, cols, 1)

    up_grad, down_grad, dense_grad, up_bias_grad = run(
        once(
            finish_hidden_kernel,
            "finish_hidden",
            (
                shape((model, hidden_cols), F32),
                shape((hidden_cols, model), F32),
                shape((width, model), F32),
                shape((QUARTERS, 1, hidden_part), F32),
            ),
            scratch=[pltpu.VMEM((hidden_cols, model), F32)],
        ),
        table,
        *lower,
        gate=1,
    )
    qkv_grad, qkv_bias_grad = run(
        once(
            finish_qkv_kernel,
            "finish_qkv",
            (shape((model, qkv_cols), F32), shape((1, qkv_cols), F32)),
        ),
        table,
        *upper,
        gate=1,
    )

    return (
        layer_out,
        input_grad,
        qkv_grad,
        qkv_bias_grad.reshape(-1),
        dense_grad,
        up_grad,
        up_bias_grad.reshape(-1),
        down_grad,
        small[4],
        small[0],
        small[1],
        small[2],
        small[3],
    )


def solution(mesh):
    in_specs = (
        P(("dp", "tensor"), None),
        P(None, "tensor"),
        P("tensor"),
        P("tensor", None),
        P(None, "tensor"),
        P("tensor"),
        P("tensor", None),
        P(),
        P(),
        P(),
        P(),
        P(),
        P(),
        P("dp", None),
        P(("dp", "tensor"), None),
    )
    out_specs = (
        P(("dp", "tensor"), None),
        P(("dp", "tensor"), None),
        P(None, "tensor"),
        P("tensor"),
        P("tensor", None),
        P(None, "tensor"),
        P("tensor"),
        P("tensor", None),
        P("tensor"),
        P("tensor"),
        P("tensor"),
        P("tensor"),
        P("tensor"),
    )
    return jax.shard_map(
        functools.partial(on_device, mesh.shape["dp"], mesh.shape["tensor"]),
        mesh=mesh,
        in_specs=in_specs,
        out_specs=out_specs,
        check_vma=False,
    )
```

time: 1270 us -> 251 us (0.20)
  waiting for transfers between devices: 783 us -> 116 us
  matrix products: 180 us -> 0 us
  local copies, waits for them, and re-layouts: 143 us -> 15.7 us
  other arithmetic: 115 us -> 2.39 us
  Pallas kernels: 0 us -> 76.5 us
  starting transfers between devices: 0.53 us -> 38.5 us
  between operations: 15.3 us -> 1.28 us
  loops' own time: 12.9 us -> 0 us
    reduce_scatter x4 -> x0, waiting for transfers between devices: 533 us -> none  [the longest x1 248 us: on_device(): lax.psum_scatter(jnp.concatenate([jnp.einsum('tc,dc->td', qkv_grad, qkv_w...]
    dot_general x133 -> x0, matrix products: 180 us -> none  [the longest x8 16.6 us: advance(): jnp.einsum('sbc,sce->sbe', weights, value_wide, precision=EXACT)]
    all_gather x3 -> x0, waiting for transfers between devices: 133 us -> none  [the longest x1 68.9 us: on_device(): lax.all_gather(norm_values[0].astype(jnp.bfloat16), 'tensor', axis=0, til...]
    ppermute x0 -> x39, waiting for transfers between devices: none -> 116 us  [the longest x37 103 us: swap(): return lax.ppermute(values, AXES, pairs)]
    psum x1 -> x0, waiting for transfers between devices: 116 us -> none  [on_device(): lax.psum((qkv_weight_grad, qkv_bias_grad, dense_weight_grad, up_weight_gr...]
    pallas_call x0 -> x24, Pallas kernels: none -> 76.5 us  [the longest x15 59.7 us: run(): result = step(*operands)]
    dynamic_update_slice x40 -> x0, local copies, waits for them, and re-layouts: 62.8 us -> none  [attend_forward(): lax.scan(advance, initial, (query_blocks, key_blocks, value_blocks, doc_b...]
    ppermute x0 -> x39, starting transfers between devices: none -> 38.5 us  [the longest x37 35.4 us: swap(): return lax.ppermute(values, AXES, pairs)]
  transfers between devices with their start and end apart: 8 -> 39, of which waited for: 7 -> 18; matrix products, arithmetic and copies ran while one was open for 31% -> 3% of each run, Pallas kernels for 0% -> 23%
where the time goes in v1:
time: 251 us; the launch traced here: 250 us
  waiting for transfers between devices  116 us (46%)
  Pallas kernels  76.5 us (30%)
  starting transfers between devices  38.5 us (15%)
  local copies, waits for them, and re-layouts  15.7 us (6%)
    ppermute x37, waiting for transfers between devices, swap(): return lax.ppermute(values, AXES, pairs)  103 us
    pallas_call x15, Pallas kernels, run(): result = step(*operands)  59.7 us
    ppermute x37, starting transfers between devices, swap(): return lax.ppermute(values, AXES, pairs)  35.4 us
    pallas_call x9, Pallas kernels, step(): call(kernel, name, listed, [spec(v) for v in operands[prefetch:]], [whole...  16.8 us
    ppermute x2, waiting for transfers between devices, across(): return lax.ppermute(values, AXES, pairs)  13 us
    unnamed x58, local copies, waits for them, and re-layouts  12.8 us
  transfers between devices with their start and end apart: 39, of which 18 were waited for; matrix products, arithmetic and copies ran while one was open for 3% of the time, Pallas kernels for 23%

profile of v1, /device:TPU:0, one launch (start us, length us, event | category | flops | bytes accessed | tf_op | source)
XLA Modules:
  0.0 250.1 jit_solution(14487341597920865191)
XLA Ops:
  0.7 3.0 %collective-permute-start = (bf16[256,1024]{1,0:T(8,128)(2,1)}, bf16[256,1024]{1,0:T(8,128)(2,1)S(1)}, u32[]{:S(2)}, u32[]{:S(2)}) collective-permute-start(bf16[256,1024]{1,0:T(8,128)(2,1)} %x_ref.3), channel_id=1, source_target_pairs={{0,1},{1,0},{2,3},{3,2},{4,5},{5,4},{6,7},{7,6},{8,9},{9,8},{10,11... | collective-permute-start | bytes 1572872 | tf_op jit(solution)/shard_map/ppermute | solution.py:723
  3.7 1.6 collective-permute-start.1
  8.7 3.1 %collective-permute-start.3 = (bf16[400,384]{1,0:T(8,128)(2,1)S(1)}, bf16[400,384]{1,0:T(8,128)(2,1)}, u32[]{:S(2)}, u32[]{:S(2)}) collective-permute-start(bf16[400,384]{1,0:T(8,128)(2,1)S(1)} %first_pack.1), channel_id=1, source_target_pairs={{0,4},{1,5},{2,6},{3,7},{4,0},{5,1},{6,2},{7,3},{8,12},{9,13},{10,... | collective-permute-start | bytes 921608 | tf_op jit(solution)/shard_map/ppermute | solution.py:723
  13.0 1.8 arrange.1
  16.8 3.2 %prepare.1 = (f32[1024,128]{1,0:T(8,128)S(1)}, f32[1024,128]{1,0:T(8,128)S(1)}, f32[1024,128]{1,0:T(8,128)S(1)}, bf16[128,128]{1,0:T(8,128)(2,1)S(1)}, bf16[128,...) custom-call(s32[3]{0:T(128)S(1)} %pad_add_fusion.table, f32[1,128]{1,0:T(1,128)S(1)} %copy-done.21, ...), custom_call_target="tpu_custom_call" | custom-call | flops 1000 | bytes 1000 | tf_op jit(solution)/shard_map/prepare/pallas_call | solution.py:743
  20.6 13.6 %collective-permute-done.3.mine.bias = bf16[400,384]{1,0:T(8,128)(2,1)} collective-permute-done((bf16[400,384]{1,0:T(8,128)(2,1)S(1)}, bf16[400,384]{1,0:T(8,128)(2,1)}, u32[]{:S(2)}, u32[]{:S(2)}) %collective-permute-start.3) | collective-permute-done | bytes 307232 | tf_op jit(solution)/shard_map/ppermute | solution.py:723
  37.3 3.5 %collective-permute-start.5 = (bf16[272,1024]{1,0:T(8,128)(2,1)}, bf16[272,1024]{1,0:T(8,128)(2,1)}, u32[]{:S(2)}, u32[]{:S(2)}) collective-permute-start(bf16[272,1024]{1,0:T(8,128)(2,1)} %get-tuple-element.128), channel_id=1, source_target_pairs={{0,4},{1,5},{2,6},{3,7},{4,0},{5,1},{6,2},{7,3},{8,12},{9,13},{10,... | collective-permute-start | bytes 1671176 | tf_op jit(solution)/shard_map/ppermute | solution.py:723
  44.4 7.1 %own_features.1 = (bf16[1024,1024]{1,0:T(8,128)(2,1)S(1)}, bf16[1024,1024]{1,0:T(8,128)(2,1)S(1)}, bf16[1024,1024]{1,0:T(8,128)(2,1)S(1)}, f32[1024,256]{1,0:T(8...) custom-call(s32[3]{0:T(128)S(1)} %pad_add_fusion.table, s32[2048]{0:T(1024)S(1)} %bitcast.71, ...), custom_call_target="tpu_custom_call" | custom-call | flops 1000 | bytes 1000 | tf_op jit(solution)/shard_map/own_features/pallas_call | solution.py:743
  55.3 1.9 collective-permute-start.9
  57.2 7.1 %collective-permute-done.5.mine = bf16[272,1024]{1,0:T(8,128)(2,1)} collective-permute-done((bf16[272,1024]{1,0:T(8,128)(2,1)}, bf16[272,1024]{1,0:T(8,128)(2,1)}, u32[]{:S(2)}, u32[]{:S(2)}) %collective-permute-start.5) | collective-permute-done | bytes 557088 | tf_op jit(solution)/shard_map/ppermute | solution.py:723
  64.8 1.7 collect_first.1
  66.5 5.4 %far_features.1 = (f32[1024,256]{1,0:T(8,128)S(1)}, bf16[1024,128]{1,0:T(8,128)(2,1)S(1)}, f32[2,128,128]{2,1,0:T(8,128)S(1)}) custom-call(s32[3]{0:T(128)S(1)} %pad_add_fusion.table, s32[2048]{0:T(1024)S(1)} %bitcast.72, bf16[1024,1024]{1,0:T(8,128)(2,1)S(1)} %get-tuple-element.189.norm_one, bf16[1024,384]{1,0:T(8,128)(2,1)S(1)} %get-tuple-element.130.weight.far_qkv, ...), custom_call_target="tpu_custom_call" | custom-call | flops 1000 | bytes 1000 | tf_op jit(solution)/shard_map/far_features/pallas_call | solution.py:743
  72.0 1.6 collective-permute-start.7
  73.6 2.6 %up.4 = (bf16[1024,512]{1,0:T(8,128)(2,1)S(1)}, bf16[1024,512]{1,0:T(8,128)(2,1)S(1)}) custom-call(bf16[1024,1024]{1,0:T(8,128)(2,1)S(1)} %get-tuple-element.160.norm_ref.norm_two, bf16[512,1024]{1,0:T(8,128)(2,1)S(1)} %copy-done.5, f32[1,512]{1,0:T(1,128)S(1)} %get-tuple-element.135.bias), custom_call_target="tpu_custom_call" | custom-call | flops 1000 | bytes 1000 | tf_op jit(solution)/shard_map/up/pallas_call | solution.py:743
  76.2 4.7 %collective-permute-done.7.first_state = f32[2,128,128]{2,1,0:T(8,128)S(1)} collective-permute-done((f32[2,128,128]{2,1,0:T(8,128)S(1)}, f32[2,128,128]{2,1,0:T(8,128)S(1)}, u32[]{:S(2)}, u32[]{:S(2)}) %collective-permute-start.7) | collective-permute-done | bytes 131104 | tf_op jit(solution)/shard_map/ppermute | solution.py:731
  80.9 3.4 %attend.1 = (f32[1024,256]{1,0:T(8,128)S(1)}, bf16[1024,256]{1,0:T(8,128)(2,1)S(1)}, f32[1024,256]{1,0:T(8,128)S(1)}, f32[4,2,128,256]{3,2,1,0:T(8,128)S(1)}) custom-call(s32[3]{0:T(128)S(1)} %pad_add_fusion.table, s32[2048]{0:T(1024)S(1)} %bitcast.73, f32[1024,256]{1,0:T(8,128)S(1)} %get-tuple-element.137.own_feat, ...), custom_call_target="tpu_custom_call" | custom-call | flops 1000 | bytes 1000 | tf_op jit(solution)/shard_map/attend/pallas_call | solution.py:743
  84.3 2.3 collective-permute-done.9.refs_2_
  88.1 5.5 %later.1 = (f32[1024,256]{1,0:T(8,128)S(1)}, f32[2,128,128]{2,1,0:T(8,128)S(1)}) custom-call(s32[3]{0:T(128)S(1)} %pad_add_fusion.table, s32[2048]{0:T(1024)S(1)} %bitcast.75, bf16[1024,1024]{1,0:T(8,128)(2,1)S(1)} %get-tuple-element.149.grad_ref.grad, bf16[128,1024]{1,0:T(8,128)(2,1)S(1)} %copy-done.9, bf16[128,1024]{1,0:T(8,128)(2,1)S(1)} %get-tuple-element.150.far_dense, ...), custom_call_target="tpu_custom_call" | custom-call | flops 1000 | bytes 1000 | tf_op jit(solution)/shard_map/later/pallas_call | solution.py:743
  93.6 2.1 down_back.2
  95.7 3.3 %hidden_weights.2 = (bf16[2,304,1024]{2,1,0:T(8,128)(2,1)S(1)}, bf16[2,304,1024]{2,1,0:T(8,128)(2,1)S(1)}) custom-call(s32[3]{0:T(128)S(1)} %pad_add_fusion.table, bf16[1024,512]{1,0:T(8,128)(2,1)S(1)} %get-tuple-element.136.active.own_active, bf16[1024,512]{1,0:T(8,128)(2,1)S(1)} %get-tuple-element.155.hidden_grad.own_hg, ...), custom_call_target="tpu_custom_call" | custom-call | flops 1000 | bytes 1000 | tf_op jit(solution)/shard_map/hidden_weights/pallas_call | solution.py:743
  99.6 3.9 %collective-permute-done.12.others = bf16[544,1024]{1,0:T(8,128)(2,1)S(1)} collective-permute-done((bf16[544,1024]{1,0:T(8,128)(2,1)S(1)}, bf16[544,1024]{1,0:T(8,128)(2,1)S(1)}, u32[]{:S(2)}, u32[]{:S(2)}) %collective-permute-start.12) | collective-permute-done | bytes 1114144 | tf_op jit(solution)/shard_map/ppermute | solution.py:723
  103.6 1.7 collect_second.1
  105.3 2.6 %up.5 = (bf16[1024,512]{1,0:T(8,128)(2,1)S(1)}, bf16[1024,512]{1,0:T(8,128)(2,1)S(1)}) custom-call(bf16[1024,1024]{1,0:T(8,128)(2,1)S(1)} %get-tuple-element.160.norm_ref.norm_two, bf16[512,1024]{1,0:T(8,128)(2,1)S(1)} %get-tuple-element.159.weight.far_up, f32[1,512]{1,0:T(1,128)S(1)} %get-tuple-element.161.bias), custom_call_target="tpu_custom_call" | custom-call | flops 1000 | bytes 1000 | tf_op jit(solution)/shard_map/up/pallas_call | solution.py:743
  107.9 4.2 %out.1 = (bf16[256,1024]{1,0:T(8,128)(2,1)S(1)}, bf16[256,1024]{1,0:T(8,128)(2,1)S(1)}, bf16[256,1024]{1,0:T(8,128)(2,1)S(1)}, bf16[256,1024]{1,0:T(8,128)(2,1)S(1)}) custom-call(bf16[1024,256]{1,0:T(8,128)(2,1)S(1)} %get-tuple-element.163.merged, bf16[1024,512]{1,0:T(8,128)(2,1)S(1)} %get-tuple-element.136.active.own_active, ...), custom_call_target="tpu_custom_call" | custom-call | flops 1000 | bytes 1000 | tf_op jit(solution)/shard_map/out/pallas_call | solution.py:743
  112.2 2.1 down_back.3
  114.5 3.3 %hidden_weights.3 = (bf16[2,304,1024]{2,1,0:T(8,128)(2,1)S(1)}, bf16[2,304,1024]{2,1,0:T(8,128)(2,1)S(1)}) custom-call(s32[3]{0:T(128)S(1)} %pad_add_fusion.table, bf16[1024,512]{1,0:T(8,128)(2,1)S(1)} %get-tuple-element.162.far_active.active, bf16[1024,512]{1,0:T(8,128)(2,1)S(1)} %get-tuple-element.171.hidden_grad.far_hg, ...), custom_call_target="tpu_custom_call" | custom-call | flops 1000 | bytes 1000 | tf_op jit(solution)/shard_map/hidden_weights/pallas_call | solution.py:743
  121.4 8.3 %collective-permute-done.14.first_later = f32[2,128,128]{2,1,0:T(8,128)S(1)} collective-permute-done((f32[2,128,128]{2,1,0:T(8,128)S(1)}, f32[2,128,128]{2,1,0:T(8,128)S(1)}, u32[]{:S(2)}, u32[]{:S(2)}) %collective-permute-start.14) | collective-permute-done | bytes 131104 | tf_op jit(solution)/shard_map/ppermute | solution.py:731
  130.1 8.6 %attend_back.1 = (bf16[1024,384]{1,0:T(8,128)(2,1)S(1)}, bf16[1024,384]{1,0:T(8,128)(2,1)S(1)}) custom-call(s32[3]{0:T(128)S(1)} %pad_add_fusion.table, s32[2048]{0:T(1024)S(1)} %bitcast.76, f32[1024,256]{1,0:T(8,128)S(1)} %get-tuple-element.137.own_feat, f32[1024,256]{1,0:T(8,128)S(1)} %get-tuple-element.133.far_feat, ...), custom_call_target="tpu_custom_call" | custom-call | flops 1000 | bytes 1000 | tf_op jit(solution)/shard_map/attend_back/pallas_call | solution.py:743
  139.4 9.9 %collective-permute-done.19.refs_3_ = bf16[256,1024]{1,0:T(8,128)(2,1)S(1)} collective-permute-done((bf16[256,1024]{1,0:T(8,128)(2,1)S(1)}, bf16[256,1024]{1,0:T(8,128)(2,1)S(1)}, u32[]{:S(2)}, u32[]{:S(2)}) %collective-permute-start.19) | collective-permute-done | bytes 524320 | tf_op jit(solution)/shard_map/ppermute | solution.py:723
  150.5 3.0 %qkv_weights.1 = (bf16[4,272,384]{2,1,0:T(8,128)(2,1)S(1)}, bf16[4,272,384]{2,1,0:T(8,128)(2,1)S(1)}) custom-call(s32[3]{0:T(128)S(1)} %pad_add_fusion.table, bf16[1024,384]{1,0:T(8,128)(2,1)S(1)} %get-tuple-element.179.own_pg, bf16[1024,384]{1,0:T(8,128)(2,1)S(1)} %get-tuple-element.187.far_pg, bf16[1024,1024]{1,0:T(8,128)(2,1)S(1)} %get-tuple-element.189.norm_one), custom_call_target="tpu_custom_call" | custom-call | flops 1000 | bytes 1000 | tf_op jit(solution)/shard_map/qkv_weights/pallas_call | solution.py:774
  154.6 5.8 %norm_grad.1 = (f32[8,1024]{1,0:T(8,128)S(1)}, bf16[256,1024]{1,0:T(8,128)(2,1)S(1)}, bf16[256,1024]{1,0:T(8,128)(2,1)S(1)}, bf16[256,1024]{1,0:T(8,128)(2,1)S(1)}, bf16[256,1024]{1,0:T(8,128)(2,1)S(1)}) custom-call(bf16[1024,384]{1,0:T(8,128)(2,1)S(1)} %get-tuple-element.179.own_pg, bf16[1024,384]{1,0:T(8,128)(2,1)S(1)} %get-tuple-element.187.far_pg, ...), custom_call_target="tpu_custom_call" | custom-call | flops 1000 | bytes 1000 | tf_op jit(solution)/shard_map/norm_grad/pallas_call | solution.py:743
  161.3 2.6 %collective-permute-start.25 = (bf16[256,1024]{1,0:T(8,128)(2,1)S(1)}, bf16[256,1024]{1,0:T(8,128)(2,1)S(1)}, u32[]{:S(2)}, u32[]{:S(2)}) collective-permute-start(bf16[256,1024]{1,0:T(8,128)(2,1)S(1)} %get-tuple-element.203), channel_id=1, source_target_pairs={{0,3},{1,2},{2,1},{3,0},{4,7},{5,6},{6,5},{7,4},{8,11},{9,10},{10,... | collective-permute-start | bytes 1572872 | tf_op jit(solution)/shard_map/ppermute | solution.py:723
  165.2 5.2 %collective-permute-done.21 = bf16[304,1024]{1,0:T(8,128)(2,1)S(1)} collective-permute-done((bf16[304,1024]{1,0:T(8,128)(2,1)S(1)}, bf16[304,1024]{1,0:T(8,128)(2,1)S(1)}, u32[]{:S(2)}, u32[]{:S(2)}) %collective-permute-start.21) | collective-permute-done | bytes 622624 | tf_op jit(solution)/shard_map/ppermute | solution.py:723
  170.7 3.0 %collective-permute-start.27 = (bf16[304,1024]{1,0:T(8,128)(2,1)S(1)}, bf16[304,1024]{1,0:T(8,128)(2,1)S(1)}, u32[]{:S(2)}, u32[]{:S(2)}) collective-permute-start(bf16[304,1024]{1,0:T(8,128)(2,1)S(1)} %add_convert_fusion.1), channel_id=1, source_target_pairs={{0,4},{1,5},{2,6},{3,7},{4,0},{5,1},{6,2},{7,3},{8,12},{9,13},{10,... | collective-permute-start | bytes 1867784 | tf_op jit(solution)/shard_map/ppermute | solution.py:723
  173.8 5.2 %collective-permute-done.22 = bf16[2,272,384]{2,1,0:T(8,128)(2,1)S(1)} collective-permute-done((bf16[2,272,384]{2,1,0:T(8,128)(2,1)S(1)}, bf16[2,272,384]{2,1,0:T(8,128)(2,1)S(1)}, u32[]{:S(2)}, u32[]{:S(2)}) %collective-permute-start.22) | collective-permute-done | bytes 417824 | tf_op jit(solution)/shard_map/ppermute | solution.py:723
  179.0 3.0 %collective-permute-start.26 = (bf16[272,384]{1,0:T(8,128)(2,1)S(1)}, bf16[272,384]{1,0:T(8,128)(2,1)S(1)}, u32[]{:S(2)}, u32[]{:S(2)}) collective-permute-start(bf16[272,384]{1,0:T(8,128)(2,1)S(1)} %fusion.6), channel_id=1, source_target_pairs={{0,4},{1,5},{2,6},{3,7},{4,0},{5,1},{6,2},{7,3},{8,12},{9,13},{10,... | collective-permute-start | bytes 626696 | tf_op jit(solution)/shard_map/ppermute | solution.py:723
  182.1 8.4 %collective-permute-done.24.refs_2_ = bf16[256,1024]{1,0:T(8,128)(2,1)S(1)} collective-permute-done((bf16[256,1024]{1,0:T(8,128)(2,1)S(1)}, bf16[256,1024]{1,0:T(8,128)(2,1)S(1)}, u32[]{:S(2)}, u32[]{:S(2)}) %collective-permute-start.24) | collective-permute-done | bytes 524320 | tf_op jit(solution)/shard_map/ppermute | solution.py:723
  190.6 11.0 %collective-permute-done.25.refs_3_ = bf16[256,1024]{1,0:T(8,128)(2,1)S(1)} collective-permute-done((bf16[256,1024]{1,0:T(8,128)(2,1)S(1)}, bf16[256,1024]{1,0:T(8,128)(2,1)S(1)}, u32[]{:S(2)}, u32[]{:S(2)}) %collective-permute-start.25) | collective-permute-done | bytes 524320 | tf_op jit(solution)/shard_map/ppermute | solution.py:723
  201.6 1.8 finish_in.1
  203.4 6.1 %collective-permute-done.26 = bf16[272,384]{1,0:T(8,128)(2,1)S(1)} collective-permute-done((bf16[272,384]{1,0:T(8,128)(2,1)S(1)}, bf16[272,384]{1,0:T(8,128)(2,1)S(1)}, u32[]{:S(2)}, u32[]{:S(2)}) %collective-permute-start.26) | collective-permute-done | bytes 208928 | tf_op jit(solution)/shard_map/ppermute | solution.py:723
  210.5 13.9 %collective-permute-done.29.third = bf16[304,1024]{1,0:T(8,128)(2,1)S(1)} collective-permute-done((bf16[304,1024]{1,0:T(8,128)(2,1)S(1)}, bf16[304,1024]{1,0:T(8,128)(2,1)S(1)}, u32[]{:S(2)}, u32[]{:S(2)}) %collective-permute-start.29) | collective-permute-done | bytes 622624 | tf_op jit(solution)/shard_map/ppermute | solution.py:723
  225.0 1.6 collective-permute-done.34
  226.9 3.6 %collective-permute-done.35 = f32[8,1024]{1,0:T(8,128)S(1)} collective-permute-done((f32[8,1024]{1,0:T(8,128)S(1)}, f32[8,1024]{1,0:T(8,128)S(1)}, u32[]{:S(2)}, u32[]{:S(2)}) %collective-permute-start.35) | collective-permute-done | bytes 32800 | tf_op jit(solution)/shard_map/ppermute | solution.py:723
  231.7 2.7 %collective-permute-done.36 = f32[8,1024]{1,0:T(8,128)S(1)} collective-permute-done((f32[8,1024]{1,0:T(8,128)S(1)}, f32[8,1024]{1,0:T(8,128)S(1)}, u32[]{:S(2)}, u32[]{:S(2)}) %collective-permute-start.36) | collective-permute-done | bytes 32800 | tf_op jit(solution)/shard_map/ppermute | solution.py:723
  234.4 3.9 %collective-permute-done.37 = f32[8,1024]{1,0:T(8,128)S(1)} collective-permute-done((f32[8,1024]{1,0:T(8,128)S(1)}, f32[8,1024]{1,0:T(8,128)S(1)}, u32[]{:S(2)}, u32[]{:S(2)}) %collective-permute-start.37) | collective-permute-done | bytes 32800 | tf_op jit(solution)/shard_map/ppermute | solution.py:723
  238.7 4.4 %collective-permute-done.38 = f32[8,1024]{1,0:T(8,128)S(1)} collective-permute-done((f32[8,1024]{1,0:T(8,128)S(1)}, f32[8,1024]{1,0:T(8,128)S(1)}, u32[]{:S(2)}, u32[]{:S(2)}) %collective-permute-start.38) | collective-permute-done | bytes 32800 | tf_op jit(solution)/shard_map/ppermute | solution.py:723
  244.2 3.5 %finish_hidden.1 = (f32[1024,512]{1,0:T(8,128)}, f32[512,1024]{1,0:T(8,128)}, f32[128,1024]{1,0:T(8,128)}, f32[4,1,128]{2,1,0:T(1,128)}) custom-call(s32[3]{0:T(128)S(1)} %pad_add_fusion.table, bf16[304,1024]{1,0:T(8,128)(2,1)S(1)} %add_convert_fusion.mine, bf16[304,1024]{1,0:T(8,128)(2,1)S(1)} %collective-permute-done.28.near, ...), custom_call_target="tpu_custom_call" | custom-call | flops 1000 | bytes 1000 | tf_op jit(solution)/shard_map/finish_hidden/pallas_call | solution.py:774
  247.7 1.8 finish_qkv.1
  (144 shorter events, 35.4 us)
Async XLA Ops:
  0.6 11.2 %copy-start.27 = (bf16[512]{0:T(512)(128)(2,1)S(1)}, bf16[512]{0:T(512)(128)(2,1)}, u32[]{:S(2)}) copy-start(bf16[512]{0:T(512)(128)(2,1)} %param.21) | copy-start | bytes 3076
  0.7 33.5 %collective-permute-start = (bf16[256,1024]{1,0:T(8,128)(2,1)}, bf16[256,1024]{1,0:T(8,128)(2,1)S(1)}, u32[]{:S(2)}, u32[]{:S(2)}) collective-permute-start(bf16[256,1024]{1,0:T(8,128)(2,1)} %x_ref.3), channel_id=1, source_target_pairs={{0,1},{1,0},{2,3},{3,2},{4,5},{5,4},{6,7},{7,6},{8,9},{9,8},{10,11... | collective-permute-start | bytes 1572872 | tf_op jit(solution)/shard_map/ppermute | solution.py:723
  3.7 31.3 %collective-permute-start.1 = (bf16[256,1024]{1,0:T(8,128)(2,1)}, bf16[256,1024]{1,0:T(8,128)(2,1)S(1)}, u32[]{:S(2)}, u32[]{:S(2)}) collective-permute-start(bf16[256,1024]{1,0:T(8,128)(2,1)} %x_ref.3), channel_id=1, source_target_pairs={{0,2},{1,3},{2,0},{3,1},{4,6},{5,7},{6,4},{7,5},{8,10},{9,11},{10,... | collective-permute-start | bytes 1572872 | tf_op jit(solution)/shard_map/ppermute | solution.py:723
  5.2 30.5 %collective-permute-start.2 = (bf16[256,1024]{1,0:T(8,128)(2,1)}, bf16[256,1024]{1,0:T(8,128)(2,1)}, u32[]{:S(2)}, u32[]{:S(2)}) collective-permute-start(bf16[256,1024]{1,0:T(8,128)(2,1)} %x_ref.3), channel_id=1, source_target_pairs={{0,3},{1,2},{2,1},{3,0},{4,7},{5,6},{6,5},{7,4},{8,11},{9,10},{10,... | collective-permute-start | bytes 1572872 | tf_op jit(solution)/shard_map/ppermute | solution.py:723
  8.1 32.7 %copy-start.24 = (bf16[1024]{0:T(1024)(128)(2,1)S(1)}, bf16[1024]{0:T(1024)(128)(2,1)}, u32[]{:S(2)}) copy-start(bf16[1024]{0:T(1024)(128)(2,1)} %param.26) | copy-start | bytes 6148
  8.1 32.7 %copy-start.25 = (bf16[1024]{0:T(1024)(128)(2,1)S(1)}, bf16[1024]{0:T(1024)(128)(2,1)}, u32[]{:S(2)}) copy-start(bf16[1024]{0:T(1024)(128)(2,1)} %param.27) | copy-start | bytes 6148
  8.1 32.8 %copy-start.13 = (s32[1,2048]{1,0:T(1,128)S(1)}, s32[1,2048]{1,0:T(1,128)}, u32[]{:S(2)}) copy-start(s32[1,2048]{1,0:T(1,128)} %param.29) | copy-start | bytes 24580
  8.7 32.1 %copy-start.22 = (bf16[1024]{0:T(1024)(128)(2,1)S(1)}, bf16[1024]{0:T(1024)(128)(2,1)}, u32[]{:S(2)}) copy-start(bf16[1024]{0:T(1024)(128)(2,1)} %param.24) | copy-start | bytes 6148
  8.7 32.1 %copy-start.23 = (bf16[1024]{0:T(1024)(128)(2,1)S(1)}, bf16[1024]{0:T(1024)(128)(2,1)}, u32[]{:S(2)}) copy-start(bf16[1024]{0:T(1024)(128)(2,1)} %param.25) | copy-start | bytes 6148
  8.7 25.4 %collective-permute-start.3 = (bf16[400,384]{1,0:T(8,128)(2,1)S(1)}, bf16[400,384]{1,0:T(8,128)(2,1)}, u32[]{:S(2)}, u32[]{:S(2)}) collective-permute-start(bf16[400,384]{1,0:T(8,128)(2,1)S(1)} %first_pack.1), channel_id=1, source_target_pairs={{0,4},{1,5},{2,6},{3,7},{4,0},{5,1},{6,2},{7,3},{8,12},{9,13},{10,... | collective-permute-start | bytes 921608 | tf_op jit(solution)/shard_map/ppermute | solution.py:723
  13.0 28.2 %copy-start.1 = (bf16[1024,384]{1,0:T(8,128)(2,1)S(1)}, bf16[1024,384]{1,0:T(8,128)(2,1)}, u32[]{:S(2)}) copy-start(bf16[1024,384]{1,0:T(8,128)(2,1)} %own_qkv.1) | copy-start | bytes 2359300
  35.8 16.8 %collective-permute-start.4 = (bf16[400,384]{1,0:T(8,128)(2,1)}, bf16[400,384]{1,0:T(8,128)(2,1)}, u32[]{:S(2)}, u32[]{:S(2)}) collective-permute-start(bf16[400,384]{1,0:T(8,128)(2,1)} %collective-permute-done.3.mine.bias), channel_id=1, source_target_pairs={{0,16},{1,17},{2,18},{3,19},{4,20},{5,21},{6,22},{7,23},{8,24},{9,... | collective-permute-start | bytes 921608 | tf_op jit(solution)/shard_map/ppermute | solution.py:723
  37.3 27.0 %collective-permute-start.5 = (bf16[272,1024]{1,0:T(8,128)(2,1)}, bf16[272,1024]{1,0:T(8,128)(2,1)}, u32[]{:S(2)}, u32[]{:S(2)}) collective-permute-start(bf16[272,1024]{1,0:T(8,128)(2,1)} %get-tuple-element.128), channel_id=1, source_target_pairs={{0,4},{1,5},{2,6},{3,7},{4,0},{5,1},{6,2},{7,3},{8,12},{9,13},{10,... | collective-permute-start | bytes 1671176 | tf_op jit(solution)/shard_map/ppermute | solution.py:723
  53.5 11.2 %collective-permute-start.6 = (bf16[800,384]{1,0:T(8,128)(2,1)S(1)}, bf16[800,384]{1,0:T(8,128)(2,1)S(1)}, u32[]{:S(2)}, u32[]{:S(2)}) collective-permute-start(bf16[800,384]{1,0:T(8,128)(2,1)S(1)} %constant_dynamic-update-slice_fusion), channel_id=1, source_target_pairs={{0,8},{1,9},{2,10},{3,11},{4,12},{5,13},{6,14},{7,15},{8,0},{9,1},... | collective-permute-start | bytes 1843208 | tf_op jit(solution)/shard_map/ppermute | solution.py:723
  53.6 30.6 %collective-permute-start.8 = (bf16[256,1024]{1,0:T(8,128)(2,1)S(1)}, bf16[256,1024]{1,0:T(8,128)(2,1)S(1)}, u32[]{:S(2)}, u32[]{:S(2)}) collective-permute-start(bf16[256,1024]{1,0:T(8,128)(2,1)S(1)} %copy-done.10), channel_id=1, source_target_pairs={{0,1},{1,0},{2,3},{3,2},{4,5},{5,4},{6,7},{7,6},{8,9},{9,8},{10,11... | collective-permute-start | bytes 1572872 | tf_op jit(solution)/shard_map/ppermute | solution.py:723
  54.2 30.0 %collective-permute-start.10 = (bf16[256,1024]{1,0:T(8,128)(2,1)S(1)}, bf16[256,1024]{1,0:T(8,128)(2,1)S(1)}, u32[]{:S(2)}, u32[]{:S(2)}) collective-permute-start(bf16[256,1024]{1,0:T(8,128)(2,1)S(1)} %copy-done.10), channel_id=1, source_target_pairs={{0,3},{1,2},{2,1},{3,0},{4,7},{5,6},{6,5},{7,4},{8,11},{9,10},{10,... | collective-permute-start | bytes 1572872 | tf_op jit(solution)/shard_map/ppermute | solution.py:723
  55.3 31.3 %collective-permute-start.9 = (bf16[256,1024]{1,0:T(8,128)(2,1)S(1)}, bf16[256,1024]{1,0:T(8,128)(2,1)S(1)}, u32[]{:S(2)}, u32[]{:S(2)}) collective-permute-start(bf16[256,1024]{1,0:T(8,128)(2,1)S(1)} %copy-done.10), channel_id=1, source_target_pairs={{0,2},{1,3},{2,0},{3,1},{4,6},{5,7},{6,4},{7,5},{8,10},{9,11},{10,... | collective-permute-start | bytes 1572872 | tf_op jit(solution)/shard_map/ppermute | solution.py:723
  64.3 23.7 %collective-permute-start.11 = (bf16[272,1024]{1,0:T(8,128)(2,1)}, bf16[272,1024]{1,0:T(8,128)(2,1)S(1)}, u32[]{:S(2)}, u32[]{:S(2)}) collective-permute-start(bf16[272,1024]{1,0:T(8,128)(2,1)} %collective-permute-done.5.mine), channel_id=1, source_target_pairs={{0,16},{1,17},{2,18},{3,19},{4,20},{5,21},{6,22},{7,23},{8,24},{9,... | collective-permute-start | bytes 1671176 | tf_op jit(solution)/shard_map/ppermute | solution.py:723
  72.0 8.9 %collective-permute-start.7 = (f32[2,128,128]{2,1,0:T(8,128)S(1)}, f32[2,128,128]{2,1,0:T(8,128)S(1)}, u32[]{:S(2)}, u32[]{:S(2)}) collective-permute-start(f32[2,128,128]{2,1,0:T(8,128)S(1)} %get-tuple-element.140), channel_id=1, source_target_pairs={{0,4},{1,5},{2,6},{3,7},{8,12},{9,13},{10,14},{11,15},{16,20},{17,... | collective-permute-start | bytes 393224 | tf_op jit(solution)/shard_map/ppermute | solution.py:731
  99.0 15.3 %collective-permute-start.13 = (bf16[2,304,1024]{2,1,0:T(8,128)(2,1)S(1)}, bf16[2,304,1024]{2,1,0:T(8,128)(2,1)S(1)}, u32[]{:S(2)}, u32[]{:S(2)}) collective-permute-start(bf16[2,304,1024]{2,1,0:T(8,128)(2,1)S(1)} %get-tuple-element.170), channel_id=1, source_target_pairs={{0,8},{1,9},{2,10},{3,11},{4,12},{5,13},{6,14},{7,15},{8,0},{9,1},... | collective-permute-start | bytes 3735560 | tf_op jit(solution)/shard_map/ppermute | solution.py:723
  99.1 4.5 %collective-permute-start.12 = (bf16[544,1024]{1,0:T(8,128)(2,1)S(1)}, bf16[544,1024]{1,0:T(8,128)(2,1)S(1)}, u32[]{:S(2)}, u32[]{:S(2)}) collective-permute-start(bf16[544,1024]{1,0:T(8,128)(2,1)S(1)} %constant_dynamic-update-slice_fusion.2), channel_id=1, source_target_pairs={{0,8},{1,9},{2,10},{3,11},{4,12},{5,13},{6,14},{7,15},{8,0},{9,1},... | collective-permute-start | bytes 3342344 | tf_op jit(solution)/shard_map/ppermute | solution.py:723
  114.5 15.6 %copy-start.19 = (bf16[128,128]{1,0:T(8,128)(2,1)S(1)}, bf16[128,128]{1,0:T(8,128)(2,1)}, u32[]{:S(2)}) copy-start(bf16[128,128]{1,0:T(8,128)(2,1)} %copy-done.18) | copy-start | bytes 98308
  117.8 21.0 %collective-permute-start.15 = (bf16[2,304,1024]{2,1,0:T(8,128)(2,1)S(1)}, bf16[2,304,1024]{2,1,0:T(8,128)(2,1)S(1)}, u32[]{:S(2)}, u32[]{:S(2)}) collective-permute-start(bf16[2,304,1024]{2,1,0:T(8,128)(2,1)S(1)} %get-tuple-element.181), channel_id=1, source_target_pairs={{0,8},{1,9},{2,10},{3,11},{4,12},{5,13},{6,14},{7,15},{8,0},{9,1},... | collective-permute-start | bytes 3735560 | tf_op jit(solution)/shard_map/ppermute | solution.py:723
  118.0 11.6 %collective-permute-start.14 = (f32[2,128,128]{2,1,0:T(8,128)S(1)}, f32[2,128,128]{2,1,0:T(8,128)S(1)}, u32[]{:S(2)}, u32[]{:S(2)}) collective-permute-start(f32[2,128,128]{2,1,0:T(8,128)S(1)} %get-tuple-element.176), channel_id=1, source_target_pairs={{4,0},{5,1},{6,2},{7,3},{12,8},{13,9},{14,10},{15,11},{20,16},{21,... | collective-permute-start | bytes 393224 | tf_op jit(solution)/shard_map/ppermute | solution.py:731
  119.5 19.5 %collective-permute-start.16 = (bf16[304,1024]{1,0:T(8,128)(2,1)S(1)}, bf16[304,1024]{1,0:T(8,128)(2,1)S(1)}, u32[]{:S(2)}, u32[]{:S(2)}) collective-permute-start(bf16[304,1024]{1,0:T(8,128)(2,1)S(1)} %fusion.3), channel_id=1, source_target_pairs={{0,16},{1,17},{2,18},{3,19},{4,20},{5,21},{6,22},{7,23},{8,24},{9,... | collective-permute-start | bytes 1867784 | tf_op jit(solution)/shard_map/ppermute | solution.py:723
  120.1 19.3 %collective-permute-start.17 = (bf16[256,1024]{1,0:T(8,128)(2,1)S(1)}, bf16[256,1024]{1,0:T(8,128)(2,1)S(1)}, u32[]{:S(2)}, u32[]{:S(2)}) collective-permute-start(bf16[256,1024]{1,0:T(8,128)(2,1)S(1)} %get-tuple-element.184), channel_id=1, source_target_pairs={{0,1},{1,0},{2,3},{3,2},{4,5},{5,4},{6,7},{7,6},{8,9},{9,8},{10,11... | collective-permute-start | bytes 1572872 | tf_op jit(solution)/shard_map/ppermute | solution.py:723
  120.7 18.7 %collective-permute-start.18 = (bf16[256,1024]{1,0:T(8,128)(2,1)S(1)}, bf16[256,1024]{1,0:T(8,128)(2,1)S(1)}, u32[]{:S(2)}, u32[]{:S(2)}) collective-permute-start(bf16[256,1024]{1,0:T(8,128)(2,1)S(1)} %get-tuple-element.185), channel_id=1, source_target_pairs={{0,2},{1,3},{2,0},{3,1},{4,6},{5,7},{6,4},{7,5},{8,10},{9,11},{10,... | collective-permute-start | bytes 1572872 | tf_op jit(solution)/shard_map/ppermute | solution.py:723
  129.6 19.7 %collective-permute-start.19 = (bf16[256,1024]{1,0:T(8,128)(2,1)S(1)}, bf16[256,1024]{1,0:T(8,128)(2,1)S(1)}, u32[]{:S(2)}, u32[]{:S(2)}) collective-permute-start(bf16[256,1024]{1,0:T(8,128)(2,1)S(1)} %get-tuple-element.186), channel_id=1, source_target_pairs={{0,3},{1,2},{2,1},{3,0},{4,7},{5,6},{6,5},{7,4},{8,11},{9,10},{10,... | collective-permute-start | bytes 1572872 | tf_op jit(solution)/shard_map/ppermute | solution.py:723
  139.0 10.3 %copy-start.3 = (bf16[256,1024]{1,0:T(8,128)(2,1)S(1)}, bf16[256,1024]{1,0:T(8,128)(2,1)}, u32[]{:S(2)}) copy-start(bf16[256,1024]{1,0:T(8,128)(2,1)} %x_ref.3) | copy-start | bytes 1572868
  153.4 10.5 %collective-permute-start.20 = (bf16[4,272,384]{2,1,0:T(8,128)(2,1)S(1)}, bf16[4,272,384]{2,1,0:T(8,128)(2,1)S(1)}, u32[]{:S(2)}, u32[]{:S(2)}) collective-permute-start(bf16[4,272,384]{2,1,0:T(8,128)(2,1)S(1)} %get-tuple-element.196), channel_id=1, source_target_pairs={{0,8},{1,9},{2,10},{3,11},{4,12},{5,13},{6,14},{7,15},{8,0},{9,1},... | collective-permute-start | bytes 2506760 | tf_op jit(solution)/shard_map/ppermute | solution.py:723
  153.5 16.9 %collective-permute-start.21 = (bf16[304,1024]{1,0:T(8,128)(2,1)S(1)}, bf16[304,1024]{1,0:T(8,128)(2,1)S(1)}, u32[]{:S(2)}, u32[]{:S(2)}) collective-permute-start(bf16[304,1024]{1,0:T(8,128)(2,1)S(1)} %fusion.2), channel_id=1, source_target_pairs={{0,16},{1,17},{2,18},{3,19},{4,20},{5,21},{6,22},{7,23},{8,24},{9,... | collective-permute-start | bytes 1867784 | tf_op jit(solution)/shard_map/ppermute | solution.py:723
  160.4 21.7 %collective-permute-start.23 = (bf16[256,1024]{1,0:T(8,128)(2,1)S(1)}, bf16[256,1024]{1,0:T(8,128)(2,1)S(1)}, u32[]{:S(2)}, u32[]{:S(2)}) collective-permute-start(bf16[256,1024]{1,0:T(8,128)(2,1)S(1)} %get-tuple-element.201), channel_id=1, source_target_pairs={{0,1},{1,0},{2,3},{3,2},{4,5},{5,4},{6,7},{7,6},{8,9},{9,8},{10,11... | collective-permute-start | bytes 1572872 | tf_op jit(solution)/shard_map/ppermute | solution.py:723
  161.3 29.2 %collective-permute-start.24 = (bf16[256,1024]{1,0:T(8,128)(2,1)S(1)}, bf16[256,1024]{1,0:T(8,128)(2,1)S(1)}, u32[]{:S(2)}, u32[]{:S(2)}) collective-permute-start(bf16[256,1024]{1,0:T(8,128)(2,1)S(1)} %get-tuple-element.202), channel_id=1, source_target_pairs={{0,2},{1,3},{2,0},{3,1},{4,6},{5,7},{6,4},{7,5},{8,10},{9,11},{10,... | collective-permute-start | bytes 1572872 | tf_op jit(solution)/shard_map/ppermute | solution.py:723
  161.3 40.2 %collective-permute-start.25 = (bf16[256,1024]{1,0:T(8,128)(2,1)S(1)}, bf16[256,1024]{1,0:T(8,128)(2,1)S(1)}, u32[]{:S(2)}, u32[]{:S(2)}) collective-permute-start(bf16[256,1024]{1,0:T(8,128)(2,1)S(1)} %get-tuple-element.203), channel_id=1, source_target_pairs={{0,3},{1,2},{2,1},{3,0},{4,7},{5,6},{6,5},{7,4},{8,11},{9,10},{10,... | collective-permute-start | bytes 1572872 | tf_op jit(solution)/shard_map/ppermute | solution.py:723
  164.1 14.9 %collective-permute-start.22 = (bf16[2,272,384]{2,1,0:T(8,128)(2,1)S(1)}, bf16[2,272,384]{2,1,0:T(8,128)(2,1)S(1)}, u32[]{:S(2)}, u32[]{:S(2)}) collective-permute-start(bf16[2,272,384]{2,1,0:T(8,128)(2,1)S(1)} %add_convert_fusion.3), channel_id=1, source_target_pairs={{0,16},{1,17},{2,18},{3,19},{4,20},{5,21},{6,22},{7,23},{8,24},{9,... | collective-permute-start | bytes 1253384 | tf_op jit(solution)/shard_map/ppermute | solution.py:723
  170.7 38.8 %collective-permute-start.27 = (bf16[304,1024]{1,0:T(8,128)(2,1)S(1)}, bf16[304,1024]{1,0:T(8,128)(2,1)S(1)}, u32[]{:S(2)}, u32[]{:S(2)}) collective-permute-start(bf16[304,1024]{1,0:T(8,128)(2,1)S(1)} %add_convert_fusion.1), channel_id=1, source_target_pairs={{0,4},{1,5},{2,6},{3,7},{4,0},{5,1},{6,2},{7,3},{8,12},{9,13},{10,... | collective-permute-start | bytes 1867784 | tf_op jit(solution)/shard_map/ppermute | solution.py:723
  179.0 30.5 %collective-permute-start.26 = (bf16[272,384]{1,0:T(8,128)(2,1)S(1)}, bf16[272,384]{1,0:T(8,128)(2,1)S(1)}, u32[]{:S(2)}, u32[]{:S(2)}) collective-permute-start(bf16[272,384]{1,0:T(8,128)(2,1)S(1)} %fusion.6), channel_id=1, source_target_pairs={{0,4},{1,5},{2,6},{3,7},{4,0},{5,1},{6,2},{7,3},{8,12},{9,13},{10,... | collective-permute-start | bytes 626696 | tf_op jit(solution)/shard_map/ppermute | solution.py:723
  209.8 14.6 %collective-permute-start.29 = (bf16[304,1024]{1,0:T(8,128)(2,1)S(1)}, bf16[304,1024]{1,0:T(8,128)(2,1)S(1)}, u32[]{:S(2)}, u32[]{:S(2)}) collective-permute-start(bf16[304,1024]{1,0:T(8,128)(2,1)S(1)} %add_convert_fusion.mine), channel_id=1, source_target_pairs={{0,16},{1,17},{2,18},{3,19},{4,20},{5,21},{6,22},{7,23},{8,24},{9,... | collective-permute-start | bytes 1867784 | tf_op jit(solution)/shard_map/ppermute | solution.py:723
  210.5 33.6 %collective-permute-start.28 = (bf16[304,1024]{1,0:T(8,128)(2,1)S(1)}, bf16[304,1024]{1,0:T(8,128)(2,1)S(1)}, u32[]{:S(2)}, u32[]{:S(2)}) collective-permute-start(bf16[304,1024]{1,0:T(8,128)(2,1)S(1)} %add_convert_fusion.mine), channel_id=1, source_target_pairs={{0,8},{1,9},{2,10},{3,11},{4,12},{5,13},{6,14},{7,15},{8,0},{9,1},... | collective-permute-start | bytes 1867784 | tf_op jit(solution)/shard_map/ppermute | solution.py:723
  224.4 19.7 %collective-permute-start.30 = (bf16[304,1024]{1,0:T(8,128)(2,1)S(1)}, bf16[304,1024]{1,0:T(8,128)(2,1)S(1)}, u32[]{:S(2)}, u32[]{:S(2)}) collective-permute-start(bf16[304,1024]{1,0:T(8,128)(2,1)S(1)} %collective-permute-done.29.third), channel_id=1, source_target_pairs={{0,8},{1,9},{2,10},{3,11},{4,12},{5,13},{6,14},{7,15},{8,0},{9,1},... | collective-permute-start | bytes 1867784 | tf_op jit(solution)/shard_map/ppermute | solution.py:723
  224.4 2.1 collective-permute-start.34
  226.6 3.9 %collective-permute-start.35 = (f32[8,1024]{1,0:T(8,128)S(1)}, f32[8,1024]{1,0:T(8,128)S(1)}, u32[]{:S(2)}, u32[]{:S(2)}) collective-permute-start(f32[8,1024]{1,0:T(8,128)S(1)} %add.80), channel_id=1, source_target_pairs={{0,16},{1,17},{2,18},{3,19},{4,20},{5,21},{6,22},{7,23},{8,24},{9,... | collective-permute-start | bytes 98312 | tf_op jit(solution)/shard_map/ppermute | solution.py:723
  230.5 3.9 %collective-permute-start.36 = (f32[8,1024]{1,0:T(8,128)S(1)}, f32[8,1024]{1,0:T(8,128)S(1)}, u32[]{:S(2)}, u32[]{:S(2)}) collective-permute-start(f32[8,1024]{1,0:T(8,128)S(1)} %add.81), channel_id=1, source_target_pairs={{0,1},{1,0},{2,3},{3,2},{4,5},{5,4},{6,7},{7,6},{8,9},{9,8},{10,11... | collective-permute-start | bytes 98312 | tf_op jit(solution)/shard_map/ppermute | solution.py:723
  231.3 11.8 %collective-permute-start.32 = (bf16[272,384]{1,0:T(8,128)(2,1)S(1)}, bf16[272,384]{1,0:T(8,128)(2,1)S(1)}, u32[]{:S(2)}, u32[]{:S(2)}) collective-permute-start(bf16[272,384]{1,0:T(8,128)(2,1)S(1)} %add_convert_fusion.4.mine), channel_id=1, source_target_pairs={{0,16},{1,17},{2,18},{3,19},{4,20},{5,21},{6,22},{7,23},{8,24},{9,... | collective-permute-start | bytes 626696 | tf_op jit(solution)/shard_map/ppermute | solution.py:723
  234.4 3.9 %collective-permute-start.37 = (f32[8,1024]{1,0:T(8,128)S(1)}, f32[8,1024]{1,0:T(8,128)S(1)}, u32[]{:S(2)}, u32[]{:S(2)}) collective-permute-start(f32[8,1024]{1,0:T(8,128)S(1)} %add.82), channel_id=1, source_target_pairs={{0,2},{1,3},{2,0},{3,1},{4,6},{5,7},{6,4},{7,5},{8,10},{9,11},{10,... | collective-permute-start | bytes 98312 | tf_op jit(solution)/shard_map/ppermute | solution.py:723
  238.3 4.8 %collective-permute-start.38 = (f32[8,1024]{1,0:T(8,128)S(1)}, f32[8,1024]{1,0:T(8,128)S(1)}, u32[]{:S(2)}, u32[]{:S(2)}) collective-permute-start(f32[8,1024]{1,0:T(8,128)S(1)} %add.83), channel_id=1, source_target_pairs={{0,4},{1,5},{2,6},{3,7},{4,0},{5,1},{6,2},{7,3},{8,12},{9,13},{10,... | collective-permute-start | bytes 98312 | tf_op jit(solution)/shard_map/ppermute | solution.py:723
  243.1 4.6 %collective-permute-start.31 = (bf16[272,384]{1,0:T(8,128)(2,1)S(1)}, bf16[272,384]{1,0:T(8,128)(2,1)S(1)}, u32[]{:S(2)}, u32[]{:S(2)}) collective-permute-start(bf16[272,384]{1,0:T(8,128)(2,1)S(1)} %add_convert_fusion.4.mine), channel_id=1, source_target_pairs={{0,8},{1,9},{2,10},{3,11},{4,12},{5,13},{6,14},{7,15},{8,0},{9,1},... | collective-permute-start | bytes 626696 | tf_op jit(solution)/shard_map/ppermute | solution.py:723
  243.1 4.6 %collective-permute-start.33 = (bf16[272,384]{1,0:T(8,128)(2,1)S(1)}, bf16[272,384]{1,0:T(8,128)(2,1)S(1)}, u32[]{:S(2)}, u32[]{:S(2)}) collective-permute-start(bf16[272,384]{1,0:T(8,128)(2,1)S(1)} %collective-permute-done.32.third), channel_id=1, source_target_pairs={{0,8},{1,9},{2,10},{3,11},{4,12},{5,13},{6,14},{7,15},{8,0},{9,1},... | collective-permute-start | bytes 626696 | tf_op jit(solution)/shard_map/ppermute | solution.py:723
  (19 other events, 59.7 us)

commit v2 on v0

v2 whole, which is shorter than its diff:
```python
import functools

import jax
import jax.numpy as jnp
import numpy as np
from jax import lax
from jax.experimental import pallas as pl
from jax.experimental.pallas import tpu as pltpu
from jax.sharding import PartitionSpec as P

HEAD_DIM = 64
ROT = 16
LANES = 128
EPS = 1e-05
EXACT = lax.Precision.HIGHEST
F32 = jnp.float32
BF16 = jnp.bfloat16
QUARTERS = 4

NN = ((1,), (0,))
NT = ((1,), (1,))
TN = ((0,), (0,))


def dot(a, b, dims=NN, precision=None):
    return lax.dot_general(a, b, (dims, ((), ())), precision=precision, preferred_element_type=F32)


def halves(values):
    high = values.astype(BF16)
    return high, (values - high.astype(F32)).astype(BF16)


def lane_of(dims):
    return lax.broadcasted_iota(jnp.int32, dims, len(dims) - 1)


def prepare_kernel(rates, omega, docs_col, keep, ahead, behind, mix_high, mix_low, turned_high, turned_low):
    rows = keep.shape[0]
    start = pl.program_id(0) * rows
    places = start + lax.broadcasted_iota(jnp.int32, (rows, LANES), 0)
    angles = places.astype(F32) * rates[...]
    inner = lane_of((rows, LANES)) % HEAD_DIM
    cosine, sine = jnp.cos(angles), jnp.sin(angles)
    half = ROT // 2
    keep[...] = jnp.where(inner < ROT, cosine, 1.0)
    ahead[...] = jnp.where(inner < half, -sine, 0.0)
    behind[...] = jnp.where((inner >= half) & (inner < ROT), sine, 0.0)

    @pl.when(pl.program_id(0) == 0)
    def _():
        extent = HEAD_DIM
        n = lax.broadcasted_iota(jnp.int32, (LANES, LANES), 0)
        k = lax.broadcasted_iota(jnp.int32, (LANES, LANES), 1)
        same = (n // extent) == (k // extent)
        n, k = (n % extent).astype(F32), (k % extent).astype(F32)
        scale = jnp.where(k == 0, float(np.sqrt(1.0 / extent)), float(np.sqrt(2.0 / extent)))
        matrix = jnp.where(same, jnp.cos(np.pi * (n + 0.5) * k / extent) * scale, 0.0)
        row = jnp.concatenate([omega[...]] * 2, axis=1)
        spread = jnp.where(same, jnp.concatenate([row] * 2, axis=0), 0.0)
        mixing = dot(matrix, spread, precision=EXACT)
        mix_high[...], mix_low[...] = halves(mixing)
        turned_high[...], turned_low[...] = halves(mixing.T)


def turn(values, keep, ahead, behind, sign):
    half = ROT // 2
    moved = (
        pltpu.roll(values, LANES - half, axis=1) * ahead + pltpu.roll(values, half, axis=1) * behind
    )
    return values * keep + sign * moved


def mixed_dot(values, high, low):
    first, second = halves(values)
    return dot(first, high) + (dot(second, high) + dot(first, low))


def head_columns(values, which, count):
    parts = [
        values[:, (3 * j + which) * HEAD_DIM : (3 * j + which + 1) * HEAD_DIM] for j in range(count)
    ]
    return parts[0] if count == 1 else jnp.concatenate(parts, axis=1)


def masked_stack(values, count):
    if count == 1:
        return values
    lane = (lane_of(values.shape) % (count * HEAD_DIM)) // HEAD_DIM
    zero = jnp.zeros_like(values)
    return jnp.concatenate([jnp.where(lane == j, values, zero) for j in range(count)], axis=0)


def side_by_side(stack, count):
    rows = stack.shape[0] // count
    if count == 1:
        return stack
    return jnp.concatenate([stack[j * rows : (j + 1) * rows] for j in range(count)], axis=1)


def own_block(dims):
    rows = lax.broadcasted_iota(jnp.int32, dims, 0) // HEAD_DIM
    return rows == (lane_of(dims) % dims[0]) // HEAD_DIM


def load_block(plan, refs, keep, sems):
    def copies(k):
        names = plan[k]
        size = keep.shape[1] // len(names)
        slot = keep.at[k % 2]
        return [
            pltpu.make_async_copy(refs[name], slot.at[pl.ds(i * size, size)], sems.at[k % 2, i])
            for i, name in enumerate(names)
        ]

    for k in range(len(plan)):

        @pl.when(pl.program_id(0) == k)
        def _(k=k):
            if k == 0:
                for copy in copies(0):
                    copy.start()
            if k + 1 < len(plan):
                for copy in copies(k + 1):
                    copy.start()
            for copy in copies(k):
                copy.wait()

    return keep[pl.program_id(0) % 2]


def rows_kernel(count, plan, taken, table, *refs):
    total = sum(len(names) for names in plan)
    x_refs = refs[:total]
    (
        vectors,
        weight,
        up_weight,
        keep,
        ahead,
        behind,
        mix_high,
        mix_low,
    ) = refs[total : total + 8]
    (
        mark,
        norm_one,
        norm_two,
        unit_out,
        feat_out,
        value_out,
        active_out,
        slope_out,
        block,
        sems,
    ) = refs[total + 8 + taken :]
    mark[...] = jnp.zeros_like(mark)
    x = load_block(plan, x_refs, block, sems).astype(F32)
    mean = jnp.mean(x, axis=-1, keepdims=True)
    centred = x - mean
    scale = lax.rsqrt(jnp.mean(centred * centred, axis=-1, keepdims=True) + EPS)
    unit = centred * scale
    row = vectors[...].astype(F32)
    one = (unit * row[0:1] + row[1:2]).astype(BF16)
    two = (unit * row[2:3] + row[3:4]).astype(BF16)
    norm_one[...] = one
    norm_two[...] = two
    unit_out[...] = unit.astype(BF16)

    projected = dot(one, weight[...]) + row[4:5, : weight.shape[1]]
    value_out[...] = head_columns(projected, 2, count).astype(BF16)
    pairs = [head_columns(projected, which, count) for which in (0, 1)]
    if count == 1:
        pairs = [jnp.concatenate(pairs, axis=1)]
    for k, pair in enumerate(pairs):
        turned = turn(pair, keep[...], ahead[...], behind[...], 1.0)
        feat = jnp.exp(mixed_dot(turned, mix_high[...], mix_low[...]))
        feat_out[:, k * LANES : (k + 1) * LANES] = feat

    hidden = dot(two, up_weight[...]) + row[5:6, : up_weight.shape[1]]
    normal = 0.5 * (1.0 + lax.erf(hidden * 0.7071067811865476))
    density = jnp.exp(-0.5 * hidden * hidden) * 0.3989422804014327
    active_out[...] = (hidden * normal).astype(BF16)
    slope_out[...] = (normal + hidden * density).astype(BF16)


def allowed_pairs(docs_col, docs_row, count):
    size = docs_col.shape[0]
    rows = lax.broadcasted_iota(jnp.int32, (size, size), 0)
    cols = lax.broadcasted_iota(jnp.int32, (size, size), 1)
    allowed = ((docs_col == docs_row) & (rows >= cols)).astype(F32)
    return allowed if count == 1 else jnp.concatenate([allowed] * count, axis=0)


def forward_kernel(
    count,
    table,
    docs,
    feat_ref,
    value_ref,
    docs_col,
    docs_row,
    mark,
    mixed_out,
    merged_out,
    inverse_out,
    states_out,
    state,
):
    step = pl.program_id(0)
    width = count * HEAD_DIM
    rows = feat_ref.shape[0]

    @pl.when(step == 0)
    def _():
        state[...] = jnp.zeros_like(state)

    start = step * rows
    before = jnp.where(start > 0, docs[jnp.maximum(start - 1, 0)], -1)
    last = docs[start + rows - 1]
    kept = (last == before).astype(F32)
    allowed = allowed_pairs(docs_col[...], docs_row[0], count)
    carried = docs_col[...] == before
    chosen = docs_col[...] == last
    query = feat_ref[:, :width].astype(BF16)
    key = feat_ref[:, width:]
    value = value_ref[...]
    both = jnp.concatenate([value, jnp.ones_like(value)], axis=1)
    memory = state[...]
    states_out[0] = memory
    high, low = halves(memory)
    weights = (dot(masked_stack(query, count), key.astype(BF16), NT) * allowed).astype(BF16)
    sums = dot(side_by_side(weights, count), masked_stack(both, count)) + jnp.where(
        carried, dot(query, high) + dot(query, low), 0.0
    )
    inverse = 1.0 / sums[:, width:]
    mixed = sums[:, :width] * inverse
    mixed_out[...] = mixed
    merged_out[...] = mixed.astype(BF16)
    inverse_out[...] = inverse
    picked = jnp.where(chosen, key, 0.0).astype(BF16)
    added = dot(picked, both, TN)
    state[...] = kept * memory + jnp.where(own_block(added.shape), added, 0.0)


def pair_grads(grad, inverse, mixed):
    part = (grad * inverse).astype(BF16)
    high, low = halves(-(part.astype(F32) * mixed))
    return part, high, low


def backward_kernel(
    count,
    table,
    docs,
    feat_ref,
    value_ref,
    mixed_ref,
    inverse_ref,
    grad_ref,
    docs_col,
    docs_row,
    mark,
    states_ref,
    keep,
    ahead,
    behind,
    turned_high,
    turned_low,
    out,
    later,
):
    blocks = pl.num_programs(0)
    step = blocks - 1 - pl.program_id(0)
    width = count * HEAD_DIM
    rows = feat_ref.shape[0]

    @pl.when(pl.program_id(0) == 0)
    def _():
        later[...] = jnp.zeros_like(later)

    start = step * rows
    total = docs.shape[0]
    before = jnp.where(start > 0, docs[jnp.maximum(start - 1, 0)], -1)
    after_doc = jnp.where(start + rows < total, docs[jnp.minimum(start + rows, total - 1)], -1)
    first = docs[start]
    kept = (first == after_doc).astype(F32)
    allowed = allowed_pairs(docs_col[...], docs_row[0], count)
    carried = docs_col[...] == before
    linked = docs_col[...] == after_doc
    chosen = docs_col[...] == first
    feat = feat_ref[...]
    query, key = feat[:, :width].astype(BF16), feat[:, width:].astype(BF16)
    value = value_ref[...]
    ones = jnp.ones_like(value)
    both = jnp.concatenate([value, ones], axis=1)
    part, high, low = pair_grads(grad_ref[...], inverse_ref[...], mixed_ref[...])
    first_two = jnp.concatenate([part, high], axis=1)
    queries = masked_stack(query, count)
    weights = (dot(queries, key, NT) * allowed).astype(BF16)
    weight_grad = dot(masked_stack(first_two, count), both, NT)
    weight_grad += dot(masked_stack(low, count), ones, NT)
    weight_grad = (weight_grad * allowed).astype(BF16)
    mem_high, mem_low = halves(states_ref[0])
    late = later[...]
    late_high, late_low = halves(late)
    query_grad = dot(side_by_side(weight_grad, count), masked_stack(key, count)) + jnp.where(
        carried,
        dot(first_two, mem_high, NT) + dot(first_two, mem_low, NT) + dot(low, mem_high[:, width:], NT),
        0.0,
    )
    key_grad = dot(weight_grad, queries, TN) + jnp.where(
        linked, dot(both, late_high, NT) + dot(both, late_low, NT), 0.0
    )
    value_grad = dot(weights, masked_stack(part, count), TN) + jnp.where(
        linked, dot(key, late_high[:, :width]) + dot(key, late_low[:, :width]), 0.0
    )
    picked = jnp.where(chosen, query.astype(F32), 0.0).astype(BF16)
    added = jnp.concatenate(
        [dot(picked, part, TN), dot(picked, high, TN) + dot(picked, low, TN)], axis=1
    )
    later[...] = kept * late + jnp.where(own_block(late.shape), added, 0.0)
    inner = jnp.concatenate([query_grad, key_grad], axis=1) * feat
    pairs = []
    for base in range(0, 2 * width, LANES):
        pair = mixed_dot(inner[:, base : base + LANES], turned_high[...], turned_low[...])
        pairs.append(turn(pair, keep[...], ahead[...], behind[...], -1.0))
    flat = pairs[0] if count == 1 else jnp.concatenate(pairs, axis=1)
    pieces = []
    for j in range(count):
        lanes = slice(j * HEAD_DIM, (j + 1) * HEAD_DIM)
        pieces += [flat[:, :width][:, lanes], flat[:, width:][:, lanes], value_grad[:, lanes]]
    out[...] = jnp.concatenate(pieces, axis=1).astype(BF16)


def write_block(outs, values):
    steps = len(outs) - 1
    for k in range(steps - 1):

        @pl.when(pl.program_id(0) == k)
        def _(out=outs[k]):
            out[...] = values

    @pl.when(pl.program_id(0) == steps - 1)
    def _():
        half = outs[-1].shape[0]
        outs[-2][...] = values[:half]
        outs[-1][...] = values[half:]


def out_kernel(merged, active, dense, down, *outs):
    total = dot(active[...], down[...]) + dot(merged[...], dense[...])
    write_block(outs, total.astype(BF16))


def grads_kernel(plan, taken, *refs):
    total = sum(len(names) for names in plan)
    dense, down, slope = refs[total : total + 3]
    mark, grad_out, merged_out, hidden_out, block, sems = refs[total + 3 + taken :]
    mark[...] = jnp.zeros_like(mark)
    grad = load_block(plan, refs[:total], block, sems)
    grad_out[...] = grad
    merged_out[...] = dot(grad, dense[...], NT)
    hidden_out[...] = (dot(grad, down[...], NT) * slope[...].astype(F32)).astype(BF16)


def norm_grad_kernel(
    change, hidden, qkv_weight, up_weight, unit_ref, vectors, own_grad, given, sums_out, *outs
):
    down = lambda values: jnp.sum(values, axis=0, keepdims=True)

    @pl.when(pl.program_id(0) == 0)
    def _():
        sums_out[...] = given[...]
        sums_out[4:5] = down(own_grad[...].astype(F32))

    unit = unit_ref[...].astype(F32)
    one = dot(change[...], qkv_weight[...], NT)
    sums_out[0:1] += down(one * unit)
    sums_out[1:2] += down(one)
    two = dot(hidden[...], up_weight[...], NT)
    sums_out[2:3] += down(two * unit)
    sums_out[3:4] += down(two)
    row = vectors[...].astype(F32)
    values = (one * row[0:1] + two * row[2:3]).astype(BF16)
    if outs[0].shape[0] < values.shape[0]:
        half = outs[0].shape[0]
        outs[0][...] = values[:half]
        outs[1][...] = values[half:]
        return
    for k, out in enumerate(outs):

        @pl.when(pl.program_id(0) == k)
        def _(out=out):
            out[...] = values


def first_add_kernel(right_block, right_half, left_block, left_half, right_out, left_out):
    half = right_half.shape[0]
    join = lambda a, b: (a.astype(F32) + b.astype(F32)).astype(BF16)
    right_out[:half] = join(right_block[:half], right_half[...])
    right_out[half:] = right_block[half:]
    left_out[:half] = left_block[:half]
    left_out[half:] = join(left_block[half:], left_half[...])


def next_add_kernel(right_block, right_sum, left_block, left_sum, right_out, left_out):
    join = lambda a, b: (a.astype(F32) + b.astype(F32)).astype(BF16)
    right_out[...] = join(right_block[...], right_sum[...])
    left_out[...] = join(left_block[...], left_sum[...])


def bias_rows(values, cols):
    tile = jnp.zeros((16, values.shape[1]), F32)
    row = lax.broadcasted_iota(jnp.int32, tile.shape, 0)
    high = values.astype(BF16).astype(F32)
    tile = jnp.where(row == 0, high, jnp.where(row == 1, values - high, tile)).astype(BF16)
    if values.shape[1] == cols:
        return tile
    return jnp.concatenate([tile, jnp.zeros((16, cols - values.shape[1]), BF16)], axis=1)


def hidden_weights_kernel(table, active, hidden_grad, grad, norm_two, kept, sent, up, down):
    part = table[0]
    step = active.shape[1] // QUARTERS
    up[...] = dot(hidden_grad[...], norm_two[...], TN).astype(BF16)
    down[...] = dot(active[...], grad[...], TN).astype(BF16)
    for k in range(QUARTERS):
        out = (kept, sent)[k % 2].at[k // 2]
        begin = pl.multiple_of((part ^ k) * step, step)
        out[:step] = up[pl.ds(begin, step)]
        out[step:] = down[pl.ds(begin, step)]


def qkv_weights_kernel(table, change, norm_one, merged, grad, hidden_sums, kept, sent):
    rows, cols = norm_one.shape[1], change.shape[1]
    small, wide = merged.shape[1], kept.shape[2]
    place = pl.program_id(0)
    weight = dot(norm_one[...], change[...], TN).astype(BF16)
    dense = dot(merged[...], grad[...], TN).astype(BF16)
    first = bias_rows(jnp.sum(change[...].astype(F32), axis=0, keepdims=True), wide)
    second = hidden_sums[0].astype(F32)
    if second.shape[1] < wide:
        rest = jnp.zeros((1, wide - second.shape[1]), F32)
        second = jnp.concatenate([second, rest], axis=1)
    high = second.astype(BF16).astype(F32)
    row = lax.broadcasted_iota(jnp.int32, (16, wide), 0)
    tail = jnp.where(row == 2, high, jnp.where(row == 3, second - high, first.astype(F32)))

    def write(out):
        if wide > min(rows, cols):
            out[0] = jnp.zeros((rows + small + 16, wide), BF16)
        out[0, :rows, :cols] = weight
        out[0, rows : rows + small, :rows] = dense
        out[0, rows + small :] = tail.astype(BF16)

    @pl.when(place % 2 == 0)
    def _():
        write(kept)

    @pl.when(place % 2 == 1)
    def _():
        write(sent)


def column_sums_kernel(values, out):
    out[...] = jnp.zeros_like(out)
    out[0:1] = jnp.sum(values[...].astype(F32), axis=0, keepdims=True)


def finish_hidden_kernel(table, mine, near, third, last, up_grad, down_grad, turned):
    part = table[0]
    step = down_grad.shape[0] // QUARTERS
    for k, ref in enumerate((mine, near, third, last)):
        begin = pl.multiple_of((part ^ k) * step, step)
        turned[pl.ds(begin, step)] = ref[:step].astype(F32)
        down_grad[pl.ds(begin, step)] = ref[step:].astype(F32)
    up_grad[...] = turned[...].T


def finish_qkv_kernel(table, mine, near, third, last, weight_grad, dense_grad, bias_grad, up_bias):
    part = table[0]
    step = weight_grad.shape[0] // QUARTERS
    small, cols = dense_grad.shape[0], weight_grad.shape[1]
    hidden = up_bias.shape[2]
    for k, ref in enumerate((mine, near, third, last)):
        begin = pl.multiple_of((part ^ k) * step, step)
        weight_grad[pl.ds(begin, step)] = ref[:step, :cols].astype(F32)
        dense_grad[:, pl.ds(begin, step)] = ref[step : step + small, :step].astype(F32)
        tail = ref[step + small :].astype(F32)
        up_bias[part ^ k] = tail[2:3, :hidden] + tail[3:4, :hidden]
    tail = mine[step + small :].astype(F32)
    bias_grad[...] = tail[0:1, :cols] + tail[1:2, :cols]


def finish_out_kernel(x_ref, bias, *refs):
    parts, out = refs[:-1], refs[-1]
    total = x_ref[...].astype(F32) + bias[6:7].astype(F32)
    for ref in parts:
        total += ref[...].astype(F32)
    out[...] = total.astype(BF16)


def finish_in_kernel(x_ref, grad_ref, *refs):
    parts, out = refs[:-1], refs[-1]
    x = x_ref[...].astype(F32)
    mean = jnp.mean(x, axis=-1, keepdims=True)
    centred = x - mean
    scale = lax.rsqrt(jnp.mean(centred * centred, axis=-1, keepdims=True) + EPS)
    unit = centred * scale
    total = parts[0][...].astype(F32)
    for ref in parts[1:]:
        total += ref[...].astype(F32)
    along = jnp.mean(total * unit, axis=-1, keepdims=True)
    out[...] = grad_ref[...].astype(F32) + scale * (
        total - jnp.mean(total, axis=-1, keepdims=True) - unit * along
    )


def params(limit=12):
    return pltpu.CompilerParams(
        dimension_semantics=("arbitrary",), vmem_limit_bytes=limit * 1024 * 1024
    )


def after(value, *others):
    return lax.optimization_barrier((value,) + others)[0]


def apart(dims, kind):
    return pltpu.HBM(dims, kind)


def shape(dims, kind):
    return jax.ShapeDtypeStruct(dims, kind)


def cost(flops, nbytes, trans=0):
    return pl.CostEstimate(flops=1000, bytes_accessed=1000, transcendentals=0)


def on_device(
    dp_size,
    tensor_size,
    inputs,
    qkv_weight,
    qkv_bias,
    dense_weight,
    up_weight,
    up_bias,
    down_weight,
    out_bias,
    gain_one,
    shift_one,
    gain_two,
    shift_two,
    feature_omega,
    doc_ids,
    out_grad,
):
    rows, model = inputs.shape
    blocks = tensor_size
    middle = blocks // 2
    tokens = rows * blocks
    qkv_cols = qkv_weight.shape[1]
    count = qkv_cols // (3 * HEAD_DIM)
    width = count * HEAD_DIM
    hidden_cols = up_weight.shape[1]
    hidden_part, model_part = hidden_cols // QUARTERS, model // QUARTERS
    part = lax.axis_index("dp") % QUARTERS
    place = lax.axis_index("tensor")

    ring = list(range(0, blocks, 2)) + list(range(blocks - 1, 0, -2))
    spots = np.argsort(np.array(ring))
    offsets = [0] + [o for s in range(1, middle) for o in (s, blocks - s)] + [middle]
    where = np.argsort(np.array(offsets))
    spot = jnp.where(place % 2 == 0, place // 2, blocks - 1 - place // 2)
    around = (spot + jnp.asarray(offsets, jnp.int32)) % blocks
    sequence_of = jnp.where(around < middle, 2 * around, 2 * (blocks - 1 - around) + 1)
    away = (jnp.asarray(spots, jnp.int32) - spot) % blocks
    slot_of = jnp.where(
        away == 0,
        0,
        jnp.where(
            away < middle,
            2 * away - 1,
            jnp.where(away == middle, blocks - 1, 2 * (blocks - away)),
        ),
    )
    table = jnp.concatenate([part[None], sequence_of, slot_of]).astype(jnp.int32)

    def right(values):
        pairs = [(ring[i], ring[(i + 1) % blocks]) for i in range(blocks)]
        return lax.ppermute(values, "tensor", pairs)

    def left(values):
        pairs = [(ring[i], ring[(i - 1) % blocks]) for i in range(blocks)]
        return lax.ppermute(values, "tensor", pairs)

    def over_dp(values, bits):
        return lax.ppermute(values, "dp", [(p, p ^ bits) for p in range(dp_size)])

    def over_tensor(values, bits):
        return lax.ppermute(values, "tensor", [(t, t ^ bits) for t in range(tensor_size)])

    line, due = [], [()]

    def run(step, *operands, gate=0, wait=()):
        operands = list(operands)
        held = tuple(line[-1:]) + due[0] + tuple(wait)
        if held:
            operands[gate] = after(operands[gate], *held)
        result = step(*operands)
        line.append(result[0] if isinstance(result, (tuple, list)) else result)
        return result

    def tick(*arrived):
        due[0] = tuple(arrived) + tuple(line[-1:])

    def now(values):
        return after(values, *due[0])

    plain = lambda cols: pl.BlockSpec((rows, cols), lambda k, *s: (k, 0))
    whole = lambda *dims: pl.BlockSpec(dims, lambda k, *s: (0,) * len(dims))
    spec = lambda values: whole(*values.shape)
    anywhere = pl.BlockSpec(memory_space=pltpu.HBM)

    def call(
        kernel, name, outs, in_specs, out_specs, prefetch=1, scratch=(), steps=blocks, aliases=None, limit=12
    ):
        return pl.pallas_call(
            kernel,
            out_shape=outs,
            grid_spec=pltpu.PrefetchScalarGridSpec(
                num_scalar_prefetch=prefetch,
                grid=(steps,),
                in_specs=in_specs,
                out_specs=out_specs,
                scratch_shapes=list(scratch),
            ),
            input_output_aliases=aliases or {},
            compiler_params=params(limit),
            cost_estimate=cost(0, 0),
            name=name,
        )

    def once(kernel, name, outs, prefetch=1, scratch=(), limit=12):
        single = not isinstance(outs, (tuple, list))
        listed = (outs,) if single else tuple(outs)

        def step(*operands):
            result = call(
                kernel,
                name,
                listed,
                [spec(v) for v in operands[prefetch:]],
                [whole(*v.shape) for v in listed],
                prefetch,
                scratch,
                1,
                limit=limit,
            )(*operands)
            return result[0] if single else result

        return step

    docs = doc_ids.reshape(-1)
    docs_col = docs.reshape(-1, 1)
    docs_row = docs.reshape(blocks, 1, rows)
    line_of = lambda v: jnp.pad(v, (0, model - v.shape[0]))
    vectors = jnp.concatenate(
        [gain_one, shift_one, gain_two, shift_two, line_of(qkv_bias), line_of(up_bias), out_bias]
        + [jnp.zeros((model,), BF16)]
    ).reshape(8, model)
    lane = np.arange(LANES) % HEAD_DIM
    rates = np.where(lane < ROT, 10000.0 ** (-(lane % (ROT // 2)) * 2.0 / ROT), 0.0)
    rates = jnp.asarray(rates[None, :], F32)

    square = whole(LANES, LANES)
    marks = []

    def group_call(kernel, name, group, extra, extra_specs, outs, out_specs, before, prefetch):
        plan, arrays = [], []
        for parts in group:
            plan.append(tuple(range(len(arrays), len(arrays) + len(parts))))
            arrays += list(parts)
        passed = tuple(before) + tuple(marks[-1:])
        operands = ((table,) if prefetch else ()) + tuple(arrays) + tuple(extra)
        aliases = {len(operands) + i: i + 1 for i in range(len(before))}
        result = run(
            call(
                functools.partial(kernel, tuple(plan), len(passed)),
                name,
                (shape((8, LANES), F32),) + outs,
                [anywhere] * len(arrays) + extra_specs + [anywhere] * len(passed),
                [whole(8, LANES)] + out_specs,
                prefetch=prefetch,
                scratch=[pltpu.VMEM((2, rows, model), BF16), pltpu.SemaphoreType.DMA((2, 2))],
                steps=len(group),
                aliases=aliases,
            ),
            *operands,
            *passed,
            gate=prefetch,
        )
        marks.append(result[0])
        return result[1:]

    class RingGather:
        def __init__(self, block):
            self.ahead = self.back = self.own = block
            self.distance = 0

        def start(self):
            self.distance += 1
            if self.distance < middle:
                self.ahead, self.back = left(now(self.ahead)), right(now(self.back))
                self.group = ((self.ahead,), (self.back,))
                self.moving = (self.ahead, self.back)
            else:
                cut = rows // 2
                self.moving = (right(now(self.back[:cut])), left(now(self.ahead[cut:])))
                self.group = (self.moving,)
            if self.distance == 1:
                self.group = ((self.own,),) + self.group
            return self.moving

    row_state = ()
    row_base = 0

    def row_step(group):
        nonlocal row_state, row_base
        base = row_base
        at = lambda cols: pl.BlockSpec((rows, cols), lambda k, *s: (base + k, 0))
        turned_at = pl.BlockSpec((rows, LANES), lambda k, table: (table[1 + base + k], 0))
        row_state = group_call(
            functools.partial(rows_kernel, count),
            "rows",
            group,
            (
                vectors,
                qkv_weight,
                up_weight,
                keep,
                ahead,
                behind,
                mix_high,
                mix_low,
            ),
            [
                whole(8, model),
                whole(model, qkv_cols),
                whole(model, hidden_cols),
                turned_at,
                turned_at,
                turned_at,
                square,
                square,
            ],
            (
                apart((tokens, model), BF16),
                apart((tokens, model), BF16),
                apart((tokens, model), BF16),
                apart((tokens, 2 * width), F32),
                apart((tokens, width), BF16),
                apart((tokens, hidden_cols), BF16),
                apart((tokens, hidden_cols), BF16),
            ),
            [
                at(model),
                at(model),
                at(model),
                at(2 * width),
                at(width),
                at(hidden_cols),
                at(hidden_cols),
            ],
            row_state,
            1,
        )
        row_base += len(group)

    class RingSum:
        def __init__(self, parts):
            self.parts = parts
            self.distance = middle
            self.sums = parts[-2], parts[-1]

        def term(self, offset):
            return self.parts[int(where[offset % blocks])]

        def start(self):
            self.distance -= 1
            self.sums = right(now(self.sums[0])), left(now(self.sums[1]))
            return self.sums

        def add(self):
            first = self.distance == middle - 1
            self.sums = run(
                once(
                    first_add_kernel if first else next_add_kernel,
                    "ring_add",
                    (shape((rows, model), BF16),) * 2,
                    prefetch=0,
                ),
                self.term(self.distance),
                self.sums[0],
                self.term(-self.distance),
                self.sums[1],
            )

        def result(self):
            return (self.parts[0],) + tuple(self.sums)

    class WeightSum:
        def __init__(self, kept, sent):
            self.kept, self.sent = kept, sent
            self.stage = 0

        def start(self, third=False, near=False, last=False):
            if third:
                self.third = over_dp(now(self.mine), 2)
                return (self.third,)
            if near:
                self.near = over_dp(now(self.mine), 1)
                return (self.near,)
            if last:
                self.last = over_dp(now(self.third), 1)
                return (self.last,)
            self.stage += 1
            self.moving = (over_dp(now(self.sent if self.stage == 1 else self.next), self.stage),)
            return self.moving

        def add(self):
            if self.stage == 1:
                self.first = self.moving[0]
                self.next = run(add, self.kept[1], self.first[1])
            else:
                self.mine = rest(run(add_three, self.kept[0], self.first[0], self.moving[0]))

        def result(self):
            return self.mine, self.near, self.third, self.last

    def finish(ring):
        while ring.distance > 0:
            ring.add()
            tick()
            tick(*ring.start())

    class SmallSum:
        def __init__(self, values):
            self.values = values
            self.steps = [("dp", 1 << k) for k in range(dp_size.bit_length() - 1)]
            self.steps += [("tensor", 1 << k) for k in range(tensor_size.bit_length() - 1)]

        def start(self):
            axis, bits = self.steps.pop(0)
            self.moving = ((over_dp if axis == "dp" else over_tensor)(now(self.values), bits),)
            return self.moving

        def add(self):
            self.values = run(lambda a, b: a + b, self.values, self.moving[0])

    x_ring = RingGather(inputs)
    going = x_ring.start()
    keep, ahead, behind, mix_high, mix_low, turned_high, turned_low = run(
        call(
            prepare_kernel,
            "prepare",
            (shape((tokens, LANES), F32),) * 3 + (shape((LANES, LANES), BF16),) * 4,
            [whole(1, LANES), whole(HEAD_DIM, HEAD_DIM), anywhere],
            [plain(LANES)] * 3 + [square] * 4,
            prefetch=0,
        ),
        rates,
        feature_omega,
        docs_col,
        wait=(vectors, docs_row),
    )

    pending = x_ring.group
    tick(*going)
    for _ in range(1, middle - 1):
        going = x_ring.start()
        row_step(pending)
        pending = x_ring.group
        tick(*going)
    g_ring = RingGather(out_grad)
    going = x_ring.start() + g_ring.start()
    row_step(pending)
    pending, grad_pending = x_ring.group, g_ring.group
    tick(*going)
    going = g_ring.start()
    row_step(pending)
    norm_one, norm_two, unit, feat, value, active, slope = row_state
    flow = lambda cols: pl.BlockSpec((rows, cols), lambda m, table, docs: (table[1 + blocks + m], 0))
    straight = lambda cols: pl.BlockSpec((rows, cols), lambda m, *s: (m, 0))
    wide = pltpu.VMEM((width, 2 * width), F32)
    mixed, merged, inverse, states = run(
        call(
            functools.partial(forward_kernel, count),
            "attend",
            (
                shape((tokens, width), F32),
                shape((tokens, width), BF16),
                shape((tokens, width), F32),
                shape((blocks, width, 2 * width), F32),
            ),
            [
                flow(2 * width),
                flow(width),
                straight(1),
                pl.BlockSpec((1, 1, rows), lambda m, *s: (m, 0, 0)),
                anywhere,
            ],
            [
                flow(width),
                flow(width),
                flow(width),
                pl.BlockSpec((1, width, 2 * width), lambda m, *s: (m, 0, 0)),
            ],
            prefetch=2,
            scratch=[wide],
        ),
        table,
        docs,
        feat,
        value,
        docs_col,
        docs_row,
        marks[-1],
        gate=2,
    )

    grad_state = ()
    grad_base = 0

    def grad_step(group):
        nonlocal grad_state, grad_base
        at = lambda cols, base=grad_base: pl.BlockSpec((rows, cols), lambda k, *s: (base + k, 0))
        grad_state = group_call(
            grads_kernel,
            "grads",
            group,
            (dense_weight, down_weight, slope),
            [whole(width, model), whole(hidden_cols, model), at(hidden_cols)],
            (
                apart((tokens, model), BF16),
                apart((tokens, width), F32),
                apart((tokens, hidden_cols), BF16),
            ),
            [at(model), at(width), at(hidden_cols)],
            grad_state,
            0,
        )
        grad_base += len(group)

    grad_pending = list(grad_pending)
    tick(*going)
    grad_pending += g_ring.group
    going = g_ring.start()
    halves_of = [shape((rows, model), BF16)] * (blocks - 1) + [shape((rows // 2, model), BF16)] * 2

    def out_step():
        return run(
            call(
                out_kernel,
                "out",
                tuple(halves_of),
                [
                    plain(width),
                    plain(hidden_cols),
                    whole(width, model),
                    whole(hidden_cols, model),
                ],
                [whole(*v.shape) for v in halves_of],
                prefetch=0,
            ),
            merged,
            active,
            dense_weight,
            down_weight,
        )

    partial_out = out_step()
    grad_step(grad_pending)
    tick(*going)
    while g_ring.distance < middle - 1:
        grad_pending = g_ring.group
        going = g_ring.start()
        grad_step(grad_pending)
        tick(*going)
    out_ring = RingSum(partial_out)
    grad_pending = g_ring.group
    going = g_ring.start() + out_ring.start()
    grad_step(grad_pending)
    tick(*going)
    out_ring.add()
    tick()
    going = out_ring.start()
    grad_step(g_ring.group)
    grad_all, merged_grad, hidden_grad = grad_state
    back = lambda cols: pl.BlockSpec(
        (rows, cols), lambda m, table, docs: (table[2 * blocks - m], 0)
    )
    back_straight = lambda cols: pl.BlockSpec((rows, cols), lambda m, *s: (blocks - 1 - m, 0))
    change = run(
        call(
            functools.partial(backward_kernel, count),
            "attend_back",
            shape((tokens, qkv_cols), BF16),
            [
                back(2 * width),
                back(width),
                back(width),
                back(width),
                back(width),
                back_straight(1),
                pl.BlockSpec((1, 1, rows), lambda m, *s: (blocks - 1 - m, 0, 0)),
                anywhere,
                pl.BlockSpec((1, width, 2 * width), lambda m, *s: (blocks - 1 - m, 0, 0)),
                back_straight(LANES),
                back_straight(LANES),
                back_straight(LANES),
                square,
                square,
            ],
            back(qkv_cols),
            prefetch=2,
            scratch=[wide],
        ),
        table,
        docs,
        feat,
        value,
        mixed,
        inverse,
        merged_grad,
        docs_col,
        docs_row,
        marks[-1],
        states,
        keep,
        ahead,
        behind,
        turned_high,
        turned_low,
        gate=6,
    )
    tick(*going)
    out_ring.add()
    tick()
    going = out_ring.start()
    def norm_step(start, outs, given):
        at = lambda cols: pl.BlockSpec((rows, cols), lambda k, *s: (start + k, 0))
        return run(
            call(
                norm_grad_kernel,
                "norm_grad",
                (shape((8, model), F32),) + tuple(outs),
                [
                    at(qkv_cols),
                    at(hidden_cols),
                    whole(model, qkv_cols),
                    whole(model, hidden_cols),
                    at(model),
                    whole(8, model),
                    whole(rows, model),
                    whole(8, model),
                ],
                [whole(8, model)] + [whole(*v.shape) for v in outs],
                prefetch=0,
                steps=1 if start else blocks - 1,
            ),
            change,
            hidden_grad,
            qkv_weight,
            up_weight,
            unit,
            vectors,
            out_grad,
            given,
            gate=5,
        )

    def add(a, b):
        return (a.astype(F32) + b.astype(F32)).astype(BF16)

    def add_three(a, b, c):
        return (a.astype(F32) + b.astype(F32) + c.astype(F32)).astype(BF16)

    def rest(total):
        step = QUARTERS
        while step < dp_size:
            total = add(total, over_dp(total, step))
            step *= 2
        return total

    last_sums, top, bottom = norm_step(blocks - 1, halves_of[-2:], jnp.zeros((8, model), F32))
    e_ring = RingSum((top, bottom))
    going += e_ring.start()
    norm_grads = norm_step(0, halves_of[:-2], last_sums)
    e_ring.parts = tuple(norm_grads[1:]) + (top, bottom)
    small = SmallSum(norm_grads[0])
    cut_cols = model // QUARTERS
    kept, sent = run(
        call(
            hidden_weights_kernel,
            "hidden_weights",
            (shape((2, 2 * hidden_part, model), BF16),) * 2,
            [
                whole(tokens, hidden_cols),
                whole(tokens, hidden_cols),
                pl.BlockSpec((tokens, cut_cols), lambda k, *s: (0, k)),
                pl.BlockSpec((tokens, cut_cols), lambda k, *s: (0, k)),
            ],
            [pl.BlockSpec((2, 2 * hidden_part, cut_cols), lambda k, *s: (0, 0, k))] * 2,
            scratch=[pltpu.VMEM((hidden_cols, cut_cols), BF16)] * 2,
            steps=QUARTERS,
            limit=20,
        ),
        table,
        active,
        hidden_grad,
        grad_all,
        norm_two,
        gate=2,
    )
    hidden_sums = run(
        once(column_sums_kernel, "column_sums", shape((8, hidden_cols), F32), prefetch=0), hidden_grad
    )
    lower = WeightSum(kept, sent)
    tick(*going)
    out_ring.add()
    e_ring.add()
    tick()
    going = out_ring.start() + e_ring.start() + lower.start()
    first_rows, first_cols = model_part + width + 16, max(qkv_cols, model_part)
    sums_parts = hidden_sums[0].reshape(QUARTERS, 1, hidden_part)
    upper_kept, upper_sent = run(
        call(
            qkv_weights_kernel,
            "qkv_weights",
            (shape((2, first_rows, first_cols), BF16),) * 2,
            [
                whole(tokens, qkv_cols),
                pl.BlockSpec((tokens, model_part), lambda k, table: (0, table[0] ^ k)),
                whole(tokens, width),
                pl.BlockSpec((tokens, model_part), lambda k, table: (0, table[0] ^ k)),
                pl.BlockSpec((1, 1, hidden_part), lambda k, table: (table[0] ^ k, 0, 0)),
            ],
            [pl.BlockSpec((1, first_rows, first_cols), lambda k, table: (k // 2, 0, 0))] * 2,
            steps=QUARTERS,
            limit=16,
        ),
        table,
        change,
        norm_one,
        merged,
        grad_all,
        sums_parts,
        gate=2,
    )
    upper = WeightSum(upper_kept, upper_sent)
    tick(*going)
    if out_ring.distance > 0:
        finish(out_ring)
    e_ring.add()
    lower.add()
    tick()
    going = e_ring.start() + upper.start() + lower.start() + small.start()
    layer_out = run(
        once(finish_out_kernel, "finish_out", shape((rows, model), BF16), prefetch=0),
        inputs,
        vectors,
        *out_ring.result(),
        gate=2,
    )
    tick(*going)
    e_ring.add()
    upper.add()
    lower.add()
    small.add()
    tick()
    going = e_ring.start() + upper.start() + lower.start(third=True) + small.start()
    tick(*going)
    upper.add()
    small.add()
    finish(e_ring)
    tick()
    going = upper.start(third=True) + lower.start(last=True) + lower.start(near=True)
    going += upper.start(near=True) + small.start()
    input_grad = run(
        once(finish_in_kernel, "finish_in", shape((rows, model), F32), prefetch=0),
        inputs,
        out_grad,
        *e_ring.result(),
        gate=2,
    )

    tick(*going)
    small.add()
    tick()
    going = upper.start(last=True) + small.start()
    up_grad, down_grad = run(
        once(
            finish_hidden_kernel,
            "finish_hidden",
            (shape((model, hidden_cols), F32), shape((hidden_cols, model), F32)),
            scratch=[pltpu.VMEM((hidden_cols, model), F32)],
            limit=16,
        ),
        table,
        *lower.result(),
        gate=1,
    )
    tick(*going)
    small.add()
    tick()
    small.start()
    qkv_grad, dense_grad, qkv_bias_grad, up_bias_grad = run(
        once(
            finish_qkv_kernel,
            "finish_qkv",
            (
                shape((model, qkv_cols), F32),
                shape((width, model), F32),
                shape((1, qkv_cols), F32),
                shape((QUARTERS, 1, hidden_part), F32),
            ),
        ),
        table,
        *upper.result(),
        gate=1,
    )

    small.add()
    while small.steps:
        tick()
        small.start()
        small.add()
    cols = model // tensor_size
    small = lax.dynamic_slice_in_dim(small.values, place * cols, cols, 1)

    return (
        layer_out,
        input_grad,
        qkv_grad,
        qkv_bias_grad.reshape(-1),
        dense_grad,
        up_grad,
        up_bias_grad.reshape(-1),
        down_grad,
        small[4],
        small[0],
        small[1],
        small[2],
        small[3],
    )


def solution(mesh):
    in_specs = (
        P(("dp", "tensor"), None),
        P(None, "tensor"),
        P("tensor"),
        P("tensor", None),
        P(None, "tensor"),
        P("tensor"),
        P("tensor", None),
        P(),
        P(),
        P(),
        P(),
        P(),
        P(),
        P("dp", None),
        P(("dp", "tensor"), None),
    )
    out_specs = (
        P(("dp", "tensor"), None),
        P(("dp", "tensor"), None),
        P(None, "tensor"),
        P("tensor"),
        P("tensor", None),
        P(None, "tensor"),
        P("tensor"),
        P("tensor", None),
        P("tensor"),
        P("tensor"),
        P("tensor"),
        P("tensor"),
        P("tensor"),
    )
    return jax.shard_map(
        functools.partial(on_device, mesh.shape["dp"], mesh.shape["tensor"]),
        mesh=mesh,
        in_specs=in_specs,
        out_specs=out_specs,
        check_vma=False,
    )
```

time: 1270 us -> 229 us (0.18); the launches traced: 1260 us -> 228 us
  waiting for transfers between devices: 783 us -> 80.1 us
  matrix products: 180 us -> 0 us
  local copies, waits for them, and re-layouts: 143 us -> 21.3 us
  other arithmetic: 115 us -> 1.38 us
  Pallas kernels: 0 us -> 81.2 us
  starting transfers between devices: 0.53 us -> 43.1 us
  between operations: 15.3 us -> 1.22 us
  loops' own time: 12.9 us -> 0 us
    reduce_scatter x4 -> x0, waiting for transfers between devices: 533 us -> none  [the longest x1 248 us: on_device(): lax.psum_scatter(jnp.concatenate([jnp.einsum('tc,dc->td', qkv_grad, qkv_w...]
    dot_general x133 -> x0, matrix products: 180 us -> none  [the longest x8 16.6 us: advance(): jnp.einsum('sbc,sce->sbe', weights, value_wide, precision=EXACT)]
    all_gather x3 -> x0, waiting for transfers between devices: 133 us -> none  [the longest x1 68.9 us: on_device(): lax.all_gather(norm_values[0].astype(jnp.bfloat16), 'tensor', axis=0, til...]
    psum x1 -> x0, waiting for transfers between devices: 116 us -> none  [on_device(): lax.psum((qkv_weight_grad, qkv_bias_grad, dense_weight_grad, up_weight_gr...]
    pallas_call x0 -> x26, Pallas kernels: none -> 81.2 us  [the longest x15 71.4 us: run(): result = step(*operands)]
    ppermute x0 -> x47, waiting for transfers between devices: none -> 80.1 us  [the longest x16 43.6 us: left(): return lax.ppermute(values, 'tensor', pairs)]
    dynamic_update_slice x40 -> x0, local copies, waits for them, and re-layouts: 62.8 us -> none  [attend_forward(): lax.scan(advance, initial, (query_blocks, key_blocks, value_blocks, doc_b...]
    ppermute x0 -> x47, starting transfers between devices: none -> 43.1 us  [the longest x16 20.3 us: left(): return lax.ppermute(values, 'tensor', pairs)]
  transfers between devices with their start and end apart: 8 -> 47, of which waited for: 7 -> 20; matrix products, arithmetic and copies ran while one was open for 31% -> 3% of each run, Pallas kernels for 0% -> 35%
where the time goes in v2:
time: 229 us; the launch traced here: 228 us
  Pallas kernels  81.2 us (35%)
  waiting for transfers between devices  80.1 us (35%)
  starting transfers between devices  43.1 us (19%)
  local copies, waits for them, and re-layouts  21.3 us (9%)
    pallas_call x15, Pallas kernels, run(): result = step(*operands)  71.4 us
    ppermute x16, waiting for transfers between devices, left(): return lax.ppermute(values, 'tensor', pairs)  43.6 us
    ppermute x16, starting transfers between devices, left(): return lax.ppermute(values, 'tensor', pairs)  20.3 us
    ppermute x12, waiting for transfers between devices, over_dp(): return lax.ppermute(values, 'dp', [(p, p ^ bits) for p in range(dp_size)])  19.9 us
    unnamed x75, local copies, waits for them, and re-layouts  18.5 us
    ppermute x16, starting transfers between devices, right(): return lax.ppermute(values, 'tensor', pairs)  13.9 us
    ppermute x16, waiting for transfers between devices, right(): return lax.ppermute(values, 'tensor', pairs)  12.6 us
    pallas_call x11, Pallas kernels, step(): call(kernel, name, listed, [spec(v) for v in operands[prefetch:]], [whole...  9.8 us
  transfers between devices with their start and end apart: 47, of which 20 were waited for; matrix products, arithmetic and copies ran while one was open for 3% of the time, Pallas kernels for 35%

profile of v2, /device:TPU:0, one launch (start us, length us, event | category | flops | bytes accessed | tf_op | source)
XLA Modules:
  0.0 228.2 jit_solution(3094704174535448358)
XLA Ops:
  0.7 3.1 %collective-permute-start = (bf16[256,1024]{1,0:T(8,128)(2,1)}, bf16[256,1024]{1,0:T(8,128)(2,1)}, u32[]{:S(2)}, u32[]{:S(2)}) collective-permute-start(bf16[256,1024]{1,0:T(8,128)(2,1)} %x_ref.3), channel_id=1, source_target_pairs={{0,2},{2,4},{4,6},{6,7},{7,5},{5,3},{3,1},{1,0},{8,10},{10,12},{12... | collective-permute-start | bytes 1572872 | tf_op jit(solution)/shard_map/ppermute | solution.py:594
  8.6 2.0 copy.58.docs_col
  13.3 4.7 %prepare.1 = (f32[2048,128]{1,0:T(8,128)S(1)}, f32[2048,128]{1,0:T(8,128)S(1)}, f32[2048,128]{1,0:T(8,128)S(1)}, bf16[128,128]{1,0:T(8,128)(2,1)S(1)}, bf16[128,...) custom-call(f32[1,128]{1,0:T(1,128)S(1)} %copy-done.31, f32[64,64]{1,0:T(8,128)S(1)} %copy-done.30, ...), custom_call_target="tpu_custom_call" | custom-call | flops 1000 | bytes 1000 | tf_op jit(solution)/shard_map/prepare/pallas_call | solution.py:613
  20.5 2.0 collective-permute-start.2
  26.2 6.2 %rows.4 = (f32[8,128]{1,0:T(8,128)S(1)}, bf16[2048,1024]{1,0:T(8,128)(2,1)}, bf16[2048,1024]{1,0:T(8,128)(2,1)}, bf16[2048,1024]{1,0:T(8,128)(2,1)}, f32[2048,25...) custom-call(s32[17]{0:T(128)S(1)} %pad_add_fusion.table, ...), custom_call_target="tpu_custom_call" | custom-call | flops 1000 | bytes 1000 | tf_op jit(solution)/shard_map/rows/pallas_call | solution.py:613
  32.4 1.7 collective-permute-done.2.refs_1_
  34.1 1.6 collective-permute-done.3.refs_0_
  36.0 1.7 collective-permute-start.4
  37.7 5.6 %rows.5 = (f32[8,128]{1,0:T(8,128)S(1)}, bf16[2048,1024]{1,0:T(8,128)(2,1)}, bf16[2048,1024]{1,0:T(8,128)(2,1)}, bf16[2048,1024]{1,0:T(8,128)(2,1)}, f32[2048,25...) custom-call(s32[17]{0:T(128)S(1)} %pad_add_fusion.table, ...), custom_call_target="tpu_custom_call", output_to_operand_aliasing={{1}: (11, {}), {2}: (12, {}), {3}: (13, {}), {4}: (14, {}),... | custom-call | flops 1000 | bytes 1000 | tf_op jit(solution)/shard_map/rows/pallas_call | solution.py:613
  43.3 4.6 %collective-permute-done.5.refs_0_ = bf16[256,1024]{1,0:T(8,128)(2,1)S(1)} collective-permute-done((bf16[256,1024]{1,0:T(8,128)(2,1)}, bf16[256,1024]{1,0:T(8,128)(2,1)S(1)}, u32[]{:S(2)}, u32[]{:S(2)}) %collective-permute-start.5) | collective-permute-done | bytes 524320 | tf_op jit(solution)/shard_map/ppermute | solution.py:598
  52.1 4.6 %rows.6 = (f32[8,128]{1,0:T(8,128)S(1)}, bf16[2048,1024]{1,0:T(8,128)(2,1)}, bf16[2048,1024]{1,0:T(8,128)(2,1)}, bf16[2048,1024]{1,0:T(8,128)(2,1)}, f32[2048,25...) custom-call(s32[17]{0:T(128)S(1)} %pad_add_fusion.table, ...), custom_call_target="tpu_custom_call", output_to_operand_aliasing={{1}: (11, {}), {2}: (12, {}), {3}: (13, {}), {4}: (14, {}),... | custom-call | flops 1000 | bytes 1000 | tf_op jit(solution)/shard_map/rows/pallas_call | solution.py:613
  56.8 7.9 %collective-permute-done.7.refs_1_ = bf16[128,1024]{1,0:T(8,128)(2,1)S(1)} collective-permute-done((bf16[128,1024]{1,0:T(8,128)(2,1)S(1)}, bf16[128,1024]{1,0:T(8,128)(2,1)S(1)}, u32[]{:S(2)}, u32[]{:S(2)}) %collective-permute-start.7) | collective-permute-done | bytes 262176 | tf_op jit(solution)/shard_map/ppermute | solution.py:598
  64.6 2.4 %collective-permute-done.6.refs_0_ = bf16[128,1024]{1,0:T(8,128)(2,1)S(1)} collective-permute-done((bf16[128,1024]{1,0:T(8,128)(2,1)S(1)}, bf16[128,1024]{1,0:T(8,128)(2,1)S(1)}, u32[]{:S(2)}, u32[]{:S(2)}) %collective-permute-start.6) | collective-permute-done | bytes 262176 | tf_op jit(solution)/shard_map/ppermute | solution.py:594
  67.2 1.9 collective-permute-start.10
  69.1 2.9 %rows.7 = (f32[8,128]{1,0:T(8,128)S(1)}, bf16[2048,1024]{1,0:T(8,128)(2,1)}, bf16[2048,1024]{1,0:T(8,128)(2,1)}, bf16[2048,1024]{1,0:T(8,128)(2,1)}, f32[2048,25...) custom-call(s32[17]{0:T(128)S(1)} %pad_add_fusion.table, ...), custom_call_target="tpu_custom_call", output_to_operand_aliasing={{1}: (11, {}), {2}: (12, {}), {3}: (13, {}), {4}: (14, {}),... | custom-call | flops 1000 | bytes 1000 | tf_op jit(solution)/shard_map/rows/pallas_call | solution.py:613
  72.1 1.7 copy-done.7
  74.8 4.2 %attend.1 = (f32[2048,128]{1,0:T(8,128)S(1)}, bf16[2048,128]{1,0:T(8,128)(2,1)S(1)}, f32[2048,128]{1,0:T(8,128)S(1)}, f32[8,128,256]{2,1,0:T(8,128)S(1)}) custom-call(s32[17]{0:T(128)S(1)} %pad_add_fusion.table, s32[2048]{0:T(1024)S(1)} %bitcast.46, f32[2048,256]{1,0:T(8,128)S(1)} %copy-done.7, bf16[2048,128]{1,0:T(8,128)(2,1)S(1)} %copy-done.20, ...), custom_call_target="tpu_custom_call" | custom-call | flops 1000 | bytes 1000 | tf_op jit(solution)/shard_map/attend/pallas_call | solution.py:613
  79.1 1.6 collective-permute-start.13
  81.2 5.1 %out.1 = (bf16[256,1024]{1,0:T(8,128)(2,1)S(1)}, bf16[256,1024]{1,0:T(8,128)(2,1)S(1)}, bf16[256,1024]{1,0:T(8,128)(2,1)S(1)}, bf16[256,1024]{1,0:T(8,128)(2,1)S...) custom-call(bf16[2048,128]{1,0:T(8,128)(2,1)S(1)} %get-tuple-element, ...), custom_call_target="tpu_custom_call" | custom-call | flops 1000 | bytes 1000 | tf_op jit(solution)/shard_map/out/pallas_call | solution.py:613
  86.3 4.1 %grads.3 = (f32[8,128]{1,0:T(8,128)S(1)}, bf16[2048,1024]{1,0:T(8,128)(2,1)}, f32[2048,128]{1,0:T(8,128)}, bf16[2048,512]{1,0:T(8,128)(2,1)}) custom-call(bf16[256,1024]{1,0:T(8,128)(2,1)S(1)} %copy-done.23, bf16[256,1024]{1,0:T(8,128)(2,1)S(1)} %collective-permute-done.8.refs_1_, bf16[256,1024]{1,0:T(8,128)(2,1)S(1)} %collective-permute-done.9.refs_2_, ...), custom_call_target="tpu_custom_call" | custom-call | flops 1000 | bytes 1000 | tf_op jit(solution)/shard_map/grads/pallas_call | solution.py:613
  90.5 1.8 collective-permute-done.12.refs_1_
  92.3 1.6 collective-permute-start.17
  94.4 1.6 collective-permute-start.15
  96.5 2.0 grads.4
  98.9 1.9 collective-permute-done.16.right_half
  100.8 3.7 %collective-permute-done.15.refs_1_ = bf16[128,1024]{1,0:T(8,128)(2,1)S(1)} collective-permute-done((bf16[128,1024]{1,0:T(8,128)(2,1)S(1)}, bf16[128,1024]{1,0:T(8,128)(2,1)S(1)}, u32[]{:S(2)}, u32[]{:S(2)}) %collective-permute-start.15) | collective-permute-done | bytes 262176 | tf_op jit(solution)/shard_map/ppermute | solution.py:598
  104.5 1.9 collective-permute-done.14.refs_0_
  106.6 2.2 collective-permute-start.19
  112.4 10.1 %attend_back.1.change = bf16[2048,384]{1,0:T(8,128)(2,1)S(1)} custom-call(s32[17]{0:T(128)S(1)} %pad_add_fusion.table, s32[2048]{0:T(1024)S(1)} %bitcast.48, f32[2048,256]{1,0:T(8,128)S(1)} %copy-done.8, bf16[2048,128]{1,0:T(8,128)(2,1)S(1)} %copy-done.21, f32[2048,128]{1,0:T(8,128)S(1)} %get-tuple-element.234.mixed_ref, ...), custom_call_target="tpu_custom_call" | custom-call | flops 1000 | bytes 1000 | tf_op jit(solution)/shard_map/attend_back/pallas_call | solution.py:613
  122.8 2.0 collective-permute-start.21
  125.8 2.0 collective-permute-start.23
  127.9 6.7 %norm_grad.3 = (f32[8,1024]{1,0:T(8,128)S(1)}, bf16[256,1024]{1,0:T(8,128)(2,1)S(1)}, bf16[256,1024]{1,0:T(8,128)(2,1)S(1)}, bf16[256,1024]{1,0:T(8,128)(2,1)S(1...) custom-call(bf16[2048,384]{1,0:T(8,128)(2,1)S(1)} %attend_back.1.cha, ...), custom_call_target="tpu_custom_call" | custom-call | flops 1000 | bytes 1000 | tf_op jit(solution)/shard_map/norm_grad/pallas_call | solution.py:613
  134.6 7.3 %hidden_weights.1 = (bf16[2,256,1024]{2,1,0:T(8,128)(2,1)S(1)}, bf16[2,256,1024]{2,1,0:T(8,128)(2,1)S(1)}) custom-call(s32[17]{0:T(128)S(1)} %pad_add_fusion.table, bf16[2048,512]{1,0:T(8,128)(2,1)S(1)} %copy-done.6, bf16[2048,512]{1,0:T(8,128)(2,1)S(1)} %copy-done.1, bf16[2048,1024]{1,0:T(8,128)(2,1)S(1)} %copy-done.3, bf16[2048,1024]{1,0:T(8,128)(2,1)S(1)} %copy-done.5), custom_call_target="tpu_custom_call" | custom-call | flops 1000 | bytes 1000 | tf_op jit(solution)/shard_map/hidden_weights/pallas_call | solution.py:613
  142.7 2.0 collective-permute-start.27
  146.9 5.6 %qkv_weights.1 = (bf16[2,400,384]{2,1,0:T(8,128)(2,1)S(1)}, bf16[2,400,384]{2,1,0:T(8,128)(2,1)S(1)}) custom-call(s32[17]{0:T(128)S(1)} %pad_add_fusion.table, bf16[2048,384]{1,0:T(8,128)(2,1)S(1)} %attend_back.1.change, bf16[2048,1024]{1,0:T(8,128)(2,1)S(1)} %copy-done.4, bf16[2048,128]{1,0:T(8,128)(2,1)S(1)} %get-tuple-element.237.merged, ...), custom_call_target="tpu_custom_call" | custom-call | flops 1000 | bytes 1000 | tf_op jit(solution)/shard_map/qkv_weights/pallas_call | solution.py:613
  152.5 5.0 %collective-permute-done.27.left_sum = bf16[256,1024]{1,0:T(8,128)(2,1)S(1)} collective-permute-done((bf16[256,1024]{1,0:T(8,128)(2,1)S(1)}, bf16[256,1024]{1,0:T(8,128)(2,1)S(1)}, u32[]{:S(2)}, u32[]{:S(2)}) %collective-permute-start.27) | collective-permute-done | bytes 524320 | tf_op jit(solution)/shard_map/ppermute | solution.py:598
  157.5 10.8 %collective-permute-done.25.refs_2_ = bf16[256,1024]{1,0:T(8,128)(2,1)S(1)} collective-permute-done((bf16[256,1024]{1,0:T(8,128)(2,1)S(1)}, bf16[256,1024]{1,0:T(8,128)(2,1)S(1)}, u32[]{:S(2)}, u32[]{:S(2)}) %collective-permute-start.25) | collective-permute-done | bytes 524320 | tf_op jit(solution)/shard_map/ppermute | solution.py:598
  168.3 2.9 %collective-permute-done.26.right_sum = bf16[256,1024]{1,0:T(8,128)(2,1)S(1)} collective-permute-done((bf16[256,1024]{1,0:T(8,128)(2,1)S(1)}, bf16[256,1024]{1,0:T(8,128)(2,1)S(1)}, u32[]{:S(2)}, u32[]{:S(2)}) %collective-permute-start.26) | collective-permute-done | bytes 524320 | tf_op jit(solution)/shard_map/ppermute | solution.py:594
  172.0 1.7 collective-permute-start.29
  176.5 9.5 %collective-permute-done.30.left_sum = bf16[256,1024]{1,0:T(8,128)(2,1)S(1)} collective-permute-done((bf16[256,1024]{1,0:T(8,128)(2,1)S(1)}, bf16[256,1024]{1,0:T(8,128)(2,1)S(1)}, u32[]{:S(2)}, u32[]{:S(2)}) %collective-permute-start.30) | collective-permute-done | bytes 524320 | tf_op jit(solution)/shard_map/ppermute | solution.py:598
  190.0 1.7 collective-permute-start.34
  193.7 14.6 %collective-permute-done.38 = f32[8,1024]{1,0:T(8,128)S(1)} collective-permute-done((f32[8,1024]{1,0:T(8,128)S(1)}, f32[8,1024]{1,0:T(8,128)S(1)}, u32[]{:S(2)}, u32[]{:S(2)}) %collective-permute-start.38) | collective-permute-done | bytes 32800 | tf_op jit(solution)/shard_map/ppermute | solution.py:601
  210.9 1.8 finish_in.1
  212.6 1.8 collective-permute-done.43
  214.5 3.8 %collective-permute-done.39.third = bf16[400,384]{1,0:T(8,128)(2,1)S(1)} collective-permute-done((bf16[400,384]{1,0:T(8,128)(2,1)S(1)}, bf16[400,384]{1,0:T(8,128)(2,1)S(1)}, u32[]{:S(2)}, u32[]{:S(2)}) %collective-permute-start.39) | collective-permute-done | bytes 307232 | tf_op jit(solution)/shard_map/ppermute | solution.py:601
  219.1 3.4 %finish_hidden.1 = (f32[1024,512]{1,0:T(8,128)}, f32[512,1024]{1,0:T(8,128)}) custom-call(s32[17]{0:T(128)S(1)} %pad_add_fusion.table, bf16[256,1024]{1,0:T(8,128)(2,1)S(1)} %fusion.1.mine, bf16[256,1024]{1,0:T(8,128)(2,1)S(1)} %collective-permute-done.41.near, bf16[256,1024]{1,0:T(8,128)(2,1)S(1)} %collective-permute-done.37.third, ...), custom_call_target="tpu_custom_call" | custom-call | flops 1000 | bytes 1000 | tf_op jit(solution)/shard_map/finish_hidden/pallas_call | solution.py:652
  223.1 2.0 finish_qkv.1
  225.6 2.1 collective-permute-done.46
  (171 shorter events, 43.8 us)
Async XLA Ops:
  0.7 22.0 %copy-start.10 = (bf16[1024,384]{1,0:T(8,128)(2,1)S(1)}, bf16[1024,384]{1,0:T(8,128)(2,1)}, u32[]{:S(2)}) copy-start(bf16[1024,384]{1,0:T(8,128)(2,1)} %qkv_weight.3) | copy-start | bytes 2359300
  0.7 19.8 %collective-permute-start = (bf16[256,1024]{1,0:T(8,128)(2,1)}, bf16[256,1024]{1,0:T(8,128)(2,1)}, u32[]{:S(2)}, u32[]{:S(2)}) collective-permute-start(bf16[256,1024]{1,0:T(8,128)(2,1)} %x_ref.3), channel_id=1, source_target_pairs={{0,2},{2,4},{4,6},{6,7},{7,5},{5,3},{3,1},{1,0},{8,10},{10,12},{12... | collective-permute-start | bytes 1572872 | tf_op jit(solution)/shard_map/ppermute | solution.py:594
  3.8 16.7 %collective-permute-start.1 = (bf16[256,1024]{1,0:T(8,128)(2,1)}, bf16[256,1024]{1,0:T(8,128)(2,1)}, u32[]{:S(2)}, u32[]{:S(2)}) collective-permute-start(bf16[256,1024]{1,0:T(8,128)(2,1)} %x_ref.3), channel_id=1, source_target_pairs={{0,1},{2,0},{4,2},{6,4},{7,6},{5,7},{3,5},{1,3},{8,9},{10,8},{12,1... | collective-permute-start | bytes 1572872 | tf_op jit(solution)/shard_map/ppermute | solution.py:598
  20.5 13.6 %collective-permute-start.2 = (bf16[256,1024]{1,0:T(8,128)(2,1)}, bf16[256,1024]{1,0:T(8,128)(2,1)S(1)}, u32[]{:S(2)}, u32[]{:S(2)}) collective-permute-start(bf16[256,1024]{1,0:T(8,128)(2,1)} %collective-permute-done.refs_2_), channel_id=1, source_target_pairs={{0,2},{2,4},{4,6},{6,7},{7,5},{5,3},{3,1},{1,0},{8,10},{10,12},{12... | collective-permute-start | bytes 1572872 | tf_op jit(solution)/shard_map/ppermute | solution.py:594
  22.5 13.1 %collective-permute-start.3 = (bf16[256,1024]{1,0:T(8,128)(2,1)}, bf16[256,1024]{1,0:T(8,128)(2,1)}, u32[]{:S(2)}, u32[]{:S(2)}) collective-permute-start(bf16[256,1024]{1,0:T(8,128)(2,1)} %collective-permute-done.1.refs_1_), channel_id=1, source_target_pairs={{0,1},{2,0},{4,2},{6,4},{7,6},{5,7},{3,5},{1,3},{8,9},{10,8},{12,1... | collective-permute-start | bytes 1572872 | tf_op jit(solution)/shard_map/ppermute | solution.py:598
  35.7 12.2 %collective-permute-start.5 = (bf16[256,1024]{1,0:T(8,128)(2,1)}, bf16[256,1024]{1,0:T(8,128)(2,1)S(1)}, u32[]{:S(2)}, u32[]{:S(2)}) collective-permute-start(bf16[256,1024]{1,0:T(8,128)(2,1)} %collective-permute-done.3.refs_0_), channel_id=1, source_target_pairs={{0,1},{2,0},{4,2},{6,4},{7,6},{5,7},{3,5},{1,3},{8,9},{10,8},{12,1... | collective-permute-start | bytes 1572872 | tf_op jit(solution)/shard_map/ppermute | solution.py:598
  36.0 11.9 %collective-permute-start.4 = (bf16[256,1024]{1,0:T(8,128)(2,1)S(1)}, bf16[256,1024]{1,0:T(8,128)(2,1)S(1)}, u32[]{:S(2)}, u32[]{:S(2)}) collective-permute-start(bf16[256,1024]{1,0:T(8,128)(2,1)S(1)} %collective-permute-done.2.refs_1_), channel_id=1, source_target_pairs={{0,2},{2,4},{4,6},{6,7},{7,5},{5,3},{3,1},{1,0},{8,10},{10,12},{12... | collective-permute-start | bytes 1572872 | tf_op jit(solution)/shard_map/ppermute | solution.py:594
  47.9 19.1 %collective-permute-start.8 = (bf16[256,1024]{1,0:T(8,128)(2,1)S(1)}, bf16[256,1024]{1,0:T(8,128)(2,1)S(1)}, u32[]{:S(2)}, u32[]{:S(2)}) collective-permute-start(bf16[256,1024]{1,0:T(8,128)(2,1)S(1)} %copy-done.23), channel_id=1, source_target_pairs={{0,1},{2,0},{4,2},{6,4},{7,6},{5,7},{3,5},{1,3},{8,9},{10,8},{12,1... | collective-permute-start | bytes 1572872 | tf_op jit(solution)/shard_map/ppermute | solution.py:598
  49.4 17.7 %collective-permute-start.9 = (bf16[256,1024]{1,0:T(8,128)(2,1)S(1)}, bf16[256,1024]{1,0:T(8,128)(2,1)S(1)}, u32[]{:S(2)}, u32[]{:S(2)}) collective-permute-start(bf16[256,1024]{1,0:T(8,128)(2,1)S(1)} %copy-done.23), channel_id=1, source_target_pairs={{0,2},{2,4},{4,6},{6,7},{7,5},{5,3},{3,1},{1,0},{8,10},{10,12},{12... | collective-permute-start | bytes 1572872 | tf_op jit(solution)/shard_map/ppermute | solution.py:594
  50.0 14.7 %collective-permute-start.7 = (bf16[128,1024]{1,0:T(8,128)(2,1)S(1)}, bf16[128,1024]{1,0:T(8,128)(2,1)S(1)}, u32[]{:S(2)}, u32[]{:S(2)}) collective-permute-start(bf16[128,1024]{1,0:T(8,128)(2,1)S(1)} %slice.73), channel_id=1, source_target_pairs={{0,1},{2,0},{4,2},{6,4},{7,6},{5,7},{3,5},{1,3},{8,9},{10,8},{12,1... | collective-permute-start | bytes 786440 | tf_op jit(solution)/shard_map/ppermute | solution.py:598
  51.5 15.6 %collective-permute-start.6 = (bf16[128,1024]{1,0:T(8,128)(2,1)S(1)}, bf16[128,1024]{1,0:T(8,128)(2,1)S(1)}, u32[]{:S(2)}, u32[]{:S(2)}) collective-permute-start(bf16[128,1024]{1,0:T(8,128)(2,1)S(1)} %slice.72), channel_id=1, source_target_pairs={{0,2},{2,4},{4,6},{6,7},{7,5},{5,3},{3,1},{1,0},{8,10},{10,12},{12... | collective-permute-start | bytes 786440 | tf_op jit(solution)/shard_map/ppermute | solution.py:594
  67.1 12.0 %collective-permute-start.11 = (bf16[256,1024]{1,0:T(8,128)(2,1)S(1)}, bf16[256,1024]{1,0:T(8,128)(2,1)S(1)}, u32[]{:S(2)}, u32[]{:S(2)}) collective-permute-start(bf16[256,1024]{1,0:T(8,128)(2,1)S(1)} %collective-permute-done.9.refs_2_), channel_id=1, source_target_pairs={{0,2},{2,4},{4,6},{6,7},{7,5},{5,3},{3,1},{1,0},{8,10},{10,12},{12... | collective-permute-start | bytes 1572872 | tf_op jit(solution)/shard_map/ppermute | solution.py:594
  67.2 12.0 %collective-permute-start.10 = (bf16[256,1024]{1,0:T(8,128)(2,1)S(1)}, bf16[256,1024]{1,0:T(8,128)(2,1)S(1)}, u32[]{:S(2)}, u32[]{:S(2)}) collective-permute-start(bf16[256,1024]{1,0:T(8,128)(2,1)S(1)} %collective-permute-done.8.refs_1_), channel_id=1, source_target_pairs={{0,1},{2,0},{4,2},{6,4},{7,6},{5,7},{3,5},{1,3},{8,9},{10,8},{12,1... | collective-permute-start | bytes 1572872 | tf_op jit(solution)/shard_map/ppermute | solution.py:598
  79.1 11.4 %collective-permute-start.13 = (bf16[256,1024]{1,0:T(8,128)(2,1)S(1)}, bf16[256,1024]{1,0:T(8,128)(2,1)S(1)}, u32[]{:S(2)}, u32[]{:S(2)}) collective-permute-start(bf16[256,1024]{1,0:T(8,128)(2,1)S(1)} %collective-permute-done.10.refs_3_), channel_id=1, source_target_pairs={{0,1},{2,0},{4,2},{6,4},{7,6},{5,7},{3,5},{1,3},{8,9},{10,8},{12,1... | collective-permute-start | bytes 1572872 | tf_op jit(solution)/shard_map/ppermute | solution.py:598
  80.8 11.6 %collective-permute-start.12 = (bf16[256,1024]{1,0:T(8,128)(2,1)S(1)}, bf16[256,1024]{1,0:T(8,128)(2,1)S(1)}, u32[]{:S(2)}, u32[]{:S(2)}) collective-permute-start(bf16[256,1024]{1,0:T(8,128)(2,1)S(1)} %collective-permute-done.11.refs_4_), channel_id=1, source_target_pairs={{0,2},{2,4},{4,6},{6,7},{7,5},{5,3},{3,1},{1,0},{8,10},{10,12},{12... | collective-permute-start | bytes 1572872 | tf_op jit(solution)/shard_map/ppermute | solution.py:594
  92.3 6.6 %collective-permute-start.17 = (bf16[128,1024]{1,0:T(8,128)(2,1)S(1)}, bf16[128,1024]{1,0:T(8,128)(2,1)S(1)}, u32[]{:S(2)}, u32[]{:S(2)}) collective-permute-start(bf16[128,1024]{1,0:T(8,128)(2,1)S(1)} %get-tuple-element.256), channel_id=1, source_target_pairs={{0,1},{2,0},{4,2},{6,4},{7,6},{5,7},{3,5},{1,3},{8,9},{10,8},{12,1... | collective-permute-start | bytes 786440 | tf_op jit(solution)/shard_map/ppermute | solution.py:598
  93.9 6.9 %collective-permute-start.16 = (bf16[128,1024]{1,0:T(8,128)(2,1)S(1)}, bf16[128,1024]{1,0:T(8,128)(2,1)S(1)}, u32[]{:S(2)}, u32[]{:S(2)}) collective-permute-start(bf16[128,1024]{1,0:T(8,128)(2,1)S(1)} %get-tuple-element.254), channel_id=1, source_target_pairs={{0,2},{2,4},{4,6},{6,7},{7,5},{5,3},{3,1},{1,0},{8,10},{10,12},{12... | collective-permute-start | bytes 786440 | tf_op jit(solution)/shard_map/ppermute | solution.py:594
  94.4 10.2 %collective-permute-start.15 = (bf16[128,1024]{1,0:T(8,128)(2,1)S(1)}, bf16[128,1024]{1,0:T(8,128)(2,1)S(1)}, u32[]{:S(2)}, u32[]{:S(2)}) collective-permute-start(bf16[128,1024]{1,0:T(8,128)(2,1)S(1)} %slice.75), channel_id=1, source_target_pairs={{0,1},{2,0},{4,2},{6,4},{7,6},{5,7},{3,5},{1,3},{8,9},{10,8},{12,1... | collective-permute-start | bytes 786440 | tf_op jit(solution)/shard_map/ppermute | solution.py:598
  96.0 10.4 %collective-permute-start.14 = (bf16[128,1024]{1,0:T(8,128)(2,1)S(1)}, bf16[128,1024]{1,0:T(8,128)(2,1)S(1)}, u32[]{:S(2)}, u32[]{:S(2)}) collective-permute-start(bf16[128,1024]{1,0:T(8,128)(2,1)S(1)} %slice.74), channel_id=1, source_target_pairs={{0,2},{2,4},{4,6},{6,7},{7,5},{5,3},{3,1},{1,0},{8,10},{10,12},{12... | collective-permute-start | bytes 786440 | tf_op jit(solution)/shard_map/ppermute | solution.py:594
  106.6 15.9 %collective-permute-start.19 = (bf16[256,1024]{1,0:T(8,128)(2,1)S(1)}, bf16[256,1024]{1,0:T(8,128)(2,1)S(1)}, u32[]{:S(2)}, u32[]{:S(2)}) collective-permute-start(bf16[256,1024]{1,0:T(8,128)(2,1)S(1)} %get-tuple-element.276), channel_id=1, source_target_pairs={{0,1},{2,0},{4,2},{6,4},{7,6},{5,7},{3,5},{1,3},{8,9},{10,8},{12,1... | collective-permute-start | bytes 1572872 | tf_op jit(solution)/shard_map/ppermute | solution.py:598
  108.7 13.8 %collective-permute-start.18 = (bf16[256,1024]{1,0:T(8,128)(2,1)S(1)}, bf16[256,1024]{1,0:T(8,128)(2,1)S(1)}, u32[]{:S(2)}, u32[]{:S(2)}) collective-permute-start(bf16[256,1024]{1,0:T(8,128)(2,1)S(1)} %get-tuple-element.274), channel_id=1, source_target_pairs={{0,2},{2,4},{4,6},{6,7},{7,5},{5,3},{3,1},{1,0},{8,10},{10,12},{12... | collective-permute-start | bytes 1572872 | tf_op jit(solution)/shard_map/ppermute | solution.py:594
  122.8 19.4 %collective-permute-start.21 = (bf16[256,1024]{1,0:T(8,128)(2,1)S(1)}, bf16[256,1024]{1,0:T(8,128)(2,1)S(1)}, u32[]{:S(2)}, u32[]{:S(2)}) collective-permute-start(bf16[256,1024]{1,0:T(8,128)(2,1)S(1)} %get-tuple-element.295), channel_id=1, source_target_pairs={{0,1},{2,0},{4,2},{6,4},{7,6},{5,7},{3,5},{1,3},{8,9},{10,8},{12,1... | collective-permute-start | bytes 1572872 | tf_op jit(solution)/shard_map/ppermute | solution.py:598
  124.8 17.4 %collective-permute-start.20 = (bf16[256,1024]{1,0:T(8,128)(2,1)S(1)}, bf16[256,1024]{1,0:T(8,128)(2,1)S(1)}, u32[]{:S(2)}, u32[]{:S(2)}) collective-permute-start(bf16[256,1024]{1,0:T(8,128)(2,1)S(1)} %get-tuple-element.293), channel_id=1, source_target_pairs={{0,2},{2,4},{4,6},{6,7},{7,5},{5,3},{3,1},{1,0},{8,10},{10,12},{12... | collective-permute-start | bytes 1572872 | tf_op jit(solution)/shard_map/ppermute | solution.py:594
  125.8 16.4 %collective-permute-start.23 = (bf16[128,1024]{1,0:T(8,128)(2,1)S(1)}, bf16[128,1024]{1,0:T(8,128)(2,1)S(1)}, u32[]{:S(2)}, u32[]{:S(2)}) collective-permute-start(bf16[128,1024]{1,0:T(8,128)(2,1)S(1)} %get-tuple-element.299), channel_id=1, source_target_pairs={{0,1},{2,0},{4,2},{6,4},{7,6},{5,7},{3,5},{1,3},{8,9},{10,8},{12,1... | collective-permute-start | bytes 786440 | tf_op jit(solution)/shard_map/ppermute | solution.py:598
  127.8 14.4 %collective-permute-start.22 = (bf16[128,1024]{1,0:T(8,128)(2,1)S(1)}, bf16[128,1024]{1,0:T(8,128)(2,1)S(1)}, u32[]{:S(2)}, u32[]{:S(2)}) collective-permute-start(bf16[128,1024]{1,0:T(8,128)(2,1)S(1)} %get-tuple-element.297), channel_id=1, source_target_pairs={{0,2},{2,4},{4,6},{6,7},{7,5},{5,3},{3,1},{1,0},{8,10},{10,12},{12... | collective-permute-start | bytes 786440 | tf_op jit(solution)/shard_map/ppermute | solution.py:594
  142.6 28.5 %collective-permute-start.28 = (bf16[2,256,1024]{2,1,0:T(8,128)(2,1)S(1)}, bf16[2,256,1024]{2,1,0:T(8,128)(2,1)S(1)}, u32[]{:S(2)}, u32[]{:S(2)}) collective-permute-start(bf16[2,256,1024]{2,1,0:T(8,128)(2,1)S(1)} %get-tuple-element.315), channel_id=1, source_target_pairs={{0,8},{8,0},{16,24},{24,16},{1,9},{9,1},{17,25},{25,17},{2,10},{10... | collective-permute-start | bytes 3145736 | tf_op jit(solution)/shard_map/ppermute | solution.py:601
  142.7 14.8 %collective-permute-start.27 = (bf16[256,1024]{1,0:T(8,128)(2,1)S(1)}, bf16[256,1024]{1,0:T(8,128)(2,1)S(1)}, u32[]{:S(2)}, u32[]{:S(2)}) collective-permute-start(bf16[256,1024]{1,0:T(8,128)(2,1)S(1)} %get-tuple-element.313), channel_id=1, source_target_pairs={{0,1},{2,0},{4,2},{6,4},{7,6},{5,7},{3,5},{1,3},{8,9},{10,8},{12,1... | collective-permute-start | bytes 1572872 | tf_op jit(solution)/shard_map/ppermute | solution.py:598
  144.7 23.6 %collective-permute-start.25 = (bf16[256,1024]{1,0:T(8,128)(2,1)S(1)}, bf16[256,1024]{1,0:T(8,128)(2,1)S(1)}, u32[]{:S(2)}, u32[]{:S(2)}) collective-permute-start(bf16[256,1024]{1,0:T(8,128)(2,1)S(1)} %get-tuple-element.310), channel_id=1, source_target_pairs={{0,1},{2,0},{4,2},{6,4},{7,6},{5,7},{3,5},{1,3},{8,9},{10,8},{12,1... | collective-permute-start | bytes 1572872 | tf_op jit(solution)/shard_map/ppermute | solution.py:598
  146.2 22.1 %collective-permute-start.24 = (bf16[256,1024]{1,0:T(8,128)(2,1)S(1)}, bf16[256,1024]{1,0:T(8,128)(2,1)S(1)}, u32[]{:S(2)}, u32[]{:S(2)}) collective-permute-start(bf16[256,1024]{1,0:T(8,128)(2,1)S(1)} %get-tuple-element.308), channel_id=1, source_target_pairs={{0,2},{2,4},{4,6},{6,7},{7,5},{5,3},{3,1},{1,0},{8,10},{10,12},{12... | collective-permute-start | bytes 1572872 | tf_op jit(solution)/shard_map/ppermute | solution.py:594
  146.7 24.4 %collective-permute-start.26 = (bf16[256,1024]{1,0:T(8,128)(2,1)S(1)}, bf16[256,1024]{1,0:T(8,128)(2,1)S(1)}, u32[]{:S(2)}, u32[]{:S(2)}) collective-permute-start(bf16[256,1024]{1,0:T(8,128)(2,1)S(1)} %get-tuple-element.311), channel_id=1, source_target_pairs={{0,2},{2,4},{4,6},{6,7},{7,5},{5,3},{3,1},{1,0},{8,10},{10,12},{12... | collective-permute-start | bytes 1572872 | tf_op jit(solution)/shard_map/ppermute | solution.py:594
  171.6 15.9 %collective-permute-start.31 = (bf16[2,400,384]{2,1,0:T(8,128)(2,1)S(1)}, bf16[2,400,384]{2,1,0:T(8,128)(2,1)S(1)}, u32[]{:S(2)}, u32[]{:S(2)}) collective-permute-start(bf16[2,400,384]{2,1,0:T(8,128)(2,1)S(1)} %get-tuple-element.327), channel_id=1, source_target_pairs={{0,8},{8,0},{16,24},{24,16},{1,9},{9,1},{17,25},{25,17},{2,10},{10... | collective-permute-start | bytes 1843208 | tf_op jit(solution)/shard_map/ppermute | solution.py:601
  171.7 14.3 %collective-permute-start.30 = (bf16[256,1024]{1,0:T(8,128)(2,1)S(1)}, bf16[256,1024]{1,0:T(8,128)(2,1)S(1)}, u32[]{:S(2)}, u32[]{:S(2)}) collective-permute-start(bf16[256,1024]{1,0:T(8,128)(2,1)S(1)} %get-tuple-element.325), channel_id=1, source_target_pairs={{0,1},{2,0},{4,2},{6,4},{7,6},{5,7},{3,5},{1,3},{8,9},{10,8},{12,1... | collective-permute-start | bytes 1572872 | tf_op jit(solution)/shard_map/ppermute | solution.py:598
  172.0 14.0 %collective-permute-start.29 = (bf16[256,1024]{1,0:T(8,128)(2,1)S(1)}, bf16[256,1024]{1,0:T(8,128)(2,1)S(1)}, u32[]{:S(2)}, u32[]{:S(2)}) collective-permute-start(bf16[256,1024]{1,0:T(8,128)(2,1)S(1)} %get-tuple-element.323), channel_id=1, source_target_pairs={{0,2},{2,4},{4,6},{6,7},{7,5},{5,3},{3,1},{1,0},{8,10},{10,12},{12... | collective-permute-start | bytes 1572872 | tf_op jit(solution)/shard_map/ppermute | solution.py:594
  173.8 13.7 %collective-permute-start.32 = (bf16[256,1024]{1,0:T(8,128)(2,1)S(1)}, bf16[256,1024]{1,0:T(8,128)(2,1)S(1)}, u32[]{:S(2)}, u32[]{:S(2)}) collective-permute-start(bf16[256,1024]{1,0:T(8,128)(2,1)S(1)} %fusion.2), channel_id=1, source_target_pairs={{0,16},{8,24},{16,0},{24,8},{1,17},{9,25},{17,1},{25,9},{2,18},{10... | collective-permute-start | bytes 1572872 | tf_op jit(solution)/shard_map/ppermute | solution.py:601
  175.3 1.2 collective-permute-start.33
  188.1 20.2 %collective-permute-start.37 = (bf16[256,1024]{1,0:T(8,128)(2,1)S(1)}, bf16[256,1024]{1,0:T(8,128)(2,1)S(1)}, u32[]{:S(2)}, u32[]{:S(2)}) collective-permute-start(bf16[256,1024]{1,0:T(8,128)(2,1)S(1)} %fusion.1.mine), channel_id=1, source_target_pairs={{0,16},{8,24},{16,0},{24,8},{1,17},{9,25},{17,1},{25,9},{2,18},{10... | collective-permute-start | bytes 1572872 | tf_op jit(solution)/shard_map/ppermute | solution.py:601
  189.7 18.6 %collective-permute-start.35 = (bf16[256,1024]{1,0:T(8,128)(2,1)S(1)}, bf16[256,1024]{1,0:T(8,128)(2,1)S(1)}, u32[]{:S(2)}, u32[]{:S(2)}) collective-permute-start(bf16[256,1024]{1,0:T(8,128)(2,1)S(1)} %get-tuple-element.338), channel_id=1, source_target_pairs={{0,1},{2,0},{4,2},{6,4},{7,6},{5,7},{3,5},{1,3},{8,9},{10,8},{12,1... | collective-permute-start | bytes 1572872 | tf_op jit(solution)/shard_map/ppermute | solution.py:598
  190.0 18.3 %collective-permute-start.34 = (bf16[256,1024]{1,0:T(8,128)(2,1)S(1)}, bf16[256,1024]{1,0:T(8,128)(2,1)S(1)}, u32[]{:S(2)}, u32[]{:S(2)}) collective-permute-start(bf16[256,1024]{1,0:T(8,128)(2,1)S(1)} %get-tuple-element.336), channel_id=1, source_target_pairs={{0,2},{2,4},{4,6},{6,7},{7,5},{5,3},{3,1},{1,0},{8,10},{10,12},{12... | collective-permute-start | bytes 1572872 | tf_op jit(solution)/shard_map/ppermute | solution.py:594
  191.7 16.6 %collective-permute-start.36 = (bf16[400,384]{1,0:T(8,128)(2,1)S(1)}, bf16[400,384]{1,0:T(8,128)(2,1)S(1)}, u32[]{:S(2)}, u32[]{:S(2)}) collective-permute-start(bf16[400,384]{1,0:T(8,128)(2,1)S(1)} %fusion.5), channel_id=1, source_target_pairs={{0,16},{8,24},{16,0},{24,8},{1,17},{9,25},{17,1},{25,9},{2,18},{10... | collective-permute-start | bytes 921608 | tf_op jit(solution)/shard_map/ppermute | solution.py:601
  192.2 16.1 %collective-permute-start.38 = (f32[8,1024]{1,0:T(8,128)S(1)}, f32[8,1024]{1,0:T(8,128)S(1)}, u32[]{:S(2)}, u32[]{:S(2)}) collective-permute-start(f32[8,1024]{1,0:T(8,128)S(1)} %add.79), channel_id=1, source_target_pairs={{0,16},{8,24},{16,0},{24,8},{1,17},{9,25},{17,1},{25,9},{2,18},{10... | collective-permute-start | bytes 98312 | tf_op jit(solution)/shard_map/ppermute | solution.py:601
  208.5 9.8 %collective-permute-start.41 = (bf16[256,1024]{1,0:T(8,128)(2,1)S(1)}, bf16[256,1024]{1,0:T(8,128)(2,1)S(1)}, u32[]{:S(2)}, u32[]{:S(2)}) collective-permute-start(bf16[256,1024]{1,0:T(8,128)(2,1)S(1)} %fusion.1.mine), channel_id=1, source_target_pairs={{0,8},{8,0},{16,24},{24,16},{1,9},{9,1},{17,25},{25,17},{2,10},{10... | collective-permute-start | bytes 1572872 | tf_op jit(solution)/shard_map/ppermute | solution.py:601
  208.6 9.8 %collective-permute-start.40 = (bf16[256,1024]{1,0:T(8,128)(2,1)S(1)}, bf16[256,1024]{1,0:T(8,128)(2,1)S(1)}, u32[]{:S(2)}, u32[]{:S(2)}) collective-permute-start(bf16[256,1024]{1,0:T(8,128)(2,1)S(1)} %collective-permute-done.37.third), channel_id=1, source_target_pairs={{0,8},{8,0},{16,24},{24,16},{1,9},{9,1},{17,25},{25,17},{2,10},{10... | collective-permute-start | bytes 1572872 | tf_op jit(solution)/shard_map/ppermute | solution.py:601
  209.1 9.3 %collective-permute-start.39 = (bf16[400,384]{1,0:T(8,128)(2,1)S(1)}, bf16[400,384]{1,0:T(8,128)(2,1)S(1)}, u32[]{:S(2)}, u32[]{:S(2)}) collective-permute-start(bf16[400,384]{1,0:T(8,128)(2,1)S(1)} %fusion.4.mine), channel_id=1, source_target_pairs={{0,16},{8,24},{16,0},{24,8},{1,17},{9,25},{17,1},{25,9},{2,18},{10... | collective-permute-start | bytes 921608 | tf_op jit(solution)/shard_map/ppermute | solution.py:601
  210.6 7.8 %collective-permute-start.42 = (bf16[400,384]{1,0:T(8,128)(2,1)S(1)}, bf16[400,384]{1,0:T(8,128)(2,1)S(1)}, u32[]{:S(2)}, u32[]{:S(2)}) collective-permute-start(bf16[400,384]{1,0:T(8,128)(2,1)S(1)} %fusion.4.mine), channel_id=1, source_target_pairs={{0,8},{8,0},{16,24},{24,16},{1,9},{9,1},{17,25},{25,17},{2,10},{10... | collective-permute-start | bytes 921608 | tf_op jit(solution)/shard_map/ppermute | solution.py:601
  210.6 3.9 %collective-permute-start.43 = (f32[8,1024]{1,0:T(8,128)S(1)}, f32[8,1024]{1,0:T(8,128)S(1)}, u32[]{:S(2)}, u32[]{:S(2)}) collective-permute-start(f32[8,1024]{1,0:T(8,128)S(1)} %add.82), channel_id=1, source_target_pairs={{0,1},{1,0},{2,3},{3,2},{4,5},{5,4},{6,7},{7,6},{8,9},{9,8},{10,11... | collective-permute-start | bytes 98312 | tf_op jit(solution)/shard_map/ppermute | solution.py:604
  218.3 4.1 %collective-permute-start.44 = (bf16[400,384]{1,0:T(8,128)(2,1)S(1)}, bf16[400,384]{1,0:T(8,128)(2,1)S(1)}, u32[]{:S(2)}, u32[]{:S(2)}) collective-permute-start(bf16[400,384]{1,0:T(8,128)(2,1)S(1)} %collective-permute-done.39.third), channel_id=1, source_target_pairs={{0,8},{8,0},{16,24},{24,16},{1,9},{9,1},{17,25},{25,17},{2,10},{10... | collective-permute-start | bytes 921608 | tf_op jit(solution)/shard_map/ppermute | solution.py:601
  218.4 4.0 %collective-permute-start.45 = (f32[8,1024]{1,0:T(8,128)S(1)}, f32[8,1024]{1,0:T(8,128)S(1)}, u32[]{:S(2)}, u32[]{:S(2)}) collective-permute-start(f32[8,1024]{1,0:T(8,128)S(1)} %add.83), channel_id=1, source_target_pairs={{0,2},{1,3},{2,0},{3,1},{4,6},{5,7},{6,4},{7,5},{8,10},{9,11},{10,... | collective-permute-start | bytes 98312 | tf_op jit(solution)/shard_map/ppermute | solution.py:604
  222.5 5.2 %collective-permute-start.46 = (f32[8,1024]{1,0:T(8,128)S(1)}, f32[8,1024]{1,0:T(8,128)S(1)}, u32[]{:S(2)}, u32[]{:S(2)}) collective-permute-start(f32[8,1024]{1,0:T(8,128)S(1)} %add.84), channel_id=1, source_target_pairs={{0,4},{1,5},{2,6},{3,7},{4,0},{5,1},{6,2},{7,3},{8,12},{9,13},{10,... | collective-permute-start | bytes 98312 | tf_op jit(solution)/shard_map/ppermute | solution.py:604
  (33 other events, 192.6 us)

commit v3 on v1

--- a/solution.py
+++ b/solution.py
@@ -37,7 +37,7 @@
     return lax.broadcasted_iota(jnp.int32, dims, len(dims) - 1)
 
 
-def prepare_kernel(table, rates, omega, keep, ahead, behind, mix_high, mix_low, turned_high, turned_low):
+def prepare_kernel(table, rates, omega, docs_col, keep, ahead, behind, mix_high, mix_low, turned_high, turned_low):
     rows = keep.shape[0]
     start = (table[1] * pl.num_programs(0) + pl.program_id(0)) * rows
     places = start + lax.broadcasted_iota(jnp.int32, (rows, LANES), 0)
@@ -139,6 +139,23 @@
     value_out[...] = value
     key = jnp.where(chosen, feat[:, width:], 0.0).astype(BF16)
     state[...] += dot(key, jnp.concatenate([value, jnp.ones_like(value)], axis=1), TN)
+
+
+def load_block(refs, keep, sems):
+    def copy(k):
+        return pltpu.make_async_copy(refs[k], keep.at[k % 2], sems.at[k % 2])
+
+    for k in range(len(refs)):
+
+        @pl.when(pl.program_id(0) == k)
+        def _(k=k):
+            if k == 0:
+                copy(0).start()
+            if k + 1 < len(refs):
+                copy(k + 1).start()
+            copy(k).wait()
+
+    return keep[pl.program_id(0) % 2]
 
 
 def own_features_kernel(count, blocks, table, docs, *refs):
@@ -161,20 +178,15 @@
         state_out,
         state,
         x_keep,
+        x_sems,
     ) = refs[blocks:]
 
     @pl.when(pl.program_id(0) == 0)
     def _():
         state[...] = jnp.zeros_like(state)
 
-    for k in range(blocks):
-
-        @pl.when(pl.program_id(0) == k)
-        def _(k=k):
-            x_keep[...] = x_refs[k][...]
-
-    rows = x_keep.shape[0]
-    x = x_keep[...].astype(F32)
+    rows = x_keep.shape[1]
+    x = load_block(x_refs, x_keep, x_sems).astype(F32)
     mean = jnp.mean(x, axis=-1, keepdims=True)
     centred = x - mean
     scale = lax.rsqrt(jnp.mean(centred * centred, axis=-1, keepdims=True) + EPS)
@@ -476,11 +488,12 @@
 
 
 def write_block(outs, values):
-    for k, out in enumerate(outs):
+    kept, sent = outs
+    for k in range(2 * kept.shape[0]):
 
         @pl.when(pl.program_id(0) == k)
-        def _(out=out):
-            out[...] = values
+        def _(k=k):
+            (sent if k % 2 else kept)[k // 2] = values
 
 
 def norm_grad_kernel(
@@ -514,13 +527,19 @@
     write_block(outs, (one * affine[0:1] + two * affine[2:3]).astype(BF16))
 
 
-def first_pack_kernel(table, weight, dense, bias, out):
+def first_pack_kernel(table, weight, dense, bias, up_bias, out):
     rows, small = weight.shape[0], dense.shape[0]
     if out.shape[1] > min(weight.shape[1], dense.shape[1]):
         out[...] = jnp.zeros_like(out)
     out[:rows, : weight.shape[1]] = weight[...]
     out[rows : rows + small, : dense.shape[1]] = dense[...]
-    out[rows + small :, : bias.shape[1]] = jnp.broadcast_to(bias[...], (16, bias.shape[1]))
+    first = bias[...].astype(F32)
+    second = up_bias[table[2]].astype(F32)
+    if first.shape[1] > second.shape[1]:
+        rest = jnp.zeros((1, first.shape[1] - second.shape[1]), F32)
+        second = jnp.concatenate([second, rest], axis=1)
+    row = lax.broadcasted_iota(jnp.int32, (16, first.shape[1]), 0)
+    out[rows + small :, : first.shape[1]] = jnp.where(row < 8, first, second).astype(BF16)
 
 
 def arrange_kernel(table, up, down, bias, own_up, own_down, own_bias, pack, turned):
@@ -533,32 +552,29 @@
         own_down[k * step : (k + 1) * step] = down[pl.ds(begin, step)]
     own_bias[...] = jnp.concatenate([bias[part ^ k].astype(F32) for k in range(QUARTERS)], axis=1)
     pack[:step] = own_up[:step]
-    pack[step : 2 * step] = own_down[:step]
-    pack[2 * step :] = jnp.zeros((16, pack.shape[1]), BF16)
-    pack[2 * step :, :step] = jnp.broadcast_to(bias[part], (16, step))
-
-
-def collect_first_kernel(table, mine, others, third, far_qkv, far_dense):
+    pack[step:] = own_down[:step]
+
+
+def collect_first_kernel(table, mine, near, third, last, far_qkv, far_dense, far_up_bias):
     part = table[2]
     step = far_qkv.shape[0] // QUARTERS
     small = far_dense.shape[0]
-    size = mine.shape[0]
-    for k, (ref, base) in enumerate(((mine, 0), (others, 0), (third, 0), (others, size))):
+    hidden = far_up_bias.shape[1] // QUARTERS
+    biases = []
+    for k, ref in enumerate((mine, near, third, last)):
         begin = pl.multiple_of((part ^ k) * step, step)
-        far_qkv[pl.ds(begin, step)] = ref[base : base + step, : far_qkv.shape[1]]
-        far_dense[:, pl.ds(begin, step)] = ref[base + step : base + step + small, :step]
-
-
-def collect_second_kernel(table, mine, others, third, far_up, far_down, far_bias):
-    step = far_down.shape[0] // QUARTERS
-    size = mine.shape[0]
-    biases = []
-    for k, (ref, base) in enumerate(((mine, 0), (others, 0), (third, 0), (others, size))):
-        far_up[k * step : (k + 1) * step] = ref[base : base + step]
-        far_down[k * step : (k + 1) * step] = ref[base + step : base + 2 * step]
-        tail = ref[base + 2 * step : base + size].astype(F32)
-        biases.append(tail[0:1, :step])
-    far_bias[...] = jnp.concatenate(biases, axis=1)
+        far_qkv[pl.ds(begin, step)] = ref[:step, : far_qkv.shape[1]]
+        far_dense[:, pl.ds(begin, step)] = ref[step : step + small, :step]
+        tail = ref[step + small :].astype(F32)
+        biases.append(tail[8:9, :hidden])
+    far_up_bias[...] = jnp.concatenate(biases, axis=1)
+
+
+def collect_second_kernel(mine, near, third, last, far_up, far_down):
+    step = mine.shape[0] // 2
+    for k, ref in enumerate((mine, near, third, last)):
+        far_up[k * step : (k + 1) * step] = ref[:step]
+        far_down[k * step : (k + 1) * step] = ref[step:]
 
 
 def collect_grad_kernel(*refs):
@@ -708,7 +724,7 @@
     count = qkv_cols // (3 * HEAD_DIM)
     width = count * HEAD_DIM
     hidden_cols = up_weight.shape[1]
-    dense_part, hidden_part, model_part = width // QUARTERS, hidden_cols // QUARTERS, model // QUARTERS
+    hidden_part, model_part = hidden_cols // QUARTERS, model // QUARTERS
     member = lax.axis_index("dp")
     place = lax.axis_index("tensor")
     half, slot = place // inner, place % inner
@@ -733,16 +749,22 @@
     def gather(block):
         return [block] + [swap(block, 0, k) for k in range(1, inner)]
 
-    line = []
-
-    def run(step, *operands, gate=0, wait=()):
+    line, due = [], [()]
+
+    def run(step, *operands, gate=0):
         operands = list(operands)
-        held = tuple(line[-1:]) + tuple(wait)
+        held = tuple(line[-1:]) + due[0]
         if held:
             operands[gate] = after(operands[gate], *held)
         result = step(*operands)
         line.append(result[0] if isinstance(result, (tuple, list)) else result)
         return result
+
+    def tick(*arrived):
+        due[0] = tuple(arrived) + tuple(line[-1:])
+
+    def now(values):
+        return after(values, *due[0])
 
     table = jnp.stack([slot, half, part]).astype(jnp.int32)
     plain = lambda cols: pl.BlockSpec((rows, cols), lambda k, *s: (k, 0))
@@ -786,6 +808,7 @@
 
         return step
 
+    first_rows, first_cols = model_part + width + 16, max(qkv_cols, model_part)
     docs = doc_ids.reshape(-1)
     docs_col = docs.reshape(-1, 1)
     docs_row = docs.reshape(tensor_size, 1, rows)
@@ -794,9 +817,118 @@
     rates = np.where(lane < ROT, 10000.0 ** (-(lane % (ROT // 2)) * 2.0 / ROT), 0.0)
     rates = jnp.asarray(rates[None, :], F32)
     own_bias = qkv_bias.reshape(1, -1)
-
-    x_blocks = gather(inputs)
-    first_rows, first_cols = model_part + width + 16, max(qkv_cols, model_part)
+    up_bias_parts = up_bias.reshape(QUARTERS, 1, hidden_part)
+
+    dense_part = width // QUARTERS
+    pack_rows = 2 * hidden_part + dense_part + 16
+    second_rows = 2 * hidden_part
+    wide = pltpu.VMEM((2, width, 2 * width), F32)
+    narrow = pltpu.VMEM((width, 2 * width), F32)
+    mine_col = pl.BlockSpec(
+        (rows, 1), lambda k, table, docs: ((k ^ table[0]) + table[1] * inner, 0)
+    )
+    def simple(kernel, name, outs, in_specs, out_specs, price):
+        return call(kernel, name, outs, in_specs, out_specs, price, prefetch=0)
+
+    def up_projection(weight, bias):
+        return run(
+            simple(
+                up_kernel,
+                "up",
+                (shape((tokens, hidden_cols), BF16),) * 2,
+                [plain(model), whole(hidden_cols, model), whole(1, hidden_cols)],
+                [plain(hidden_cols)] * 2,
+                cost(2 * tokens * model * hidden_cols, 5e6, 2 * tokens * hidden_cols),
+            ),
+            norm_two,
+            weight,
+            bias,
+        )
+
+    def down_back(weight, slope):
+        return run(
+            simple(
+                down_back_kernel,
+                "down_back",
+                (shape((tokens, hidden_cols), BF16), shape((8, hidden_cols), F32)),
+                [plain(model), whole(hidden_cols, model), plain(hidden_cols)],
+                [plain(hidden_cols), whole(8, hidden_cols)],
+                cost(2 * tokens * model * hidden_cols, 5e6),
+            ),
+            grad_all,
+            weight,
+            slope,
+            gate=2,
+        )
+
+    def add(a, b):
+        return (a.astype(F32) + b.astype(F32)).astype(BF16)
+
+    def rest(total):
+        step = QUARTERS
+        while step < dp_size:
+            total = add(total, swap(total, step, 0))
+            step *= 2
+        return total
+
+    def add_three(a, b, c):
+        return (a.astype(F32) + b.astype(F32) + c.astype(F32)).astype(BF16)
+
+    class PairSum:
+        def __init__(self, parts):
+            self.kept, self.sent = parts
+            self.bit = 1
+
+        def start(self):
+            self.moving = swap(now(self.sent), 0, self.bit)
+            self.bit *= 2
+            return self.moving
+
+        def more(self):
+            return self.bit < inner
+
+        def add(self):
+            def halve(a, b):
+                total = add(a, b)
+                return total[0::2], total[1::2]
+
+            self.kept, self.sent = run(halve, self.kept, self.moving)
+
+        def result(self):
+            return self.kept[0], self.moving[0]
+
+    def hidden_weights(active, hidden_grad, side, sums_row):
+        return run(
+            call(
+                hidden_weights_kernel,
+                "hidden_weights",
+                (shape((2, pack_rows, model), BF16),) * 2,
+                [
+                    whole(tokens, hidden_cols),
+                    whole(tokens, hidden_cols),
+                    pl.BlockSpec((tokens, width), lambda k, table: (0, side))
+                    if width % LANES == 0
+                    else whole(tokens, width),
+                    whole(tokens, model),
+                    whole(tokens, model),
+                    whole(8, hidden_cols),
+                ],
+                [whole(2, pack_rows, model)] * 2,
+                cost(2 * tokens * model * (2 * hidden_cols + width), 9e6),
+                scratch=[pltpu.VMEM((width, model), BF16)],
+                steps=1,
+            ),
+            table,
+            active,
+            hidden_grad,
+            merged if width % LANES == 0 else merged[:, side * width : (side + 1) * width],
+            grad_all,
+            norm_two,
+            sums_row,
+            gate=2,
+        )
+
+    x_blocks = [inputs] + [swap(inputs, 0, k) for k in range(1, inner)]
     first_pack = run(
         call(
             first_pack_kernel,
@@ -806,6 +938,7 @@
                 pl.BlockSpec((model_part, qkv_cols), lambda k, table: (table[2], 0)),
                 pl.BlockSpec((width, model_part), lambda k, table: (0, table[2])),
                 whole(1, qkv_cols),
+                whole(QUARTERS, 1, hidden_part),
             ],
             whole(first_rows, first_cols),
             cost(1e5, 4e5),
@@ -815,10 +948,9 @@
         qkv_weight,
         dense_weight,
         own_bias,
+        up_bias_parts,
     )
     first_mine = swap(first_pack, 0, inner)
-    pack_rows = 2 * hidden_part + dense_part + 16
-    second_rows = 2 * hidden_part + 16
     own_up, own_down, own_up_bias, second_pack = run(
         once(
             arrange_kernel,
@@ -834,31 +966,30 @@
         table,
         up_weight,
         down_weight,
-        up_bias.reshape(QUARTERS, 1, hidden_part),
+        up_bias_parts,
         gate=3,
     )
-    second_mine = swap(second_pack, 0, inner)
     square = whole(LANES, LANES)
     keep, ahead, behind, mix_high, mix_low, turned_high, turned_low = run(
         call(
             prepare_kernel,
             "prepare",
             (shape((tokens, LANES), F32),) * 3 + (shape((LANES, LANES), BF16),) * 4,
-            [whole(1, LANES), whole(HEAD_DIM, HEAD_DIM)],
+            [whole(1, LANES), whole(HEAD_DIM, HEAD_DIM), pl.BlockSpec(memory_space=pl.ANY)],
             [plain(LANES)] * 3 + [square] * 4,
             cost(1e6, 2e6),
         ),
         table,
-        rates,
+        after(rates, affine, docs_row),
         feature_omega,
+        docs_col,
         gate=2,
     )
 
-    wide = pltpu.VMEM((2, width, 2 * width), F32)
-    narrow = pltpu.VMEM((width, 2 * width), F32)
-    mine_col = pl.BlockSpec(
-        (rows, 1), lambda k, table, docs: ((k ^ table[0]) + table[1] * inner, 0)
-    )
+    tick(first_mine, *x_blocks[1:])
+    first_third, first_near = swap(now(first_mine), 2, 0), swap(now(first_mine), 1, 0)
+    second_mine = swap(now(second_pack), 0, inner)
+    grad_blocks = [out_grad] + [swap(now(out_grad), 0, k) for k in range(1, inner - 1)]
     norm_one, norm_two, unit, own_feat, own_value, near_state = run(
         call(
             functools.partial(own_features_kernel, count, inner),
@@ -871,7 +1002,7 @@
                 shape((tokens, width), BF16),
                 shape((width, LANES), F32),
             ),
-            [whole(rows, model)] * inner
+            [pl.BlockSpec(memory_space=pltpu.HBM)] * inner
             + [
                 whole(4, model),
                 whole(model, qkv_cols),
@@ -893,7 +1024,11 @@
             ],
             cost(2 * tokens * model * qkv_cols, 12e6),
             prefetch=2,
-            scratch=[narrow, pltpu.VMEM((rows, model), BF16)],
+            scratch=[
+                narrow,
+                pltpu.VMEM((2, rows, model), BF16),
+                pltpu.SemaphoreType.DMA((2,)),
+            ],
         ),
         table,
         docs,
@@ -908,28 +1043,30 @@
         mix_low,
         docs_col,
         gate=2 + inner,
-        wait=(first_mine,),
-    )
-    here_x = tuple(x_blocks[1:]) + (keep,)
-    first_third = swap(after(first_mine, *here_x), 2, 0)
-    grad_blocks = gather(after(out_grad, *here_x))
-    first_others = swap(
-        run(lambda a, b: jnp.concatenate([a, b], axis=0), first_mine, first_third), 1, 0
-    )
-    far_qkv, far_dense = run(
+    )
+    tick(first_third, first_near)
+    first_last = swap(now(first_third), 1, 0)
+    grad_blocks.append(swap(now(out_grad), 0, inner - 1))
+    own_active, own_slope = up_projection(own_up, own_up_bias)
+
+    tick(first_last)
+    far_qkv, far_dense, far_up_bias = run(
         once(
             collect_first_kernel,
             "collect_first",
-            (shape((model, qkv_cols), BF16), shape((width, model), BF16)),
+            (
+                shape((model, qkv_cols), BF16),
+                shape((width, model), BF16),
+                shape((1, hidden_cols), F32),
+            ),
         ),
         table,
         first_mine,
-        first_others,
+        first_near,
         first_third,
+        first_last,
         gate=1,
-        wait=(second_mine,),
-    )
-    second_third = swap(second_mine, 2, 0)
+    )
     far_feat, far_value, state = run(
         call(
             functools.partial(far_features_kernel, count),
@@ -971,27 +1108,8 @@
         gate=2,
     )
     first_state = across(state, 0)
-
-    def simple(kernel, name, outs, in_specs, out_specs, price):
-        return call(kernel, name, outs, in_specs, out_specs, price, prefetch=0)
-
-    def up_projection(weight, bias):
-        return run(
-            simple(
-                up_kernel,
-                "up",
-                (shape((tokens, hidden_cols), BF16),) * 2,
-                [plain(model), whole(hidden_cols, model), whole(1, hidden_cols)],
-                [plain(hidden_cols)] * 2,
-                cost(2 * tokens * model * hidden_cols, 5e6, 2 * tokens * hidden_cols),
-            ),
-            norm_two,
-            weight,
-            bias,
-        )
-
-    own_active, own_slope = up_projection(own_up, own_up_bias)
-
+    tick(first_state, second_mine, *grad_blocks[1:])
+    second_third, second_near = swap(now(second_mine), 2, 0), swap(now(second_mine), 1, 0)
     block_row = pl.BlockSpec((1, 1, rows), lambda m, table, docs: (m + table[1] * inner, 0, 0))
     block_col = pl.BlockSpec((rows, 1), lambda m, table, docs: (m + table[1] * inner, 0))
     mixed, merged, inverse, states = run(
@@ -1044,8 +1162,6 @@
         *grad_blocks,
         gate=1,
     )
-    both_second = run(lambda a, b: jnp.concatenate([a, b], axis=0), second_mine, second_third)
-    second_others = swap(both_second, 1, 0)
     merged_grad, later = run(
         call(
             functools.partial(later_kernel, count),
@@ -1070,89 +1186,36 @@
         gate=2,
     )
     first_later = across(later, 1)
-
-    def down_back(weight, slope):
-        return run(
-            simple(
-                down_back_kernel,
-                "down_back",
-                (shape((tokens, hidden_cols), BF16), shape((8, hidden_cols), F32)),
-                [plain(model), whole(hidden_cols, model), plain(hidden_cols)],
-                [plain(hidden_cols), whole(8, hidden_cols)],
-                cost(2 * tokens * model * hidden_cols, 5e6),
-            ),
-            grad_all,
-            weight,
-            slope,
-            gate=2,
-        )
-
-    def add(a, b):
-        return (a.astype(F32) + b.astype(F32)).astype(BF16)
-
-    def rest(total):
-        step = QUARTERS
-        while step < dp_size:
-            total = add(total, swap(total, step, 0))
-            step *= 2
-        return total
-
-    def hidden_weights(active, hidden_grad, side, sums_row):
-        return run(
-            call(
-                hidden_weights_kernel,
-                "hidden_weights",
-                (shape((2, pack_rows, model), BF16),) * 2,
-                [
-                    whole(tokens, hidden_cols),
-                    whole(tokens, hidden_cols),
-                    pl.BlockSpec((tokens, width), lambda k, table: (0, side))
-                    if width % LANES == 0
-                    else whole(tokens, width),
-                    whole(tokens, model),
-                    whole(tokens, model),
-                    whole(8, hidden_cols),
-                ],
-                [whole(2, pack_rows, model)] * 2,
-                cost(2 * tokens * model * (2 * hidden_cols + width), 9e6),
-                scratch=[pltpu.VMEM((width, model), BF16)],
-                steps=1,
-            ),
-            table,
-            active,
-            hidden_grad,
-            merged if width % LANES == 0 else merged[:, side * width : (side + 1) * width],
-            grad_all,
-            norm_two,
-            sums_row,
-            gate=2,
-        )
-
+    tick(second_third)
+    second_last = swap(now(second_third), 1, 0)
     own_hidden_grad, own_up_sums = down_back(own_down, own_slope)
     own_kept, own_sent = hidden_weights(own_active, own_hidden_grad, 0, own_up_sums)
-    own_got = swap(own_sent, 1, 0)
-    far_up, far_down, far_up_bias = run(
+    tick(second_last, second_near, first_later)
+    own_got = swap(now(own_sent), 1, 0)
+    far_up, far_down = run(
         once(
             collect_second_kernel,
             "collect_second",
-            (
-                shape((hidden_cols, model), BF16),
-                shape((hidden_cols, model), BF16),
-                shape((1, hidden_cols), F32),
-            ),
+            (shape((hidden_cols, model), BF16),) * 2,
+            prefetch=0,
         ),
-        table,
         second_mine,
-        second_others,
+        second_near,
         second_third,
-        gate=1,
+        second_last,
     )
     far_active, far_slope = up_projection(far_up, far_up_bias)
+    far_hidden_grad, far_up_sums = down_back(far_down, far_slope)
+    far_kept, far_sent = hidden_weights(far_active, far_hidden_grad, 1, far_up_sums)
+    tick(own_got)
+    own_next = run(add, own_kept[1], own_got[1])
+    tick()
+    far_got = swap(now(far_sent), 1, 0)
     partial_out = run(
         simple(
             out_kernel,
             "out",
-            (shape((rows, model), BF16),) * inner,
+            (shape((inner // 2, rows, model), BF16),) * 2,
             [
                 plain(2 * width),
                 plain(hidden_cols),
@@ -1162,7 +1225,7 @@
                 whole(hidden_cols, model),
                 whole(hidden_cols, model),
             ],
-            [whole(rows, model)] * inner,
+            [whole(inner // 2, rows, model)] * 2,
             cost(4 * tokens * model * (width + hidden_cols), 8e6),
         ),
         merged,
@@ -1174,17 +1237,12 @@
         far_down,
     )
 
-    def scatter(blocks):
-        return [blocks[0]] + [swap(blocks[k], 0, k) for k in range(1, inner)]
-
-    out_parts = scatter(partial_out)
-
-    far_hidden_grad, far_up_sums = down_back(far_down, far_slope)
-    own_next = run(add, own_kept[1], own_got[1])
-    own_cross = swap(own_next, 2, 0)
-    far_kept, far_sent = hidden_weights(far_active, far_hidden_grad, 1, far_up_sums)
-    far_got = swap(far_sent, 1, 0)
-
+    tick(far_got)
+    far_next = run(add, far_kept[1], far_got[1])
+    tick()
+    far_cross = swap(now(far_next), 2, 0)
+    out_sum = PairSum(partial_out)
+    out_moving = out_sum.start()
     back = lambda cols: pl.BlockSpec((rows, cols), lambda m, table, docs: ((inner - 1 - m) ^ table[0], 0))
     back_straight = lambda cols: pl.BlockSpec((rows, cols), lambda m, *s: (inner - 1 - m, 0))
     own_pg, far_pg = run(
@@ -1239,16 +1297,6 @@
         turned_low,
         gate=8,
     )
-    far_next = run(add, far_kept[1], far_got[1])
-    far_cross = swap(far_next, 2, 0)
-    own_quad = run(lambda a, b, c: add(add(a, b), c), own_kept[0], own_got[0], own_cross)
-    layer_out = run(
-        once(finish_out_kernel, "finish_out", shape((rows, model), BF16), prefetch=0),
-        inputs,
-        out_bias.reshape(1, -1),
-        *out_parts,
-        gate=2,
-    )
     kept, sent = run(
         once(
             qkv_weights_kernel,
@@ -1262,12 +1310,15 @@
         norm_one,
         gate=3,
     )
-    got = swap(sent, 1, 0)
+    tick(far_cross)
+    far_quad = run(add_three, far_kept[0], far_got[0], far_cross)
+    tick()
+    far_home = swap(now(far_quad), 0, inner)
     norm_grads = run(
         simple(
             norm_grad_kernel,
             "norm_grad",
-            (shape((8, model), F32),) + (shape((rows, model), BF16),) * inner,
+            (shape((8, model), F32),) + (shape((inner // 2, rows, model), BF16),) * 2,
             [
                 plain(qkv_cols),
                 plain(qkv_cols),
@@ -1281,7 +1332,7 @@
                 whole(4, model),
                 whole(8, model),
             ],
-            [whole(8, model)] + [whole(rows, model)] * inner,
+            [whole(8, model)] + [whole(inner // 2, rows, model)] * 2,
             cost(4 * tokens * model * (qkv_cols + hidden_cols), 12e6),
         ),
         own_pg,
@@ -1297,42 +1348,80 @@
         grad_sums,
         gate=8,
     )
-    e_parts = scatter(norm_grads[1:])
+    e_sum = PairSum(norm_grads[1:])
+    steps = [(1 << k, 0) for k in range(dp_size.bit_length() - 1)]
+    steps += [(0, 1 << k) for k in range(tensor_size.bit_length() - 1)]
+    small = norm_grads[0]
+
+    def small_start():
+        return swap(now(small), *steps.pop(0))
+
+    def small_add(moved):
+        return run(lambda a, b: a + b, small, moved)
+
+    tick(out_moving)
+    out_sum.add()
+    tick()
+    e_moving = e_sum.start()
+    out_moving = out_sum.start()
+    got, own_cross = swap(now(sent), 1, 0), swap(now(own_next), 2, 0)
+    tick(got)
     cross_sent = run(add, kept[2:], got[2:])
-    crossed = swap(cross_sent, 2, 0)
-    far_quad = run(lambda a, b, c: add(add(a, b), c), far_kept[0], far_got[0], far_cross)
-    far_home = swap(far_quad, 0, inner)
-    far_piece = run(lambda a, b, c: add(add(a, b), c), kept[1], got[1], crossed[1])
-    far_piece_home = swap(far_piece, 0, inner)
-    own_piece = run(lambda a, b, c: add(add(a, b), c), kept[0], got[0], crossed[0])
+    tick()
+    crossed = swap(now(cross_sent), 2, 0)
+    tick(out_moving)
+    while out_sum.more():
+        out_sum.add()
+        tick(out_sum.start())
+    layer_out = run(
+        once(finish_out_kernel, "finish_out", shape((rows, model), BF16), prefetch=0),
+        inputs,
+        out_bias.reshape(1, -1),
+        *out_sum.result(),
+        gate=2,
+    )
+    tick(crossed)
+    far_piece = run(add_three, kept[1], got[1], crossed[1])
+    own_piece = run(add_three, kept[0], got[0], crossed[0])
+    tick()
+    far_piece_home = swap(now(far_piece), 0, inner)
+    tick(far_home, own_cross)
+    own_quad = run(add_three, own_kept[0], own_got[0], own_cross)
+    lower_mine = rest(run(add, own_quad, far_home))
+    tick()
+    lower_third, lower_near = swap(now(lower_mine), 2, 0), swap(now(lower_mine), 1, 0)
+    tick(e_moving)
+    e_sum.add()
+    tick()
+    e_moving = e_sum.start()
+    moved_small = small_start()
+    tick(far_piece_home, lower_near, moved_small)
+    upper_mine = rest(run(add, own_piece, far_piece_home))
+    small = small_add(moved_small)
+    tick()
+    upper_third, upper_near = swap(now(upper_mine), 2, 0), swap(now(upper_mine), 1, 0)
+    moved_small = small_start()
+    tick(e_moving)
+    while e_sum.more():
+        e_sum.add()
+        tick(e_sum.start())
     input_grad = run(
         once(finish_in_kernel, "finish_in", shape((rows, model), F32), prefetch=0),
         inputs,
         out_grad,
-        *e_parts,
+        *e_sum.result(),
         gate=2,
     )
-    upper_mine = rest(run(add, own_piece, far_piece_home))
-    upper_third = swap(upper_mine, 2, 0)
-    upper_near = swap(upper_mine, 1, 0)
-    lower_mine = rest(run(add, own_quad, far_home))
-    lower_third = swap(lower_mine, 2, 0)
-    lower_near = swap(lower_mine, 1, 0)
-    upper = (upper_mine, upper_near, upper_third, swap(upper_third, 1, 0))
-    lower = (lower_mine, lower_near, lower_third, swap(lower_third, 1, 0))
-
-    small = after(norm_grads[0], input_grad)
-    step = 1
-    while step < dp_size:
-        small = small + swap(small, step, 0)
-        step *= 2
-    step = 1
-    while step < tensor_size:
-        small = small + swap(small, 0, step)
-        step *= 2
-    cols = model // tensor_size
-    small = lax.dynamic_slice_in_dim(small, place * cols, cols, 1)
-
+    tick(lower_third, moved_small)
+    lower = (lower_mine, lower_near, lower_third, swap(now(lower_third), 1, 0))
+    small = small_add(moved_small)
+    tick(upper_third, upper_near)
+    upper = (upper_mine, upper_near, upper_third, swap(now(upper_third), 1, 0))
+    moved_small = small_start()
+    tick(lower[3], moved_small)
+    small = small_add(moved_small)
+    tick()
+    moved_small = small_start()
     up_grad, down_grad, dense_grad, up_bias_grad = run(
         once(
             finish_hidden_kernel,
@@ -1349,6 +1438,10 @@
         *lower,
         gate=1,
     )
+    tick(moved_small, upper[3])
+    small = small_add(moved_small)
+    tick()
+    moved_small = small_start()
     qkv_grad, qkv_bias_grad = run(
         once(
             finish_qkv_kernel,
@@ -1359,6 +1452,13 @@
         *upper,
         gate=1,
     )
+
+    small = small + moved_small
+    while steps:
+        tick()
+        small = small_add(small_start())
+    cols = model // tensor_size
+    small = lax.dynamic_slice_in_dim(small, place * cols, cols, 1)
 
     return (
         layer_out,

time: 251 us -> 221 us (0.88)
  waiting for transfers between devices: 116 us -> 101 us
  local copies, waits for them, and re-layouts: 15.7 us -> 8.51 us
  starting transfers between devices: 38.5 us -> 32.9 us
  Pallas kernels: 76.5 us -> 73.4 us
    ppermute x37, waiting for transfers between devices: 103 us -> 85.6 us  [swap(): return lax.ppermute(values, AXES, pairs)]
    unnamed x58 -> x40, local copies, waits for them, and re-layouts: 12.8 us -> 5.82 us
    ppermute x37, starting transfers between devices: 35.4 us -> 28.5 us  [swap(): return lax.ppermute(values, AXES, pairs)]
    pallas_call x9, Pallas kernels: 16.8 us -> 14.1 us  [step(): call(kernel, name, listed, [spec(v) for v in operands[prefetch:]], [whole...]
  transfers between devices with their start and end apart: 39 -> 39, of which waited for: 18 -> 18; matrix products, arithmetic and copies ran while one was open for 3% -> 2% of each run, Pallas kernels for 23% -> 33%
where the time goes in v3:
time: 221 us; the launch traced here: 220 us
  waiting for transfers between devices  101 us (46%)
  Pallas kernels  73.4 us (33%)
  starting transfers between devices  32.9 us (15%)
  local copies, waits for them, and re-layouts  8.51 us (4%)
  other arithmetic  3.2 us (1%)
    ppermute x37, waiting for transfers between devices, swap(): return lax.ppermute(values, AXES, pairs)  85.6 us
    pallas_call x15, Pallas kernels, run(): result = step(*operands)  59.3 us
    ppermute x37, starting transfers between devices, swap(): return lax.ppermute(values, AXES, pairs)  28.5 us
    ppermute x2, waiting for transfers between devices, across(): return lax.ppermute(values, AXES, pairs)  15.4 us
    pallas_call x9, Pallas kernels, step(): call(kernel, name, listed, [spec(v) for v in operands[prefetch:]], [whole...  14.1 us
    unnamed x40, local copies, waits for them, and re-layouts  5.82 us
  transfers between devices with their start and end apart: 39, of which 18 were waited for; matrix products, arithmetic and copies ran while one was open for 2% of the time, Pallas kernels for 33%

profile of v3, /device:TPU:0, one launch (start us, length us, event | category | flops | bytes accessed | tf_op | source)
XLA Modules:
  0.0 220.2 jit_solution(17713639443740402182)
XLA Ops:
  0.7 3.0 %collective-permute-start = (bf16[256,1024]{1,0:T(8,128)(2,1)}, bf16[256,1024]{1,0:T(8,128)(2,1)}, u32[]{:S(2)}, u32[]{:S(2)}) collective-permute-start(bf16[256,1024]{1,0:T(8,128)(2,1)} %x_ref.3), channel_id=1, source_target_pairs={{0,1},{1,0},{2,3},{3,2},{4,5},{5,4},{6,7},{7,6},{8,9},{9,8},{10,11... | collective-permute-start | bytes 1572872 | tf_op jit(solution)/shard_map/ppermute | solution.py:739
  3.7 1.6 collective-permute-start.1
  8.8 1.3 first_pack.1
  10.1 3.0 %collective-permute-start.3 = (bf16[400,384]{1,0:T(8,128)(2,1)}, bf16[400,384]{1,0:T(8,128)(2,1)}, u32[]{:S(2)}, u32[]{:S(2)}) collective-permute-start(bf16[400,384]{1,0:T(8,128)(2,1)} %first_pack.1), channel_id=1, source_target_pairs={{0,4},{1,5},{2,6},{3,7},{4,0},{5,1},{6,2},{7,3},{8,12},{9,13},{10,... | collective-permute-start | bytes 921608 | tf_op jit(solution)/shard_map/ppermute | solution.py:739
  13.1 1.2 copy-done.9
  17.7 3.2 %prepare.1 = (f32[1024,128]{1,0:T(8,128)S(1)}, f32[1024,128]{1,0:T(8,128)S(1)}, f32[1024,128]{1,0:T(8,128)S(1)}, bf16[128,128]{1,0:T(8,128)(2,1)S(1)}, bf16[128,...) custom-call(s32[3]{0:T(128)S(1)} %pad_add_fusion.table, f32[1,128]{1,0:T(1,128)S(1)} %copy-done.12, ...), custom_call_target="tpu_custom_call" | custom-call | flops 1000 | bytes 1000 | tf_op jit(solution)/shard_map/prepare/pallas_call | solution.py:759
  20.9 13.4 %collective-permute-done.3.mine.bias = bf16[400,384]{1,0:T(8,128)(2,1)} collective-permute-done((bf16[400,384]{1,0:T(8,128)(2,1)}, bf16[400,384]{1,0:T(8,128)(2,1)}, u32[]{:S(2)}, u32[]{:S(2)}) %collective-permute-start.3) | collective-permute-done | bytes 307232 | tf_op jit(solution)/shard_map/ppermute | solution.py:739
  35.0 1.7 collective-permute-start.4
  36.7 2.7 %collective-permute-start.10 = (bf16[256,1024]{1,0:T(8,128)(2,1)}, bf16[256,1024]{1,0:T(8,128)(2,1)S(1)}, u32[]{:S(2)}, u32[]{:S(2)}) collective-permute-start(bf16[256,1024]{1,0:T(8,128)(2,1)} %grad_ref.1), channel_id=1, source_target_pairs={{0,2},{1,3},{2,0},{3,1},{4,6},{5,7},{6,4},{7,5},{8,10},{9,11},{10,... | collective-permute-start | bytes 1572872 | tf_op jit(solution)/shard_map/ppermute | solution.py:739
  39.9 2.4 %collective-permute-start.8 = (bf16[256,1024]{1,0:T(8,128)(2,1)}, bf16[256,1024]{1,0:T(8,128)(2,1)S(1)}, u32[]{:S(2)}, u32[]{:S(2)}) collective-permute-start(bf16[256,1024]{1,0:T(8,128)(2,1)} %copy-done.13), channel_id=1, source_target_pairs={{0,4},{1,5},{2,6},{3,7},{4,0},{5,1},{6,2},{7,3},{8,12},{9,13},{10,... | collective-permute-start | bytes 1572872 | tf_op jit(solution)/shard_map/ppermute | solution.py:739
  42.3 6.0 %own_features.1 = (bf16[1024,1024]{1,0:T(8,128)(2,1)S(1)}, bf16[1024,1024]{1,0:T(8,128)(2,1)S(1)}, bf16[1024,1024]{1,0:T(8,128)(2,1)S(1)}, f32[1024,256]{1,0:T(8...) custom-call(s32[3]{0:T(128)S(1)} %pad_add_fusion.table, s32[2048]{0:T(1024)S(1)} %bitcast.77, ...), custom_call_target="tpu_custom_call" | custom-call | flops 1000 | bytes 1000 | tf_op jit(solution)/shard_map/own_features/pallas_call | solution.py:759
  48.8 2.6 %up.4 = (bf16[1024,512]{1,0:T(8,128)(2,1)S(1)}, bf16[1024,512]{1,0:T(8,128)(2,1)S(1)}) custom-call(bf16[1024,1024]{1,0:T(8,128)(2,1)S(1)} %get-tuple-element.191.norm_ref.norm_two, bf16[512,1024]{1,0:T(8,128)(2,1)S(1)} %get-tuple-element.142.weight.own_up, f32[1,512]{1,0:T(1,128)S(1)} %get-tuple-element.155.bias), custom_call_target="tpu_custom_call" | custom-call | flops 1000 | bytes 1000 | tf_op jit(solution)/shard_map/up/pallas_call | solution.py:759
  51.5 1.6 collect_first.1
  53.1 5.4 %far_features.1 = (f32[1024,256]{1,0:T(8,128)S(1)}, bf16[1024,128]{1,0:T(8,128)(2,1)S(1)}, f32[2,128,128]{2,1,0:T(8,128)S(1)}) custom-call(s32[3]{0:T(128)S(1)} %pad_add_fusion.table, s32[2048]{0:T(1024)S(1)} %bitcast.78, bf16[1024,1024]{1,0:T(8,128)(2,1)S(1)} %get-tuple-element.216.norm_one, bf16[1024,384]{1,0:T(8,128)(2,1)S(1)} %get-tuple-element.159.weight.far_qkv, ...), custom_call_target="tpu_custom_call" | custom-call | flops 1000 | bytes 1000 | tf_op jit(solution)/shard_map/far_features/pallas_call | solution.py:759
  58.5 2.9 %collective-permute-start.7 = (f32[2,128,128]{2,1,0:T(8,128)S(1)}, f32[2,128,128]{2,1,0:T(8,128)S(1)}, u32[]{:S(2)}, u32[]{:S(2)}) collective-permute-start(f32[2,128,128]{2,1,0:T(8,128)S(1)} %get-tuple-element.163), channel_id=1, source_target_pairs={{0,4},{1,5},{2,6},{3,7},{8,12},{9,13},{10,14},{11,15},{16,20},{17,... | collective-permute-start | bytes 393224 | tf_op jit(solution)/shard_map/ppermute | solution.py:747
  61.5 4.7 %collective-permute-done.8.mine = bf16[256,1024]{1,0:T(8,128)(2,1)S(1)} collective-permute-done((bf16[256,1024]{1,0:T(8,128)(2,1)}, bf16[256,1024]{1,0:T(8,128)(2,1)S(1)}, u32[]{:S(2)}, u32[]{:S(2)}) %collective-permute-start.8) | collective-permute-done | bytes 524320 | tf_op jit(solution)/shard_map/ppermute | solution.py:739
  66.2 10.6 %collective-permute-done.7.first_state = f32[2,128,128]{2,1,0:T(8,128)S(1)} collective-permute-done((f32[2,128,128]{2,1,0:T(8,128)S(1)}, f32[2,128,128]{2,1,0:T(8,128)S(1)}, u32[]{:S(2)}, u32[]{:S(2)}) %collective-permute-start.7) | collective-permute-done | bytes 131104 | tf_op jit(solution)/shard_map/ppermute | solution.py:747
  77.3 3.4 %attend.1 = (f32[1024,256]{1,0:T(8,128)S(1)}, bf16[1024,256]{1,0:T(8,128)(2,1)S(1)}, f32[1024,256]{1,0:T(8,128)S(1)}, f32[4,2,128,256]{3,2,1,0:T(8,128)S(1)}) custom-call(s32[3]{0:T(128)S(1)} %pad_add_fusion.table, s32[2048]{0:T(1024)S(1)} %bitcast.79, f32[1024,256]{1,0:T(8,128)S(1)} %get-tuple-element.168.own_feat, ...), custom_call_target="tpu_custom_call" | custom-call | flops 1000 | bytes 1000 | tf_op jit(solution)/shard_map/attend/pallas_call | solution.py:759
  81.6 5.4 %later.1 = (f32[1024,256]{1,0:T(8,128)S(1)}, f32[2,128,128]{2,1,0:T(8,128)S(1)}) custom-call(s32[3]{0:T(128)S(1)} %pad_add_fusion.table, s32[2048]{0:T(1024)S(1)} %bitcast.81, bf16[1024,1024]{1,0:T(8,128)(2,1)S(1)} %get-tuple-element.177.grad_ref.grad, bf16[128,1024]{1,0:T(8,128)(2,1)S(1)} %copy-done.6, bf16[128,1024]{1,0:T(8,128)(2,1)S(1)} %get-tuple-element.178.far_dense, ...), custom_call_target="tpu_custom_call" | custom-call | flops 1000 | bytes 1000 | tf_op jit(solution)/shard_map/later/pallas_call | solution.py:759
  87.0 3.3 %collective-permute-done.12.third = bf16[256,1024]{1,0:T(8,128)(2,1)S(1)} collective-permute-done((bf16[256,1024]{1,0:T(8,128)(2,1)S(1)}, bf16[256,1024]{1,0:T(8,128)(2,1)S(1)}, u32[]{:S(2)}, u32[]{:S(2)}) %collective-permute-start.12) | collective-permute-done | bytes 524320 | tf_op jit(solution)/shard_map/ppermute | solution.py:739
  90.3 1.5 collective-permute-start.15
  91.8 2.1 down_back.2
  93.9 3.2 %hidden_weights.2 = (bf16[2,304,1024]{2,1,0:T(8,128)(2,1)S(1)}, bf16[2,304,1024]{2,1,0:T(8,128)(2,1)S(1)}) custom-call(s32[3]{0:T(128)S(1)} %pad_add_fusion.table, bf16[1024,512]{1,0:T(8,128)(2,1)S(1)} %get-tuple-element.156.active.own_active, bf16[1024,512]{1,0:T(8,128)(2,1)S(1)} %get-tuple-element.184.hidden_grad.own_hg, ...), custom_call_target="tpu_custom_call" | custom-call | flops 1000 | bytes 1000 | tf_op jit(solution)/shard_map/hidden_weights/pallas_call | solution.py:759
  97.1 4.8 %collective-permute-done.15.first_later = f32[2,128,128]{2,1,0:T(8,128)S(1)} collective-permute-done((f32[2,128,128]{2,1,0:T(8,128)S(1)}, f32[2,128,128]{2,1,0:T(8,128)S(1)}, u32[]{:S(2)}, u32[]{:S(2)}) %collective-permute-start.15) | collective-permute-done | bytes 131104 | tf_op jit(solution)/shard_map/ppermute | solution.py:747
  102.2 2.6 %up.5 = (bf16[1024,512]{1,0:T(8,128)(2,1)S(1)}, bf16[1024,512]{1,0:T(8,128)(2,1)S(1)}) custom-call(bf16[1024,1024]{1,0:T(8,128)(2,1)S(1)} %get-tuple-element.191.norm_ref.norm_two, bf16[512,1024]{1,0:T(8,128)(2,1)S(1)} %get-tuple-element.190.weight.far_up, f32[1,512]{1,0:T(1,128)S(1)} %get-tuple-element.192.bias), custom_call_target="tpu_custom_call" | custom-call | flops 1000 | bytes 1000 | tf_op jit(solution)/shard_map/up/pallas_call | solution.py:759
  104.8 2.1 down_back.3
  106.9 3.2 %hidden_weights.3 = (bf16[2,304,1024]{2,1,0:T(8,128)(2,1)S(1)}, bf16[2,304,1024]{2,1,0:T(8,128)(2,1)S(1)}) custom-call(s32[3]{0:T(128)S(1)} %pad_add_fusion.table, bf16[1024,512]{1,0:T(8,128)(2,1)S(1)} %get-tuple-element.193.active.far_active, bf16[1024,512]{1,0:T(8,128)(2,1)S(1)} %get-tuple-element.198.hidden_grad.far_hg, ...), custom_call_target="tpu_custom_call" | custom-call | flops 1000 | bytes 1000 | tf_op jit(solution)/shard_map/hidden_weights/pallas_call | solution.py:759
  111.1 4.2 %out.1 = (bf16[2,256,1024]{2,1,0:T(8,128)(2,1)S(1)}, bf16[2,256,1024]{2,1,0:T(8,128)(2,1)S(1)}) custom-call(bf16[1024,256]{1,0:T(8,128)(2,1)S(1)} %get-tuple-element.204.merged, bf16[1024,512]{1,0:T(8,128)(2,1)S(1)} %get-tuple-element.156.active.own_active, bf16[1024,512]{1,0:T(8,128)(2,1)S(1)} %get-tuple-element.193.active.far_active, ...), custom_call_target="tpu_custom_call" | custom-call | flops 1000 | bytes 1000 | tf_op jit(solution)/shard_map/out/pallas_call | solution.py:759
  116.6 8.6 %attend_back.1 = (bf16[1024,384]{1,0:T(8,128)(2,1)S(1)}, bf16[1024,384]{1,0:T(8,128)(2,1)S(1)}) custom-call(s32[3]{0:T(128)S(1)} %pad_add_fusion.table, s32[2048]{0:T(1024)S(1)} %bitcast.82, f32[1024,256]{1,0:T(8,128)S(1)} %get-tuple-element.168.own_feat, f32[1024,256]{1,0:T(8,128)S(1)} %get-tuple-element.162.far_feat, ...), custom_call_target="tpu_custom_call" | custom-call | flops 1000 | bytes 1000 | tf_op jit(solution)/shard_map/attend_back/pallas_call | solution.py:759
  125.2 3.0 %qkv_weights.1 = (bf16[4,272,384]{2,1,0:T(8,128)(2,1)S(1)}, bf16[4,272,384]{2,1,0:T(8,128)(2,1)S(1)}) custom-call(s32[3]{0:T(128)S(1)} %pad_add_fusion.table, bf16[1024,384]{1,0:T(8,128)(2,1)S(1)} %get-tuple-element.213.own_pg, bf16[1024,384]{1,0:T(8,128)(2,1)S(1)} %get-tuple-element.214.far_pg, bf16[1024,1024]{1,0:T(8,128)(2,1)S(1)} %get-tuple-element.216.norm_one), custom_call_target="tpu_custom_call" | custom-call | flops 1000 | bytes 1000 | tf_op jit(solution)/shard_map/qkv_weights/pallas_call | solution.py:796
  128.2 3.6 %collective-permute-done.18 = bf16[304,1024]{1,0:T(8,128)(2,1)S(1)} collective-permute-done((bf16[304,1024]{1,0:T(8,128)(2,1)S(1)}, bf16[304,1024]{1,0:T(8,128)(2,1)S(1)}, u32[]{:S(2)}, u32[]{:S(2)}) %collective-permute-start.18) | collective-permute-done | bytes 622624 | tf_op jit(solution)/shard_map/ppermute | solution.py:739
  132.1 6.0 %norm_grad.1 = (f32[8,1024]{1,0:T(8,128)S(1)}, bf16[2,256,1024]{2,1,0:T(8,128)(2,1)S(1)}, bf16[2,256,1024]{2,1,0:T(8,128)(2,1)S(1)}) custom-call(bf16[1024,384]{1,0:T(8,128)(2,1)S(1)} %get-tuple-element.213.own_pg, bf16[1024,384]{1,0:T(8,128)(2,1)S(1)} %get-tuple-element.214.far_pg, bf16[1024,512]{1,0:T(8,128)(2,1)S(1)} %get-tuple-element.184.hidden_grad.own_hg, ...), custom_call_target="tpu_custom_call" | custom-call | flops 1000 | bytes 1000 | tf_op jit(solution)/shard_map/norm_grad/pallas_call | solution.py:759
  138.2 2.5 %collective-permute-done.19 = bf16[2,256,1024]{2,1,0:T(8,128)(2,1)S(1)} collective-permute-done((bf16[2,256,1024]{2,1,0:T(8,128)(2,1)S(1)}, bf16[2,256,1024]{2,1,0:T(8,128)(2,1)S(1)}, u32[]{:S(2)}, u32[]{:S(2)}) %collective-permute-start.19) | collective-permute-done | bytes 1048608 | tf_op jit(solution)/shard_map/ppermute | solution.py:739
  141.4 2.2 %collective-permute-done.20 = bf16[4,272,384]{2,1,0:T(8,128)(2,1)S(1)} collective-permute-done((bf16[4,272,384]{2,1,0:T(8,128)(2,1)S(1)}, bf16[4,272,384]{2,1,0:T(8,128)(2,1)S(1)}, u32[]{:S(2)}, u32[]{:S(2)}) %collective-permute-start.20) | collective-permute-done | bytes 835616 | tf_op jit(solution)/shard_map/ppermute | solution.py:739
  144.4 1.6 collective-permute-start.24
  146.6 16.1 %collective-permute-done.21 = bf16[1,256,1024]{2,1,0:T(8,128)(2,1)S(1)} collective-permute-done((bf16[1,256,1024]{2,1,0:T(8,128)(2,1)S(1)}, bf16[1,256,1024]{2,1,0:T(8,128)(2,1)S(1)}, u32[]{:S(2)}, u32[]{:S(2)}) %collective-permute-start.21) | collective-permute-done | bytes 524320 | tf_op jit(solution)/shard_map/ppermute | solution.py:739
  163.9 10.5 %collective-permute-done.23 = bf16[304,1024]{1,0:T(8,128)(2,1)S(1)} collective-permute-done((bf16[304,1024]{1,0:T(8,128)(2,1)S(1)}, bf16[304,1024]{1,0:T(8,128)(2,1)S(1)}, u32[]{:S(2)}, u32[]{:S(2)}) %collective-permute-start.23) | collective-permute-done | bytes 622624 | tf_op jit(solution)/shard_map/ppermute | solution.py:739
  175.1 1.6 collective-permute-start.30
  177.8 1.2 collective-permute-done.28
  179.0 14.5 %collective-permute-done.26 = bf16[272,384]{1,0:T(8,128)(2,1)S(1)} collective-permute-done((bf16[272,384]{1,0:T(8,128)(2,1)S(1)}, bf16[272,384]{1,0:T(8,128)(2,1)S(1)}, u32[]{:S(2)}, u32[]{:S(2)}) %collective-permute-start.26) | collective-permute-done | bytes 208928 | tf_op jit(solution)/shard_map/ppermute | solution.py:739
  194.1 1.6 collective-permute-done.29
  195.7 1.7 finish_in.1
  198.3 6.8 %collective-permute-done.33.third = bf16[272,384]{1,0:T(8,128)(2,1)S(1)} collective-permute-done((bf16[272,384]{1,0:T(8,128)(2,1)S(1)}, bf16[272,384]{1,0:T(8,128)(2,1)S(1)}, u32[]{:S(2)}, u32[]{:S(2)}) %collective-permute-start.33) | collective-permute-done | bytes 208928 | tf_op jit(solution)/shard_map/ppermute | solution.py:739
  205.7 3.4 %collective-permute-done.35 = f32[8,1024]{1,0:T(8,128)S(1)} collective-permute-done((f32[8,1024]{1,0:T(8,128)S(1)}, f32[8,1024]{1,0:T(8,128)S(1)}, u32[]{:S(2)}, u32[]{:S(2)}) %collective-permute-start.35) | collective-permute-done | bytes 32800 | tf_op jit(solution)/shard_map/ppermute | solution.py:739
  209.1 1.8 collective-permute-start.36
  210.9 3.5 %finish_hidden.1 = (f32[1024,512]{1,0:T(8,128)}, f32[512,1024]{1,0:T(8,128)}, f32[128,1024]{1,0:T(8,128)}, f32[4,1,128]{2,1,0:T(1,128)}) custom-call(s32[3]{0:T(128)S(1)} %pad_add_fusion.table, bf16[304,1024]{1,0:T(8,128)(2,1)S(1)} %add_convert_fusion.2.mine, bf16[304,1024]{1,0:T(8,128)(2,1)S(1)} %collective-permute-done.27.near, ...), custom_call_target="tpu_custom_call" | custom-call | flops 1000 | bytes 1000 | tf_op jit(solution)/shard_map/finish_hidden/pallas_call | solution.py:796
  214.4 2.0 collective-permute-start.38
  216.4 1.8 finish_qkv.1
  (129 shorter events, 21.9 us)
Async XLA Ops:
  0.6 12.4 %copy-start.14 = (bf16[512]{0:T(512)(128)(2,1)S(1)}, bf16[512]{0:T(512)(128)(2,1)}, u32[]{:S(2)}) copy-start(bf16[512]{0:T(512)(128)(2,1)} %param.21) | copy-start | bytes 3076
  0.7 33.6 %collective-permute-start = (bf16[256,1024]{1,0:T(8,128)(2,1)}, bf16[256,1024]{1,0:T(8,128)(2,1)}, u32[]{:S(2)}, u32[]{:S(2)}) collective-permute-start(bf16[256,1024]{1,0:T(8,128)(2,1)} %x_ref.3), channel_id=1, source_target_pairs={{0,1},{1,0},{2,3},{3,2},{4,5},{5,4},{6,7},{7,6},{8,9},{9,8},{10,11... | collective-permute-start | bytes 1572872 | tf_op jit(solution)/shard_map/ppermute | solution.py:739
  3.7 30.6 %collective-permute-start.1 = (bf16[256,1024]{1,0:T(8,128)(2,1)}, bf16[256,1024]{1,0:T(8,128)(2,1)}, u32[]{:S(2)}, u32[]{:S(2)}) collective-permute-start(bf16[256,1024]{1,0:T(8,128)(2,1)} %x_ref.3), channel_id=1, source_target_pairs={{0,2},{1,3},{2,0},{3,1},{4,6},{5,7},{6,4},{7,5},{8,10},{9,11},{10,... | collective-permute-start | bytes 1572872 | tf_op jit(solution)/shard_map/ppermute | solution.py:739
  5.2 29.8 %collective-permute-start.2 = (bf16[256,1024]{1,0:T(8,128)(2,1)}, bf16[256,1024]{1,0:T(8,128)(2,1)}, u32[]{:S(2)}, u32[]{:S(2)}) collective-permute-start(bf16[256,1024]{1,0:T(8,128)(2,1)} %x_ref.3), channel_id=1, source_target_pairs={{0,3},{1,2},{2,1},{3,0},{4,7},{5,6},{6,5},{7,4},{8,11},{9,10},{10,... | collective-permute-start | bytes 1572872 | tf_op jit(solution)/shard_map/ppermute | solution.py:739
  8.8 4.3 %copy-start.8 = (bf16[1024,512]{1,0:T(8,128)(2,1)S(1)}, bf16[1024,512]{1,0:T(8,128)(2,1)}, u32[]{:S(2)}) copy-start(bf16[1024,512]{1,0:T(8,128)(2,1)} %up.3) | copy-start | bytes 3145732
  8.8 8.4 %copy-start.10 = (s32[1,2048]{1,0:T(1,128)S(1)}, s32[1,2048]{1,0:T(1,128)}, u32[]{:S(2)}) copy-start(s32[1,2048]{1,0:T(1,128)} %param.29) | copy-start | bytes 24580
  10.1 24.2 %collective-permute-start.3 = (bf16[400,384]{1,0:T(8,128)(2,1)}, bf16[400,384]{1,0:T(8,128)(2,1)}, u32[]{:S(2)}, u32[]{:S(2)}) collective-permute-start(bf16[400,384]{1,0:T(8,128)(2,1)} %first_pack.1), channel_id=1, source_target_pairs={{0,4},{1,5},{2,6},{3,7},{4,0},{5,1},{6,2},{7,3},{8,12},{9,13},{10,... | collective-permute-start | bytes 921608 | tf_op jit(solution)/shard_map/ppermute | solution.py:739
  14.3 3.3 %copy-start.11 = (f32[64,64]{1,0:T(8,128)S(1)}, f32[64,64]{1,0:T(8,128)}, u32[]{:S(2)}) copy-start(f32[64,64]{1,0:T(8,128)} %omega) | copy-start | bytes 49156
  14.3 3.3 %copy-start.12 = (f32[1,128]{1,0:T(1,128)S(1)}, f32[1,128]{1,0:T(1,128)}, u32[]{:S(2)}) copy-start(f32[1,128]{1,0:T(1,128)} %constant.45.clone.rates) | copy-start | bytes 1540
  17.2 25.2 %copy-start.1 = (bf16[1024,384]{1,0:T(8,128)(2,1)S(1)}, bf16[1024,384]{1,0:T(8,128)(2,1)}, u32[]{:S(2)}) copy-start(bf16[1024,384]{1,0:T(8,128)(2,1)} %own_qkv.1) | copy-start | bytes 2359300
  17.2 25.2 %copy-start.2 = (bf16[256,1024]{1,0:T(8,128)(2,1)S(1)}, bf16[256,1024]{1,0:T(8,128)(2,1)}, u32[]{:S(2)}) copy-start(bf16[256,1024]{1,0:T(8,128)(2,1)} %x_ref.3) | copy-start | bytes 1572868
  35.0 13.3 %collective-permute-start.4 = (bf16[400,384]{1,0:T(8,128)(2,1)}, bf16[400,384]{1,0:T(8,128)(2,1)S(1)}, u32[]{:S(2)}, u32[]{:S(2)}) collective-permute-start(bf16[400,384]{1,0:T(8,128)(2,1)} %collective-permute-done.3.mine.bias), channel_id=1, source_target_pairs={{0,16},{1,17},{2,18},{3,19},{4,20},{5,21},{6,22},{7,23},{8,24},{9,... | collective-permute-start | bytes 921608 | tf_op jit(solution)/shard_map/ppermute | solution.py:739
  36.7 11.7 %collective-permute-start.5 = (bf16[400,384]{1,0:T(8,128)(2,1)}, bf16[400,384]{1,0:T(8,128)(2,1)S(1)}, u32[]{:S(2)}, u32[]{:S(2)}) collective-permute-start(bf16[400,384]{1,0:T(8,128)(2,1)} %collective-permute-done.3.mine.bias), channel_id=1, source_target_pairs={{0,8},{1,9},{2,10},{3,11},{4,12},{5,13},{6,14},{7,15},{8,0},{9,1},... | collective-permute-start | bytes 921608 | tf_op jit(solution)/shard_map/ppermute | solution.py:739
  36.7 29.5 %collective-permute-start.10 = (bf16[256,1024]{1,0:T(8,128)(2,1)}, bf16[256,1024]{1,0:T(8,128)(2,1)S(1)}, u32[]{:S(2)}, u32[]{:S(2)}) collective-permute-start(bf16[256,1024]{1,0:T(8,128)(2,1)} %grad_ref.1), channel_id=1, source_target_pairs={{0,2},{1,3},{2,0},{3,1},{4,6},{5,7},{6,4},{7,5},{8,10},{9,11},{10,... | collective-permute-start | bytes 1572872 | tf_op jit(solution)/shard_map/ppermute | solution.py:739
  39.4 26.8 %collective-permute-start.9 = (bf16[256,1024]{1,0:T(8,128)(2,1)}, bf16[256,1024]{1,0:T(8,128)(2,1)S(1)}, u32[]{:S(2)}, u32[]{:S(2)}) collective-permute-start(bf16[256,1024]{1,0:T(8,128)(2,1)} %grad_ref.1), channel_id=1, source_target_pairs={{0,1},{1,0},{2,3},{3,2},{4,5},{5,4},{6,7},{7,6},{8,9},{9,8},{10,11... | collective-permute-start | bytes 1572872 | tf_op jit(solution)/shard_map/ppermute | solution.py:739
  39.9 26.3 %collective-permute-start.8 = (bf16[256,1024]{1,0:T(8,128)(2,1)}, bf16[256,1024]{1,0:T(8,128)(2,1)S(1)}, u32[]{:S(2)}, u32[]{:S(2)}) collective-permute-start(bf16[256,1024]{1,0:T(8,128)(2,1)} %copy-done.13), channel_id=1, source_target_pairs={{0,4},{1,5},{2,6},{3,7},{4,0},{5,1},{6,2},{7,3},{8,12},{9,13},{10,... | collective-permute-start | bytes 1572872 | tf_op jit(solution)/shard_map/ppermute | solution.py:739
  42.3 6.0 %copy-start.7 = (bf16[256,1024]{1,0:T(8,128)(2,1)S(1)}, bf16[256,1024]{1,0:T(8,128)(2,1)}, u32[]{:S(2)}) copy-start(bf16[256,1024]{1,0:T(8,128)(2,1)} %grad_ref.1) | copy-start | bytes 1572868
  48.3 28.4 %collective-permute-start.11 = (bf16[256,1024]{1,0:T(8,128)(2,1)S(1)}, bf16[256,1024]{1,0:T(8,128)(2,1)S(1)}, u32[]{:S(2)}, u32[]{:S(2)}) collective-permute-start(bf16[256,1024]{1,0:T(8,128)(2,1)S(1)} %copy-done.7), channel_id=1, source_target_pairs={{0,3},{1,2},{2,1},{3,0},{4,7},{5,6},{6,5},{7,4},{8,11},{9,10},{10,... | collective-permute-start | bytes 1572872 | tf_op jit(solution)/shard_map/ppermute | solution.py:739
  48.8 2.6 %collective-permute-start.6 = (bf16[400,384]{1,0:T(8,128)(2,1)S(1)}, bf16[400,384]{1,0:T(8,128)(2,1)S(1)}, u32[]{:S(2)}, u32[]{:S(2)}) collective-permute-start(bf16[400,384]{1,0:T(8,128)(2,1)S(1)} %collective-permute-done.4.third), channel_id=1, source_target_pairs={{0,8},{1,9},{2,10},{3,11},{4,12},{5,13},{6,14},{7,15},{8,0},{9,1},... | collective-permute-start | bytes 921608 | tf_op jit(solution)/shard_map/ppermute | solution.py:739
  58.5 18.2 %collective-permute-start.7 = (f32[2,128,128]{2,1,0:T(8,128)S(1)}, f32[2,128,128]{2,1,0:T(8,128)S(1)}, u32[]{:S(2)}, u32[]{:S(2)}) collective-permute-start(f32[2,128,128]{2,1,0:T(8,128)S(1)} %get-tuple-element.163), channel_id=1, source_target_pairs={{0,4},{1,5},{2,6},{3,7},{8,12},{9,13},{10,14},{11,15},{16,20},{17,... | collective-permute-start | bytes 393224 | tf_op jit(solution)/shard_map/ppermute | solution.py:747
  76.8 13.6 %collective-permute-start.12 = (bf16[256,1024]{1,0:T(8,128)(2,1)S(1)}, bf16[256,1024]{1,0:T(8,128)(2,1)S(1)}, u32[]{:S(2)}, u32[]{:S(2)}) collective-permute-start(bf16[256,1024]{1,0:T(8,128)(2,1)S(1)} %collective-permute-done.8.mine), channel_id=1, source_target_pairs={{0,16},{1,17},{2,18},{3,19},{4,20},{5,21},{6,22},{7,23},{8,24},{9,... | collective-permute-start | bytes 1572872 | tf_op jit(solution)/shard_map/ppermute | solution.py:739
  77.3 24.7 %collective-permute-start.14 = (bf16[256,1024]{1,0:T(8,128)(2,1)S(1)}, bf16[256,1024]{1,0:T(8,128)(2,1)S(1)}, u32[]{:S(2)}, u32[]{:S(2)}) collective-permute-start(bf16[256,1024]{1,0:T(8,128)(2,1)S(1)} %collective-permute-done.8.mine), channel_id=1, source_target_pairs={{0,8},{1,9},{2,10},{3,11},{4,12},{5,13},{6,14},{7,15},{8,0},{9,1},... | collective-permute-start | bytes 1572872 | tf_op jit(solution)/shard_map/ppermute | solution.py:739
  81.6 10.2 %copy-start.4 = (bf16[512,1024]{1,0:T(8,128)(2,1)S(1)}, bf16[512,1024]{1,0:T(8,128)(2,1)}, u32[]{:S(2)}) copy-start(bf16[512,1024]{1,0:T(8,128)(2,1)} %copy-done.3) | copy-start | bytes 3145732
  90.3 11.6 %collective-permute-start.13 = (bf16[256,1024]{1,0:T(8,128)(2,1)S(1)}, bf16[256,1024]{1,0:T(8,128)(2,1)S(1)}, u32[]{:S(2)}, u32[]{:S(2)}) collective-permute-start(bf16[256,1024]{1,0:T(8,128)(2,1)S(1)} %collective-permute-done.12.third), channel_id=1, source_target_pairs={{0,8},{1,9},{2,10},{3,11},{4,12},{5,13},{6,14},{7,15},{8,0},{9,1},... | collective-permute-start | bytes 1572872 | tf_op jit(solution)/shard_map/ppermute | solution.py:739
  90.3 11.6 %collective-permute-start.15 = (f32[2,128,128]{2,1,0:T(8,128)S(1)}, f32[2,128,128]{2,1,0:T(8,128)S(1)}, u32[]{:S(2)}, u32[]{:S(2)}) collective-permute-start(f32[2,128,128]{2,1,0:T(8,128)S(1)} %get-tuple-element.188), channel_id=1, source_target_pairs={{4,0},{5,1},{6,2},{7,3},{12,8},{13,9},{14,10},{15,11},{20,16},{21,... | collective-permute-start | bytes 393224 | tf_op jit(solution)/shard_map/ppermute | solution.py:747
  101.9 8.2 %collective-permute-start.16 = (bf16[2,304,1024]{2,1,0:T(8,128)(2,1)S(1)}, bf16[2,304,1024]{2,1,0:T(8,128)(2,1)S(1)}, u32[]{:S(2)}, u32[]{:S(2)}) collective-permute-start(bf16[2,304,1024]{2,1,0:T(8,128)(2,1)S(1)} %get-tuple-element.202), channel_id=1, source_target_pairs={{0,8},{1,9},{2,10},{3,11},{4,12},{5,13},{6,14},{7,15},{8,0},{9,1},... | collective-permute-start | bytes 3735560 | tf_op jit(solution)/shard_map/ppermute | solution.py:739
  110.4 4.9 %collective-permute-start.17 = (bf16[2,304,1024]{2,1,0:T(8,128)(2,1)S(1)}, bf16[2,304,1024]{2,1,0:T(8,128)(2,1)S(1)}, u32[]{:S(2)}, u32[]{:S(2)}) collective-permute-start(bf16[2,304,1024]{2,1,0:T(8,128)(2,1)S(1)} %get-tuple-element.207), channel_id=1, source_target_pairs={{0,8},{1,9},{2,10},{3,11},{4,12},{5,13},{6,14},{7,15},{8,0},{9,1},... | collective-permute-start | bytes 3735560 | tf_op jit(solution)/shard_map/ppermute | solution.py:739
  115.5 25.1 %collective-permute-start.19 = (bf16[2,256,1024]{2,1,0:T(8,128)(2,1)S(1)}, bf16[2,256,1024]{2,1,0:T(8,128)(2,1)S(1)}, u32[]{:S(2)}, u32[]{:S(2)}) collective-permute-start(bf16[2,256,1024]{2,1,0:T(8,128)(2,1)S(1)} %get-tuple-element.224), channel_id=1, source_target_pairs={{0,1},{1,0},{2,3},{3,2},{4,5},{5,4},{6,7},{7,6},{8,9},{9,8},{10,11... | collective-permute-start | bytes 3145736 | tf_op jit(solution)/shard_map/ppermute | solution.py:739
  116.1 15.7 %collective-permute-start.18 = (bf16[304,1024]{1,0:T(8,128)(2,1)S(1)}, bf16[304,1024]{1,0:T(8,128)(2,1)S(1)}, u32[]{:S(2)}, u32[]{:S(2)}) collective-permute-start(bf16[304,1024]{1,0:T(8,128)(2,1)S(1)} %fusion.4), channel_id=1, source_target_pairs={{0,16},{1,17},{2,18},{3,19},{4,20},{5,21},{6,22},{7,23},{8,24},{9,... | collective-permute-start | bytes 1867784 | tf_op jit(solution)/shard_map/ppermute | solution.py:739
  141.2 2.4 %collective-permute-start.20 = (bf16[4,272,384]{2,1,0:T(8,128)(2,1)S(1)}, bf16[4,272,384]{2,1,0:T(8,128)(2,1)S(1)}, u32[]{:S(2)}, u32[]{:S(2)}) collective-permute-start(bf16[4,272,384]{2,1,0:T(8,128)(2,1)S(1)} %get-tuple-element.227), channel_id=1, source_target_pairs={{0,8},{1,9},{2,10},{3,11},{4,12},{5,13},{6,14},{7,15},{8,0},{9,1},... | collective-permute-start | bytes 2506760 | tf_op jit(solution)/shard_map/ppermute | solution.py:739
  141.3 21.4 %collective-permute-start.21 = (bf16[1,256,1024]{2,1,0:T(8,128)(2,1)S(1)}, bf16[1,256,1024]{2,1,0:T(8,128)(2,1)S(1)}, u32[]{:S(2)}, u32[]{:S(2)}) collective-permute-start(bf16[1,256,1024]{2,1,0:T(8,128)(2,1)S(1)} %get-tuple-element.229), channel_id=1, source_target_pairs={{0,2},{1,3},{2,0},{3,1},{4,6},{5,7},{6,4},{7,5},{8,10},{9,11},{10,... | collective-permute-start | bytes 1572872 | tf_op jit(solution)/shard_map/ppermute | solution.py:739
  143.7 20.0 %collective-permute-start.22 = (bf16[2,272,384]{2,1,0:T(8,128)(2,1)S(1)}, bf16[2,272,384]{2,1,0:T(8,128)(2,1)S(1)}, u32[]{:S(2)}, u32[]{:S(2)}) collective-permute-start(bf16[2,272,384]{2,1,0:T(8,128)(2,1)S(1)} %add_convert_fusion.3), channel_id=1, source_target_pairs={{0,16},{1,17},{2,18},{3,19},{4,20},{5,21},{6,22},{7,23},{8,24},{9,... | collective-permute-start | bytes 1253384 | tf_op jit(solution)/shard_map/ppermute | solution.py:739
  144.3 30.1 %collective-permute-start.23 = (bf16[304,1024]{1,0:T(8,128)(2,1)S(1)}, bf16[304,1024]{1,0:T(8,128)(2,1)S(1)}, u32[]{:S(2)}, u32[]{:S(2)}) collective-permute-start(bf16[304,1024]{1,0:T(8,128)(2,1)S(1)} %fusion.3), channel_id=1, source_target_pairs={{0,4},{1,5},{2,6},{3,7},{4,0},{5,1},{6,2},{7,3},{8,12},{9,13},{10,... | collective-permute-start | bytes 1867784 | tf_op jit(solution)/shard_map/ppermute | solution.py:739
  144.4 30.1 %collective-permute-start.24 = (bf16[304,1024]{1,0:T(8,128)(2,1)S(1)}, bf16[304,1024]{1,0:T(8,128)(2,1)S(1)}, u32[]{:S(2)}, u32[]{:S(2)}) collective-permute-start(bf16[304,1024]{1,0:T(8,128)(2,1)S(1)} %fusion.5), channel_id=1, source_target_pairs={{0,16},{1,17},{2,18},{3,19},{4,20},{5,21},{6,22},{7,23},{8,24},{9,... | collective-permute-start | bytes 1867784 | tf_op jit(solution)/shard_map/ppermute | solution.py:739
  146.0 30.7 %collective-permute-start.25 = (bf16[2,256,1024]{2,1,0:T(8,128)(2,1)S(1)}, bf16[2,256,1024]{2,1,0:T(8,128)(2,1)S(1)}, u32[]{:S(2)}, u32[]{:S(2)}) collective-permute-start(bf16[2,256,1024]{2,1,0:T(8,128)(2,1)S(1)} %get-tuple-element.240), channel_id=1, source_target_pairs={{0,1},{1,0},{2,3},{3,2},{4,5},{5,4},{6,7},{7,6},{8,9},{9,8},{10,11... | collective-permute-start | bytes 3145736 | tf_op jit(solution)/shard_map/ppermute | solution.py:739
  175.0 18.5 %collective-permute-start.27 = (bf16[304,1024]{1,0:T(8,128)(2,1)S(1)}, bf16[304,1024]{1,0:T(8,128)(2,1)S(1)}, u32[]{:S(2)}, u32[]{:S(2)}) collective-permute-start(bf16[304,1024]{1,0:T(8,128)(2,1)S(1)} %add_convert_fusion.2.mine), channel_id=1, source_target_pairs={{0,8},{1,9},{2,10},{3,11},{4,12},{5,13},{6,14},{7,15},{8,0},{9,1},... | collective-permute-start | bytes 1867784 | tf_op jit(solution)/shard_map/ppermute | solution.py:739
  175.1 22.3 %collective-permute-start.30 = (bf16[304,1024]{1,0:T(8,128)(2,1)S(1)}, bf16[304,1024]{1,0:T(8,128)(2,1)S(1)}, u32[]{:S(2)}, u32[]{:S(2)}) collective-permute-start(bf16[304,1024]{1,0:T(8,128)(2,1)S(1)} %add_convert_fusion.2.mine), channel_id=1, source_target_pairs={{0,16},{1,17},{2,18},{3,19},{4,20},{5,21},{6,22},{7,23},{8,24},{9,... | collective-permute-start | bytes 1867784 | tf_op jit(solution)/shard_map/ppermute | solution.py:739
  177.2 18.5 %collective-permute-start.29 = (bf16[1,256,1024]{2,1,0:T(8,128)(2,1)S(1)}, bf16[1,256,1024]{2,1,0:T(8,128)(2,1)S(1)}, u32[]{:S(2)}, u32[]{:S(2)}) collective-permute-start(bf16[1,256,1024]{2,1,0:T(8,128)(2,1)S(1)} %get-tuple-element.247), channel_id=1, source_target_pairs={{0,2},{1,3},{2,0},{3,1},{4,6},{5,7},{6,4},{7,5},{8,10},{9,11},{10,... | collective-permute-start | bytes 1572872 | tf_op jit(solution)/shard_map/ppermute | solution.py:739
  177.2 16.3 %collective-permute-start.26 = (bf16[272,384]{1,0:T(8,128)(2,1)S(1)}, bf16[272,384]{1,0:T(8,128)(2,1)S(1)}, u32[]{:S(2)}, u32[]{:S(2)}) collective-permute-start(bf16[272,384]{1,0:T(8,128)(2,1)S(1)} %fusion.7), channel_id=1, source_target_pairs={{0,4},{1,5},{2,6},{3,7},{4,0},{5,1},{6,2},{7,3},{8,12},{9,13},{10,... | collective-permute-start | bytes 626696 | tf_op jit(solution)/shard_map/ppermute | solution.py:739
  177.8 1.2 collective-permute-start.28
  193.6 4.0 %collective-permute-start.31 = (f32[8,1024]{1,0:T(8,128)S(1)}, f32[8,1024]{1,0:T(8,128)S(1)}, u32[]{:S(2)}, u32[]{:S(2)}) collective-permute-start(f32[8,1024]{1,0:T(8,128)S(1)} %add.88), channel_id=1, source_target_pairs={{0,16},{1,17},{2,18},{3,19},{4,20},{5,21},{6,22},{7,23},{8,24},{9,... | collective-permute-start | bytes 98312 | tf_op jit(solution)/shard_map/ppermute | solution.py:739
  197.6 11.5 %collective-permute-start.32 = (bf16[304,1024]{1,0:T(8,128)(2,1)S(1)}, bf16[304,1024]{1,0:T(8,128)(2,1)S(1)}, u32[]{:S(2)}, u32[]{:S(2)}) collective-permute-start(bf16[304,1024]{1,0:T(8,128)(2,1)S(1)} %collective-permute-done.30.third), channel_id=1, source_target_pairs={{0,8},{1,9},{2,10},{3,11},{4,12},{5,13},{6,14},{7,15},{8,0},{9,1},... | collective-permute-start | bytes 1867784 | tf_op jit(solution)/shard_map/ppermute | solution.py:739
  197.6 7.6 %collective-permute-start.33 = (bf16[272,384]{1,0:T(8,128)(2,1)S(1)}, bf16[272,384]{1,0:T(8,128)(2,1)S(1)}, u32[]{:S(2)}, u32[]{:S(2)}) collective-permute-start(bf16[272,384]{1,0:T(8,128)(2,1)S(1)} %add_convert_fusion.4.mine), channel_id=1, source_target_pairs={{0,16},{1,17},{2,18},{3,19},{4,20},{5,21},{6,22},{7,23},{8,24},{9,... | collective-permute-start | bytes 626696 | tf_op jit(solution)/shard_map/ppermute | solution.py:739
  198.1 7.1 %collective-permute-start.34 = (bf16[272,384]{1,0:T(8,128)(2,1)S(1)}, bf16[272,384]{1,0:T(8,128)(2,1)S(1)}, u32[]{:S(2)}, u32[]{:S(2)}) collective-permute-start(bf16[272,384]{1,0:T(8,128)(2,1)S(1)} %add_convert_fusion.4.mine), channel_id=1, source_target_pairs={{0,8},{1,9},{2,10},{3,11},{4,12},{5,13},{6,14},{7,15},{8,0},{9,1},... | collective-permute-start | bytes 626696 | tf_op jit(solution)/shard_map/ppermute | solution.py:739
  205.1 9.3 %collective-permute-start.37 = (bf16[272,384]{1,0:T(8,128)(2,1)S(1)}, bf16[272,384]{1,0:T(8,128)(2,1)S(1)}, u32[]{:S(2)}, u32[]{:S(2)}) collective-permute-start(bf16[272,384]{1,0:T(8,128)(2,1)S(1)} %collective-permute-done.33.third), channel_id=1, source_target_pairs={{0,8},{1,9},{2,10},{3,11},{4,12},{5,13},{6,14},{7,15},{8,0},{9,1},... | collective-permute-start | bytes 626696 | tf_op jit(solution)/shard_map/ppermute | solution.py:739
  205.1 3.9 %collective-permute-start.35 = (f32[8,1024]{1,0:T(8,128)S(1)}, f32[8,1024]{1,0:T(8,128)S(1)}, u32[]{:S(2)}, u32[]{:S(2)}) collective-permute-start(f32[8,1024]{1,0:T(8,128)S(1)} %add.89), channel_id=1, source_target_pairs={{0,1},{1,0},{2,3},{3,2},{4,5},{5,4},{6,7},{7,6},{8,9},{9,8},{10,11... | collective-permute-start | bytes 98312 | tf_op jit(solution)/shard_map/ppermute | solution.py:739
  209.1 5.3 %collective-permute-start.36 = (f32[8,1024]{1,0:T(8,128)S(1)}, f32[8,1024]{1,0:T(8,128)S(1)}, u32[]{:S(2)}, u32[]{:S(2)}) collective-permute-start(f32[8,1024]{1,0:T(8,128)S(1)} %add.90), channel_id=1, source_target_pairs={{0,2},{1,3},{2,0},{3,1},{4,6},{5,7},{6,4},{7,5},{8,10},{9,11},{10,... | collective-permute-start | bytes 98312 | tf_op jit(solution)/shard_map/ppermute | solution.py:739
  214.4 5.2 %collective-permute-start.38 = (f32[8,1024]{1,0:T(8,128)S(1)}, f32[8,1024]{1,0:T(8,128)S(1)}, u32[]{:S(2)}, u32[]{:S(2)}) collective-permute-start(f32[8,1024]{1,0:T(8,128)S(1)} %add.91), channel_id=1, source_target_pairs={{0,4},{1,5},{2,6},{3,7},{4,0},{5,1},{6,2},{7,3},{8,12},{9,13},{10,... | collective-permute-start | bytes 98312 | tf_op jit(solution)/shard_map/ppermute | solution.py:739
  (11 other events, 22.2 us)

commit v4 on v3

--- a/solution.py
+++ b/solution.py
@@ -928,7 +928,9 @@
             gate=2,
         )
 
-    x_blocks = [inputs] + [swap(inputs, 0, k) for k in range(1, inner)]
+    x_blocks = [inputs] + [
+        None if k & (k - 1) else swap(inputs, 0, k) for k in range(1, inner)
+    ]
     first_pack = run(
         call(
             first_pack_kernel,
@@ -986,10 +988,16 @@
         gate=2,
     )
 
+    for k in range(1, inner):
+        if k & (k - 1):
+            tick(x_blocks[k & (k - 1)])
+            x_blocks[k] = swap(now(x_blocks[k & (k - 1)]), 0, k & -k)
     tick(first_mine, *x_blocks[1:])
     first_third, first_near = swap(now(first_mine), 2, 0), swap(now(first_mine), 1, 0)
     second_mine = swap(now(second_pack), 0, inner)
-    grad_blocks = [out_grad] + [swap(now(out_grad), 0, k) for k in range(1, inner - 1)]
+    grad_blocks = [out_grad] + [
+        None if k & (k - 1) else swap(now(out_grad), 0, k) for k in range(1, inner)
+    ]
     norm_one, norm_two, unit, own_feat, own_value, near_state = run(
         call(
             functools.partial(own_features_kernel, count, inner),
@@ -1046,7 +1054,6 @@
     )
     tick(first_third, first_near)
     first_last = swap(now(first_third), 1, 0)
-    grad_blocks.append(swap(now(out_grad), 0, inner - 1))
     own_active, own_slope = up_projection(own_up, own_up_bias)
 
     tick(first_last)
@@ -1108,8 +1115,10 @@
         gate=2,
     )
     first_state = across(state, 0)
-    tick(first_state, second_mine, *grad_blocks[1:])
-    second_third, second_near = swap(now(second_mine), 2, 0), swap(now(second_mine), 1, 0)
+    for k in range(1, inner):
+        if k & (k - 1):
+            tick(first_state, grad_blocks[k & (k - 1)])
+            grad_blocks[k] = swap(now(grad_blocks[k & (k - 1)]), 0, k & -k)
     block_row = pl.BlockSpec((1, 1, rows), lambda m, table, docs: (m + table[1] * inner, 0, 0))
     block_col = pl.BlockSpec((rows, 1), lambda m, table, docs: (m + table[1] * inner, 0))
     mixed, merged, inverse, states = run(
@@ -1152,6 +1161,9 @@
         first_state,
         gate=2,
     )
+    tick(second_mine)
+    second_third, second_near = swap(now(second_mine), 2, 0), swap(now(second_mine), 1, 0)
+    tick(*grad_blocks[1:])
     grad_all, grad_sums = run(
         once(
             collect_grad_kernel,
@@ -1190,7 +1202,7 @@
     second_last = swap(now(second_third), 1, 0)
     own_hidden_grad, own_up_sums = down_back(own_down, own_slope)
     own_kept, own_sent = hidden_weights(own_active, own_hidden_grad, 0, own_up_sums)
-    tick(second_last, second_near, first_later)
+    tick(second_last, second_near)
     own_got = swap(now(own_sent), 1, 0)
     far_up, far_down = run(
         once(
@@ -1207,7 +1219,7 @@
     far_active, far_slope = up_projection(far_up, far_up_bias)
     far_hidden_grad, far_up_sums = down_back(far_down, far_slope)
     far_kept, far_sent = hidden_weights(far_active, far_hidden_grad, 1, far_up_sums)
-    tick(own_got)
+    tick(own_got, first_later)
     own_next = run(add, own_kept[1], own_got[1])
     tick()
     far_got = swap(now(far_sent), 1, 0)

time: 221 us -> 216 us (0.977)
  waiting for transfers between devices: 101 us -> 89.4 us
  starting transfers between devices: 32.9 us -> 41.8 us
    ppermute x2, waiting for transfers between devices: 15.4 us -> 2.21 us  [across(): return lax.ppermute(values, AXES, pairs)]
    ppermute x37, starting transfers between devices: 28.5 us -> 38.2 us  [swap(): return lax.ppermute(values, AXES, pairs)]
    unnamed x40 -> x42, local copies, waits for them, and re-layouts: 5.82 us -> 5.85 us
where the time goes in v4:
time: 216 us
  waiting for transfers between devices  89.4 us (41%)
  Pallas kernels  71.4 us (33%)
  starting transfers between devices  41.8 us (19%)
  local copies, waits for them, and re-layouts  8.54 us (4%)
  other arithmetic  3.21 us (1%)
    ppermute x37, waiting for transfers between devices, swap(): return lax.ppermute(values, AXES, pairs)  87.2 us
    pallas_call x15, Pallas kernels, run(): result = step(*operands)  58.3 us
    ppermute x37, starting transfers between devices, swap(): return lax.ppermute(values, AXES, pairs)  38.2 us
    pallas_call x9, Pallas kernels, step(): call(kernel, name, listed, [spec(v) for v in operands[prefetch:]], [whole...  13.1 us
    unnamed x42, local copies, waits for them, and re-layouts  5.85 us
  transfers between devices with their start and end apart: 39, of which 18 were waited for; matrix products, arithmetic and copies ran while one was open for 2% of the time, Pallas kernels for 33%

profile of v4, /device:TPU:0, one launch (start us, length us, event | category | flops | bytes accessed | tf_op | source)
XLA Modules:
  0.0 215.6 jit_solution(8317378000494183598)
XLA Ops:
  0.7 3.1 %collective-permute-start.1 = (bf16[256,1024]{1,0:T(8,128)(2,1)}, bf16[256,1024]{1,0:T(8,128)(2,1)}, u32[]{:S(2)}, u32[]{:S(2)}) collective-permute-start(bf16[256,1024]{1,0:T(8,128)(2,1)} %x_ref.3), channel_id=1, source_target_pairs={{0,2},{1,3},{2,0},{3,1},{4,6},{5,7},{6,4},{7,5},{8,10},{9,11},{10,... | collective-permute-start | bytes 1572872 | tf_op jit(solution)/shard_map/ppermute | solution.py:739
  3.7 1.5 collective-permute-start
  14.7 3.2 %prepare.1 = (f32[1024,128]{1,0:T(8,128)S(1)}, f32[1024,128]{1,0:T(8,128)S(1)}, f32[1024,128]{1,0:T(8,128)S(1)}, bf16[128,128]{1,0:T(8,128)(2,1)S(1)}, bf16[128,...) custom-call(s32[3]{0:T(128)S(1)} %pad_add_fusion.table, f32[1,128]{1,0:T(1,128)S(1)} %copy-done.13, ...), custom_call_target="tpu_custom_call" | custom-call | flops 1000 | bytes 1000 | tf_op jit(solution)/shard_map/prepare/pallas_call | solution.py:759
  18.5 2.6 %collective-permute-start.3 = (bf16[400,384]{1,0:T(8,128)(2,1)}, bf16[400,384]{1,0:T(8,128)(2,1)S(1)}, u32[]{:S(2)}, u32[]{:S(2)}) collective-permute-start(bf16[400,384]{1,0:T(8,128)(2,1)} %copy-done.11), channel_id=1, source_target_pairs={{0,4},{1,5},{2,6},{3,7},{4,0},{5,1},{6,2},{7,3},{8,12},{9,13},{10,... | collective-permute-start | bytes 921608 | tf_op jit(solution)/shard_map/ppermute | solution.py:739
  21.1 13.1 %collective-permute-done.3.mine.bias = bf16[400,384]{1,0:T(8,128)(2,1)S(1)} collective-permute-done((bf16[400,384]{1,0:T(8,128)(2,1)}, bf16[400,384]{1,0:T(8,128)(2,1)S(1)}, u32[]{:S(2)}, u32[]{:S(2)}) %collective-permute-start.3) | collective-permute-done | bytes 307232 | tf_op jit(solution)/shard_map/ppermute | solution.py:739
  34.2 1.5 collective-permute-start.4
  35.8 3.1 %collective-permute-start.11 = (bf16[256,1024]{1,0:T(8,128)(2,1)}, bf16[256,1024]{1,0:T(8,128)(2,1)S(1)}, u32[]{:S(2)}, u32[]{:S(2)}) collective-permute-start(bf16[256,1024]{1,0:T(8,128)(2,1)} %copy-done.14), channel_id=1, source_target_pairs={{0,4},{1,5},{2,6},{3,7},{4,0},{5,1},{6,2},{7,3},{8,12},{9,13},{10,... | collective-permute-start | bytes 1572872 | tf_op jit(solution)/shard_map/ppermute | solution.py:739
  38.9 6.1 %own_features.1 = (bf16[1024,1024]{1,0:T(8,128)(2,1)S(1)}, bf16[1024,1024]{1,0:T(8,128)(2,1)S(1)}, bf16[1024,1024]{1,0:T(8,128)(2,1)S(1)}, f32[1024,256]{1,0:T(8...) custom-call(s32[3]{0:T(128)S(1)} %pad_add_fusion.table, s32[2048]{0:T(1024)S(1)} %bitcast.77, ...), custom_call_target="tpu_custom_call" | custom-call | flops 1000 | bytes 1000 | tf_op jit(solution)/shard_map/own_features/pallas_call | solution.py:759
  45.1 2.6 %up.4 = (bf16[1024,512]{1,0:T(8,128)(2,1)S(1)}, bf16[1024,512]{1,0:T(8,128)(2,1)S(1)}) custom-call(bf16[1024,1024]{1,0:T(8,128)(2,1)S(1)} %get-tuple-element.192.norm_ref.norm_two, bf16[512,1024]{1,0:T(8,128)(2,1)S(1)} %get-tuple-element.143.weight.own_up, f32[1,512]{1,0:T(1,128)S(1)} %get-tuple-element.157.bias), custom_call_target="tpu_custom_call" | custom-call | flops 1000 | bytes 1000 | tf_op jit(solution)/shard_map/up/pallas_call | solution.py:759
  48.4 4.7 %far_features.1 = (f32[1024,256]{1,0:T(8,128)S(1)}, bf16[1024,128]{1,0:T(8,128)(2,1)S(1)}, f32[2,128,128]{2,1,0:T(8,128)S(1)}) custom-call(s32[3]{0:T(128)S(1)} %pad_add_fusion.table, s32[2048]{0:T(1024)S(1)} %bitcast.78, bf16[1024,1024]{1,0:T(8,128)(2,1)S(1)} %get-tuple-element.218.norm_one, bf16[1024,384]{1,0:T(8,128)(2,1)S(1)} %get-tuple-element.161.weight.far_qkv, ...), custom_call_target="tpu_custom_call" | custom-call | flops 1000 | bytes 1000 | tf_op jit(solution)/shard_map/far_features/pallas_call | solution.py:759
  53.2 2.1 collective-permute-start.7
  55.3 1.6 collective-permute-start.9
  56.9 4.4 %collective-permute-done.8.refs_2_ = bf16[256,1024]{1,0:T(8,128)(2,1)S(1)} collective-permute-done((bf16[256,1024]{1,0:T(8,128)(2,1)}, bf16[256,1024]{1,0:T(8,128)(2,1)S(1)}, u32[]{:S(2)}, u32[]{:S(2)}) %collective-permute-start.8) | collective-permute-done | bytes 524320 | tf_op jit(solution)/shard_map/ppermute | solution.py:739
  62.2 1.5 collective-permute-start.10
  63.7 3.4 %attend.1 = (f32[1024,256]{1,0:T(8,128)S(1)}, bf16[1024,256]{1,0:T(8,128)(2,1)S(1)}, f32[1024,256]{1,0:T(8,128)S(1)}, f32[4,2,128,256]{3,2,1,0:T(8,128)S(1)}) custom-call(s32[3]{0:T(128)S(1)} %pad_add_fusion.table, s32[2048]{0:T(1024)S(1)} %bitcast.79, f32[1024,256]{1,0:T(8,128)S(1)} %get-tuple-element.167.own_feat, ...), custom_call_target="tpu_custom_call" | custom-call | flops 1000 | bytes 1000 | tf_op jit(solution)/shard_map/attend/pallas_call | solution.py:759
  67.7 2.5 %collective-permute-done.9.refs_1_ = bf16[256,1024]{1,0:T(8,128)(2,1)S(1)} collective-permute-done((bf16[256,1024]{1,0:T(8,128)(2,1)S(1)}, bf16[256,1024]{1,0:T(8,128)(2,1)S(1)}, u32[]{:S(2)}, u32[]{:S(2)}) %collective-permute-start.9) | collective-permute-done | bytes 524320 | tf_op jit(solution)/shard_map/ppermute | solution.py:739
  70.2 10.3 %collective-permute-done.10.refs_3_ = bf16[256,1024]{1,0:T(8,128)(2,1)S(1)} collective-permute-done((bf16[256,1024]{1,0:T(8,128)(2,1)S(1)}, bf16[256,1024]{1,0:T(8,128)(2,1)S(1)}, u32[]{:S(2)}, u32[]{:S(2)}) %collective-permute-start.10) | collective-permute-done | bytes 524320 | tf_op jit(solution)/shard_map/ppermute | solution.py:739
  80.7 5.4 %later.1 = (f32[1024,256]{1,0:T(8,128)S(1)}, f32[2,128,128]{2,1,0:T(8,128)S(1)}) custom-call(s32[3]{0:T(128)S(1)} %pad_add_fusion.table, s32[2048]{0:T(1024)S(1)} %bitcast.81, bf16[1024,1024]{1,0:T(8,128)(2,1)S(1)} %get-tuple-element.177.grad_ref.grad, bf16[128,1024]{1,0:T(8,128)(2,1)S(1)} %copy-done.6, bf16[128,1024]{1,0:T(8,128)(2,1)S(1)} %get-tuple-element.178.far_dense, ...), custom_call_target="tpu_custom_call" | custom-call | flops 1000 | bytes 1000 | tf_op jit(solution)/shard_map/later/pallas_call | solution.py:759
  86.2 2.1 down_back.2
  88.4 3.2 %hidden_weights.2 = (bf16[2,304,1024]{2,1,0:T(8,128)(2,1)S(1)}, bf16[2,304,1024]{2,1,0:T(8,128)(2,1)S(1)}) custom-call(s32[3]{0:T(128)S(1)} %pad_add_fusion.table, bf16[1024,512]{1,0:T(8,128)(2,1)S(1)} %get-tuple-element.158.active.own_active, bf16[1024,512]{1,0:T(8,128)(2,1)S(1)} %get-tuple-element.186.hidden_grad.own_hg, ...), custom_call_target="tpu_custom_call" | custom-call | flops 1000 | bytes 1000 | tf_op jit(solution)/shard_map/hidden_weights/pallas_call | solution.py:759
  92.2 1.5 collective-permute-start.16
  93.9 2.6 %up.5 = (bf16[1024,512]{1,0:T(8,128)(2,1)S(1)}, bf16[1024,512]{1,0:T(8,128)(2,1)S(1)}) custom-call(bf16[1024,1024]{1,0:T(8,128)(2,1)S(1)} %get-tuple-element.192.norm_ref.norm_two, bf16[512,1024]{1,0:T(8,128)(2,1)S(1)} %get-tuple-element.191.weight.far_up, f32[1,512]{1,0:T(1,128)S(1)} %get-tuple-element.193.bias), custom_call_target="tpu_custom_call" | custom-call | flops 1000 | bytes 1000 | tf_op jit(solution)/shard_map/up/pallas_call | solution.py:759
  96.5 2.1 down_back.3
  98.6 3.2 %hidden_weights.3 = (bf16[2,304,1024]{2,1,0:T(8,128)(2,1)S(1)}, bf16[2,304,1024]{2,1,0:T(8,128)(2,1)S(1)}) custom-call(s32[3]{0:T(128)S(1)} %pad_add_fusion.table, bf16[1024,512]{1,0:T(8,128)(2,1)S(1)} %get-tuple-element.194.active.far_active, bf16[1024,512]{1,0:T(8,128)(2,1)S(1)} %get-tuple-element.199.hidden_grad.far_hg, ...), custom_call_target="tpu_custom_call" | custom-call | flops 1000 | bytes 1000 | tf_op jit(solution)/shard_map/hidden_weights/pallas_call | solution.py:759
  103.6 4.2 %out.1 = (bf16[2,256,1024]{2,1,0:T(8,128)(2,1)S(1)}, bf16[2,256,1024]{2,1,0:T(8,128)(2,1)S(1)}) custom-call(bf16[1024,256]{1,0:T(8,128)(2,1)S(1)} %get-tuple-element.206.merged, bf16[1024,512]{1,0:T(8,128)(2,1)S(1)} %get-tuple-element.158.active.own_active, bf16[1024,512]{1,0:T(8,128)(2,1)S(1)} %get-tuple-element.194.active.far_active, ...), custom_call_target="tpu_custom_call" | custom-call | flops 1000 | bytes 1000 | tf_op jit(solution)/shard_map/out/pallas_call | solution.py:759
  108.0 1.6 collective-permute-start.19
  110.1 8.7 %attend_back.1 = (bf16[1024,384]{1,0:T(8,128)(2,1)S(1)}, bf16[1024,384]{1,0:T(8,128)(2,1)S(1)}) custom-call(s32[3]{0:T(128)S(1)} %pad_add_fusion.table, s32[2048]{0:T(1024)S(1)} %bitcast.82, f32[1024,256]{1,0:T(8,128)S(1)} %get-tuple-element.167.own_feat, f32[1024,256]{1,0:T(8,128)S(1)} %get-tuple-element.164.far_feat, ...), custom_call_target="tpu_custom_call" | custom-call | flops 1000 | bytes 1000 | tf_op jit(solution)/shard_map/attend_back/pallas_call | solution.py:759
  118.8 3.0 %qkv_weights.1 = (bf16[4,272,384]{2,1,0:T(8,128)(2,1)S(1)}, bf16[4,272,384]{2,1,0:T(8,128)(2,1)S(1)}) custom-call(s32[3]{0:T(128)S(1)} %pad_add_fusion.table, bf16[1024,384]{1,0:T(8,128)(2,1)S(1)} %get-tuple-element.215.own_pg, bf16[1024,384]{1,0:T(8,128)(2,1)S(1)} %get-tuple-element.216.far_pg, bf16[1024,1024]{1,0:T(8,128)(2,1)S(1)} %get-tuple-element.218.norm_one), custom_call_target="tpu_custom_call" | custom-call | flops 1000 | bytes 1000 | tf_op jit(solution)/shard_map/qkv_weights/pallas_call | solution.py:796
  121.8 4.0 %collective-permute-done.18 = bf16[304,1024]{1,0:T(8,128)(2,1)S(1)} collective-permute-done((bf16[304,1024]{1,0:T(8,128)(2,1)S(1)}, bf16[304,1024]{1,0:T(8,128)(2,1)S(1)}, u32[]{:S(2)}, u32[]{:S(2)}) %collective-permute-start.18) | collective-permute-done | bytes 622624 | tf_op jit(solution)/shard_map/ppermute | solution.py:739
  126.1 6.1 %norm_grad.1 = (f32[8,1024]{1,0:T(8,128)S(1)}, bf16[2,256,1024]{2,1,0:T(8,128)(2,1)S(1)}, bf16[2,256,1024]{2,1,0:T(8,128)(2,1)S(1)}) custom-call(bf16[1024,384]{1,0:T(8,128)(2,1)S(1)} %get-tuple-element.215.own_pg, bf16[1024,384]{1,0:T(8,128)(2,1)S(1)} %get-tuple-element.216.far_pg, bf16[1024,512]{1,0:T(8,128)(2,1)S(1)} %get-tuple-element.186.hidden_grad.own_hg, ...), custom_call_target="tpu_custom_call" | custom-call | flops 1000 | bytes 1000 | tf_op jit(solution)/shard_map/norm_grad/pallas_call | solution.py:759
  132.2 1.5 collective-permute-done.19
  134.8 1.8 collective-permute-done.20
  137.3 2.3 %collective-permute-start.23 = (bf16[304,1024]{1,0:T(8,128)(2,1)S(1)}, bf16[304,1024]{1,0:T(8,128)(2,1)S(1)}, u32[]{:S(2)}, u32[]{:S(2)}) collective-permute-start(bf16[304,1024]{1,0:T(8,128)(2,1)S(1)} %fusion.3), channel_id=1, source_target_pairs={{0,4},{1,5},{2,6},{3,7},{4,0},{5,1},{6,2},{7,3},{8,12},{9,13},{10,... | collective-permute-start | bytes 1867784 | tf_op jit(solution)/shard_map/ppermute | solution.py:739
  139.6 1.5 collective-permute-start.24
  141.1 1.6 collective-permute-start.25
  142.7 15.7 %collective-permute-done.21 = bf16[1,256,1024]{2,1,0:T(8,128)(2,1)S(1)} collective-permute-done((bf16[1,256,1024]{2,1,0:T(8,128)(2,1)S(1)}, bf16[1,256,1024]{2,1,0:T(8,128)(2,1)S(1)}, u32[]{:S(2)}, u32[]{:S(2)}) %collective-permute-start.21) | collective-permute-done | bytes 524320 | tf_op jit(solution)/shard_map/ppermute | solution.py:739
  159.6 7.8 %collective-permute-done.23 = bf16[304,1024]{1,0:T(8,128)(2,1)S(1)} collective-permute-done((bf16[304,1024]{1,0:T(8,128)(2,1)S(1)}, bf16[304,1024]{1,0:T(8,128)(2,1)S(1)}, u32[]{:S(2)}, u32[]{:S(2)}) %collective-permute-start.23) | collective-permute-done | bytes 622624 | tf_op jit(solution)/shard_map/ppermute | solution.py:739
  168.1 1.6 collective-permute-start.30
  170.8 3.4 %collective-permute-start.26 = (bf16[272,384]{1,0:T(8,128)(2,1)S(1)}, bf16[272,384]{1,0:T(8,128)(2,1)S(1)}, u32[]{:S(2)}, u32[]{:S(2)}) collective-permute-start(bf16[272,384]{1,0:T(8,128)(2,1)S(1)} %fusion.7), channel_id=1, source_target_pairs={{0,4},{1,5},{2,6},{3,7},{4,0},{5,1},{6,2},{7,3},{8,12},{9,13},{10,... | collective-permute-start | bytes 626696 | tf_op jit(solution)/shard_map/ppermute | solution.py:739
  175.4 11.4 %collective-permute-done.26 = bf16[272,384]{1,0:T(8,128)(2,1)S(1)} collective-permute-done((bf16[272,384]{1,0:T(8,128)(2,1)S(1)}, bf16[272,384]{1,0:T(8,128)(2,1)S(1)}, u32[]{:S(2)}, u32[]{:S(2)}) %collective-permute-start.26) | collective-permute-done | bytes 208928 | tf_op jit(solution)/shard_map/ppermute | solution.py:739
  188.7 1.7 finish_in.1
  191.6 6.9 %collective-permute-done.33.third = bf16[272,384]{1,0:T(8,128)(2,1)S(1)} collective-permute-done((bf16[272,384]{1,0:T(8,128)(2,1)S(1)}, bf16[272,384]{1,0:T(8,128)(2,1)S(1)}, u32[]{:S(2)}, u32[]{:S(2)}) %collective-permute-start.33) | collective-permute-done | bytes 208928 | tf_op jit(solution)/shard_map/ppermute | solution.py:739
  198.5 1.5 collective-permute-start.35
  200.0 2.4 %collective-permute-done.35 = f32[8,1024]{1,0:T(8,128)S(1)} collective-permute-done((f32[8,1024]{1,0:T(8,128)S(1)}, f32[8,1024]{1,0:T(8,128)S(1)}, u32[]{:S(2)}, u32[]{:S(2)}) %collective-permute-start.35) | collective-permute-done | bytes 32800 | tf_op jit(solution)/shard_map/ppermute | solution.py:739
  202.4 4.2 %collective-permute-start.36 = (f32[8,1024]{1,0:T(8,128)S(1)}, f32[8,1024]{1,0:T(8,128)S(1)}, u32[]{:S(2)}, u32[]{:S(2)}) collective-permute-start(f32[8,1024]{1,0:T(8,128)S(1)} %add.90), channel_id=1, source_target_pairs={{0,2},{1,3},{2,0},{3,1},{4,6},{5,7},{6,4},{7,5},{8,10},{9,11},{10,... | collective-permute-start | bytes 98312 | tf_op jit(solution)/shard_map/ppermute | solution.py:739
  206.6 3.5 %finish_hidden.1 = (f32[1024,512]{1,0:T(8,128)}, f32[512,1024]{1,0:T(8,128)}, f32[128,1024]{1,0:T(8,128)}, f32[4,1,128]{2,1,0:T(1,128)}) custom-call(s32[3]{0:T(128)S(1)} %pad_add_fusion.table, bf16[304,1024]{1,0:T(8,128)(2,1)S(1)} %add_convert_fusion.2.mine, bf16[304,1024]{1,0:T(8,128)(2,1)S(1)} %collective-permute-done.27.near, ...), custom_call_target="tpu_custom_call" | custom-call | flops 1000 | bytes 1000 | tf_op jit(solution)/shard_map/finish_hidden/pallas_call | solution.py:796
  210.2 1.8 finish_qkv.1
  212.6 2.5 %collective-permute-done.38 = f32[8,1024]{1,0:T(8,128)S(1)} collective-permute-done((f32[8,1024]{1,0:T(8,128)S(1)}, f32[8,1024]{1,0:T(8,128)S(1)}, u32[]{:S(2)}, u32[]{:S(2)}) %collective-permute-start.38) | collective-permute-done | bytes 32800 | tf_op jit(solution)/shard_map/ppermute | solution.py:739
  (131 shorter events, 26.3 us)
Async XLA Ops:
  0.6 9.4 %copy-start.15 = (bf16[512]{0:T(512)(128)(2,1)S(1)}, bf16[512]{0:T(512)(128)(2,1)}, u32[]{:S(2)}) copy-start(bf16[512]{0:T(512)(128)(2,1)} %param.21) | copy-start | bytes 3076
  0.7 17.2 %collective-permute-start.1 = (bf16[256,1024]{1,0:T(8,128)(2,1)}, bf16[256,1024]{1,0:T(8,128)(2,1)}, u32[]{:S(2)}, u32[]{:S(2)}) collective-permute-start(bf16[256,1024]{1,0:T(8,128)(2,1)} %x_ref.3), channel_id=1, source_target_pairs={{0,2},{1,3},{2,0},{3,1},{4,6},{5,7},{6,4},{7,5},{8,10},{9,11},{10,... | collective-permute-start | bytes 1572872 | tf_op jit(solution)/shard_map/ppermute | solution.py:739
  3.7 30.5 %collective-permute-start = (bf16[256,1024]{1,0:T(8,128)(2,1)}, bf16[256,1024]{1,0:T(8,128)(2,1)}, u32[]{:S(2)}, u32[]{:S(2)}) collective-permute-start(bf16[256,1024]{1,0:T(8,128)(2,1)} %x_ref.3), channel_id=1, source_target_pairs={{0,1},{1,0},{2,3},{3,2},{4,5},{5,4},{6,7},{7,6},{8,9},{9,8},{10,11... | collective-permute-start | bytes 1572872 | tf_op jit(solution)/shard_map/ppermute | solution.py:739
  11.3 3.3 %copy-start.19 = (bf16[1024]{0:T(1024)(128)(2,1)S(1)}, bf16[1024]{0:T(1024)(128)(2,1)}, u32[]{:S(2)}) copy-start(bf16[1024]{0:T(1024)(128)(2,1)} %param.27) | copy-start | bytes 6148
  11.3 3.3 %copy-start.12 = (f32[64,64]{1,0:T(8,128)S(1)}, f32[64,64]{1,0:T(8,128)}, u32[]{:S(2)}) copy-start(f32[64,64]{1,0:T(8,128)} %omega) | copy-start | bytes 49156
  11.3 3.3 %copy-start.13 = (f32[1,128]{1,0:T(1,128)S(1)}, f32[1,128]{1,0:T(1,128)}, u32[]{:S(2)}) copy-start(f32[1,128]{1,0:T(1,128)} %constant.45.clone.rates) | copy-start | bytes 1540
  14.2 24.7 %copy-start.1 = (bf16[1024,384]{1,0:T(8,128)(2,1)S(1)}, bf16[1024,384]{1,0:T(8,128)(2,1)}, u32[]{:S(2)}) copy-start(bf16[1024,384]{1,0:T(8,128)(2,1)} %own_qkv.1) | copy-start | bytes 2359300
  14.2 24.7 %copy-start.2 = (bf16[256,1024]{1,0:T(8,128)(2,1)S(1)}, bf16[256,1024]{1,0:T(8,128)(2,1)}, u32[]{:S(2)}) copy-start(bf16[256,1024]{1,0:T(8,128)(2,1)} %x_ref.3) | copy-start | bytes 1572868
  17.9 16.3 %collective-permute-start.2 = (bf16[256,1024]{1,0:T(8,128)(2,1)}, bf16[256,1024]{1,0:T(8,128)(2,1)S(1)}, u32[]{:S(2)}, u32[]{:S(2)}) collective-permute-start(bf16[256,1024]{1,0:T(8,128)(2,1)} %collective-permute-done.1.refs_2_), channel_id=1, source_target_pairs={{0,1},{1,0},{2,3},{3,2},{4,5},{5,4},{6,7},{7,6},{8,9},{9,8},{10,11... | collective-permute-start | bytes 1572872 | tf_op jit(solution)/shard_map/ppermute | solution.py:739
  18.5 15.7 %collective-permute-start.3 = (bf16[400,384]{1,0:T(8,128)(2,1)}, bf16[400,384]{1,0:T(8,128)(2,1)S(1)}, u32[]{:S(2)}, u32[]{:S(2)}) collective-permute-start(bf16[400,384]{1,0:T(8,128)(2,1)} %copy-done.11), channel_id=1, source_target_pairs={{0,4},{1,5},{2,6},{3,7},{4,0},{5,1},{6,2},{7,3},{8,12},{9,13},{10,... | collective-permute-start | bytes 921608 | tf_op jit(solution)/shard_map/ppermute | solution.py:739
  34.2 10.8 %collective-permute-start.4 = (bf16[400,384]{1,0:T(8,128)(2,1)S(1)}, bf16[400,384]{1,0:T(8,128)(2,1)S(1)}, u32[]{:S(2)}, u32[]{:S(2)}) collective-permute-start(bf16[400,384]{1,0:T(8,128)(2,1)S(1)} %collective-permute-done.3.mine.bias), channel_id=1, source_target_pairs={{0,16},{1,17},{2,18},{3,19},{4,20},{5,21},{6,22},{7,23},{8,24},{9,... | collective-permute-start | bytes 921608 | tf_op jit(solution)/shard_map/ppermute | solution.py:739
  35.8 9.3 %collective-permute-start.5 = (bf16[400,384]{1,0:T(8,128)(2,1)S(1)}, bf16[400,384]{1,0:T(8,128)(2,1)S(1)}, u32[]{:S(2)}, u32[]{:S(2)}) collective-permute-start(bf16[400,384]{1,0:T(8,128)(2,1)S(1)} %collective-permute-done.3.mine.bias), channel_id=1, source_target_pairs={{0,8},{1,9},{2,10},{3,11},{4,12},{5,13},{6,14},{7,15},{8,0},{9,1},... | collective-permute-start | bytes 921608 | tf_op jit(solution)/shard_map/ppermute | solution.py:739
  35.8 25.6 %collective-permute-start.8 = (bf16[256,1024]{1,0:T(8,128)(2,1)}, bf16[256,1024]{1,0:T(8,128)(2,1)S(1)}, u32[]{:S(2)}, u32[]{:S(2)}) collective-permute-start(bf16[256,1024]{1,0:T(8,128)(2,1)} %grad_ref.1), channel_id=1, source_target_pairs={{0,2},{1,3},{2,0},{3,1},{4,6},{5,7},{6,4},{7,5},{8,10},{9,11},{10,... | collective-permute-start | bytes 1572872 | tf_op jit(solution)/shard_map/ppermute | solution.py:739
  35.8 31.4 %collective-permute-start.11 = (bf16[256,1024]{1,0:T(8,128)(2,1)}, bf16[256,1024]{1,0:T(8,128)(2,1)S(1)}, u32[]{:S(2)}, u32[]{:S(2)}) collective-permute-start(bf16[256,1024]{1,0:T(8,128)(2,1)} %copy-done.14), channel_id=1, source_target_pairs={{0,4},{1,5},{2,6},{3,7},{4,0},{5,1},{6,2},{7,3},{8,12},{9,13},{10,... | collective-permute-start | bytes 1572872 | tf_op jit(solution)/shard_map/ppermute | solution.py:739
  45.1 2.7 %collective-permute-start.6 = (bf16[400,384]{1,0:T(8,128)(2,1)S(1)}, bf16[400,384]{1,0:T(8,128)(2,1)S(1)}, u32[]{:S(2)}, u32[]{:S(2)}) collective-permute-start(bf16[400,384]{1,0:T(8,128)(2,1)S(1)} %collective-permute-done.4.third), channel_id=1, source_target_pairs={{0,8},{1,9},{2,10},{3,11},{4,12},{5,13},{6,14},{7,15},{8,0},{9,1},... | collective-permute-start | bytes 921608 | tf_op jit(solution)/shard_map/ppermute | solution.py:739
  48.4 6.9 %copy-start.7 = (bf16[256,1024]{1,0:T(8,128)(2,1)S(1)}, bf16[256,1024]{1,0:T(8,128)(2,1)}, u32[]{:S(2)}) copy-start(bf16[256,1024]{1,0:T(8,128)(2,1)} %grad_ref.1) | copy-start | bytes 1572868
  53.2 9.0 %collective-permute-start.7 = (f32[2,128,128]{2,1,0:T(8,128)S(1)}, f32[2,128,128]{2,1,0:T(8,128)S(1)}, u32[]{:S(2)}, u32[]{:S(2)}) collective-permute-start(f32[2,128,128]{2,1,0:T(8,128)S(1)} %get-tuple-element.165), channel_id=1, source_target_pairs={{0,4},{1,5},{2,6},{3,7},{8,12},{9,13},{10,14},{11,15},{16,20},{17,... | collective-permute-start | bytes 393224 | tf_op jit(solution)/shard_map/ppermute | solution.py:747
  55.3 14.9 %collective-permute-start.9 = (bf16[256,1024]{1,0:T(8,128)(2,1)S(1)}, bf16[256,1024]{1,0:T(8,128)(2,1)S(1)}, u32[]{:S(2)}, u32[]{:S(2)}) collective-permute-start(bf16[256,1024]{1,0:T(8,128)(2,1)S(1)} %copy-done.7), channel_id=1, source_target_pairs={{0,1},{1,0},{2,3},{3,2},{4,5},{5,4},{6,7},{7,6},{8,9},{9,8},{10,11... | collective-permute-start | bytes 1572872 | tf_op jit(solution)/shard_map/ppermute | solution.py:739
  62.2 18.3 %collective-permute-start.10 = (bf16[256,1024]{1,0:T(8,128)(2,1)S(1)}, bf16[256,1024]{1,0:T(8,128)(2,1)S(1)}, u32[]{:S(2)}, u32[]{:S(2)}) collective-permute-start(bf16[256,1024]{1,0:T(8,128)(2,1)S(1)} %collective-permute-done.8.refs_2_), channel_id=1, source_target_pairs={{0,1},{1,0},{2,3},{3,2},{4,5},{5,4},{6,7},{7,6},{8,9},{9,8},{10,11... | collective-permute-start | bytes 1572872 | tf_op jit(solution)/shard_map/ppermute | solution.py:739
  67.1 13.6 %copy-start.6 = (bf16[128,1024]{1,0:T(8,128)(2,1)S(1)}, bf16[128,1024]{1,0:T(8,128)(2,1)}, u32[]{:S(2)}) copy-start(bf16[128,1024]{1,0:T(8,128)(2,1)} %own_dense.3) | copy-start | bytes 786436
  67.1 19.0 %collective-permute-start.12 = (bf16[256,1024]{1,0:T(8,128)(2,1)S(1)}, bf16[256,1024]{1,0:T(8,128)(2,1)S(1)}, u32[]{:S(2)}, u32[]{:S(2)}) collective-permute-start(bf16[256,1024]{1,0:T(8,128)(2,1)S(1)} %collective-permute-done.11.mine), channel_id=1, source_target_pairs={{0,16},{1,17},{2,18},{3,19},{4,20},{5,21},{6,22},{7,23},{8,24},{9,... | collective-permute-start | bytes 1572872 | tf_op jit(solution)/shard_map/ppermute | solution.py:739
  67.7 23.9 %collective-permute-start.14 = (bf16[256,1024]{1,0:T(8,128)(2,1)S(1)}, bf16[256,1024]{1,0:T(8,128)(2,1)S(1)}, u32[]{:S(2)}, u32[]{:S(2)}) collective-permute-start(bf16[256,1024]{1,0:T(8,128)(2,1)S(1)} %collective-permute-done.11.mine), channel_id=1, source_target_pairs={{0,8},{1,9},{2,10},{3,11},{4,12},{5,13},{6,14},{7,15},{8,0},{9,1},... | collective-permute-start | bytes 1572872 | tf_op jit(solution)/shard_map/ppermute | solution.py:739
  80.7 5.5 %copy-start.4 = (bf16[512,1024]{1,0:T(8,128)(2,1)S(1)}, bf16[512,1024]{1,0:T(8,128)(2,1)}, u32[]{:S(2)}) copy-start(bf16[512,1024]{1,0:T(8,128)(2,1)} %copy-done.3) | copy-start | bytes 3145732
  86.2 5.5 %collective-permute-start.13 = (bf16[256,1024]{1,0:T(8,128)(2,1)S(1)}, bf16[256,1024]{1,0:T(8,128)(2,1)S(1)}, u32[]{:S(2)}, u32[]{:S(2)}) collective-permute-start(bf16[256,1024]{1,0:T(8,128)(2,1)S(1)} %collective-permute-done.12.third), channel_id=1, source_target_pairs={{0,8},{1,9},{2,10},{3,11},{4,12},{5,13},{6,14},{7,15},{8,0},{9,1},... | collective-permute-start | bytes 1572872 | tf_op jit(solution)/shard_map/ppermute | solution.py:739
  91.6 11.6 %collective-permute-start.15 = (bf16[2,304,1024]{2,1,0:T(8,128)(2,1)S(1)}, bf16[2,304,1024]{2,1,0:T(8,128)(2,1)S(1)}, u32[]{:S(2)}, u32[]{:S(2)}) collective-permute-start(bf16[2,304,1024]{2,1,0:T(8,128)(2,1)S(1)} %get-tuple-element.203), channel_id=1, source_target_pairs={{0,8},{1,9},{2,10},{3,11},{4,12},{5,13},{6,14},{7,15},{8,0},{9,1},... | collective-permute-start | bytes 3735560 | tf_op jit(solution)/shard_map/ppermute | solution.py:739
  92.2 11.0 %collective-permute-start.16 = (f32[2,128,128]{2,1,0:T(8,128)S(1)}, f32[2,128,128]{2,1,0:T(8,128)S(1)}, u32[]{:S(2)}, u32[]{:S(2)}) collective-permute-start(f32[2,128,128]{2,1,0:T(8,128)S(1)} %get-tuple-element.204), channel_id=1, source_target_pairs={{4,0},{5,1},{6,2},{7,3},{12,8},{13,9},{14,10},{15,11},{20,16},{21,... | collective-permute-start | bytes 393224 | tf_op jit(solution)/shard_map/ppermute | solution.py:747
  103.4 4.4 %collective-permute-start.17 = (bf16[2,304,1024]{2,1,0:T(8,128)(2,1)S(1)}, bf16[2,304,1024]{2,1,0:T(8,128)(2,1)S(1)}, u32[]{:S(2)}, u32[]{:S(2)}) collective-permute-start(bf16[2,304,1024]{2,1,0:T(8,128)(2,1)S(1)} %get-tuple-element.209), channel_id=1, source_target_pairs={{0,8},{1,9},{2,10},{3,11},{4,12},{5,13},{6,14},{7,15},{8,0},{9,1},... | collective-permute-start | bytes 3735560 | tf_op jit(solution)/shard_map/ppermute | solution.py:739
  108.0 25.6 %collective-permute-start.19 = (bf16[2,256,1024]{2,1,0:T(8,128)(2,1)S(1)}, bf16[2,256,1024]{2,1,0:T(8,128)(2,1)S(1)}, u32[]{:S(2)}, u32[]{:S(2)}) collective-permute-start(bf16[2,256,1024]{2,1,0:T(8,128)(2,1)S(1)} %get-tuple-element.226), channel_id=1, source_target_pairs={{0,1},{1,0},{2,3},{3,2},{4,5},{5,4},{6,7},{7,6},{8,9},{9,8},{10,11... | collective-permute-start | bytes 3145736 | tf_op jit(solution)/shard_map/ppermute | solution.py:739
  109.6 16.1 %collective-permute-start.18 = (bf16[304,1024]{1,0:T(8,128)(2,1)S(1)}, bf16[304,1024]{1,0:T(8,128)(2,1)S(1)}, u32[]{:S(2)}, u32[]{:S(2)}) collective-permute-start(bf16[304,1024]{1,0:T(8,128)(2,1)S(1)} %fusion.4), channel_id=1, source_target_pairs={{0,16},{1,17},{2,18},{3,19},{4,20},{5,21},{6,22},{7,23},{8,24},{9,... | collective-permute-start | bytes 1867784 | tf_op jit(solution)/shard_map/ppermute | solution.py:739
  134.2 2.4 %collective-permute-start.20 = (bf16[4,272,384]{2,1,0:T(8,128)(2,1)S(1)}, bf16[4,272,384]{2,1,0:T(8,128)(2,1)S(1)}, u32[]{:S(2)}, u32[]{:S(2)}) collective-permute-start(bf16[4,272,384]{2,1,0:T(8,128)(2,1)S(1)} %get-tuple-element.229), channel_id=1, source_target_pairs={{0,8},{1,9},{2,10},{3,11},{4,12},{5,13},{6,14},{7,15},{8,0},{9,1},... | collective-permute-start | bytes 2506760 | tf_op jit(solution)/shard_map/ppermute | solution.py:739
  134.3 24.1 %collective-permute-start.21 = (bf16[1,256,1024]{2,1,0:T(8,128)(2,1)S(1)}, bf16[1,256,1024]{2,1,0:T(8,128)(2,1)S(1)}, u32[]{:S(2)}, u32[]{:S(2)}) collective-permute-start(bf16[1,256,1024]{2,1,0:T(8,128)(2,1)S(1)} %get-tuple-element.231), channel_id=1, source_target_pairs={{0,2},{1,3},{2,0},{3,1},{4,6},{5,7},{6,4},{7,5},{8,10},{9,11},{10,... | collective-permute-start | bytes 1572872 | tf_op jit(solution)/shard_map/ppermute | solution.py:739
  136.7 22.8 %collective-permute-start.22 = (bf16[2,272,384]{2,1,0:T(8,128)(2,1)S(1)}, bf16[2,272,384]{2,1,0:T(8,128)(2,1)S(1)}, u32[]{:S(2)}, u32[]{:S(2)}) collective-permute-start(bf16[2,272,384]{2,1,0:T(8,128)(2,1)S(1)} %add_convert_fusion.3), channel_id=1, source_target_pairs={{0,16},{1,17},{2,18},{3,19},{4,20},{5,21},{6,22},{7,23},{8,24},{9,... | collective-permute-start | bytes 1253384 | tf_op jit(solution)/shard_map/ppermute | solution.py:739
  137.3 30.1 %collective-permute-start.23 = (bf16[304,1024]{1,0:T(8,128)(2,1)S(1)}, bf16[304,1024]{1,0:T(8,128)(2,1)S(1)}, u32[]{:S(2)}, u32[]{:S(2)}) collective-permute-start(bf16[304,1024]{1,0:T(8,128)(2,1)S(1)} %fusion.3), channel_id=1, source_target_pairs={{0,4},{1,5},{2,6},{3,7},{4,0},{5,1},{6,2},{7,3},{8,12},{9,13},{10,... | collective-permute-start | bytes 1867784 | tf_op jit(solution)/shard_map/ppermute | solution.py:739
  139.6 27.9 %collective-permute-start.24 = (bf16[304,1024]{1,0:T(8,128)(2,1)S(1)}, bf16[304,1024]{1,0:T(8,128)(2,1)S(1)}, u32[]{:S(2)}, u32[]{:S(2)}) collective-permute-start(bf16[304,1024]{1,0:T(8,128)(2,1)S(1)} %fusion.5), channel_id=1, source_target_pairs={{0,16},{1,17},{2,18},{3,19},{4,20},{5,21},{6,22},{7,23},{8,24},{9,... | collective-permute-start | bytes 1867784 | tf_op jit(solution)/shard_map/ppermute | solution.py:739
  141.1 28.5 %collective-permute-start.25 = (bf16[2,256,1024]{2,1,0:T(8,128)(2,1)S(1)}, bf16[2,256,1024]{2,1,0:T(8,128)(2,1)S(1)}, u32[]{:S(2)}, u32[]{:S(2)}) collective-permute-start(bf16[2,256,1024]{2,1,0:T(8,128)(2,1)S(1)} %get-tuple-element.242), channel_id=1, source_target_pairs={{0,1},{1,0},{2,3},{3,2},{4,5},{5,4},{6,7},{7,6},{8,9},{9,8},{10,11... | collective-permute-start | bytes 3145736 | tf_op jit(solution)/shard_map/ppermute | solution.py:739
  168.0 18.8 %collective-permute-start.27 = (bf16[304,1024]{1,0:T(8,128)(2,1)S(1)}, bf16[304,1024]{1,0:T(8,128)(2,1)S(1)}, u32[]{:S(2)}, u32[]{:S(2)}) collective-permute-start(bf16[304,1024]{1,0:T(8,128)(2,1)S(1)} %add_convert_fusion.2.mine), channel_id=1, source_target_pairs={{0,8},{1,9},{2,10},{3,11},{4,12},{5,13},{6,14},{7,15},{8,0},{9,1},... | collective-permute-start | bytes 1867784 | tf_op jit(solution)/shard_map/ppermute | solution.py:739
  168.1 22.3 %collective-permute-start.30 = (bf16[304,1024]{1,0:T(8,128)(2,1)S(1)}, bf16[304,1024]{1,0:T(8,128)(2,1)S(1)}, u32[]{:S(2)}, u32[]{:S(2)}) collective-permute-start(bf16[304,1024]{1,0:T(8,128)(2,1)S(1)} %add_convert_fusion.2.mine), channel_id=1, source_target_pairs={{0,16},{1,17},{2,18},{3,19},{4,20},{5,21},{6,22},{7,23},{8,24},{9,... | collective-permute-start | bytes 1867784 | tf_op jit(solution)/shard_map/ppermute | solution.py:739
  170.1 18.5 %collective-permute-start.29 = (bf16[1,256,1024]{2,1,0:T(8,128)(2,1)S(1)}, bf16[1,256,1024]{2,1,0:T(8,128)(2,1)S(1)}, u32[]{:S(2)}, u32[]{:S(2)}) collective-permute-start(bf16[1,256,1024]{2,1,0:T(8,128)(2,1)S(1)} %get-tuple-element.249), channel_id=1, source_target_pairs={{0,2},{1,3},{2,0},{3,1},{4,6},{5,7},{6,4},{7,5},{8,10},{9,11},{10,... | collective-permute-start | bytes 1572872 | tf_op jit(solution)/shard_map/ppermute | solution.py:739
  170.8 16.0 %collective-permute-start.26 = (bf16[272,384]{1,0:T(8,128)(2,1)S(1)}, bf16[272,384]{1,0:T(8,128)(2,1)S(1)}, u32[]{:S(2)}, u32[]{:S(2)}) collective-permute-start(bf16[272,384]{1,0:T(8,128)(2,1)S(1)} %fusion.7), channel_id=1, source_target_pairs={{0,4},{1,5},{2,6},{3,7},{4,0},{5,1},{6,2},{7,3},{8,12},{9,13},{10,... | collective-permute-start | bytes 626696 | tf_op jit(solution)/shard_map/ppermute | solution.py:739
  174.2 1.2 collective-permute-start.28
  186.9 4.0 %collective-permute-start.31 = (f32[8,1024]{1,0:T(8,128)S(1)}, f32[8,1024]{1,0:T(8,128)S(1)}, u32[]{:S(2)}, u32[]{:S(2)}) collective-permute-start(f32[8,1024]{1,0:T(8,128)S(1)} %add.88), channel_id=1, source_target_pairs={{0,16},{1,17},{2,18},{3,19},{4,20},{5,21},{6,22},{7,23},{8,24},{9,... | collective-permute-start | bytes 98312 | tf_op jit(solution)/shard_map/ppermute | solution.py:739
  190.9 11.5 %collective-permute-start.32 = (bf16[304,1024]{1,0:T(8,128)(2,1)S(1)}, bf16[304,1024]{1,0:T(8,128)(2,1)S(1)}, u32[]{:S(2)}, u32[]{:S(2)}) collective-permute-start(bf16[304,1024]{1,0:T(8,128)(2,1)S(1)} %collective-permute-done.30.third), channel_id=1, source_target_pairs={{0,8},{1,9},{2,10},{3,11},{4,12},{5,13},{6,14},{7,15},{8,0},{9,1},... | collective-permute-start | bytes 1867784 | tf_op jit(solution)/shard_map/ppermute | solution.py:739
  190.9 7.6 %collective-permute-start.33 = (bf16[272,384]{1,0:T(8,128)(2,1)S(1)}, bf16[272,384]{1,0:T(8,128)(2,1)S(1)}, u32[]{:S(2)}, u32[]{:S(2)}) collective-permute-start(bf16[272,384]{1,0:T(8,128)(2,1)S(1)} %add_convert_fusion.4.mine), channel_id=1, source_target_pairs={{0,16},{1,17},{2,18},{3,19},{4,20},{5,21},{6,22},{7,23},{8,24},{9,... | collective-permute-start | bytes 626696 | tf_op jit(solution)/shard_map/ppermute | solution.py:739
  191.4 7.1 %collective-permute-start.34 = (bf16[272,384]{1,0:T(8,128)(2,1)S(1)}, bf16[272,384]{1,0:T(8,128)(2,1)S(1)}, u32[]{:S(2)}, u32[]{:S(2)}) collective-permute-start(bf16[272,384]{1,0:T(8,128)(2,1)S(1)} %add_convert_fusion.4.mine), channel_id=1, source_target_pairs={{0,8},{1,9},{2,10},{3,11},{4,12},{5,13},{6,14},{7,15},{8,0},{9,1},... | collective-permute-start | bytes 626696 | tf_op jit(solution)/shard_map/ppermute | solution.py:739
  198.5 11.7 %collective-permute-start.37 = (bf16[272,384]{1,0:T(8,128)(2,1)S(1)}, bf16[272,384]{1,0:T(8,128)(2,1)S(1)}, u32[]{:S(2)}, u32[]{:S(2)}) collective-permute-start(bf16[272,384]{1,0:T(8,128)(2,1)S(1)} %collective-permute-done.33.third), channel_id=1, source_target_pairs={{0,8},{1,9},{2,10},{3,11},{4,12},{5,13},{6,14},{7,15},{8,0},{9,1},... | collective-permute-start | bytes 626696 | tf_op jit(solution)/shard_map/ppermute | solution.py:739
  198.5 3.9 %collective-permute-start.35 = (f32[8,1024]{1,0:T(8,128)S(1)}, f32[8,1024]{1,0:T(8,128)S(1)}, u32[]{:S(2)}, u32[]{:S(2)}) collective-permute-start(f32[8,1024]{1,0:T(8,128)S(1)} %add.89), channel_id=1, source_target_pairs={{0,1},{1,0},{2,3},{3,2},{4,5},{5,4},{6,7},{7,6},{8,9},{9,8},{10,11... | collective-permute-start | bytes 98312 | tf_op jit(solution)/shard_map/ppermute | solution.py:739
  202.4 7.7 %collective-permute-start.36 = (f32[8,1024]{1,0:T(8,128)S(1)}, f32[8,1024]{1,0:T(8,128)S(1)}, u32[]{:S(2)}, u32[]{:S(2)}) collective-permute-start(f32[8,1024]{1,0:T(8,128)S(1)} %add.90), channel_id=1, source_target_pairs={{0,2},{1,3},{2,0},{3,1},{4,6},{5,7},{6,4},{7,5},{8,10},{9,11},{10,... | collective-permute-start | bytes 98312 | tf_op jit(solution)/shard_map/ppermute | solution.py:739
  210.1 5.0 %collective-permute-start.38 = (f32[8,1024]{1,0:T(8,128)S(1)}, f32[8,1024]{1,0:T(8,128)S(1)}, u32[]{:S(2)}, u32[]{:S(2)}) collective-permute-start(f32[8,1024]{1,0:T(8,128)S(1)} %add.91), channel_id=1, source_target_pairs={{0,4},{1,5},{2,6},{3,7},{4,0},{5,1},{6,2},{7,3},{8,12},{9,13},{10,... | collective-permute-start | bytes 98312 | tf_op jit(solution)/shard_map/ppermute | solution.py:739
  (12 other events, 22.9 us)

commit v5 on v4

--- a/solution.py
+++ b/solution.py
@@ -1427,13 +1427,9 @@
     tick(lower_third, moved_small)
     lower = (lower_mine, lower_near, lower_third, swap(now(lower_third), 1, 0))
     small = small_add(moved_small)
-    tick(upper_third, upper_near)
-    upper = (upper_mine, upper_near, upper_third, swap(now(upper_third), 1, 0))
-    moved_small = small_start()
-    tick(lower[3], moved_small)
-    small = small_add(moved_small)
     tick()
     moved_small = small_start()
+    tick(lower[3])
     up_grad, down_grad, dense_grad, up_bias_grad = run(
         once(
             finish_hidden_kernel,
@@ -1450,7 +1446,12 @@
         *lower,
         gate=1,
     )
-    tick(moved_small, upper[3])
+    tick(upper_third, upper_near, moved_small)
+    upper = (upper_mine, upper_near, upper_third, swap(now(upper_third), 1, 0))
+    small = small_add(moved_small)
+    tick()
+    moved_small = small_start()
+    tick(upper[3], moved_small)
     small = small_add(moved_small)
     tick()
     moved_small = small_start()

time: 216 us -> 210 us (0.972)
  waiting for transfers between devices: 89.4 us -> 82.7 us
    ppermute x37, waiting for transfers between devices: 87.2 us -> 80.5 us  [swap(): return lax.ppermute(values, AXES, pairs)]
  transfers between devices with their start and end apart: 39 -> 39, of which waited for: 18 -> 18; matrix products, arithmetic and copies ran while one was open for 2% -> 2% of each run, Pallas kernels for 33% -> 34%
where the time goes in v5:
time: 210 us
  waiting for transfers between devices  82.7 us (39%)
  Pallas kernels  71.4 us (34%)
  starting transfers between devices  43 us (20%)
  local copies, waits for them, and re-layouts  8.54 us (4%)
  other arithmetic  3.21 us (2%)
    ppermute x37, waiting for transfers between devices, swap(): return lax.ppermute(values, AXES, pairs)  80.5 us
    pallas_call x15, Pallas kernels, run(): result = step(*operands)  58.3 us
    ppermute x37, starting transfers between devices, swap(): return lax.ppermute(values, AXES, pairs)  39.4 us
    pallas_call x9, Pallas kernels, step(): call(kernel, name, listed, [spec(v) for v in operands[prefetch:]], [whole...  13.1 us
    unnamed x42, local copies, waits for them, and re-layouts  5.85 us
  transfers between devices with their start and end apart: 39, of which 18 were waited for; matrix products, arithmetic and copies ran while one was open for 2% of the time, Pallas kernels for 34%

profile of v5, /device:TPU:0, one launch (start us, length us, event | category | flops | bytes accessed | tf_op | source)
XLA Modules:
  0.0 210.1 jit_solution(4525808844828523966)
XLA Ops:
  0.7 3.1 %collective-permute-start.1 = (bf16[256,1024]{1,0:T(8,128)(2,1)}, bf16[256,1024]{1,0:T(8,128)(2,1)}, u32[]{:S(2)}, u32[]{:S(2)}) collective-permute-start(bf16[256,1024]{1,0:T(8,128)(2,1)} %x_ref.3), channel_id=1, source_target_pairs={{0,2},{1,3},{2,0},{3,1},{4,6},{5,7},{6,4},{7,5},{8,10},{9,11},{10,... | collective-permute-start | bytes 1572872 | tf_op jit(solution)/shard_map/ppermute | solution.py:739
  3.7 1.5 collective-permute-start
  14.7 3.2 %prepare.1 = (f32[1024,128]{1,0:T(8,128)S(1)}, f32[1024,128]{1,0:T(8,128)S(1)}, f32[1024,128]{1,0:T(8,128)S(1)}, bf16[128,128]{1,0:T(8,128)(2,1)S(1)}, bf16[128,...) custom-call(s32[3]{0:T(128)S(1)} %pad_add_fusion.table, f32[1,128]{1,0:T(1,128)S(1)} %copy-done.13, ...), custom_call_target="tpu_custom_call" | custom-call | flops 1000 | bytes 1000 | tf_op jit(solution)/shard_map/prepare/pallas_call | solution.py:759
  18.5 2.6 %collective-permute-start.3 = (bf16[400,384]{1,0:T(8,128)(2,1)}, bf16[400,384]{1,0:T(8,128)(2,1)S(1)}, u32[]{:S(2)}, u32[]{:S(2)}) collective-permute-start(bf16[400,384]{1,0:T(8,128)(2,1)} %copy-done.11), channel_id=1, source_target_pairs={{0,4},{1,5},{2,6},{3,7},{4,0},{5,1},{6,2},{7,3},{8,12},{9,13},{10,... | collective-permute-start | bytes 921608 | tf_op jit(solution)/shard_map/ppermute | solution.py:739
  21.1 13.1 %collective-permute-done.3.mine.bias = bf16[400,384]{1,0:T(8,128)(2,1)S(1)} collective-permute-done((bf16[400,384]{1,0:T(8,128)(2,1)}, bf16[400,384]{1,0:T(8,128)(2,1)S(1)}, u32[]{:S(2)}, u32[]{:S(2)}) %collective-permute-start.3) | collective-permute-done | bytes 307232 | tf_op jit(solution)/shard_map/ppermute | solution.py:739
  34.2 1.5 collective-permute-start.4
  35.8 3.1 %collective-permute-start.11 = (bf16[256,1024]{1,0:T(8,128)(2,1)}, bf16[256,1024]{1,0:T(8,128)(2,1)S(1)}, u32[]{:S(2)}, u32[]{:S(2)}) collective-permute-start(bf16[256,1024]{1,0:T(8,128)(2,1)} %copy-done.14), channel_id=1, source_target_pairs={{0,4},{1,5},{2,6},{3,7},{4,0},{5,1},{6,2},{7,3},{8,12},{9,13},{10,... | collective-permute-start | bytes 1572872 | tf_op jit(solution)/shard_map/ppermute | solution.py:739
  38.9 6.1 %own_features.1 = (bf16[1024,1024]{1,0:T(8,128)(2,1)S(1)}, bf16[1024,1024]{1,0:T(8,128)(2,1)S(1)}, bf16[1024,1024]{1,0:T(8,128)(2,1)S(1)}, f32[1024,256]{1,0:T(8...) custom-call(s32[3]{0:T(128)S(1)} %pad_add_fusion.table, s32[2048]{0:T(1024)S(1)} %bitcast.77, ...), custom_call_target="tpu_custom_call" | custom-call | flops 1000 | bytes 1000 | tf_op jit(solution)/shard_map/own_features/pallas_call | solution.py:759
  45.1 2.6 %up.4 = (bf16[1024,512]{1,0:T(8,128)(2,1)S(1)}, bf16[1024,512]{1,0:T(8,128)(2,1)S(1)}) custom-call(bf16[1024,1024]{1,0:T(8,128)(2,1)S(1)} %get-tuple-element.192.norm_ref.norm_two, bf16[512,1024]{1,0:T(8,128)(2,1)S(1)} %get-tuple-element.143.weight.own_up, f32[1,512]{1,0:T(1,128)S(1)} %get-tuple-element.157.bias), custom_call_target="tpu_custom_call" | custom-call | flops 1000 | bytes 1000 | tf_op jit(solution)/shard_map/up/pallas_call | solution.py:759
  48.4 4.7 %far_features.1 = (f32[1024,256]{1,0:T(8,128)S(1)}, bf16[1024,128]{1,0:T(8,128)(2,1)S(1)}, f32[2,128,128]{2,1,0:T(8,128)S(1)}) custom-call(s32[3]{0:T(128)S(1)} %pad_add_fusion.table, s32[2048]{0:T(1024)S(1)} %bitcast.78, bf16[1024,1024]{1,0:T(8,128)(2,1)S(1)} %get-tuple-element.218.norm_one, bf16[1024,384]{1,0:T(8,128)(2,1)S(1)} %get-tuple-element.161.weight.far_qkv, ...), custom_call_target="tpu_custom_call" | custom-call | flops 1000 | bytes 1000 | tf_op jit(solution)/shard_map/far_features/pallas_call | solution.py:759
  53.2 2.1 %collective-permute-start.7 = (f32[2,128,128]{2,1,0:T(8,128)S(1)}, f32[2,128,128]{2,1,0:T(8,128)S(1)}, u32[]{:S(2)}, u32[]{:S(2)}) collective-permute-start(f32[2,128,128]{2,1,0:T(8,128)S(1)} %get-tuple-element.165), channel_id=1, source_target_pairs={{0,4},{1,5},{2,6},{3,7},{8,12},{9,13},{10,14},{11,15},{16,20},{17,... | collective-permute-start | bytes 393224 | tf_op jit(solution)/shard_map/ppermute | solution.py:747
  55.3 1.6 collective-permute-start.9
  56.9 4.4 %collective-permute-done.8.refs_2_ = bf16[256,1024]{1,0:T(8,128)(2,1)S(1)} collective-permute-done((bf16[256,1024]{1,0:T(8,128)(2,1)}, bf16[256,1024]{1,0:T(8,128)(2,1)S(1)}, u32[]{:S(2)}, u32[]{:S(2)}) %collective-permute-start.8) | collective-permute-done | bytes 524320 | tf_op jit(solution)/shard_map/ppermute | solution.py:739
  62.2 1.5 collective-permute-start.10
  63.7 3.4 %attend.1 = (f32[1024,256]{1,0:T(8,128)S(1)}, bf16[1024,256]{1,0:T(8,128)(2,1)S(1)}, f32[1024,256]{1,0:T(8,128)S(1)}, f32[4,2,128,256]{3,2,1,0:T(8,128)S(1)}) custom-call(s32[3]{0:T(128)S(1)} %pad_add_fusion.table, s32[2048]{0:T(1024)S(1)} %bitcast.79, f32[1024,256]{1,0:T(8,128)S(1)} %get-tuple-element.167.own_feat, ...), custom_call_target="tpu_custom_call" | custom-call | flops 1000 | bytes 1000 | tf_op jit(solution)/shard_map/attend/pallas_call | solution.py:759
  67.7 2.5 %collective-permute-done.9.refs_1_ = bf16[256,1024]{1,0:T(8,128)(2,1)S(1)} collective-permute-done((bf16[256,1024]{1,0:T(8,128)(2,1)S(1)}, bf16[256,1024]{1,0:T(8,128)(2,1)S(1)}, u32[]{:S(2)}, u32[]{:S(2)}) %collective-permute-start.9) | collective-permute-done | bytes 524320 | tf_op jit(solution)/shard_map/ppermute | solution.py:739
  70.2 10.3 %collective-permute-done.10.refs_3_ = bf16[256,1024]{1,0:T(8,128)(2,1)S(1)} collective-permute-done((bf16[256,1024]{1,0:T(8,128)(2,1)S(1)}, bf16[256,1024]{1,0:T(8,128)(2,1)S(1)}, u32[]{:S(2)}, u32[]{:S(2)}) %collective-permute-start.10) | collective-permute-done | bytes 524320 | tf_op jit(solution)/shard_map/ppermute | solution.py:739
  80.7 5.4 %later.1 = (f32[1024,256]{1,0:T(8,128)S(1)}, f32[2,128,128]{2,1,0:T(8,128)S(1)}) custom-call(s32[3]{0:T(128)S(1)} %pad_add_fusion.table, s32[2048]{0:T(1024)S(1)} %bitcast.81, bf16[1024,1024]{1,0:T(8,128)(2,1)S(1)} %get-tuple-element.177.grad_ref.grad, bf16[128,1024]{1,0:T(8,128)(2,1)S(1)} %copy-done.6, bf16[128,1024]{1,0:T(8,128)(2,1)S(1)} %get-tuple-element.178.far_dense, ...), custom_call_target="tpu_custom_call" | custom-call | flops 1000 | bytes 1000 | tf_op jit(solution)/shard_map/later/pallas_call | solution.py:759
  86.2 2.1 down_back.2
  88.4 3.2 %hidden_weights.2 = (bf16[2,304,1024]{2,1,0:T(8,128)(2,1)S(1)}, bf16[2,304,1024]{2,1,0:T(8,128)(2,1)S(1)}) custom-call(s32[3]{0:T(128)S(1)} %pad_add_fusion.table, bf16[1024,512]{1,0:T(8,128)(2,1)S(1)} %get-tuple-element.158.active.own_active, bf16[1024,512]{1,0:T(8,128)(2,1)S(1)} %get-tuple-element.186.hidden_grad.own_hg, ...), custom_call_target="tpu_custom_call" | custom-call | flops 1000 | bytes 1000 | tf_op jit(solution)/shard_map/hidden_weights/pallas_call | solution.py:759
  92.2 1.5 collective-permute-start.16
  93.9 2.6 %up.5 = (bf16[1024,512]{1,0:T(8,128)(2,1)S(1)}, bf16[1024,512]{1,0:T(8,128)(2,1)S(1)}) custom-call(bf16[1024,1024]{1,0:T(8,128)(2,1)S(1)} %get-tuple-element.192.norm_ref.norm_two, bf16[512,1024]{1,0:T(8,128)(2,1)S(1)} %get-tuple-element.191.weight.far_up, f32[1,512]{1,0:T(1,128)S(1)} %get-tuple-element.193.bias), custom_call_target="tpu_custom_call" | custom-call | flops 1000 | bytes 1000 | tf_op jit(solution)/shard_map/up/pallas_call | solution.py:759
  96.5 2.1 %down_back.3 = (bf16[1024,512]{1,0:T(8,128)(2,1)S(1)}, f32[8,512]{1,0:T(8,128)S(1)}) custom-call(bf16[1024,1024]{1,0:T(8,128)(2,1)S(1)} %get-tuple-element.177.grad_ref.grad, bf16[512,1024]{1,0:T(8,128)(2,1)S(1)} %get-tuple-element.195.weight.far_down, bf16[1024,512]{1,0:T(8,128)(2,1)S(1)} %get-tuple-element.197.slope), custom_call_target="tpu_custom_call" | custom-call | flops 1000 | bytes 1000 | tf_op jit(solution)/shard_map/down_back/pallas_call | solution.py:759
  98.6 3.2 %hidden_weights.3 = (bf16[2,304,1024]{2,1,0:T(8,128)(2,1)S(1)}, bf16[2,304,1024]{2,1,0:T(8,128)(2,1)S(1)}) custom-call(s32[3]{0:T(128)S(1)} %pad_add_fusion.table, bf16[1024,512]{1,0:T(8,128)(2,1)S(1)} %get-tuple-element.194.active.far_active, bf16[1024,512]{1,0:T(8,128)(2,1)S(1)} %get-tuple-element.199.hidden_grad.far_hg, ...), custom_call_target="tpu_custom_call" | custom-call | flops 1000 | bytes 1000 | tf_op jit(solution)/shard_map/hidden_weights/pallas_call | solution.py:759
  101.9 1.3 collective-permute-done.16.first_later
  103.6 4.2 %out.1 = (bf16[2,256,1024]{2,1,0:T(8,128)(2,1)S(1)}, bf16[2,256,1024]{2,1,0:T(8,128)(2,1)S(1)}) custom-call(bf16[1024,256]{1,0:T(8,128)(2,1)S(1)} %get-tuple-element.206.merged, bf16[1024,512]{1,0:T(8,128)(2,1)S(1)} %get-tuple-element.158.active.own_active, bf16[1024,512]{1,0:T(8,128)(2,1)S(1)} %get-tuple-element.194.active.far_active, ...), custom_call_target="tpu_custom_call" | custom-call | flops 1000 | bytes 1000 | tf_op jit(solution)/shard_map/out/pallas_call | solution.py:759
  108.0 1.6 collective-permute-start.19
  110.1 8.7 %attend_back.1 = (bf16[1024,384]{1,0:T(8,128)(2,1)S(1)}, bf16[1024,384]{1,0:T(8,128)(2,1)S(1)}) custom-call(s32[3]{0:T(128)S(1)} %pad_add_fusion.table, s32[2048]{0:T(1024)S(1)} %bitcast.82, f32[1024,256]{1,0:T(8,128)S(1)} %get-tuple-element.167.own_feat, f32[1024,256]{1,0:T(8,128)S(1)} %get-tuple-element.164.far_feat, ...), custom_call_target="tpu_custom_call" | custom-call | flops 1000 | bytes 1000 | tf_op jit(solution)/shard_map/attend_back/pallas_call | solution.py:759
  118.8 3.0 %qkv_weights.1 = (bf16[4,272,384]{2,1,0:T(8,128)(2,1)S(1)}, bf16[4,272,384]{2,1,0:T(8,128)(2,1)S(1)}) custom-call(s32[3]{0:T(128)S(1)} %pad_add_fusion.table, bf16[1024,384]{1,0:T(8,128)(2,1)S(1)} %get-tuple-element.215.own_pg, bf16[1024,384]{1,0:T(8,128)(2,1)S(1)} %get-tuple-element.216.far_pg, bf16[1024,1024]{1,0:T(8,128)(2,1)S(1)} %get-tuple-element.218.norm_one), custom_call_target="tpu_custom_call" | custom-call | flops 1000 | bytes 1000 | tf_op jit(solution)/shard_map/qkv_weights/pallas_call | solution.py:796
  121.8 4.0 %collective-permute-done.18 = bf16[304,1024]{1,0:T(8,128)(2,1)S(1)} collective-permute-done((bf16[304,1024]{1,0:T(8,128)(2,1)S(1)}, bf16[304,1024]{1,0:T(8,128)(2,1)S(1)}, u32[]{:S(2)}, u32[]{:S(2)}) %collective-permute-start.18) | collective-permute-done | bytes 622624 | tf_op jit(solution)/shard_map/ppermute | solution.py:739
  126.1 6.1 %norm_grad.1 = (f32[8,1024]{1,0:T(8,128)S(1)}, bf16[2,256,1024]{2,1,0:T(8,128)(2,1)S(1)}, bf16[2,256,1024]{2,1,0:T(8,128)(2,1)S(1)}) custom-call(bf16[1024,384]{1,0:T(8,128)(2,1)S(1)} %get-tuple-element.215.own_pg, bf16[1024,384]{1,0:T(8,128)(2,1)S(1)} %get-tuple-element.216.far_pg, bf16[1024,512]{1,0:T(8,128)(2,1)S(1)} %get-tuple-element.186.hidden_grad.own_hg, ...), custom_call_target="tpu_custom_call" | custom-call | flops 1000 | bytes 1000 | tf_op jit(solution)/shard_map/norm_grad/pallas_call | solution.py:759
  132.2 1.5 collective-permute-done.19
  134.8 1.8 collective-permute-done.20
  137.3 2.3 %collective-permute-start.23 = (bf16[304,1024]{1,0:T(8,128)(2,1)S(1)}, bf16[304,1024]{1,0:T(8,128)(2,1)S(1)}, u32[]{:S(2)}, u32[]{:S(2)}) collective-permute-start(bf16[304,1024]{1,0:T(8,128)(2,1)S(1)} %fusion.3), channel_id=1, source_target_pairs={{0,4},{1,5},{2,6},{3,7},{4,0},{5,1},{6,2},{7,3},{8,12},{9,13},{10,... | collective-permute-start | bytes 1867784 | tf_op jit(solution)/shard_map/ppermute | solution.py:739
  139.6 1.5 collective-permute-start.24
  141.1 1.6 collective-permute-start.25
  142.7 15.7 %collective-permute-done.21 = bf16[1,256,1024]{2,1,0:T(8,128)(2,1)S(1)} collective-permute-done((bf16[1,256,1024]{2,1,0:T(8,128)(2,1)S(1)}, bf16[1,256,1024]{2,1,0:T(8,128)(2,1)S(1)}, u32[]{:S(2)}, u32[]{:S(2)}) %collective-permute-start.21) | collective-permute-done | bytes 524320 | tf_op jit(solution)/shard_map/ppermute | solution.py:739
  159.6 7.8 %collective-permute-done.23 = bf16[304,1024]{1,0:T(8,128)(2,1)S(1)} collective-permute-done((bf16[304,1024]{1,0:T(8,128)(2,1)S(1)}, bf16[304,1024]{1,0:T(8,128)(2,1)S(1)}, u32[]{:S(2)}, u32[]{:S(2)}) %collective-permute-start.23) | collective-permute-done | bytes 622624 | tf_op jit(solution)/shard_map/ppermute | solution.py:739
  168.1 1.6 collective-permute-start.30
  170.8 3.4 %collective-permute-start.26 = (bf16[272,384]{1,0:T(8,128)(2,1)S(1)}, bf16[272,384]{1,0:T(8,128)(2,1)S(1)}, u32[]{:S(2)}, u32[]{:S(2)}) collective-permute-start(bf16[272,384]{1,0:T(8,128)(2,1)S(1)} %fusion.7), channel_id=1, source_target_pairs={{0,4},{1,5},{2,6},{3,7},{4,0},{5,1},{6,2},{7,3},{8,12},{9,13},{10,... | collective-permute-start | bytes 626696 | tf_op jit(solution)/shard_map/ppermute | solution.py:739
  175.4 11.4 %collective-permute-done.26 = bf16[272,384]{1,0:T(8,128)(2,1)S(1)} collective-permute-done((bf16[272,384]{1,0:T(8,128)(2,1)S(1)}, bf16[272,384]{1,0:T(8,128)(2,1)S(1)}, u32[]{:S(2)}, u32[]{:S(2)}) %collective-permute-start.26) | collective-permute-done | bytes 208928 | tf_op jit(solution)/shard_map/ppermute | solution.py:739
  188.7 1.7 finish_in.1
  191.6 1.5 collective-permute-start.35
  193.1 3.5 %finish_hidden.1 = (f32[1024,512]{1,0:T(8,128)}, f32[512,1024]{1,0:T(8,128)}, f32[128,1024]{1,0:T(8,128)}, f32[4,1,128]{2,1,0:T(1,128)}) custom-call(s32[3]{0:T(128)S(1)} %pad_add_fusion.table, bf16[304,1024]{1,0:T(8,128)(2,1)S(1)} %add_convert_fusion.2.mine, bf16[304,1024]{1,0:T(8,128)(2,1)S(1)} %collective-permute-done.27.near, ...), custom_call_target="tpu_custom_call" | custom-call | flops 1000 | bytes 1000 | tf_op jit(solution)/shard_map/finish_hidden/pallas_call | solution.py:796
  196.7 1.8 collective-permute-done.33.third
  198.5 4.2 %collective-permute-start.37 = (f32[8,1024]{1,0:T(8,128)S(1)}, f32[8,1024]{1,0:T(8,128)S(1)}, u32[]{:S(2)}, u32[]{:S(2)}) collective-permute-start(f32[8,1024]{1,0:T(8,128)S(1)} %add.90), channel_id=1, source_target_pairs={{0,2},{1,3},{2,0},{3,1},{4,6},{5,7},{6,4},{7,5},{8,10},{9,11},{10,... | collective-permute-start | bytes 98312 | tf_op jit(solution)/shard_map/ppermute | solution.py:739
  202.7 2.0 collective-permute-done.37
  205.9 1.8 finish_qkv.1
  (131 shorter events, 27.4 us)
Async XLA Ops:
  0.6 9.4 %copy-start.15 = (bf16[512]{0:T(512)(128)(2,1)S(1)}, bf16[512]{0:T(512)(128)(2,1)}, u32[]{:S(2)}) copy-start(bf16[512]{0:T(512)(128)(2,1)} %param.21) | copy-start | bytes 3076
  0.7 17.2 %collective-permute-start.1 = (bf16[256,1024]{1,0:T(8,128)(2,1)}, bf16[256,1024]{1,0:T(8,128)(2,1)}, u32[]{:S(2)}, u32[]{:S(2)}) collective-permute-start(bf16[256,1024]{1,0:T(8,128)(2,1)} %x_ref.3), channel_id=1, source_target_pairs={{0,2},{1,3},{2,0},{3,1},{4,6},{5,7},{6,4},{7,5},{8,10},{9,11},{10,... | collective-permute-start | bytes 1572872 | tf_op jit(solution)/shard_map/ppermute | solution.py:739
  3.7 30.5 %collective-permute-start = (bf16[256,1024]{1,0:T(8,128)(2,1)}, bf16[256,1024]{1,0:T(8,128)(2,1)}, u32[]{:S(2)}, u32[]{:S(2)}) collective-permute-start(bf16[256,1024]{1,0:T(8,128)(2,1)} %x_ref.3), channel_id=1, source_target_pairs={{0,1},{1,0},{2,3},{3,2},{4,5},{5,4},{6,7},{7,6},{8,9},{9,8},{10,11... | collective-permute-start | bytes 1572872 | tf_op jit(solution)/shard_map/ppermute | solution.py:739
  11.3 3.3 %copy-start.19 = (bf16[1024]{0:T(1024)(128)(2,1)S(1)}, bf16[1024]{0:T(1024)(128)(2,1)}, u32[]{:S(2)}) copy-start(bf16[1024]{0:T(1024)(128)(2,1)} %param.27) | copy-start | bytes 6148
  11.3 3.3 %copy-start.12 = (f32[64,64]{1,0:T(8,128)S(1)}, f32[64,64]{1,0:T(8,128)}, u32[]{:S(2)}) copy-start(f32[64,64]{1,0:T(8,128)} %omega) | copy-start | bytes 49156
  11.3 3.3 %copy-start.13 = (f32[1,128]{1,0:T(1,128)S(1)}, f32[1,128]{1,0:T(1,128)}, u32[]{:S(2)}) copy-start(f32[1,128]{1,0:T(1,128)} %constant.45.clone.rates) | copy-start | bytes 1540
  14.2 24.7 %copy-start.1 = (bf16[1024,384]{1,0:T(8,128)(2,1)S(1)}, bf16[1024,384]{1,0:T(8,128)(2,1)}, u32[]{:S(2)}) copy-start(bf16[1024,384]{1,0:T(8,128)(2,1)} %own_qkv.1) | copy-start | bytes 2359300
  14.2 24.7 %copy-start.2 = (bf16[256,1024]{1,0:T(8,128)(2,1)S(1)}, bf16[256,1024]{1,0:T(8,128)(2,1)}, u32[]{:S(2)}) copy-start(bf16[256,1024]{1,0:T(8,128)(2,1)} %x_ref.3) | copy-start | bytes 1572868
  17.9 16.3 %collective-permute-start.2 = (bf16[256,1024]{1,0:T(8,128)(2,1)}, bf16[256,1024]{1,0:T(8,128)(2,1)S(1)}, u32[]{:S(2)}, u32[]{:S(2)}) collective-permute-start(bf16[256,1024]{1,0:T(8,128)(2,1)} %collective-permute-done.1.refs_2_), channel_id=1, source_target_pairs={{0,1},{1,0},{2,3},{3,2},{4,5},{5,4},{6,7},{7,6},{8,9},{9,8},{10,11... | collective-permute-start | bytes 1572872 | tf_op jit(solution)/shard_map/ppermute | solution.py:739
  18.5 15.7 %collective-permute-start.3 = (bf16[400,384]{1,0:T(8,128)(2,1)}, bf16[400,384]{1,0:T(8,128)(2,1)S(1)}, u32[]{:S(2)}, u32[]{:S(2)}) collective-permute-start(bf16[400,384]{1,0:T(8,128)(2,1)} %copy-done.11), channel_id=1, source_target_pairs={{0,4},{1,5},{2,6},{3,7},{4,0},{5,1},{6,2},{7,3},{8,12},{9,13},{10,... | collective-permute-start | bytes 921608 | tf_op jit(solution)/shard_map/ppermute | solution.py:739
  34.2 10.8 %collective-permute-start.4 = (bf16[400,384]{1,0:T(8,128)(2,1)S(1)}, bf16[400,384]{1,0:T(8,128)(2,1)S(1)}, u32[]{:S(2)}, u32[]{:S(2)}) collective-permute-start(bf16[400,384]{1,0:T(8,128)(2,1)S(1)} %collective-permute-done.3.mine.bias), channel_id=1, source_target_pairs={{0,16},{1,17},{2,18},{3,19},{4,20},{5,21},{6,22},{7,23},{8,24},{9,... | collective-permute-start | bytes 921608 | tf_op jit(solution)/shard_map/ppermute | solution.py:739
  35.8 9.3 %collective-permute-start.5 = (bf16[400,384]{1,0:T(8,128)(2,1)S(1)}, bf16[400,384]{1,0:T(8,128)(2,1)S(1)}, u32[]{:S(2)}, u32[]{:S(2)}) collective-permute-start(bf16[400,384]{1,0:T(8,128)(2,1)S(1)} %collective-permute-done.3.mine.bias), channel_id=1, source_target_pairs={{0,8},{1,9},{2,10},{3,11},{4,12},{5,13},{6,14},{7,15},{8,0},{9,1},... | collective-permute-start | bytes 921608 | tf_op jit(solution)/shard_map/ppermute | solution.py:739
  35.8 25.6 %collective-permute-start.8 = (bf16[256,1024]{1,0:T(8,128)(2,1)}, bf16[256,1024]{1,0:T(8,128)(2,1)S(1)}, u32[]{:S(2)}, u32[]{:S(2)}) collective-permute-start(bf16[256,1024]{1,0:T(8,128)(2,1)} %grad_ref.1), channel_id=1, source_target_pairs={{0,2},{1,3},{2,0},{3,1},{4,6},{5,7},{6,4},{7,5},{8,10},{9,11},{10,... | collective-permute-start | bytes 1572872 | tf_op jit(solution)/shard_map/ppermute | solution.py:739
  35.8 31.4 %collective-permute-start.11 = (bf16[256,1024]{1,0:T(8,128)(2,1)}, bf16[256,1024]{1,0:T(8,128)(2,1)S(1)}, u32[]{:S(2)}, u32[]{:S(2)}) collective-permute-start(bf16[256,1024]{1,0:T(8,128)(2,1)} %copy-done.14), channel_id=1, source_target_pairs={{0,4},{1,5},{2,6},{3,7},{4,0},{5,1},{6,2},{7,3},{8,12},{9,13},{10,... | collective-permute-start | bytes 1572872 | tf_op jit(solution)/shard_map/ppermute | solution.py:739
  45.1 2.7 %collective-permute-start.6 = (bf16[400,384]{1,0:T(8,128)(2,1)S(1)}, bf16[400,384]{1,0:T(8,128)(2,1)S(1)}, u32[]{:S(2)}, u32[]{:S(2)}) collective-permute-start(bf16[400,384]{1,0:T(8,128)(2,1)S(1)} %collective-permute-done.4.third), channel_id=1, source_target_pairs={{0,8},{1,9},{2,10},{3,11},{4,12},{5,13},{6,14},{7,15},{8,0},{9,1},... | collective-permute-start | bytes 921608 | tf_op jit(solution)/shard_map/ppermute | solution.py:739
  48.4 6.9 %copy-start.7 = (bf16[256,1024]{1,0:T(8,128)(2,1)S(1)}, bf16[256,1024]{1,0:T(8,128)(2,1)}, u32[]{:S(2)}) copy-start(bf16[256,1024]{1,0:T(8,128)(2,1)} %grad_ref.1) | copy-start | bytes 1572868
  53.2 9.0 %collective-permute-start.7 = (f32[2,128,128]{2,1,0:T(8,128)S(1)}, f32[2,128,128]{2,1,0:T(8,128)S(1)}, u32[]{:S(2)}, u32[]{:S(2)}) collective-permute-start(f32[2,128,128]{2,1,0:T(8,128)S(1)} %get-tuple-element.165), channel_id=1, source_target_pairs={{0,4},{1,5},{2,6},{3,7},{8,12},{9,13},{10,14},{11,15},{16,20},{17,... | collective-permute-start | bytes 393224 | tf_op jit(solution)/shard_map/ppermute | solution.py:747
  55.3 14.9 %collective-permute-start.9 = (bf16[256,1024]{1,0:T(8,128)(2,1)S(1)}, bf16[256,1024]{1,0:T(8,128)(2,1)S(1)}, u32[]{:S(2)}, u32[]{:S(2)}) collective-permute-start(bf16[256,1024]{1,0:T(8,128)(2,1)S(1)} %copy-done.7), channel_id=1, source_target_pairs={{0,1},{1,0},{2,3},{3,2},{4,5},{5,4},{6,7},{7,6},{8,9},{9,8},{10,11... | collective-permute-start | bytes 1572872 | tf_op jit(solution)/shard_map/ppermute | solution.py:739
  62.2 18.3 %collective-permute-start.10 = (bf16[256,1024]{1,0:T(8,128)(2,1)S(1)}, bf16[256,1024]{1,0:T(8,128)(2,1)S(1)}, u32[]{:S(2)}, u32[]{:S(2)}) collective-permute-start(bf16[256,1024]{1,0:T(8,128)(2,1)S(1)} %collective-permute-done.8.refs_2_), channel_id=1, source_target_pairs={{0,1},{1,0},{2,3},{3,2},{4,5},{5,4},{6,7},{7,6},{8,9},{9,8},{10,11... | collective-permute-start | bytes 1572872 | tf_op jit(solution)/shard_map/ppermute | solution.py:739
  67.1 13.6 %copy-start.6 = (bf16[128,1024]{1,0:T(8,128)(2,1)S(1)}, bf16[128,1024]{1,0:T(8,128)(2,1)}, u32[]{:S(2)}) copy-start(bf16[128,1024]{1,0:T(8,128)(2,1)} %own_dense.3) | copy-start | bytes 786436
  67.1 19.0 %collective-permute-start.12 = (bf16[256,1024]{1,0:T(8,128)(2,1)S(1)}, bf16[256,1024]{1,0:T(8,128)(2,1)S(1)}, u32[]{:S(2)}, u32[]{:S(2)}) collective-permute-start(bf16[256,1024]{1,0:T(8,128)(2,1)S(1)} %collective-permute-done.11.mine), channel_id=1, source_target_pairs={{0,16},{1,17},{2,18},{3,19},{4,20},{5,21},{6,22},{7,23},{8,24},{9,... | collective-permute-start | bytes 1572872 | tf_op jit(solution)/shard_map/ppermute | solution.py:739
  67.7 23.9 %collective-permute-start.14 = (bf16[256,1024]{1,0:T(8,128)(2,1)S(1)}, bf16[256,1024]{1,0:T(8,128)(2,1)S(1)}, u32[]{:S(2)}, u32[]{:S(2)}) collective-permute-start(bf16[256,1024]{1,0:T(8,128)(2,1)S(1)} %collective-permute-done.11.mine), channel_id=1, source_target_pairs={{0,8},{1,9},{2,10},{3,11},{4,12},{5,13},{6,14},{7,15},{8,0},{9,1},... | collective-permute-start | bytes 1572872 | tf_op jit(solution)/shard_map/ppermute | solution.py:739
  80.7 5.5 %copy-start.4 = (bf16[512,1024]{1,0:T(8,128)(2,1)S(1)}, bf16[512,1024]{1,0:T(8,128)(2,1)}, u32[]{:S(2)}) copy-start(bf16[512,1024]{1,0:T(8,128)(2,1)} %copy-done.3) | copy-start | bytes 3145732
  86.2 5.5 %collective-permute-start.13 = (bf16[256,1024]{1,0:T(8,128)(2,1)S(1)}, bf16[256,1024]{1,0:T(8,128)(2,1)S(1)}, u32[]{:S(2)}, u32[]{:S(2)}) collective-permute-start(bf16[256,1024]{1,0:T(8,128)(2,1)S(1)} %collective-permute-done.12.third), channel_id=1, source_target_pairs={{0,8},{1,9},{2,10},{3,11},{4,12},{5,13},{6,14},{7,15},{8,0},{9,1},... | collective-permute-start | bytes 1572872 | tf_op jit(solution)/shard_map/ppermute | solution.py:739
  91.6 11.6 %collective-permute-start.15 = (bf16[2,304,1024]{2,1,0:T(8,128)(2,1)S(1)}, bf16[2,304,1024]{2,1,0:T(8,128)(2,1)S(1)}, u32[]{:S(2)}, u32[]{:S(2)}) collective-permute-start(bf16[2,304,1024]{2,1,0:T(8,128)(2,1)S(1)} %get-tuple-element.203), channel_id=1, source_target_pairs={{0,8},{1,9},{2,10},{3,11},{4,12},{5,13},{6,14},{7,15},{8,0},{9,1},... | collective-permute-start | bytes 3735560 | tf_op jit(solution)/shard_map/ppermute | solution.py:739
  92.2 11.0 %collective-permute-start.16 = (f32[2,128,128]{2,1,0:T(8,128)S(1)}, f32[2,128,128]{2,1,0:T(8,128)S(1)}, u32[]{:S(2)}, u32[]{:S(2)}) collective-permute-start(f32[2,128,128]{2,1,0:T(8,128)S(1)} %get-tuple-element.204), channel_id=1, source_target_pairs={{4,0},{5,1},{6,2},{7,3},{12,8},{13,9},{14,10},{15,11},{20,16},{21,... | collective-permute-start | bytes 393224 | tf_op jit(solution)/shard_map/ppermute | solution.py:747
  103.4 4.4 %collective-permute-start.17 = (bf16[2,304,1024]{2,1,0:T(8,128)(2,1)S(1)}, bf16[2,304,1024]{2,1,0:T(8,128)(2,1)S(1)}, u32[]{:S(2)}, u32[]{:S(2)}) collective-permute-start(bf16[2,304,1024]{2,1,0:T(8,128)(2,1)S(1)} %get-tuple-element.209), channel_id=1, source_target_pairs={{0,8},{1,9},{2,10},{3,11},{4,12},{5,13},{6,14},{7,15},{8,0},{9,1},... | collective-permute-start | bytes 3735560 | tf_op jit(solution)/shard_map/ppermute | solution.py:739
  108.0 25.6 %collective-permute-start.19 = (bf16[2,256,1024]{2,1,0:T(8,128)(2,1)S(1)}, bf16[2,256,1024]{2,1,0:T(8,128)(2,1)S(1)}, u32[]{:S(2)}, u32[]{:S(2)}) collective-permute-start(bf16[2,256,1024]{2,1,0:T(8,128)(2,1)S(1)} %get-tuple-element.226), channel_id=1, source_target_pairs={{0,1},{1,0},{2,3},{3,2},{4,5},{5,4},{6,7},{7,6},{8,9},{9,8},{10,11... | collective-permute-start | bytes 3145736 | tf_op jit(solution)/shard_map/ppermute | solution.py:739
  109.6 16.1 %collective-permute-start.18 = (bf16[304,1024]{1,0:T(8,128)(2,1)S(1)}, bf16[304,1024]{1,0:T(8,128)(2,1)S(1)}, u32[]{:S(2)}, u32[]{:S(2)}) collective-permute-start(bf16[304,1024]{1,0:T(8,128)(2,1)S(1)} %fusion.4), channel_id=1, source_target_pairs={{0,16},{1,17},{2,18},{3,19},{4,20},{5,21},{6,22},{7,23},{8,24},{9,... | collective-permute-start | bytes 1867784 | tf_op jit(solution)/shard_map/ppermute | solution.py:739
  134.2 2.4 %collective-permute-start.20 = (bf16[4,272,384]{2,1,0:T(8,128)(2,1)S(1)}, bf16[4,272,384]{2,1,0:T(8,128)(2,1)S(1)}, u32[]{:S(2)}, u32[]{:S(2)}) collective-permute-start(bf16[4,272,384]{2,1,0:T(8,128)(2,1)S(1)} %get-tuple-element.229), channel_id=1, source_target_pairs={{0,8},{1,9},{2,10},{3,11},{4,12},{5,13},{6,14},{7,15},{8,0},{9,1},... | collective-permute-start | bytes 2506760 | tf_op jit(solution)/shard_map/ppermute | solution.py:739
  134.3 24.1 %collective-permute-start.21 = (bf16[1,256,1024]{2,1,0:T(8,128)(2,1)S(1)}, bf16[1,256,1024]{2,1,0:T(8,128)(2,1)S(1)}, u32[]{:S(2)}, u32[]{:S(2)}) collective-permute-start(bf16[1,256,1024]{2,1,0:T(8,128)(2,1)S(1)} %get-tuple-element.231), channel_id=1, source_target_pairs={{0,2},{1,3},{2,0},{3,1},{4,6},{5,7},{6,4},{7,5},{8,10},{9,11},{10,... | collective-permute-start | bytes 1572872 | tf_op jit(solution)/shard_map/ppermute | solution.py:739
  136.7 22.8 %collective-permute-start.22 = (bf16[2,272,384]{2,1,0:T(8,128)(2,1)S(1)}, bf16[2,272,384]{2,1,0:T(8,128)(2,1)S(1)}, u32[]{:S(2)}, u32[]{:S(2)}) collective-permute-start(bf16[2,272,384]{2,1,0:T(8,128)(2,1)S(1)} %add_convert_fusion.3), channel_id=1, source_target_pairs={{0,16},{1,17},{2,18},{3,19},{4,20},{5,21},{6,22},{7,23},{8,24},{9,... | collective-permute-start | bytes 1253384 | tf_op jit(solution)/shard_map/ppermute | solution.py:739
  137.3 30.1 %collective-permute-start.23 = (bf16[304,1024]{1,0:T(8,128)(2,1)S(1)}, bf16[304,1024]{1,0:T(8,128)(2,1)S(1)}, u32[]{:S(2)}, u32[]{:S(2)}) collective-permute-start(bf16[304,1024]{1,0:T(8,128)(2,1)S(1)} %fusion.3), channel_id=1, source_target_pairs={{0,4},{1,5},{2,6},{3,7},{4,0},{5,1},{6,2},{7,3},{8,12},{9,13},{10,... | collective-permute-start | bytes 1867784 | tf_op jit(solution)/shard_map/ppermute | solution.py:739
  139.6 27.9 %collective-permute-start.24 = (bf16[304,1024]{1,0:T(8,128)(2,1)S(1)}, bf16[304,1024]{1,0:T(8,128)(2,1)S(1)}, u32[]{:S(2)}, u32[]{:S(2)}) collective-permute-start(bf16[304,1024]{1,0:T(8,128)(2,1)S(1)} %fusion.5), channel_id=1, source_target_pairs={{0,16},{1,17},{2,18},{3,19},{4,20},{5,21},{6,22},{7,23},{8,24},{9,... | collective-permute-start | bytes 1867784 | tf_op jit(solution)/shard_map/ppermute | solution.py:739
  141.1 28.5 %collective-permute-start.25 = (bf16[2,256,1024]{2,1,0:T(8,128)(2,1)S(1)}, bf16[2,256,1024]{2,1,0:T(8,128)(2,1)S(1)}, u32[]{:S(2)}, u32[]{:S(2)}) collective-permute-start(bf16[2,256,1024]{2,1,0:T(8,128)(2,1)S(1)} %get-tuple-element.242), channel_id=1, source_target_pairs={{0,1},{1,0},{2,3},{3,2},{4,5},{5,4},{6,7},{7,6},{8,9},{9,8},{10,11... | collective-permute-start | bytes 3145736 | tf_op jit(solution)/shard_map/ppermute | solution.py:739
  168.0 18.8 %collective-permute-start.27 = (bf16[304,1024]{1,0:T(8,128)(2,1)S(1)}, bf16[304,1024]{1,0:T(8,128)(2,1)S(1)}, u32[]{:S(2)}, u32[]{:S(2)}) collective-permute-start(bf16[304,1024]{1,0:T(8,128)(2,1)S(1)} %add_convert_fusion.2.mine), channel_id=1, source_target_pairs={{0,8},{1,9},{2,10},{3,11},{4,12},{5,13},{6,14},{7,15},{8,0},{9,1},... | collective-permute-start | bytes 1867784 | tf_op jit(solution)/shard_map/ppermute | solution.py:739
  168.1 22.3 %collective-permute-start.30 = (bf16[304,1024]{1,0:T(8,128)(2,1)S(1)}, bf16[304,1024]{1,0:T(8,128)(2,1)S(1)}, u32[]{:S(2)}, u32[]{:S(2)}) collective-permute-start(bf16[304,1024]{1,0:T(8,128)(2,1)S(1)} %add_convert_fusion.2.mine), channel_id=1, source_target_pairs={{0,16},{1,17},{2,18},{3,19},{4,20},{5,21},{6,22},{7,23},{8,24},{9,... | collective-permute-start | bytes 1867784 | tf_op jit(solution)/shard_map/ppermute | solution.py:739
  170.1 18.5 %collective-permute-start.29 = (bf16[1,256,1024]{2,1,0:T(8,128)(2,1)S(1)}, bf16[1,256,1024]{2,1,0:T(8,128)(2,1)S(1)}, u32[]{:S(2)}, u32[]{:S(2)}) collective-permute-start(bf16[1,256,1024]{2,1,0:T(8,128)(2,1)S(1)} %get-tuple-element.249), channel_id=1, source_target_pairs={{0,2},{1,3},{2,0},{3,1},{4,6},{5,7},{6,4},{7,5},{8,10},{9,11},{10,... | collective-permute-start | bytes 1572872 | tf_op jit(solution)/shard_map/ppermute | solution.py:739
  170.8 16.0 %collective-permute-start.26 = (bf16[272,384]{1,0:T(8,128)(2,1)S(1)}, bf16[272,384]{1,0:T(8,128)(2,1)S(1)}, u32[]{:S(2)}, u32[]{:S(2)}) collective-permute-start(bf16[272,384]{1,0:T(8,128)(2,1)S(1)} %fusion.7), channel_id=1, source_target_pairs={{0,4},{1,5},{2,6},{3,7},{4,0},{5,1},{6,2},{7,3},{8,12},{9,13},{10,... | collective-permute-start | bytes 626696 | tf_op jit(solution)/shard_map/ppermute | solution.py:739
  174.2 1.2 collective-permute-start.28
  186.9 4.0 %collective-permute-start.31 = (f32[8,1024]{1,0:T(8,128)S(1)}, f32[8,1024]{1,0:T(8,128)S(1)}, u32[]{:S(2)}, u32[]{:S(2)}) collective-permute-start(f32[8,1024]{1,0:T(8,128)S(1)} %add.88), channel_id=1, source_target_pairs={{0,16},{1,17},{2,18},{3,19},{4,20},{5,21},{6,22},{7,23},{8,24},{9,... | collective-permute-start | bytes 98312 | tf_op jit(solution)/shard_map/ppermute | solution.py:739
  190.9 2.2 %collective-permute-start.32 = (bf16[304,1024]{1,0:T(8,128)(2,1)S(1)}, bf16[304,1024]{1,0:T(8,128)(2,1)S(1)}, u32[]{:S(2)}, u32[]{:S(2)}) collective-permute-start(bf16[304,1024]{1,0:T(8,128)(2,1)S(1)} %collective-permute-done.30.third), channel_id=1, source_target_pairs={{0,8},{1,9},{2,10},{3,11},{4,12},{5,13},{6,14},{7,15},{8,0},{9,1},... | collective-permute-start | bytes 1867784 | tf_op jit(solution)/shard_map/ppermute | solution.py:739
  190.9 7.6 %collective-permute-start.33 = (bf16[272,384]{1,0:T(8,128)(2,1)S(1)}, bf16[272,384]{1,0:T(8,128)(2,1)S(1)}, u32[]{:S(2)}, u32[]{:S(2)}) collective-permute-start(bf16[272,384]{1,0:T(8,128)(2,1)S(1)} %add_convert_fusion.4.mine), channel_id=1, source_target_pairs={{0,16},{1,17},{2,18},{3,19},{4,20},{5,21},{6,22},{7,23},{8,24},{9,... | collective-permute-start | bytes 626696 | tf_op jit(solution)/shard_map/ppermute | solution.py:739
  191.4 7.1 %collective-permute-start.34 = (bf16[272,384]{1,0:T(8,128)(2,1)S(1)}, bf16[272,384]{1,0:T(8,128)(2,1)S(1)}, u32[]{:S(2)}, u32[]{:S(2)}) collective-permute-start(bf16[272,384]{1,0:T(8,128)(2,1)S(1)} %add_convert_fusion.4.mine), channel_id=1, source_target_pairs={{0,8},{1,9},{2,10},{3,11},{4,12},{5,13},{6,14},{7,15},{8,0},{9,1},... | collective-permute-start | bytes 626696 | tf_op jit(solution)/shard_map/ppermute | solution.py:739
  191.6 5.1 %collective-permute-start.35 = (f32[8,1024]{1,0:T(8,128)S(1)}, f32[8,1024]{1,0:T(8,128)S(1)}, u32[]{:S(2)}, u32[]{:S(2)}) collective-permute-start(f32[8,1024]{1,0:T(8,128)S(1)} %add.89), channel_id=1, source_target_pairs={{0,1},{1,0},{2,3},{3,2},{4,5},{5,4},{6,7},{7,6},{8,9},{9,8},{10,11... | collective-permute-start | bytes 98312 | tf_op jit(solution)/shard_map/ppermute | solution.py:739
  198.5 6.2 %collective-permute-start.36 = (bf16[272,384]{1,0:T(8,128)(2,1)S(1)}, bf16[272,384]{1,0:T(8,128)(2,1)S(1)}, u32[]{:S(2)}, u32[]{:S(2)}) collective-permute-start(bf16[272,384]{1,0:T(8,128)(2,1)S(1)} %collective-permute-done.33.third), channel_id=1, source_target_pairs={{0,8},{1,9},{2,10},{3,11},{4,12},{5,13},{6,14},{7,15},{8,0},{9,1},... | collective-permute-start | bytes 626696 | tf_op jit(solution)/shard_map/ppermute | solution.py:739
  198.5 6.2 %collective-permute-start.37 = (f32[8,1024]{1,0:T(8,128)S(1)}, f32[8,1024]{1,0:T(8,128)S(1)}, u32[]{:S(2)}, u32[]{:S(2)}) collective-permute-start(f32[8,1024]{1,0:T(8,128)S(1)} %add.90), channel_id=1, source_target_pairs={{0,2},{1,3},{2,0},{3,1},{4,6},{5,7},{6,4},{7,5},{8,10},{9,11},{10,... | collective-permute-start | bytes 98312 | tf_op jit(solution)/shard_map/ppermute | solution.py:739
  204.7 4.9 %collective-permute-start.38 = (f32[8,1024]{1,0:T(8,128)S(1)}, f32[8,1024]{1,0:T(8,128)S(1)}, u32[]{:S(2)}, u32[]{:S(2)}) collective-permute-start(f32[8,1024]{1,0:T(8,128)S(1)} %add.91), channel_id=1, source_target_pairs={{0,4},{1,5},{2,6},{3,7},{4,0},{5,1},{6,2},{7,3},{8,12},{9,13},{10,... | collective-permute-start | bytes 98312 | tf_op jit(solution)/shard_map/ppermute | solution.py:739
  (12 other events, 22.9 us)
